TPU v7x, 32 devices: a whole 2x2x4 slice. The times are simulated.
32 devices in a mesh: ctx: 8 (over z, x), exp: 4 (over y, core).
Axes of the slice: x: 2, y: 2, z: 4, core: 2. Of those that a mesh axis runs over, the one named last changes fastest.
Arguments:
- residual: bfloat16 [4, 1024, 2048], P('exp', 'ctx'), may hold values from -54 to 54
- queries: bfloat16 [4, 1024, 2048], P('exp', 'ctx'), may hold values from -160 to 160
- key_states: bfloat16 [4, 1024, 256], P('exp', 'ctx'), may hold values from -6.1 to 6.1
- value_states: bfloat16 [4, 1024, 256], P('exp', 'ctx'), may hold values from -6 to 6
- expert_ids: int32 [4, 1024, 1], P('exp', 'ctx'), may hold values from 0 to 7; in each aligned block of 128 rows (0 to 127, 128 to 255, ..., all dimensions but the last counted through in order) at most 32 rows name the same one
- route_weight: float32 [4, 1024, 1], P('exp', 'ctx'), may hold values from 0.2 to 1
- gate_weight: bfloat16 [4, 8, 192, 2048], P('exp', 'ctx'), may hold values from -0.125 to 0.125
- up_weight: bfloat16 [4, 8, 192, 2048], P('exp', 'ctx'), may hold values from -0.125 to 0.125
- down_weight: bfloat16 [4, 8, 192, 2048], P('exp', 'ctx'), may hold values from -0.21875 to 0.21875
Outputs:
- output: bfloat16 [4, 1024, 2048], P('exp', 'ctx')
Inputs may be any that keep to these rules, and one draw needn't show every extreme that they name: `expert_ids`: within each aligned block of 128 rows (sequence by sequence, positions in order), which is the rows of one device, no expert is named more than 32 times, a bound that some block reaches; every expert is named somewhere.
All inputs are finite; a program needn't handle non-finite values.
Results may differ from a plain program's by a relative error of at most 0.003.
Values may be sent and summed in bfloat16 or wider, within the bound.
No kernel may reach another device: no remote copies, remote signals or barrier semaphores. Data moves between devices by JAX's collectives and lax.ppermute only.
A program may use at most 64 MiB of HBM per device.

v0:
```python
from functools import partial
import math

import jax
import jax.numpy as jnp
from jax import lax
from jax.sharding import PartitionSpec as P

HD = 128
HEADS = 16
KV_HEADS = 2
PIECES = 4
TOPK = 1


negative_fill = -1e30
epsilon = 1e-06


def contract_rows(left_rows, weight_rows):
    return lax.dot_general(
        left_rows, weight_rows, (((1,), (1,)), ((), ())), preferred_element_type=jnp.float32
    )


def to_groups(half_block, heads_kv, group_size, head_dim):
    token_count = half_block.shape[0]
    shaped = half_block.reshape(token_count, heads_kv, group_size, head_dim)
    return jnp.transpose(shaped, (1, 0, 2, 3)).reshape(heads_kv, token_count * group_size, head_dim)


def keep_current(current):
    return current


def block_update(current, query_rows, query_pos, key_block, value_block, key_start, score_scale):
    running_max, running_total, accumulated = current
    scores = (
        jnp.einsum("gqd,kgd->gqk", query_rows, key_block, preferred_element_type=jnp.float32)
        * score_scale
    )
    key_pos = key_start + jnp.arange(key_block.shape[0], dtype=jnp.int32)
    allowed = key_pos[None, None, :] <= query_pos[None, :, None]
    scores = jnp.where(allowed, scores, negative_fill)
    new_max = jnp.maximum(running_max, jnp.max(scores, axis=-1))
    rescale = jnp.exp(running_max - new_max)
    exponent = jnp.where(allowed, jnp.exp(scores - new_max[..., None]), 0.0)
    new_total = running_total * rescale + jnp.sum(exponent, axis=-1)
    product = jnp.einsum(
        "gqk,kgd->gqd",
        exponent.astype(jnp.bfloat16),
        value_block,
        preferred_element_type=jnp.float32,
    )
    return (new_max, new_total, accumulated * rescale[..., None] + product)


def make_folder(query_sets, position_sets, last_positions, heads_kv, head_dim, score_scale):

    def fold_keys(running, key_piece, first_key):
        key_part, value_part = key_piece
        key_count = key_part.shape[1]
        key_width = math.gcd(key_count, 512)
        key_rows = key_part.reshape(key_count, heads_kv, head_dim)
        value_rows = value_part.reshape(key_count, heads_kv, head_dim)

        def one_block(block_index, current_sets):
            offset = block_index * key_width
            key_block = lax.dynamic_slice_in_dim(key_rows, offset, key_width, 0)
            value_block = lax.dynamic_slice_in_dim(value_rows, offset, key_width, 0)
            updated = []
            for current, query_rows, query_pos, last_pos in zip(
                current_sets, query_sets, position_sets, last_positions
            ):
                step_fn = partial(
                    block_update,
                    query_rows=query_rows,
                    query_pos=query_pos,
                    key_block=key_block,
                    value_block=value_block,
                    key_start=offset,
                    score_scale=score_scale,
                )
                updated.append(lax.cond(offset <= last_pos, step_fn, keep_current, current))
            return tuple(updated)

        return lax.fori_loop(0, key_count // key_width, one_block, running)

    return fold_keys


def finish(current, token_count, heads_kv, group_size, head_dim):
    running_max, running_total, accumulated = current
    result = accumulated / running_total[..., None]
    shaped = result.reshape(heads_kv, token_count, group_size, head_dim)
    return (
        jnp.transpose(shaped, (1, 0, 2, 3))
        .reshape(token_count, heads_kv * group_size * head_dim)
        .astype(jnp.bfloat16)
    )


def shards(
    residual,
    queries,
    key_states,
    value_states,
    expert_ids,
    route_weight,
    gate_weight,
    up_weight,
    down_weight,
):
    ctx_count = lax.axis_size("ctx")
    exp_count = lax.axis_size("exp")
    ctx_rank = lax.axis_index("ctx")
    tok_rows = residual.shape[1]
    half_rows = tok_rows // 2
    group_size = HEADS // KV_HEADS
    score_scale = 1.0 / math.sqrt(HD)
    local_queries = queries[0]
    first_half = local_queries[:half_rows]
    second_half = local_queries[half_rows:]
    first_start = ctx_rank * tok_rows
    second_start = first_start + half_rows
    offsets = jnp.repeat(jnp.arange(half_rows, dtype=jnp.int32), group_size)
    query_sets = (
        to_groups(first_half, KV_HEADS, group_size, HD),
        to_groups(second_half, KV_HEADS, group_size, HD),
    )
    position_sets = (first_start + offsets, second_start + offsets)
    last_positions = (first_start + half_rows - 1, second_start + half_rows - 1)
    row_total = half_rows * group_size
    empty_state = (
        jnp.full((KV_HEADS, row_total), negative_fill, jnp.float32),
        jnp.zeros((KV_HEADS, row_total), jnp.float32),
        jnp.zeros((KV_HEADS, row_total, HD), jnp.float32),
    )
    folder = make_folder(query_sets, position_sets, last_positions, KV_HEADS, HD, score_scale)
    final_sets = folder(
        (empty_state, empty_state),
        (
            lax.all_gather(key_states, "ctx", axis=1, tiled=True),
            lax.all_gather(value_states, "ctx", axis=1, tiled=True),
        ),
        jnp.int32(0),
    )
    first_out = finish(final_sets[0], half_rows, KV_HEADS, group_size, HD)
    second_out = finish(final_sets[1], half_rows, KV_HEADS, group_size, HD)
    attention = jnp.concatenate([first_out, second_out], axis=0)
    summed = residual[0].astype(jnp.float32) + lax.optimization_barrier(attention).astype(
        jnp.float32
    )
    normed = (
        summed * lax.rsqrt(jnp.mean(summed * summed, axis=-1, keepdims=True) + epsilon)
    ).astype(jnp.bfloat16)
    width_model = normed.shape[1]
    experts_each = ctx_count // PIECES
    expert_total = experts_each * exp_count
    pair_count = tok_rows * TOPK
    capacity = max(2, 2 * tok_rows * TOPK // expert_total)
    flat_ids = expert_ids[0].reshape(pair_count)
    onehot = (flat_ids[:, None] == jnp.arange(expert_total, dtype=jnp.int32)[None, :]).astype(
        jnp.int32
    )
    earlier = jnp.cumsum(onehot, axis=0) - onehot
    slot_index = jnp.sum(earlier * onehot, axis=1)
    owner_index = flat_ids // experts_each
    local_expert = flat_ids % experts_each
    target = (local_expert * exp_count + owner_index) * capacity + slot_index
    pair_token = jnp.arange(pair_count, dtype=jnp.int32) // TOPK
    slot_total = expert_total * capacity
    slot_table = jnp.full((slot_total,), tok_rows, jnp.int32).at[target].set(pair_token)
    padded = jnp.concatenate([normed, jnp.zeros((1, width_model), jnp.bfloat16)], axis=0)
    outgoing = padded[slot_table].reshape(experts_each, exp_count, capacity, width_model)
    arrived = lax.all_to_all(outgoing, "exp", split_axis=1, concat_axis=1, tiled=True)
    copies = jnp.broadcast_to(
        arrived[:, None], (experts_each, PIECES, exp_count, capacity, width_model)
    ).reshape(ctx_count, exp_count * capacity, width_model)
    gate_piece = gate_weight[0, 0]
    up_piece = up_weight[0, 0]
    down_piece = down_weight[0, 0]
    received = lax.all_to_all(copies, "ctx", split_axis=0, concat_axis=0, tiled=True)
    sources = received.shape[0]
    item_count = received.shape[1]
    flat_rows = received.reshape(sources * item_count, width_model)
    gate_part = contract_rows(flat_rows, gate_piece)
    up_part = contract_rows(flat_rows, up_piece)
    active = (jax.nn.silu(gate_part) * up_part).astype(jnp.bfloat16)
    partial_out = jnp.dot(active, down_piece, preferred_element_type=jnp.float32).astype(
        jnp.bfloat16
    )
    returned = lax.all_to_all(
        partial_out.reshape(sources, item_count, width_model),
        "ctx",
        split_axis=0,
        concat_axis=0,
        tiled=True,
    )
    piece_sum = jnp.sum(
        returned.reshape(experts_each, PIECES, exp_count, capacity, width_model).astype(
            jnp.float32
        ),
        axis=1,
    ).astype(jnp.bfloat16)
    arrived_back = lax.all_to_all(piece_sum, "exp", split_axis=1, concat_axis=1, tiled=True)
    gathered = arrived_back.reshape(slot_total, width_model)[target].astype(jnp.float32)
    weighted = gathered * route_weight[0]
    mixture = jnp.sum(weighted.reshape(tok_rows, TOPK, width_model), axis=1)
    return (summed + mixture).astype(jnp.bfloat16)[None]


def solution(mesh):
    in_specs = (
        P("exp", "ctx", None),
        P("exp", "ctx", None),
        P("exp", "ctx", None),
        P("exp", "ctx", None),
        P("exp", "ctx", None),
        P("exp", "ctx", None),
        P("exp", "ctx", None, None),
        P("exp", "ctx", None, None),
        P("exp", "ctx", None, None),
    )
    out_specs = P("exp", "ctx", None)
    return jax.shard_map(shards, mesh=mesh, in_specs=in_specs, out_specs=out_specs, check_vma=False)
```

profile of v0, /device:TPU:8, one launch (start us, length us, event | category | flops | bytes accessed | tf_op | source)
XLA Modules:
  0.0 326.1 jit_solution(8292580245410848761)
XLA Ops:
  0.0 1.1 slice_bitcast_fusion
  1.4 27.0 %all_gather.6 = bf16[1,1024,256]{1,2,0:T(8,128)(2,1)S(1)} all-gather(bf16[1,128,256]{1,2,0:T(8,128)(2,1)S(1)} %copy.41), channel_id=1, replica_groups=mesh['ctx'=8,'exp'=4] {'ctx'}, dimensions={1}, use_global_device_ids=true | all-gather | bytes 589824 | tf_op jit(solution)/shard_map/all_gather | solution.py:143
  28.5 27.8 %all_gather.7 = bf16[1,1024,256]{1,2,0:T(8,128)(2,1)S(1)} all-gather(bf16[1,128,256]{1,2,0:T(8,128)(2,1)S(1)} %copy.42), channel_id=1, replica_groups=mesh['ctx'=8,'exp'=4] {'ctx'}, dimensions={1}, use_global_device_ids=true | all-gather | bytes 589824 | tf_op jit(solution)/shard_map/all_gather | solution.py:144
  56.4 0.8 broadcast_in_dim.78
  57.2 0.8 broadcast_in_dim.78.clone
  58.1 9.5 %while.24 = (s32[]{:T(128)}, f32[2,512]{1,0:T(2,128)S(1)}, f32[2,512]{1,0:T(2,128)S(1)}, f32[2,512,128]{2,1,0:T(8,128)}, f32[2,512]{1,0:T(2,128)S(1)}, /*index=5...) while((s32[]{:T(128)}, f32[2,512]{1,0:T(2,128)S(1)}, ...), condition=%wide.region_9.10_spmd.clone, body=%wide.region_0.9_spmd.clone.sunk | while | flops 551557120 | bytes 29000316 | solution.py:87
  58.5 3.4 %conditional.7 = ((f32[2,512]{1,0:T(2,128)S(1)}, f32[2,512]{1,0:T(2,128)S(1)}, f32[2,512,128]{2,1,0:T(8,128)})) conditional(s32[]{:T(128)} %convert_element_type.131, (f32[2,512]{1,0:T(2,128)S(1)}, f32[2,512]{1,0:T(2,128)S(1)}, f32[2,512,128]{2,1,0:T(8,128)}) %tuple.67, (s32[]{:T(128)}, s32[]{:T(128)}, bf16[2,512,128]{2,1,0:T(8,128)(2,1)S(1)}, ...), branch_computations={%region_5.5_spmd, %region_6.8_spmd} | conditional | flops 275778560 | bytes 13449312 | solution.py:84
  59.5 0.6 fusion.17
  60.0 1.1 convolution_add_fusion.1
  61.1 0.8 copy-done.6
  61.9 2.6 conditional.6
  62.9 0.6 fusion.6
  63.4 1.1 convolution_add_fusion
  64.6 0.8 copy-done.4
  65.8 1.0 copy-done.3
  66.8 0.8 copy-done.4
  67.6 1.3 fusion.39
  70.9 1.0 scatter_custom_fusion
  71.9 1.4 gather_fusion
  73.4 17.1 %all_to_all.20 = bf16[2,4,32,2048]{3,2,0,1:T(8,128)(2,1)S(1)} all-to-all(bf16[2,4,32,2048]{3,2,0,1:T(8,128)(2,1)S(1)} %copy.49), channel_id=1, replica_groups=mesh['ctx'=8,'exp'=4] {'exp'}, dimensions={1} | all-to-all | bytes 2097152 | tf_op jit(solution)/shard_map/all_to_all | solution.py:176
  91.1 100.2 %all_to_all.21 = bf16[8,128,2048]{2,1,0:T(8,128)(2,1)S(1)} all-to-all(bf16[8,128,2048]{2,1,0:T(8,128)(2,1)S(1)} %bitcast.91), channel_id=1, replica_groups=mesh['ctx'=8,'exp'=4] {'ctx'}, dimensions={0} | all-to-all | bytes 8388608 | tf_op jit(solution)/shard_map/all_to_all | solution.py:183
  191.3 2.0 copy-done.2
  193.2 2.5 fusion.30
  195.8 7.1 %convolution_convert_fusion = bf16[1024,2048]{1,0:T(8,128)(2,1)} fusion(bf16[1024,2048]{1,0:T(8,128)(2,1)} %bitcast.97, bf16[1,1,192,2048]{3,2,1,0:T(8,128)(2,1)S(1)} %copy-done, bf16[1,1,192,2048]{3,2,1,0:T(8,128)(2,1)S(1)} %copy-done.13, f32[1024,192]{0,1:T(8,128)} %fusion.30), kind=kOutput, calls=%fused_computation.43 | convolution fusion | flops 1613889536 | bytes 10747904 | tf_op jit(solution)/shard_map/dot_general | solution.py:190
  202.8 97.0 %all_to_all.22 = bf16[8,128,2048]{2,1,0:T(8,128)(2,1)} all-to-all(bf16[8,128,2048]{2,1,0:T(8,128)(2,1)} %bitcast.98), channel_id=1, replica_groups=mesh['ctx'=8,'exp'=4] {'ctx'}, dimensions={0} | all-to-all | bytes 8388608 | tf_op jit(solution)/shard_map/all_to_all | solution.py:193
  299.8 3.1 reduce_sum.57
  302.9 1.1 copy.51
  304.0 4.2 %all-to-all-start.3 = ((bf16[2,4,32,2048]{3,2,0,1:T(8,128)(2,1)}), bf16[2,4,32,2048]{3,2,0,1:T(8,128)(2,1)}, u32[]{:S(2)}, u32[]{:S(2)}) async-start(bf16[2,4,32,2048]{3,2,0,1:T(8,128)(2,1)} %copy.51), calls=%async_computation.3 | async-start | bytes 2097152 | tf_op jit(solution)/shard_map/all_to_all | solution.py:206
  308.2 14.5 %all-to-all-done.3 = bf16[2,4,32,2048]{3,2,0,1:T(8,128)(2,1)} async-done(((bf16[2,4,32,2048]{3,2,0,1:T(8,128)(2,1)}), bf16[2,4,32,2048]{3,2,0,1:T(8,128)(2,1)}, u32[]{:S(2)}, u32[]{:S(2)}) %all-to-all-start.3) | async-done | bytes 1048608 | tf_op jit(solution)/shard_map/all_to_all | solution.py:206
  322.7 1.3 copy.52
  324.0 0.9 gather_fusion.1
  325.0 1.1 fusion.37
  (85 shorter events, 5.6 us)
Async XLA Ops:
  0.0 195.8 %copy-start = (bf16[1,1,192,2048]{3,2,1,0:T(8,128)(2,1)S(1)}, bf16[1,1,192,2048]{3,2,1,0:T(8,128)(2,1)}, u32[]{:S(2)}) copy-start(bf16[1,1,192,2048]{3,2,1,0:T(8,128)(2,1)} %param.23) | copy-start | bytes 2359300
  0.0 1.3 copy-start.8
  0.0 28.4 %copy-start.9 = (bf16[1,128,256]{2,1,0:T(8,128)(2,1)S(1)}, bf16[1,128,256]{2,1,0:T(8,128)(2,1)}, u32[]{:S(2)}) copy-start(bf16[1,128,256]{2,1,0:T(8,128)(2,1)} %param.18) | copy-start | bytes 196612
  58.5 3.4 %copy-start.3 = (f32[2,512,128]{2,1,0:T(8,128)S(1)}, f32[2,512,128]{2,1,0:T(8,128)}, u32[]{:S(2)}) copy-start(f32[2,512,128]{2,1,0:T(8,128)} %get-tuple-element.613) | copy-start | bytes 1572868 | tf_op jit(solution)/shard_map/while
  58.9 1.2 copy-start.5
  61.1 0.8 copy-start.6
  64.5 0.8 copy-start.4
  65.7 1.0 copy-start.3
  66.8 0.8 copy-start.4
  67.6 1.5 copy-start.7
  68.9 1.0 copy-start.1
  69.3 1.1 copy-start.10
  91.1 102.2 %copy-start.12 = (bf16[1,1,192,2048]{3,2,1,0:T(8,128)(2,1)S(1)}, bf16[1,1,192,2048]{3,2,1,0:T(8,128)(2,1)}, u32[]{:S(2)}) copy-start(bf16[1,1,192,2048]{3,2,1,0:T(8,128)(2,1)} %param.21) | copy-start | bytes 2359300
  191.3 2.0 copy-start.2
  193.2 2.5 copy-start.13
  304.0 18.8 %all-to-all-start.3 = ((bf16[2,4,32,2048]{3,2,0,1:T(8,128)(2,1)}), bf16[2,4,32,2048]{3,2,0,1:T(8,128)(2,1)}, u32[]{:S(2)}, u32[]{:S(2)}) async-start(bf16[2,4,32,2048]{3,2,0,1:T(8,128)(2,1)} %copy.51), calls=%async_computation.3 | async-start | bytes 2097152 | tf_op jit(solution)/shard_map/all_to_all | solution.py:206
  324.0 1.0 copy-start.11
where the time goes:
time: 329 us; the launch traced here: 326 us
  blocking collectives  269 us (82%)
  local copies, waits for them, and re-layouts  16.7 us (5%)
  waiting for transfers between devices  14.5 us (4%)
  matrix products  12.8 us (4%)
  other arithmetic  8.21 us (2%)
  starting transfers between devices  4.23 us (1%)
    all_to_all x1, blocking collectives, shards(): lax.all_to_all(copies, 'ctx', split_axis=0, concat_axis=0, tiled=True)  100 us
    all_to_all x1, blocking collectives, shards(): lax.all_to_all(partial_out.reshape(sources, item_count, width_model), 'ct...  97 us
    all_gather x1, blocking collectives, shards(): lax.all_gather(value_states, 'ctx', axis=1, tiled=True)  27.8 us
    all_gather x1, blocking collectives, shards(): lax.all_gather(key_states, 'ctx', axis=1, tiled=True)  27 us
    all_to_all x1, blocking collectives, shards(): lax.all_to_all(outgoing, 'exp', split_axis=1, concat_axis=1, tiled=True)  17.1 us
    all_to_all x1, waiting for transfers between devices, shards(): lax.all_to_all(piece_sum, 'exp', split_axis=1, concat_axis=1, tiled=True)  14.5 us
    dot_general x1, matrix products, shards(): jnp.dot(active, down_piece, preferred_element_type=jnp.float32)  7.05 us
  transfers between devices with their start and end apart: 1, of which 1 were waited for; matrix products, arithmetic and copies ran while one was open for 0% of the time, Pallas kernels for 0%

commit v1 on v0

--- a/solution.py
+++ b/solution.py
@@ -4,6 +4,8 @@
 import jax
 import jax.numpy as jnp
 from jax import lax
+from jax.experimental import pallas as pl
+from jax.experimental.pallas import tpu as pltpu
 from jax.sharding import PartitionSpec as P
 
 HD = 128
@@ -210,6 +212,270 @@
     return (summed + mixture).astype(jnp.bfloat16)[None]
 
 
+AXES = ("ctx", "exp")
+
+
+def spot(flat):
+    ctx, exp = divmod(flat, 4)
+    return ctx // 2, ctx % 2, exp // 2, exp % 2
+
+
+def flat_of(z, x, y, core):
+    return (z * 2 + x) * 4 + y * 2 + core
+
+
+def move(array, rule):
+    pairs = []
+    for flat in range(32):
+        there = rule(*spot(flat))
+        if there is not None:
+            pairs.append((flat, flat_of(*there)))
+    return lax.ppermute(array, AXES, pairs)
+
+
+def gather_pieces(weights):
+    def first(z, x, y, core):
+        return (z, x, y, 1 - core) if core == z % 2 else (z ^ 1, x, y, core)
+
+    def over_x(z, x, y, core):
+        return z, x ^ 1, y, core
+
+    def to_core(z, x, y, core):
+        return z, x, y, 1 - core
+
+    near = [move(w, first) for w in weights]
+    far = [move(w, over_x) for w in near]
+    near_twin = [move(w, to_core) for w in near]
+    far_twin = [move(w, to_core) for w in far]
+    return near, near_twin, far, far_twin
+
+
+def slot_targets(ids_row, z_here, y_here, capacity):
+    expert_count = 8
+    token_count = ids_row.shape[1]
+    lanes = lax.broadcasted_iota(jnp.int32, (expert_count, token_count), 0)
+    onehot = (lanes == ids_row).astype(jnp.float32)
+    before = (
+        lax.broadcasted_iota(jnp.int32, (token_count, token_count), 0)
+        < lax.broadcasted_iota(jnp.int32, (token_count, token_count), 1)
+    ).astype(jnp.bfloat16)
+    earlier = jnp.dot(onehot.astype(jnp.bfloat16), before, preferred_element_type=jnp.float32)
+    slot = jnp.sum(earlier * onehot, axis=0, keepdims=True).astype(jnp.int32)
+    owner = lax.shift_right_logical(ids_row, 1)
+    z_there = (ids_row & 1) * 2 + (owner & 1)
+    y_there = lax.shift_right_logical(owner, 1)
+    relative = (z_there ^ z_here) * 2 + (y_there ^ y_here)
+    return relative * capacity + slot
+
+
+def slot_matrix(ids_row, z_here, y_here, capacity):
+    target = slot_targets(ids_row, z_here, y_here, capacity)
+    rows = lax.broadcasted_iota(jnp.int32, (8 * capacity, ids_row.shape[1]), 0)
+    return (rows == target).astype(jnp.bfloat16)
+
+
+def attend_kernel(where_ref, ids_ref, queries_ref, residual_ref, *refs):
+    kv_refs, summed_ref, out_refs = refs[:8], refs[8], refs[9:17]
+    keys_ref, values_ref, bias_ref, mixed_ref = refs[17:]
+    tokens = queries_ref.shape[0]
+    group = HEADS // KV_HEADS
+    ctx_here = where_ref[0]
+    row = lax.broadcasted_iota(jnp.int32, (tokens, tokens), 0)
+    column = lax.broadcasted_iota(jnp.int32, (tokens, tokens), 1)
+    for k in range(8):
+        span = slice(k * tokens, (k + 1) * tokens)
+        block = kv_refs[k][...]
+        keys_ref[span, :] = block[:, : KV_HEADS * HD]
+        values_ref[span, :] = block[:, KV_HEADS * HD :]
+        if k == 0:
+            bias_ref[:, span] = jnp.where(column <= row, 0.0, negative_fill)
+        else:
+            bias_ref[:, span] = jnp.full(
+                (tokens, tokens), jnp.where(ctx_here >= k, 0.0, negative_fill), jnp.float32
+            )
+    factor = math.log2(math.e) / math.sqrt(HD)
+    heads_each = 2
+    for first in range(0, HEADS, heads_each):
+        kv_head = first // group
+        side = slice(kv_head * HD, (kv_head + 1) * HD)
+        rows = jnp.concatenate(
+            [queries_ref[:, h * HD : (h + 1) * HD] for h in range(first, first + heads_each)], axis=0
+        )
+        scores = contract_rows(rows, keys_ref[:, side])
+        scores = scores + jnp.concatenate([bias_ref[...]] * heads_each, axis=0)
+        largest = jnp.max(scores, axis=1, keepdims=True)
+        exponent = jnp.exp2((scores - largest) * factor)
+        total = jnp.sum(exponent, axis=1, keepdims=True)
+        product = jnp.dot(
+            exponent.astype(jnp.bfloat16), values_ref[:, side], preferred_element_type=jnp.float32
+        )
+        result = product / total
+        for j in range(heads_each):
+            mixed_ref[:, (first + j) * HD : (first + j + 1) * HD] = result[
+                j * tokens : (j + 1) * tokens
+            ].astype(jnp.bfloat16)
+    summed = residual_ref[...].astype(jnp.float32) + mixed_ref[...].astype(jnp.float32)
+    summed_ref[...] = summed
+    scale = lax.rsqrt(jnp.mean(summed * summed, axis=1, keepdims=True) + epsilon)
+    normed = (summed * scale).astype(jnp.bfloat16)
+    capacity = out_refs[0].shape[0]
+    choose = slot_matrix(ids_ref[...], where_ref[1], where_ref[2], capacity)
+    slots = jnp.dot(choose, normed, preferred_element_type=jnp.float32).astype(jnp.bfloat16)
+    for k in range(8):
+        out_refs[k][...] = slots[k * capacity : (k + 1) * capacity]
+
+
+def expert_kernel(*refs):
+    row_refs, weight_refs, out_refs = refs[:8], refs[8:20], refs[20:28]
+    gate_ref, up_ref, down_ref, semaphores = refs[28:]
+    piece = weight_refs[0].shape[0]
+    copies = []
+    for kind, target in enumerate((gate_ref, up_ref, down_ref)):
+        row_of = []
+        for j in range(PIECES):
+            copy = pltpu.make_async_copy(
+                weight_refs[kind * PIECES + j],
+                target.at[pl.ds(j * piece, piece)],
+                semaphores.at[kind, j],
+            )
+            row_of.append(copy)
+        copies.append(row_of)
+    for j in range(PIECES):
+        copies[0][j].start()
+        copies[1][j].start()
+    for j in range(PIECES):
+        copies[2][j].start()
+    rows = jnp.concatenate([ref[...] for ref in row_refs], axis=0)
+    actives = []
+    for half in range(2):
+        span = slice(half * 2 * piece, (half + 1) * 2 * piece)
+        for j in (2 * half, 2 * half + 1):
+            copies[0][j].wait()
+            copies[1][j].wait()
+        gate_part = contract_rows(rows, gate_ref[span, :])
+        up_part = contract_rows(rows, up_ref[span, :])
+        silu = gate_part / (1.0 + jnp.exp(-gate_part))
+        actives.append((silu * up_part).astype(jnp.bfloat16))
+    for j in range(PIECES):
+        copies[2][j].wait()
+    active = jnp.concatenate(actives, axis=1)
+    capacity = out_refs[0].shape[0]
+    result = jnp.dot(active, down_ref[...], preferred_element_type=jnp.float32).astype(jnp.bfloat16)
+    for k in range(8):
+        out_refs[k][...] = result[k * capacity : (k + 1) * capacity]
+
+
+def combine_kernel(where_ref, ids_ref, route_ref, summed_ref, *refs):
+    row_refs, out_ref = refs[:8], refs[8]
+    capacity = row_refs[0].shape[0]
+    choose = slot_matrix(ids_ref[...], where_ref[1], where_ref[2], capacity)
+    rows = jnp.concatenate([ref[...] for ref in row_refs], axis=0)
+    picked = lax.dot_general(
+        choose, rows, (((0,), (0,)), ((), ())), preferred_element_type=jnp.float32
+    )
+    out_ref[...] = (summed_ref[...] + picked * route_ref[...]).astype(jnp.bfloat16)
+
+
+IN_VMEM = pl.BlockSpec(memory_space=pltpu.VMEM)
+IN_SMEM = pl.BlockSpec(memory_space=pltpu.SMEM)
+ANYWHERE = pl.BlockSpec(memory_space=pl.ANY)
+
+
+def shards_cube(
+    residual,
+    queries,
+    key_states,
+    value_states,
+    expert_ids,
+    route_weight,
+    gate_weight,
+    up_weight,
+    down_weight,
+):
+    ctx_here = lax.axis_index("ctx")
+    exp_here = lax.axis_index("exp")
+    where = jnp.stack([ctx_here, ctx_here // 2, exp_here // 2]).astype(jnp.int32)
+    tokens, width = residual.shape[1:]
+    piece = gate_weight.shape[2]
+    capacity = max(2, 2 * tokens * TOPK // 8)
+    ids_row = expert_ids[0].reshape(1, tokens)
+    kv_own = jnp.concatenate([key_states[0], value_states[0]], axis=1)
+    kv_blocks = [kv_own]
+    for k in range(1, 8):
+        def later(z, x, y, core, k=k):
+            ctx = 2 * z + x + k
+            return (ctx // 2, ctx % 2, y, core) if ctx < 8 else None
+
+        kv_blocks.append(move(kv_own, later))
+    near, near_twin, far, far_twin = gather_pieces([gate_weight[0, 0], up_weight[0, 0], down_weight[0, 0]])
+    slot_shape = jax.ShapeDtypeStruct((capacity, width), jnp.bfloat16)
+    keys_all = 8 * tokens
+    first_out = pl.pallas_call(
+        attend_kernel,
+        out_shape=[jax.ShapeDtypeStruct((tokens, width), jnp.float32)] + [slot_shape] * 8,
+        in_specs=[IN_SMEM] + [IN_VMEM] * 11,
+        out_specs=[IN_VMEM] * 9,
+        scratch_shapes=[
+            pltpu.VMEM((keys_all, KV_HEADS * HD), jnp.bfloat16),
+            pltpu.VMEM((keys_all, KV_HEADS * HD), jnp.bfloat16),
+            pltpu.VMEM((tokens, keys_all), jnp.float32),
+            pltpu.VMEM((tokens, width), jnp.bfloat16),
+        ],
+        compiler_params=pltpu.CompilerParams(vmem_limit_bytes=40 << 20),
+        cost_estimate=pl.CostEstimate(
+            flops=4 * tokens * keys_all * HEADS * HD,
+            bytes_accessed=8 * tokens * width,
+            transcendentals=tokens * keys_all * HEADS,
+        ),
+        name="attend",
+    )(where, ids_row, queries[0], residual[0], *kv_blocks)
+    summed, outgoing = first_out[0], first_out[1:]
+
+    def swap(array, k):
+        if k == 0:
+            return array
+        return move(array, lambda z, x, y, core: (z ^ (k >> 1), x, y ^ (k & 1), core))
+
+    arrived = [swap(outgoing[k], k) for k in range(8)]
+    pieces = []
+    for kind in range(3):
+        pieces += [near[kind], near_twin[kind], far[kind], far_twin[kind]]
+    results = pl.pallas_call(
+        expert_kernel,
+        out_shape=[slot_shape] * 8,
+        in_specs=[IN_VMEM] * 8 + [ANYWHERE] * 12,
+        out_specs=[IN_VMEM] * 8,
+        scratch_shapes=[
+            pltpu.VMEM((PIECES * piece, width), jnp.bfloat16),
+            pltpu.VMEM((PIECES * piece, width), jnp.bfloat16),
+            pltpu.VMEM((PIECES * piece, width), jnp.bfloat16),
+            pltpu.SemaphoreType.DMA((3, PIECES)),
+        ],
+        compiler_params=pltpu.CompilerParams(vmem_limit_bytes=48 << 20),
+        cost_estimate=pl.CostEstimate(
+            flops=6 * 8 * capacity * PIECES * piece * width,
+            bytes_accessed=6 * PIECES * piece * width,
+            transcendentals=8 * capacity * PIECES * piece,
+        ),
+        name="experts",
+    )(*arrived, *pieces)
+    returned = [swap(results[k], k) for k in range(8)]
+    output = pl.pallas_call(
+        combine_kernel,
+        out_shape=jax.ShapeDtypeStruct((tokens, width), jnp.bfloat16),
+        in_specs=[IN_SMEM] + [IN_VMEM] * 11,
+        out_specs=IN_VMEM,
+        compiler_params=pltpu.CompilerParams(vmem_limit_bytes=24 << 20),
+        cost_estimate=pl.CostEstimate(
+            flops=2 * tokens * 8 * capacity * width,
+            bytes_accessed=12 * tokens * width,
+            transcendentals=0,
+        ),
+        name="combine",
+    )(where, ids_row, route_weight[0], summed, *returned)
+    return output[None]
+
+
 def solution(mesh):
     in_specs = (
         P("exp", "ctx", None),
@@ -223,4 +489,6 @@
         P("exp", "ctx", None, None),
     )
     out_specs = P("exp", "ctx", None)
-    return jax.shard_map(shards, mesh=mesh, in_specs=in_specs, out_specs=out_specs, check_vma=False)
+    cube = mesh.shape["ctx"] == 8 and mesh.shape["exp"] == 4
+    body = shards_cube if cube else shards
+    return jax.shard_map(body, mesh=mesh, in_specs=in_specs, out_specs=out_specs, check_vma=False)

time: 329 us -> 153 us (0.47)
  blocking collectives: 269 us -> 0 us
  starting transfers between devices: 4.23 us -> 76.9 us
  waiting for transfers between devices: 14.5 us -> 57.2 us
  matrix products: 12.8 us -> 0 us
  Pallas kernels: 0 us -> 12 us
  local copies, waits for them, and re-layouts: 16.7 us -> 5.32 us
  other arithmetic: 8.21 us -> 0.96 us
    all_to_all x3 -> x0, blocking collectives: 214 us -> none  [the longest x1 100 us: shards(): lax.all_to_all(copies, 'ctx', split_axis=0, concat_axis=0, tiled=True)]
    ppermute x0 -> x33, starting transfers between devices: none -> 76.9 us  [move(): return lax.ppermute(array, AXES, pairs)]
    ppermute x0 -> x33, waiting for transfers between devices: none -> 57.2 us  [move(): return lax.ppermute(array, AXES, pairs)]
    all_gather x2 -> x0, blocking collectives: 54.8 us -> none  [the longest x1 27.8 us: shards(): lax.all_gather(value_states, 'ctx', axis=1, tiled=True)]
    all_to_all x1 -> x0, waiting for transfers between devices: 14.5 us -> none  [shards(): lax.all_to_all(piece_sum, 'exp', split_axis=1, concat_axis=1, tiled=True)]
    dot_general x6 -> x0, matrix products: 12.8 us -> none  [the longest x1 7.05 us: shards(): jnp.dot(active, down_piece, preferred_element_type=jnp.float32)]
    pallas_call x0 -> x3, Pallas kernels: none -> 12 us  [the longest x1 5.22 us: shards_cube(): pl.pallas_call(attend_kernel, out_shape=[jax.ShapeDtypeStruct((tokens, wi...]
    reduce_sum x5 -> x0, other arithmetic: 4.62 us -> none  [the longest x1 3.06 us: shards(): jnp.sum(returned.reshape(experts_each, PIECES, exp_count, capacity, width...]
  transfers between devices with their start and end apart: 1 -> 33, of which waited for: 1 -> 17; matrix products, arithmetic and copies ran while one was open for 0% -> 1% of each run, Pallas kernels for 0% -> 3%
where the time goes in v1:
time: 153 us
  starting transfers between devices  76.9 us (50%)
  waiting for transfers between devices  57.2 us (37%)
  Pallas kernels  12 us (8%)
  local copies, waits for them, and re-layouts  5.32 us (3%)
    ppermute x33, starting transfers between devices, move(): return lax.ppermute(array, AXES, pairs)  76.9 us
    ppermute x33, waiting for transfers between devices, move(): return lax.ppermute(array, AXES, pairs)  57.2 us
    pallas_call x1, Pallas kernels, shards_cube(): pl.pallas_call(attend_kernel, out_shape=[jax.ShapeDtypeStruct((tokens, wi...  5.22 us
    unnamed x24, local copies, waits for them, and re-layouts  5.21 us
    pallas_call x1, Pallas kernels, shards_cube(): pl.pallas_call(expert_kernel, out_shape=[slot_shape] * 8, in_specs=[IN_VM...  4.95 us
  transfers between devices with their start and end apart: 33, of which 17 were waited for; matrix products, arithmetic and copies ran while one was open for 1% of the time, Pallas kernels for 3%

profile of v1, /device:TPU:8, one launch (start us, length us, event | category | flops | bytes accessed | tf_op | source)
XLA Modules:
  0.0 152.7 jit_solution(4602873293649032577)
XLA Ops:
  0.0 1.6 %collective-permute-start.22 = (bf16[192,2048]{1,0:T(8,128)(2,1)}, bf16[192,2048]{1,0:T(8,128)(2,1)}, u32[]{:S(2)}, u32[]{:S(2)}) collective-permute-start(bf16[192,2048]{1,0:T(8,128)(2,1)} %bitcast.22), channel_id=1, source_target_pairs={{0,1},{1,9},{2,3},{3,11},{4,5},{5,13},{6,7},{7,15},{8,0},{9,8},{10... | collective-permute-start | bytes 2359304 | tf_op jit(solution)/shard_map/ppermute | solution.py:233
  2.5 3.4 %collective-permute-start = (bf16[128,512]{1,0:T(8,128)(2,1)S(1)}, bf16[128,512]{1,0:T(8,128)(2,1)S(1)}, u32[]{:S(2)}, u32[]{:S(2)}) collective-permute-start(bf16[128,512]{1,0:T(8,128)(2,1)S(1)} %pad_maximum_fusion.refs_0_), channel_id=1, source_target_pairs={{0,4},{1,5},{2,6},{3,7},{4,8},{5,9},{6,10},{7,11},{8,12},{9,13},{1... | collective-permute-start | bytes 393224 | tf_op jit(solution)/shard_map/ppermute | solution.py:233
  5.9 3.7 %collective-permute-start.1 = (bf16[128,512]{1,0:T(8,128)(2,1)S(1)}, bf16[128,512]{1,0:T(8,128)(2,1)S(1)}, u32[]{:S(2)}, u32[]{:S(2)}) collective-permute-start(bf16[128,512]{1,0:T(8,128)(2,1)S(1)} %pad_maximum_fusion.refs_0_), channel_id=1, source_target_pairs={{0,8},{1,9},{2,10},{3,11},{4,12},{5,13},{6,14},{7,15},{8,16},{9,17... | collective-permute-start | bytes 393224 | tf_op jit(solution)/shard_map/ppermute | solution.py:233
  9.6 2.1 %collective-permute-done.refs_1_ = bf16[128,512]{1,0:T(8,128)(2,1)S(1)} collective-permute-done((bf16[128,512]{1,0:T(8,128)(2,1)S(1)}, bf16[128,512]{1,0:T(8,128)(2,1)S(1)}, u32[]{:S(2)}, u32[]{:S(2)}) %collective-permute-start) | collective-permute-done | bytes 131104 | tf_op jit(solution)/shard_map/ppermute | solution.py:233
  11.7 3.1 %collective-permute-start.2 = (bf16[128,512]{1,0:T(8,128)(2,1)S(1)}, bf16[128,512]{1,0:T(8,128)(2,1)S(1)}, u32[]{:S(2)}, u32[]{:S(2)}) collective-permute-start(bf16[128,512]{1,0:T(8,128)(2,1)S(1)} %pad_maximum_fusion.refs_0_), channel_id=1, source_target_pairs={{0,12},{1,13},{2,14},{3,15},{4,16},{5,17},{6,18},{7,19},{8,20},{9,... | collective-permute-start | bytes 393224 | tf_op jit(solution)/shard_map/ppermute | solution.py:233
  14.9 3.8 %collective-permute-start.3 = (bf16[128,512]{1,0:T(8,128)(2,1)S(1)}, bf16[128,512]{1,0:T(8,128)(2,1)S(1)}, u32[]{:S(2)}, u32[]{:S(2)}) collective-permute-start(bf16[128,512]{1,0:T(8,128)(2,1)S(1)} %pad_maximum_fusion.refs_0_), channel_id=1, source_target_pairs={{0,16},{1,17},{2,18},{3,19},{4,20},{5,21},{6,22},{7,23},{8,24},{9,... | collective-permute-start | bytes 393224 | tf_op jit(solution)/shard_map/ppermute | solution.py:233
  18.7 5.2 %collective-permute-start.4 = (bf16[128,512]{1,0:T(8,128)(2,1)S(1)}, bf16[128,512]{1,0:T(8,128)(2,1)S(1)}, u32[]{:S(2)}, u32[]{:S(2)}) collective-permute-start(bf16[128,512]{1,0:T(8,128)(2,1)S(1)} %pad_maximum_fusion.refs_0_), channel_id=1, source_target_pairs={{0,20},{1,21},{2,22},{3,23},{4,24},{5,25},{6,26},{7,27},{8,28},{9,... | collective-permute-start | bytes 393224 | tf_op jit(solution)/shard_map/ppermute | solution.py:233
  24.7 3.0 %collective-permute-done.4.refs_5_ = bf16[128,512]{1,0:T(8,128)(2,1)S(1)} collective-permute-done((bf16[128,512]{1,0:T(8,128)(2,1)S(1)}, bf16[128,512]{1,0:T(8,128)(2,1)S(1)}, u32[]{:S(2)}, u32[]{:S(2)}) %collective-permute-start.4) | collective-permute-done | bytes 131104 | tf_op jit(solution)/shard_map/ppermute | solution.py:233
  32.7 5.2 %attend.1 = (f32[128,2048]{1,0:T(8,128)S(1)}, bf16[32,2048]{1,0:T(8,128)(2,1)S(1)}, bf16[32,2048]{1,0:T(8,128)(2,1)S(1)}, bf16[32,2048]{1,0:T(8,128)(2,1)S(1)}, ...) custom-call(s32[3]{0:T(128)S(1)} %pad_add_fusion.where_ref, ...), custom_call_target="tpu_custom_call" | custom-call | flops 1073741824 | bytes 2097152 | tf_op jit(solution)/shard_map/attend/pallas_call | solution.py:413
  38.0 7.7 %collective-permute-start.10 = (bf16[32,2048]{1,0:T(8,128)(2,1)S(1)}, bf16[32,2048]{1,0:T(8,128)(2,1)S(1)}, u32[]{:S(2)}, u32[]{:S(2)}) collective-permute-start(bf16[32,2048]{1,0:T(8,128)(2,1)S(1)} %get-tuple-element.27), channel_id=1, source_target_pairs={{0,16},{1,17},{2,18},{3,19},{4,20},{5,21},{6,22},{7,23},{8,24},{9,... | collective-permute-start | bytes 393224 | tf_op jit(solution)/shard_map/ppermute | solution.py:233
  46.7 7.0 %collective-permute-start.16 = (bf16[192,2048]{1,0:T(8,128)(2,1)S(1)}, bf16[192,2048]{1,0:T(8,128)(2,1)S(1)}, u32[]{:S(2)}, u32[]{:S(2)}) collective-permute-start(bf16[192,2048]{1,0:T(8,128)(2,1)S(1)} %collective-permute-done.14.refs_8_), channel_id=1, source_target_pairs={{0,4},{1,5},{2,6},{3,7},{4,0},{5,1},{6,2},{7,3},{8,12},{9,13},{10,... | collective-permute-start | bytes 2359304 | tf_op jit(solution)/shard_map/ppermute | solution.py:233
  53.8 2.0 %collective-permute-start.24 = (bf16[192,2048]{1,0:T(8,128)(2,1)}, bf16[192,2048]{1,0:T(8,128)(2,1)S(1)}, u32[]{:S(2)}, u32[]{:S(2)}) collective-permute-start(bf16[192,2048]{1,0:T(8,128)(2,1)} %collective-permute-done.22.refs_16_), channel_id=1, source_target_pairs={{0,4},{1,5},{2,6},{3,7},{4,0},{5,1},{6,2},{7,3},{8,12},{9,13},{10,... | collective-permute-start | bytes 2359304 | tf_op jit(solution)/shard_map/ppermute | solution.py:233
  55.7 20.2 %collective-permute-start.15 = (bf16[192,2048]{1,0:T(8,128)(2,1)S(1)}, bf16[192,2048]{1,0:T(8,128)(2,1)S(1)}, u32[]{:S(2)}, u32[]{:S(2)}) collective-permute-start(bf16[192,2048]{1,0:T(8,128)(2,1)S(1)} %collective-permute-done.14.refs_8_), channel_id=1, source_target_pairs={{0,1},{1,0},{2,3},{3,2},{4,5},{5,4},{6,7},{7,6},{8,9},{9,8},{10,11... | collective-permute-start | bytes 2359304 | tf_op jit(solution)/shard_map/ppermute | solution.py:233
  75.9 8.3 %collective-permute-done.12.refs_6_ = bf16[32,2048]{1,0:T(8,128)(2,1)S(1)} collective-permute-done((bf16[32,2048]{1,0:T(8,128)(2,1)S(1)}, bf16[32,2048]{1,0:T(8,128)(2,1)S(1)}, u32[]{:S(2)}, u32[]{:S(2)}) %collective-permute-start.12) | collective-permute-done | bytes 131104 | tf_op jit(solution)/shard_map/ppermute | solution.py:233
  84.3 8.2 %collective-permute-done.13.refs_7_ = bf16[32,2048]{1,0:T(8,128)(2,1)S(1)} collective-permute-done((bf16[32,2048]{1,0:T(8,128)(2,1)S(1)}, bf16[32,2048]{1,0:T(8,128)(2,1)S(1)}, u32[]{:S(2)}, u32[]{:S(2)}) %collective-permute-start.13) | collective-permute-done | bytes 131104 | tf_op jit(solution)/shard_map/ppermute | solution.py:233
  92.5 1.6 %collective-permute-start.7 = (bf16[32,2048]{1,0:T(8,128)(2,1)S(1)}, bf16[32,2048]{1,0:T(8,128)(2,1)S(1)}, u32[]{:S(2)}, u32[]{:S(2)}) collective-permute-start(bf16[32,2048]{1,0:T(8,128)(2,1)S(1)} %get-tuple-element.24), channel_id=1, source_target_pairs={{0,2},{1,3},{2,0},{3,1},{4,6},{5,7},{6,4},{7,5},{8,10},{9,11},{10,... | collective-permute-start | bytes 393224 | tf_op jit(solution)/shard_map/ppermute | solution.py:233
  94.2 3.3 %collective-permute-done.7.refs_1_ = bf16[32,2048]{1,0:T(8,128)(2,1)S(1)} collective-permute-done((bf16[32,2048]{1,0:T(8,128)(2,1)S(1)}, bf16[32,2048]{1,0:T(8,128)(2,1)S(1)}, u32[]{:S(2)}, u32[]{:S(2)}) %collective-permute-start.7) | collective-permute-done | bytes 131104 | tf_op jit(solution)/shard_map/ppermute | solution.py:233
  97.9 4.6 %collective-permute-done.8.refs_2_ = bf16[32,2048]{1,0:T(8,128)(2,1)S(1)} collective-permute-done((bf16[32,2048]{1,0:T(8,128)(2,1)S(1)}, bf16[32,2048]{1,0:T(8,128)(2,1)S(1)}, u32[]{:S(2)}, u32[]{:S(2)}) %collective-permute-start.8) | collective-permute-done | bytes 131104 | tf_op jit(solution)/shard_map/ppermute | solution.py:233
  102.5 1.7 %collective-permute-start.9 = (bf16[32,2048]{1,0:T(8,128)(2,1)S(1)}, bf16[32,2048]{1,0:T(8,128)(2,1)S(1)}, u32[]{:S(2)}, u32[]{:S(2)}) collective-permute-start(bf16[32,2048]{1,0:T(8,128)(2,1)S(1)} %get-tuple-element.26), channel_id=1, source_target_pairs={{0,10},{1,11},{2,8},{3,9},{4,14},{5,15},{6,12},{7,13},{8,2},{9,3},... | collective-permute-start | bytes 393224 | tf_op jit(solution)/shard_map/ppermute | solution.py:233
  104.2 4.2 %collective-permute-done.9.refs_3_ = bf16[32,2048]{1,0:T(8,128)(2,1)S(1)} collective-permute-done((bf16[32,2048]{1,0:T(8,128)(2,1)S(1)}, bf16[32,2048]{1,0:T(8,128)(2,1)S(1)}, u32[]{:S(2)}, u32[]{:S(2)}) %collective-permute-start.9) | collective-permute-done | bytes 131104 | tf_op jit(solution)/shard_map/ppermute | solution.py:233
  109.5 2.2 %collective-permute-done.19.refs_13_ = bf16[192,2048]{1,0:T(8,128)(2,1)S(1)} collective-permute-done((bf16[192,2048]{1,0:T(8,128)(2,1)S(1)}, bf16[192,2048]{1,0:T(8,128)(2,1)S(1)}, u32[]{:S(2)}, u32[]{:S(2)}) %collective-permute-start.19) | collective-permute-done | bytes 786464 | tf_op jit(solution)/shard_map/ppermute | solution.py:233
  112.9 1.1 collective-permute-done.21.refs_15_
  116.0 5.0 %experts.1 = (bf16[32,2048]{1,0:T(8,128)(2,1)S(1)}, bf16[32,2048]{1,0:T(8,128)(2,1)S(1)}, bf16[32,2048]{1,0:T(8,128)(2,1)S(1)}, bf16[32,2048]{1,0:T(8,128)(2,1)S...) custom-call(bf16[32,2048]{1,0:T(8,128)(2,1)S(1)} %get-tuple-element., ...), custom_call_target="tpu_custom_call" | custom-call | flops 2415919104 | bytes 9437184 | tf_op jit(solution)/shard_map/experts/pallas_call | solution.py:443
  121.0 2.8 %collective-permute-start.26 = (bf16[32,2048]{1,0:T(8,128)(2,1)S(1)}, bf16[32,2048]{1,0:T(8,128)(2,1)S(1)}, u32[]{:S(2)}, u32[]{:S(2)}) collective-permute-start(bf16[32,2048]{1,0:T(8,128)(2,1)S(1)} %get-tuple-element.32), channel_id=1, source_target_pairs={{0,2},{1,3},{2,0},{3,1},{4,6},{5,7},{6,4},{7,5},{8,10},{9,11},{10,... | collective-permute-start | bytes 393224 | tf_op jit(solution)/shard_map/ppermute | solution.py:233
  123.8 1.5 %collective-permute-start.28 = (bf16[32,2048]{1,0:T(8,128)(2,1)S(1)}, bf16[32,2048]{1,0:T(8,128)(2,1)S(1)}, u32[]{:S(2)}, u32[]{:S(2)}) collective-permute-start(bf16[32,2048]{1,0:T(8,128)(2,1)S(1)} %get-tuple-element.34), channel_id=1, source_target_pairs={{0,10},{1,11},{2,8},{3,9},{4,14},{5,15},{6,12},{7,13},{8,2},{9,3},... | collective-permute-start | bytes 393224 | tf_op jit(solution)/shard_map/ppermute | solution.py:233
  125.3 2.0 %collective-permute-start.29 = (bf16[32,2048]{1,0:T(8,128)(2,1)S(1)}, bf16[32,2048]{1,0:T(8,128)(2,1)S(1)}, u32[]{:S(2)}, u32[]{:S(2)}) collective-permute-start(bf16[32,2048]{1,0:T(8,128)(2,1)S(1)} %get-tuple-element.35), channel_id=1, source_target_pairs={{0,16},{1,17},{2,18},{3,19},{4,20},{5,21},{6,22},{7,23},{8,24},{9,... | collective-permute-start | bytes 393224 | tf_op jit(solution)/shard_map/ppermute | solution.py:233
  127.4 2.3 %collective-permute-start.30 = (bf16[32,2048]{1,0:T(8,128)(2,1)S(1)}, bf16[32,2048]{1,0:T(8,128)(2,1)S(1)}, u32[]{:S(2)}, u32[]{:S(2)}) collective-permute-start(bf16[32,2048]{1,0:T(8,128)(2,1)S(1)} %get-tuple-element.36), channel_id=1, source_target_pairs={{0,18},{1,19},{2,16},{3,17},{4,22},{5,23},{6,20},{7,21},{8,26},{9,... | collective-permute-start | bytes 393224 | tf_op jit(solution)/shard_map/ppermute | solution.py:233
  130.7 3.2 %collective-permute-start.32 = (bf16[32,2048]{1,0:T(8,128)(2,1)S(1)}, bf16[32,2048]{1,0:T(8,128)(2,1)S(1)}, u32[]{:S(2)}, u32[]{:S(2)}) collective-permute-start(bf16[32,2048]{1,0:T(8,128)(2,1)S(1)} %get-tuple-element.38), channel_id=1, source_target_pairs={{0,26},{1,27},{2,24},{3,25},{4,30},{5,31},{6,28},{7,29},{8,18},{9,... | collective-permute-start | bytes 393224 | tf_op jit(solution)/shard_map/ppermute | solution.py:233
  134.7 10.3 %collective-permute-done.30.refs_5_ = bf16[32,2048]{1,0:T(8,128)(2,1)S(1)} collective-permute-done((bf16[32,2048]{1,0:T(8,128)(2,1)S(1)}, bf16[32,2048]{1,0:T(8,128)(2,1)S(1)}, u32[]{:S(2)}, u32[]{:S(2)}) %collective-permute-start.30) | collective-permute-done | bytes 131104 | tf_op jit(solution)/shard_map/ppermute | solution.py:233
  145.0 3.5 %collective-permute-done.31.refs_6_ = bf16[32,2048]{1,0:T(8,128)(2,1)S(1)} collective-permute-done((bf16[32,2048]{1,0:T(8,128)(2,1)S(1)}, bf16[32,2048]{1,0:T(8,128)(2,1)S(1)}, u32[]{:S(2)}, u32[]{:S(2)}) %collective-permute-start.31) | collective-permute-done | bytes 131104 | tf_op jit(solution)/shard_map/ppermute | solution.py:233
  148.5 2.3 %collective-permute-done.32.refs_7_ = bf16[32,2048]{1,0:T(8,128)(2,1)S(1)} collective-permute-done((bf16[32,2048]{1,0:T(8,128)(2,1)S(1)}, bf16[32,2048]{1,0:T(8,128)(2,1)S(1)}, u32[]{:S(2)}, u32[]{:S(2)}) %collective-permute-start.32) | collective-permute-done | bytes 131104 | tf_op jit(solution)/shard_map/ppermute | solution.py:233
  150.8 1.8 %combine.1 = bf16[128,2048]{1,0:T(8,128)(2,1)} custom-call(s32[3]{0:T(128)S(1)} %pad_add_fusion.where_ref, s32[1,128]{1,0:T(1,128)S(1)} %bitcast.14, f32[128,1]{1,0:T(8,128)S(1)} %copy.10.route_ref, f32[128,2048]{1,0:T(8,128)S(1)} %get-tuple-element.22.summed_ref, bf16[32,2048]{1,0:T(8,128)(2,1)S(1)} %get-tuple-element.31.refs_0_, ...), custom_call_target="tpu_custom_call" | custom-call | flops 134217728 | bytes 3145728 | tf_op jit(solution)/shard_map/combine/pallas_call | solution.py:463
  (64 shorter events, 14.3 us)
Async XLA Ops:
  0.0 46.7 %collective-permute-start.14 = (bf16[192,2048]{1,0:T(8,128)(2,1)}, bf16[192,2048]{1,0:T(8,128)(2,1)S(1)}, u32[]{:S(2)}, u32[]{:S(2)}) collective-permute-start(bf16[192,2048]{1,0:T(8,128)(2,1)} %bitcast.20), channel_id=1, source_target_pairs={{0,1},{1,9},{2,3},{3,11},{4,5},{5,13},{6,7},{7,15},{8,0},{9,8},{10... | collective-permute-start | bytes 2359304 | tf_op jit(solution)/shard_map/ppermute | solution.py:233
  0.0 53.7 %collective-permute-start.18 = (bf16[192,2048]{1,0:T(8,128)(2,1)}, bf16[192,2048]{1,0:T(8,128)(2,1)S(1)}, u32[]{:S(2)}, u32[]{:S(2)}) collective-permute-start(bf16[192,2048]{1,0:T(8,128)(2,1)} %bitcast.21), channel_id=1, source_target_pairs={{0,1},{1,9},{2,3},{3,11},{4,5},{5,13},{6,7},{7,15},{8,0},{9,8},{10... | collective-permute-start | bytes 2359304 | tf_op jit(solution)/shard_map/ppermute | solution.py:233
  0.0 53.8 %collective-permute-start.22 = (bf16[192,2048]{1,0:T(8,128)(2,1)}, bf16[192,2048]{1,0:T(8,128)(2,1)}, u32[]{:S(2)}, u32[]{:S(2)}) collective-permute-start(bf16[192,2048]{1,0:T(8,128)(2,1)} %bitcast.22), channel_id=1, source_target_pairs={{0,1},{1,9},{2,3},{3,11},{4,5},{5,13},{6,7},{7,15},{8,0},{9,8},{10... | collective-permute-start | bytes 2359304 | tf_op jit(solution)/shard_map/ppermute | solution.py:233
  2.5 9.2 %collective-permute-start = (bf16[128,512]{1,0:T(8,128)(2,1)S(1)}, bf16[128,512]{1,0:T(8,128)(2,1)S(1)}, u32[]{:S(2)}, u32[]{:S(2)}) collective-permute-start(bf16[128,512]{1,0:T(8,128)(2,1)S(1)} %pad_maximum_fusion.refs_0_), channel_id=1, source_target_pairs={{0,4},{1,5},{2,6},{3,7},{4,8},{5,9},{6,10},{7,11},{8,12},{9,13},{1... | collective-permute-start | bytes 393224 | tf_op jit(solution)/shard_map/ppermute | solution.py:233
  5.9 9.0 %collective-permute-start.1 = (bf16[128,512]{1,0:T(8,128)(2,1)S(1)}, bf16[128,512]{1,0:T(8,128)(2,1)S(1)}, u32[]{:S(2)}, u32[]{:S(2)}) collective-permute-start(bf16[128,512]{1,0:T(8,128)(2,1)S(1)} %pad_maximum_fusion.refs_0_), channel_id=1, source_target_pairs={{0,8},{1,9},{2,10},{3,11},{4,12},{5,13},{6,14},{7,15},{8,16},{9,17... | collective-permute-start | bytes 393224 | tf_op jit(solution)/shard_map/ppermute | solution.py:233
  11.7 7.0 %collective-permute-start.2 = (bf16[128,512]{1,0:T(8,128)(2,1)S(1)}, bf16[128,512]{1,0:T(8,128)(2,1)S(1)}, u32[]{:S(2)}, u32[]{:S(2)}) collective-permute-start(bf16[128,512]{1,0:T(8,128)(2,1)S(1)} %pad_maximum_fusion.refs_0_), channel_id=1, source_target_pairs={{0,12},{1,13},{2,14},{3,15},{4,16},{5,17},{6,18},{7,19},{8,20},{9,... | collective-permute-start | bytes 393224 | tf_op jit(solution)/shard_map/ppermute | solution.py:233
  14.9 9.1 %collective-permute-start.3 = (bf16[128,512]{1,0:T(8,128)(2,1)S(1)}, bf16[128,512]{1,0:T(8,128)(2,1)S(1)}, u32[]{:S(2)}, u32[]{:S(2)}) collective-permute-start(bf16[128,512]{1,0:T(8,128)(2,1)S(1)} %pad_maximum_fusion.refs_0_), channel_id=1, source_target_pairs={{0,16},{1,17},{2,18},{3,19},{4,20},{5,21},{6,22},{7,23},{8,24},{9,... | collective-permute-start | bytes 393224 | tf_op jit(solution)/shard_map/ppermute | solution.py:233
  18.7 9.0 %collective-permute-start.4 = (bf16[128,512]{1,0:T(8,128)(2,1)S(1)}, bf16[128,512]{1,0:T(8,128)(2,1)S(1)}, u32[]{:S(2)}, u32[]{:S(2)}) collective-permute-start(bf16[128,512]{1,0:T(8,128)(2,1)S(1)} %pad_maximum_fusion.refs_0_), channel_id=1, source_target_pairs={{0,20},{1,21},{2,22},{3,23},{4,24},{5,25},{6,26},{7,27},{8,28},{9,... | collective-permute-start | bytes 393224 | tf_op jit(solution)/shard_map/ppermute | solution.py:233
  24.0 4.5 %collective-permute-start.5 = (bf16[128,512]{1,0:T(8,128)(2,1)S(1)}, bf16[128,512]{1,0:T(8,128)(2,1)S(1)}, u32[]{:S(2)}, u32[]{:S(2)}) collective-permute-start(bf16[128,512]{1,0:T(8,128)(2,1)S(1)} %pad_maximum_fusion.refs_0_), channel_id=1, source_target_pairs={{0,24},{1,25},{2,26},{3,27},{4,28},{5,29},{6,30},{7,31}} | collective-permute-start | bytes 393224 | tf_op jit(solution)/shard_map/ppermute | solution.py:233
  38.0 17.8 %collective-permute-start.10 = (bf16[32,2048]{1,0:T(8,128)(2,1)S(1)}, bf16[32,2048]{1,0:T(8,128)(2,1)S(1)}, u32[]{:S(2)}, u32[]{:S(2)}) collective-permute-start(bf16[32,2048]{1,0:T(8,128)(2,1)S(1)} %get-tuple-element.27), channel_id=1, source_target_pairs={{0,16},{1,17},{2,18},{3,19},{4,20},{5,21},{6,22},{7,23},{8,24},{9,... | collective-permute-start | bytes 393224 | tf_op jit(solution)/shard_map/ppermute | solution.py:233
  45.7 30.2 %collective-permute-start.11 = (bf16[32,2048]{1,0:T(8,128)(2,1)S(1)}, bf16[32,2048]{1,0:T(8,128)(2,1)S(1)}, u32[]{:S(2)}, u32[]{:S(2)}) collective-permute-start(bf16[32,2048]{1,0:T(8,128)(2,1)S(1)} %get-tuple-element.28), channel_id=1, source_target_pairs={{0,18},{1,19},{2,16},{3,17},{4,22},{5,23},{6,20},{7,21},{8,26},{9,... | collective-permute-start | bytes 393224 | tf_op jit(solution)/shard_map/ppermute | solution.py:233
  46.7 61.6 %collective-permute-start.16 = (bf16[192,2048]{1,0:T(8,128)(2,1)S(1)}, bf16[192,2048]{1,0:T(8,128)(2,1)S(1)}, u32[]{:S(2)}, u32[]{:S(2)}) collective-permute-start(bf16[192,2048]{1,0:T(8,128)(2,1)S(1)} %collective-permute-done.14.refs_8_), channel_id=1, source_target_pairs={{0,4},{1,5},{2,6},{3,7},{4,0},{5,1},{6,2},{7,3},{8,12},{9,13},{10,... | collective-permute-start | bytes 2359304 | tf_op jit(solution)/shard_map/ppermute | solution.py:233
  53.7 55.1 %collective-permute-start.20 = (bf16[192,2048]{1,0:T(8,128)(2,1)S(1)}, bf16[192,2048]{1,0:T(8,128)(2,1)S(1)}, u32[]{:S(2)}, u32[]{:S(2)}) collective-permute-start(bf16[192,2048]{1,0:T(8,128)(2,1)S(1)} %collective-permute-done.18.refs_12_), channel_id=1, source_target_pairs={{0,4},{1,5},{2,6},{3,7},{4,0},{5,1},{6,2},{7,3},{8,12},{9,13},{10,... | collective-permute-start | bytes 2359304 | tf_op jit(solution)/shard_map/ppermute | solution.py:233
  53.8 55.2 %collective-permute-start.24 = (bf16[192,2048]{1,0:T(8,128)(2,1)}, bf16[192,2048]{1,0:T(8,128)(2,1)S(1)}, u32[]{:S(2)}, u32[]{:S(2)}) collective-permute-start(bf16[192,2048]{1,0:T(8,128)(2,1)} %collective-permute-done.22.refs_16_), channel_id=1, source_target_pairs={{0,4},{1,5},{2,6},{3,7},{4,0},{5,1},{6,2},{7,3},{8,12},{9,13},{10,... | collective-permute-start | bytes 2359304 | tf_op jit(solution)/shard_map/ppermute | solution.py:233
  55.7 53.6 %collective-permute-start.15 = (bf16[192,2048]{1,0:T(8,128)(2,1)S(1)}, bf16[192,2048]{1,0:T(8,128)(2,1)S(1)}, u32[]{:S(2)}, u32[]{:S(2)}) collective-permute-start(bf16[192,2048]{1,0:T(8,128)(2,1)S(1)} %collective-permute-done.14.refs_8_), channel_id=1, source_target_pairs={{0,1},{1,0},{2,3},{3,2},{4,5},{5,4},{6,7},{7,6},{8,9},{9,8},{10,11... | collective-permute-start | bytes 2359304 | tf_op jit(solution)/shard_map/ppermute | solution.py:233
  75.9 8.3 %collective-permute-start.12 = (bf16[32,2048]{1,0:T(8,128)(2,1)S(1)}, bf16[32,2048]{1,0:T(8,128)(2,1)S(1)}, u32[]{:S(2)}, u32[]{:S(2)}) collective-permute-start(bf16[32,2048]{1,0:T(8,128)(2,1)S(1)} %get-tuple-element.29), channel_id=1, source_target_pairs={{0,24},{1,25},{2,26},{3,27},{4,28},{5,29},{6,30},{7,31},{8,16},{9,... | collective-permute-start | bytes 393224 | tf_op jit(solution)/shard_map/ppermute | solution.py:233
  84.2 8.3 %collective-permute-start.13 = (bf16[32,2048]{1,0:T(8,128)(2,1)S(1)}, bf16[32,2048]{1,0:T(8,128)(2,1)S(1)}, u32[]{:S(2)}, u32[]{:S(2)}) collective-permute-start(bf16[32,2048]{1,0:T(8,128)(2,1)S(1)} %get-tuple-element.30), channel_id=1, source_target_pairs={{0,26},{1,27},{2,24},{3,25},{4,30},{5,31},{6,28},{7,29},{8,18},{9,... | collective-permute-start | bytes 393224 | tf_op jit(solution)/shard_map/ppermute | solution.py:233
  92.5 5.0 %collective-permute-start.7 = (bf16[32,2048]{1,0:T(8,128)(2,1)S(1)}, bf16[32,2048]{1,0:T(8,128)(2,1)S(1)}, u32[]{:S(2)}, u32[]{:S(2)}) collective-permute-start(bf16[32,2048]{1,0:T(8,128)(2,1)S(1)} %get-tuple-element.24), channel_id=1, source_target_pairs={{0,2},{1,3},{2,0},{3,1},{4,6},{5,7},{6,4},{7,5},{8,10},{9,11},{10,... | collective-permute-start | bytes 393224 | tf_op jit(solution)/shard_map/ppermute | solution.py:233
  97.5 5.0 %collective-permute-start.8 = (bf16[32,2048]{1,0:T(8,128)(2,1)S(1)}, bf16[32,2048]{1,0:T(8,128)(2,1)S(1)}, u32[]{:S(2)}, u32[]{:S(2)}) collective-permute-start(bf16[32,2048]{1,0:T(8,128)(2,1)S(1)} %get-tuple-element.25), channel_id=1, source_target_pairs={{0,8},{1,9},{2,10},{3,11},{4,12},{5,13},{6,14},{7,15},{8,0},{9,1},... | collective-permute-start | bytes 393224 | tf_op jit(solution)/shard_map/ppermute | solution.py:233
  102.5 5.9 %collective-permute-start.9 = (bf16[32,2048]{1,0:T(8,128)(2,1)S(1)}, bf16[32,2048]{1,0:T(8,128)(2,1)S(1)}, u32[]{:S(2)}, u32[]{:S(2)}) collective-permute-start(bf16[32,2048]{1,0:T(8,128)(2,1)S(1)} %get-tuple-element.26), channel_id=1, source_target_pairs={{0,10},{1,11},{2,8},{3,9},{4,14},{5,15},{6,12},{7,13},{8,2},{9,3},... | collective-permute-start | bytes 393224 | tf_op jit(solution)/shard_map/ppermute | solution.py:233
  108.3 3.3 %collective-permute-start.19 = (bf16[192,2048]{1,0:T(8,128)(2,1)S(1)}, bf16[192,2048]{1,0:T(8,128)(2,1)S(1)}, u32[]{:S(2)}, u32[]{:S(2)}) collective-permute-start(bf16[192,2048]{1,0:T(8,128)(2,1)S(1)} %collective-permute-done.18.refs_12_), channel_id=1, source_target_pairs={{0,1},{1,0},{2,3},{3,2},{4,5},{5,4},{6,7},{7,6},{8,9},{9,8},{10,11... | collective-permute-start | bytes 2359304 | tf_op jit(solution)/shard_map/ppermute | solution.py:233
  108.3 4.4 %collective-permute-start.23 = (bf16[192,2048]{1,0:T(8,128)(2,1)}, bf16[192,2048]{1,0:T(8,128)(2,1)S(1)}, u32[]{:S(2)}, u32[]{:S(2)}) collective-permute-start(bf16[192,2048]{1,0:T(8,128)(2,1)} %collective-permute-done.22.refs_16_), channel_id=1, source_target_pairs={{0,1},{1,0},{2,3},{3,2},{4,5},{5,4},{6,7},{7,6},{8,9},{9,8},{10,11... | collective-permute-start | bytes 2359304 | tf_op jit(solution)/shard_map/ppermute | solution.py:233
  108.9 4.0 %collective-permute-start.17 = (bf16[192,2048]{1,0:T(8,128)(2,1)S(1)}, bf16[192,2048]{1,0:T(8,128)(2,1)S(1)}, u32[]{:S(2)}, u32[]{:S(2)}) collective-permute-start(bf16[192,2048]{1,0:T(8,128)(2,1)S(1)} %collective-permute-done.16.refs_10_), channel_id=1, source_target_pairs={{0,1},{1,0},{2,3},{3,2},{4,5},{5,4},{6,7},{7,6},{8,9},{9,8},{10,11... | collective-permute-start | bytes 2359304 | tf_op jit(solution)/shard_map/ppermute | solution.py:233
  108.9 5.1 %collective-permute-start.21 = (bf16[192,2048]{1,0:T(8,128)(2,1)S(1)}, bf16[192,2048]{1,0:T(8,128)(2,1)S(1)}, u32[]{:S(2)}, u32[]{:S(2)}) collective-permute-start(bf16[192,2048]{1,0:T(8,128)(2,1)S(1)} %collective-permute-done.20.refs_14_), channel_id=1, source_target_pairs={{0,1},{1,0},{2,3},{3,2},{4,5},{5,4},{6,7},{7,6},{8,9},{9,8},{10,11... | collective-permute-start | bytes 2359304 | tf_op jit(solution)/shard_map/ppermute | solution.py:233
  109.4 5.7 %collective-permute-start.25 = (bf16[192,2048]{1,0:T(8,128)(2,1)S(1)}, bf16[192,2048]{1,0:T(8,128)(2,1)S(1)}, u32[]{:S(2)}, u32[]{:S(2)}) collective-permute-start(bf16[192,2048]{1,0:T(8,128)(2,1)S(1)} %collective-permute-done.24.refs_18_), channel_id=1, source_target_pairs={{0,1},{1,0},{2,3},{3,2},{4,5},{5,4},{6,7},{7,6},{8,9},{9,8},{10,11... | collective-permute-start | bytes 2359304 | tf_op jit(solution)/shard_map/ppermute | solution.py:233
  121.0 8.6 %collective-permute-start.26 = (bf16[32,2048]{1,0:T(8,128)(2,1)S(1)}, bf16[32,2048]{1,0:T(8,128)(2,1)S(1)}, u32[]{:S(2)}, u32[]{:S(2)}) collective-permute-start(bf16[32,2048]{1,0:T(8,128)(2,1)S(1)} %get-tuple-element.32), channel_id=1, source_target_pairs={{0,2},{1,3},{2,0},{3,1},{4,6},{5,7},{6,4},{7,5},{8,10},{9,11},{10,... | collective-permute-start | bytes 393224 | tf_op jit(solution)/shard_map/ppermute | solution.py:233
  123.8 6.9 %collective-permute-start.27 = (bf16[32,2048]{1,0:T(8,128)(2,1)S(1)}, bf16[32,2048]{1,0:T(8,128)(2,1)S(1)}, u32[]{:S(2)}, u32[]{:S(2)}) collective-permute-start(bf16[32,2048]{1,0:T(8,128)(2,1)S(1)} %get-tuple-element.33), channel_id=1, source_target_pairs={{0,8},{1,9},{2,10},{3,11},{4,12},{5,13},{6,14},{7,15},{8,0},{9,1},... | collective-permute-start | bytes 393224 | tf_op jit(solution)/shard_map/ppermute | solution.py:233
  123.8 10.3 %collective-permute-start.28 = (bf16[32,2048]{1,0:T(8,128)(2,1)S(1)}, bf16[32,2048]{1,0:T(8,128)(2,1)S(1)}, u32[]{:S(2)}, u32[]{:S(2)}) collective-permute-start(bf16[32,2048]{1,0:T(8,128)(2,1)S(1)} %get-tuple-element.34), channel_id=1, source_target_pairs={{0,10},{1,11},{2,8},{3,9},{4,14},{5,15},{6,12},{7,13},{8,2},{9,3},... | collective-permute-start | bytes 393224 | tf_op jit(solution)/shard_map/ppermute | solution.py:233
  125.3 9.4 %collective-permute-start.29 = (bf16[32,2048]{1,0:T(8,128)(2,1)S(1)}, bf16[32,2048]{1,0:T(8,128)(2,1)S(1)}, u32[]{:S(2)}, u32[]{:S(2)}) collective-permute-start(bf16[32,2048]{1,0:T(8,128)(2,1)S(1)} %get-tuple-element.35), channel_id=1, source_target_pairs={{0,16},{1,17},{2,18},{3,19},{4,20},{5,21},{6,22},{7,23},{8,24},{9,... | collective-permute-start | bytes 393224 | tf_op jit(solution)/shard_map/ppermute | solution.py:233
  127.4 17.6 %collective-permute-start.30 = (bf16[32,2048]{1,0:T(8,128)(2,1)S(1)}, bf16[32,2048]{1,0:T(8,128)(2,1)S(1)}, u32[]{:S(2)}, u32[]{:S(2)}) collective-permute-start(bf16[32,2048]{1,0:T(8,128)(2,1)S(1)} %get-tuple-element.36), channel_id=1, source_target_pairs={{0,18},{1,19},{2,16},{3,17},{4,22},{5,23},{6,20},{7,21},{8,26},{9,... | collective-permute-start | bytes 393224 | tf_op jit(solution)/shard_map/ppermute | solution.py:233
  129.6 18.9 %collective-permute-start.31 = (bf16[32,2048]{1,0:T(8,128)(2,1)S(1)}, bf16[32,2048]{1,0:T(8,128)(2,1)S(1)}, u32[]{:S(2)}, u32[]{:S(2)}) collective-permute-start(bf16[32,2048]{1,0:T(8,128)(2,1)S(1)} %get-tuple-element.37), channel_id=1, source_target_pairs={{0,24},{1,25},{2,26},{3,27},{4,28},{5,29},{6,30},{7,31},{8,16},{9,... | collective-permute-start | bytes 393224 | tf_op jit(solution)/shard_map/ppermute | solution.py:233
  130.7 20.1 %collective-permute-start.32 = (bf16[32,2048]{1,0:T(8,128)(2,1)S(1)}, bf16[32,2048]{1,0:T(8,128)(2,1)S(1)}, u32[]{:S(2)}, u32[]{:S(2)}) collective-permute-start(bf16[32,2048]{1,0:T(8,128)(2,1)S(1)} %get-tuple-element.38), channel_id=1, source_target_pairs={{0,26},{1,27},{2,24},{3,25},{4,30},{5,31},{6,28},{7,29},{8,18},{9,... | collective-permute-start | bytes 393224 | tf_op jit(solution)/shard_map/ppermute | solution.py:233
  (13 other events, 28.7 us)

commit v2 on v1

--- a/solution.py
+++ b/solution.py
@@ -233,21 +233,32 @@
     return lax.ppermute(array, AXES, pairs)
 
 
-def gather_pieces(weights):
-    def first(z, x, y, core):
-        return (z, x, y, 1 - core) if core == z % 2 else (z ^ 1, x, y, core)
-
-    def over_x(z, x, y, core):
-        return z, x ^ 1, y, core
-
-    def to_core(z, x, y, core):
-        return z, x, y, 1 - core
-
-    near = [move(w, first) for w in weights]
-    far = [move(w, over_x) for w in near]
-    near_twin = [move(w, to_core) for w in near]
-    far_twin = [move(w, to_core) for w in far]
-    return near, near_twin, far, far_twin
+def is_home(z, core):
+    return core == z % 2
+
+
+def to_twin(z, x, y, core):
+    return z, x, y, 1 - core
+
+
+def first_hop(z, x, y, core):
+    return (z, x ^ 1, y, 1 - core) if is_home(z, core) else (z ^ 1, x, y, core)
+
+
+def second_hop(z, x, y, core):
+    return (z, x ^ 1, y, core) if is_home(z, core) else None
+
+
+def home_to_twin(z, x, y, core):
+    return (z, x, y, 1 - core) if is_home(z, core) else None
+
+
+def pack_halves(gate, up, down):
+    half = gate.shape[0] // 2
+    return [
+        jnp.concatenate([w[k * half : (k + 1) * half] for w in (gate, up, down)], axis=0)
+        for k in range(2)
+    ]
 
 
 def slot_targets(ids_row, z_here, y_here, capacity):
@@ -325,39 +336,66 @@
         out_refs[k][...] = slots[k * capacity : (k + 1) * capacity]
 
 
-def expert_kernel(*refs):
-    row_refs, weight_refs, out_refs = refs[:8], refs[8:20], refs[20:28]
+def expert_kernel(where_ref, *refs):
+    row_refs, pack_refs, out_refs = refs[:8], refs[8:20], refs[20:28]
     gate_ref, up_ref, down_ref, semaphores = refs[28:]
-    piece = weight_refs[0].shape[0]
-    copies = []
-    for kind, target in enumerate((gate_ref, up_ref, down_ref)):
-        row_of = []
-        for j in range(PIECES):
-            copy = pltpu.make_async_copy(
-                weight_refs[kind * PIECES + j],
-                target.at[pl.ds(j * piece, piece)],
-                semaphores.at[kind, j],
+    own, own_twin, one, one_twin, last, last_twin = [pack_refs[2 * i : 2 * i + 2] for i in range(6)]
+    at_home = where_ref[3] == 1
+    away = jnp.logical_not(at_home)
+    strip = pack_refs[0].shape[0] // 3
+    targets = (gate_ref, up_ref, down_ref)
+
+    def copies_of(pair, place, kinds):
+        return [
+            pltpu.make_async_copy(
+                pair[h].at[pl.ds(kind * strip, strip)],
+                targets[kind].at[pl.ds((2 * place + h) * strip, strip)],
+                semaphores.at[kind, place, h],
             )
-            row_of.append(copy)
-        copies.append(row_of)
-    for j in range(PIECES):
-        copies[0][j].start()
-        copies[1][j].start()
-    for j in range(PIECES):
-        copies[2][j].start()
+            for kind in kinds
+            for h in range(2)
+        ]
+
+    def start(pair, place):
+        for copy in copies_of(pair, place, range(3)):
+            copy.start()
+
+    def wait(pair, place, kinds):
+        for copy in copies_of(pair, place, kinds):
+            copy.wait()
+
+    @pl.when(at_home)
+    def _():
+        start(own, 0)
+
+    @pl.when(away)
+    def _():
+        start(own_twin, 0)
+
+    start(one, 1)
+    start(one_twin, 2)
+
+    @pl.when(at_home)
+    def _():
+        start(last, 3)
+
+    @pl.when(away)
+    def _():
+        start(last_twin, 3)
+
     rows = jnp.concatenate([ref[...] for ref in row_refs], axis=0)
+    sources = (own, one, one_twin, last)
     actives = []
     for half in range(2):
-        span = slice(half * 2 * piece, (half + 1) * 2 * piece)
-        for j in (2 * half, 2 * half + 1):
-            copies[0][j].wait()
-            copies[1][j].wait()
+        span = slice(half * 4 * strip, (half + 1) * 4 * strip)
+        for place in (2 * half, 2 * half + 1):
+            wait(sources[place], place, (0, 1))
         gate_part = contract_rows(rows, gate_ref[span, :])
         up_part = contract_rows(rows, up_ref[span, :])
         silu = gate_part / (1.0 + jnp.exp(-gate_part))
         actives.append((silu * up_part).astype(jnp.bfloat16))
-    for j in range(PIECES):
-        copies[2][j].wait()
+    for place in range(PIECES):
+        wait(sources[place], place, (2,))
     active = jnp.concatenate(actives, axis=1)
     capacity = out_refs[0].shape[0]
     result = jnp.dot(active, down_ref[...], preferred_element_type=jnp.float32).astype(jnp.bfloat16)
@@ -394,20 +432,38 @@
 ):
     ctx_here = lax.axis_index("ctx")
     exp_here = lax.axis_index("exp")
-    where = jnp.stack([ctx_here, ctx_here // 2, exp_here // 2]).astype(jnp.int32)
+    home = ((ctx_here // 2) % 2 == exp_here % 2).astype(jnp.int32)
+    where = jnp.stack([ctx_here, ctx_here // 2, exp_here // 2, home]).astype(jnp.int32)
     tokens, width = residual.shape[1:]
     piece = gate_weight.shape[2]
     capacity = max(2, 2 * tokens * TOPK // 8)
     ids_row = expert_ids[0].reshape(1, tokens)
     kv_own = jnp.concatenate([key_states[0], value_states[0]], axis=1)
-    kv_blocks = [kv_own]
-    for k in range(1, 8):
-        def later(z, x, y, core, k=k):
+    kv_blocks = {0: kv_own}
+
+    def send_keys(block, k):
+        def later(z, x, y, core):
             ctx = 2 * z + x + k
             return (ctx // 2, ctx % 2, y, core) if ctx < 8 else None
 
-        kv_blocks.append(move(kv_own, later))
-    near, near_twin, far, far_twin = gather_pieces([gate_weight[0, 0], up_weight[0, 0], down_weight[0, 0]])
+        kv_blocks[k] = move(block, later)
+
+    own = pack_halves(gate_weight[0, 0], up_weight[0, 0], down_weight[0, 0])
+    for k in (7, 6):
+        send_keys(kv_own, k)
+    own[0], own[1], kv_blocks[7], kv_blocks[6], kv_next = lax.optimization_barrier(
+        (own[0], own[1], kv_blocks[7], kv_blocks[6], kv_own)
+    )
+    one_first = move(own[0], first_hop)
+    for k in (4, 5, 3, 2, 1):
+        send_keys(kv_next, k)
+    kv_list = [kv_blocks[k] for k in range(1, 8)]
+    one_first, own[0], own[1], *kv_list = lax.optimization_barrier(
+        (one_first, own[0], own[1], *kv_list)
+    )
+    one_second = move(own[1], first_hop)
+    own_twin = [move(w, home_to_twin) for w in own]
+    twin_first = move(one_first, to_twin)
     slot_shape = jax.ShapeDtypeStruct((capacity, width), jnp.bfloat16)
     keys_all = 8 * tokens
     first_out = pl.pallas_call(
@@ -421,51 +477,59 @@
             pltpu.VMEM((tokens, keys_all), jnp.float32),
             pltpu.VMEM((tokens, width), jnp.bfloat16),
         ],
-        compiler_params=pltpu.CompilerParams(vmem_limit_bytes=40 << 20),
+        compiler_params=pltpu.CompilerParams(vmem_limit_bytes=16 << 20),
         cost_estimate=pl.CostEstimate(
             flops=4 * tokens * keys_all * HEADS * HD,
             bytes_accessed=8 * tokens * width,
             transcendentals=tokens * keys_all * HEADS,
         ),
         name="attend",
-    )(where, ids_row, queries[0], residual[0], *kv_blocks)
-    summed, outgoing = first_out[0], first_out[1:]
+    )(where, ids_row, queries[0], residual[0], kv_own, *kv_list)
+    summed, outgoing = first_out[0], list(first_out[1:])
 
     def swap(array, k):
         if k == 0:
             return array
         return move(array, lambda z, x, y, core: (z ^ (k >> 1), x, y ^ (k & 1), core))
 
-    arrived = [swap(outgoing[k], k) for k in range(8)]
-    pieces = []
-    for kind in range(3):
-        pieces += [near[kind], near_twin[kind], far[kind], far_twin[kind]]
+    early, late = (4, 2, 3, 1), (5, 6, 7)
+    held = lax.optimization_barrier((*outgoing, *own_twin, twin_first))
+    outgoing, own_twin, twin_first = list(held[:8]), list(held[8:10]), held[10]
+    arrived = [swap(outgoing[k], k) if k in early else outgoing[k] for k in range(8)]
+    one_first, one_second, *arrived = lax.optimization_barrier((one_first, one_second, *arrived))
+    one = [one_first, one_second]
+    last = [move(w, second_hop) for w in one]
+    arrived = [swap(arrived[k], k) if k in late else arrived[k] for k in range(8)]
+    last[0], one[1], *arrived = lax.optimization_barrier((last[0], one[1], *arrived))
+    one_twin = [twin_first, move(one[1], to_twin)]
+    last_twin = [move(w, home_to_twin) for w in last]
+    packs = own + own_twin + one + one_twin + last + last_twin
     results = pl.pallas_call(
         expert_kernel,
         out_shape=[slot_shape] * 8,
-        in_specs=[IN_VMEM] * 8 + [ANYWHERE] * 12,
+        in_specs=[IN_SMEM] + [IN_VMEM] * 8 + [ANYWHERE] * 12,
         out_specs=[IN_VMEM] * 8,
         scratch_shapes=[
             pltpu.VMEM((PIECES * piece, width), jnp.bfloat16),
             pltpu.VMEM((PIECES * piece, width), jnp.bfloat16),
             pltpu.VMEM((PIECES * piece, width), jnp.bfloat16),
-            pltpu.SemaphoreType.DMA((3, PIECES)),
+            pltpu.SemaphoreType.DMA((3, PIECES, 2)),
         ],
-        compiler_params=pltpu.CompilerParams(vmem_limit_bytes=48 << 20),
+        compiler_params=pltpu.CompilerParams(vmem_limit_bytes=24 << 20),
         cost_estimate=pl.CostEstimate(
             flops=6 * 8 * capacity * PIECES * piece * width,
             bytes_accessed=6 * PIECES * piece * width,
             transcendentals=8 * capacity * PIECES * piece,
         ),
         name="experts",
-    )(*arrived, *pieces)
+    )(where, *[arrived[k] for k in range(8)], *packs)
     returned = [swap(results[k], k) for k in range(8)]
     output = pl.pallas_call(
         combine_kernel,
         out_shape=jax.ShapeDtypeStruct((tokens, width), jnp.bfloat16),
         in_specs=[IN_SMEM] + [IN_VMEM] * 11,
         out_specs=IN_VMEM,
-        compiler_params=pltpu.CompilerParams(vmem_limit_bytes=24 << 20),
+        compiler_params=pltpu.CompilerParams(vmem_limit_bytes=10 << 20),
         cost_estimate=pl.CostEstimate(
             flops=2 * tokens * 8 * capacity * width,
             bytes_accessed=12 * tokens * width,

time: 153 us -> 157 us (1.026)
  starting transfers between devices: 76.9 us -> 62.9 us
  local copies, waits for them, and re-layouts: 5.32 us -> 19 us
  Pallas kernels: 12 us -> 14.5 us
    ppermute x33 -> x31, starting transfers between devices: 76.9 us -> 62.9 us  [move(): return lax.ppermute(array, AXES, pairs)]
    unnamed x24 -> x52, local copies, waits for them, and re-layouts: 5.21 us -> 17.7 us
    pallas_call x1, Pallas kernels: 4.95 us -> 7.47 us  [shards_cube(): pl.pallas_call(expert_kernel, out_shape=[slot_shape] * 8, in_specs=[IN_SM...]
    ppermute x33 -> x31, waiting for transfers between devices: 57.2 us -> 57.4 us  [move(): return lax.ppermute(array, AXES, pairs)]
  transfers between devices with their start and end apart: 33 -> 31, of which waited for: 17 -> 16; matrix products, arithmetic and copies ran while one was open for 1% -> 1% of each run, Pallas kernels for 3% -> 3%
where the time goes in v2:
time: 157 us; the launch traced here: 156 us
  starting transfers between devices  62.9 us (40%)
  waiting for transfers between devices  57.4 us (37%)
  local copies, waits for them, and re-layouts  19 us (12%)
  Pallas kernels  14.5 us (9%)
    ppermute x31, starting transfers between devices, move(): return lax.ppermute(array, AXES, pairs)  62.9 us
    ppermute x31, waiting for transfers between devices, move(): return lax.ppermute(array, AXES, pairs)  57.4 us
    unnamed x52, local copies, waits for them, and re-layouts  17.7 us
    pallas_call x1, Pallas kernels, shards_cube(): pl.pallas_call(expert_kernel, out_shape=[slot_shape] * 8, in_specs=[IN_SM...  7.47 us
    pallas_call x1, Pallas kernels, shards_cube(): pl.pallas_call(attend_kernel, out_shape=[jax.ShapeDtypeStruct((tokens, wi...  5.22 us
  transfers between devices with their start and end apart: 31, of which 16 were waited for; matrix products, arithmetic and copies ran while one was open for 1% of the time, Pallas kernels for 3%

profile of v2, /device:TPU:8, one launch (start us, length us, event | category | flops | bytes accessed | tf_op | source)
XLA Modules:
  0.0 155.5 jit_solution(1964352486410203205)
XLA Ops:
  5.4 8.8 %collective-permute-start.2 = (bf16[288,2048]{1,0:T(8,128)(2,1)S(1)}, bf16[288,2048]{1,0:T(8,128)(2,1)S(1)}, u32[]{:S(2)}, u32[]{:S(2)}) collective-permute-start(bf16[288,2048]{1,0:T(8,128)(2,1)S(1)} %get-tuple-element.91.refs_8_), channel_id=1, source_target_pairs={{0,5},{1,9},{2,7},{3,11},{4,1},{5,13},{6,3},{7,15},{8,0},{9,12},{1... | collective-permute-start | bytes 3538952 | tf_op jit(solution)/shard_map/ppermute | solution.py:233
  14.2 1.9 %collective-permute-start.3 = (bf16[128,512]{1,0:T(8,128)(2,1)S(1)}, bf16[128,512]{1,0:T(8,128)(2,1)S(1)}, u32[]{:S(2)}, u32[]{:S(2)}) collective-permute-start(bf16[128,512]{1,0:T(8,128)(2,1)S(1)} %pad_maximum_fusion.2.refs_0_), channel_id=1, source_target_pairs={{0,4},{1,5},{2,6},{3,7},{4,8},{5,9},{6,10},{7,11},{8,12},{9,13},{1... | collective-permute-start | bytes 393224 | tf_op jit(solution)/shard_map/ppermute | solution.py:233
  16.1 1.9 %collective-permute-start.4 = (bf16[128,512]{1,0:T(8,128)(2,1)S(1)}, bf16[128,512]{1,0:T(8,128)(2,1)S(1)}, u32[]{:S(2)}, u32[]{:S(2)}) collective-permute-start(bf16[128,512]{1,0:T(8,128)(2,1)S(1)} %pad_maximum_fusion.2.refs_0_), channel_id=1, source_target_pairs={{0,8},{1,9},{2,10},{3,11},{4,12},{5,13},{6,14},{7,15},{8,16},{9,17... | collective-permute-start | bytes 393224 | tf_op jit(solution)/shard_map/ppermute | solution.py:233
  18.1 6.2 %collective-permute-start.5 = (bf16[128,512]{1,0:T(8,128)(2,1)S(1)}, bf16[128,512]{1,0:T(8,128)(2,1)S(1)}, u32[]{:S(2)}, u32[]{:S(2)}) collective-permute-start(bf16[128,512]{1,0:T(8,128)(2,1)S(1)} %pad_maximum_fusion.2.refs_0_), channel_id=1, source_target_pairs={{0,12},{1,13},{2,14},{3,15},{4,16},{5,17},{6,18},{7,19},{8,20},{9,... | collective-permute-start | bytes 393224 | tf_op jit(solution)/shard_map/ppermute | solution.py:233
  26.2 1.6 %collective-permute-start.7 = (bf16[128,512]{1,0:T(8,128)(2,1)S(1)}, bf16[128,512]{1,0:T(8,128)(2,1)S(1)}, u32[]{:S(2)}, u32[]{:S(2)}) collective-permute-start(bf16[128,512]{1,0:T(8,128)(2,1)S(1)} %pad_maximum_fusion.2.refs_0_), channel_id=1, source_target_pairs={{0,20},{1,21},{2,22},{3,23},{4,24},{5,25},{6,26},{7,27},{8,28},{9,... | collective-permute-start | bytes 393224 | tf_op jit(solution)/shard_map/ppermute | solution.py:233
  29.2 1.6 %collective-permute-done.6.refs_4_ = bf16[128,512]{1,0:T(8,128)(2,1)S(1)} collective-permute-done((bf16[128,512]{1,0:T(8,128)(2,1)S(1)}, bf16[128,512]{1,0:T(8,128)(2,1)S(1)}, u32[]{:S(2)}, u32[]{:S(2)}) %collective-permute-start.6) | collective-permute-done | bytes 131104 | tf_op jit(solution)/shard_map/ppermute | solution.py:233
  31.4 4.5 %collective-permute-done.7.refs_5_ = bf16[128,512]{1,0:T(8,128)(2,1)S(1)} collective-permute-done((bf16[128,512]{1,0:T(8,128)(2,1)S(1)}, bf16[128,512]{1,0:T(8,128)(2,1)S(1)}, u32[]{:S(2)}, u32[]{:S(2)}) %collective-permute-start.7) | collective-permute-done | bytes 131104 | tf_op jit(solution)/shard_map/ppermute | solution.py:233
  37.9 8.6 %collective-permute-start.11 = (bf16[288,2048]{1,0:T(8,128)(2,1)S(1)}, bf16[288,2048]{1,0:T(8,128)(2,1)}, u32[]{:S(2)}, u32[]{:S(2)}) collective-permute-start(bf16[288,2048]{1,0:T(8,128)(2,1)S(1)} %collective-permute-done.2.refs_12_), channel_id=1, source_target_pairs={{0,1},{1,0},{2,3},{3,2},{4,5},{5,4},{6,7},{7,6},{8,9},{9,8},{10,11... | collective-permute-start | bytes 3538952 | tf_op jit(solution)/shard_map/ppermute | solution.py:233
  47.8 2.3 %collective-permute-start.8 = (bf16[288,2048]{1,0:T(8,128)(2,1)S(1)}, bf16[288,2048]{1,0:T(8,128)(2,1)}, u32[]{:S(2)}, u32[]{:S(2)}) collective-permute-start(bf16[288,2048]{1,0:T(8,128)(2,1)S(1)} %get-tuple-element.82.refs_9_), channel_id=1, source_target_pairs={{0,5},{1,9},{2,7},{3,11},{4,1},{5,13},{6,3},{7,15},{8,0},{9,12},{1... | collective-permute-start | bytes 3538952 | tf_op jit(solution)/shard_map/ppermute | solution.py:233
  59.5 5.2 %attend.1 = (f32[128,2048]{1,0:T(8,128)S(1)}, bf16[32,2048]{1,0:T(8,128)(2,1)S(1)}, bf16[32,2048]{1,0:T(8,128)(2,1)S(1)}, bf16[32,2048]{1,0:T(8,128)(2,1)S(1)}, ...) custom-call(s32[4]{0:T(128)S(1)} %pad_add_fusion.where_ref, ...), custom_call_target="tpu_custom_call" | custom-call | flops 1073741824 | bytes 2097152 | tf_op jit(solution)/shard_map/attend/pallas_call | solution.py:469
  65.7 1.6 %collective-permute-start.12 = (bf16[32,2048]{1,0:T(8,128)(2,1)S(1)}, bf16[32,2048]{1,0:T(8,128)(2,1)S(1)}, u32[]{:S(2)}, u32[]{:S(2)}) collective-permute-start(bf16[32,2048]{1,0:T(8,128)(2,1)S(1)} %get-tuple-element.93), channel_id=1, source_target_pairs={{0,2},{1,3},{2,0},{3,1},{4,6},{5,7},{6,4},{7,5},{8,10},{9,11},{10,... | collective-permute-start | bytes 393224 | tf_op jit(solution)/shard_map/ppermute | solution.py:233
  67.3 1.5 collective-permute-start.13
  69.3 2.7 %collective-permute-start.15 = (bf16[32,2048]{1,0:T(8,128)(2,1)S(1)}, bf16[32,2048]{1,0:T(8,128)(2,1)S(1)}, u32[]{:S(2)}, u32[]{:S(2)}) collective-permute-start(bf16[32,2048]{1,0:T(8,128)(2,1)S(1)} %get-tuple-element.96), channel_id=1, source_target_pairs={{0,16},{1,17},{2,18},{3,19},{4,20},{5,21},{6,22},{7,23},{8,24},{9,... | collective-permute-start | bytes 393224 | tf_op jit(solution)/shard_map/ppermute | solution.py:233
  72.0 1.8 %collective-permute-done.13.refs_2_ = bf16[32,2048]{1,0:T(8,128)(2,1)S(1)} collective-permute-done((bf16[32,2048]{1,0:T(8,128)(2,1)S(1)}, bf16[32,2048]{1,0:T(8,128)(2,1)S(1)}, u32[]{:S(2)}, u32[]{:S(2)}) %collective-permute-start.13) | collective-permute-done | bytes 131104 | tf_op jit(solution)/shard_map/ppermute | solution.py:233
  73.7 3.5 %collective-permute-done.14.refs_3_ = bf16[32,2048]{1,0:T(8,128)(2,1)S(1)} collective-permute-done((bf16[32,2048]{1,0:T(8,128)(2,1)S(1)}, bf16[32,2048]{1,0:T(8,128)(2,1)S(1)}, u32[]{:S(2)}, u32[]{:S(2)}) %collective-permute-start.14) | collective-permute-done | bytes 131104 | tf_op jit(solution)/shard_map/ppermute | solution.py:233
  77.2 1.3 collective-permute-done.15.refs_4_
  80.0 4.2 %collective-permute-start.17 = (bf16[32,2048]{1,0:T(8,128)(2,1)S(1)}, bf16[32,2048]{1,0:T(8,128)(2,1)S(1)}, u32[]{:S(2)}, u32[]{:S(2)}) collective-permute-start(bf16[32,2048]{1,0:T(8,128)(2,1)S(1)} %get-tuple-element.107), channel_id=1, source_target_pairs={{0,18},{1,19},{2,16},{3,17},{4,22},{5,23},{6,20},{7,21},{8,26},{9,... | collective-permute-start | bytes 393224 | tf_op jit(solution)/shard_map/ppermute | solution.py:233
  84.3 3.7 %collective-permute-start.18 = (bf16[32,2048]{1,0:T(8,128)(2,1)S(1)}, bf16[32,2048]{1,0:T(8,128)(2,1)S(1)}, u32[]{:S(2)}, u32[]{:S(2)}) collective-permute-start(bf16[32,2048]{1,0:T(8,128)(2,1)S(1)} %get-tuple-element.108), channel_id=1, source_target_pairs={{0,24},{1,25},{2,26},{3,27},{4,28},{5,29},{6,30},{7,31},{8,16},{9,... | collective-permute-start | bytes 393224 | tf_op jit(solution)/shard_map/ppermute | solution.py:233
  88.0 13.9 %collective-permute-done.18.refs_6_ = bf16[32,2048]{1,0:T(8,128)(2,1)S(1)} collective-permute-done((bf16[32,2048]{1,0:T(8,128)(2,1)S(1)}, bf16[32,2048]{1,0:T(8,128)(2,1)S(1)}, u32[]{:S(2)}, u32[]{:S(2)}) %collective-permute-start.18) | collective-permute-done | bytes 131104 | tf_op jit(solution)/shard_map/ppermute | solution.py:233
  101.9 1.6 %collective-permute-done.19.refs_7_ = bf16[32,2048]{1,0:T(8,128)(2,1)S(1)} collective-permute-done((bf16[32,2048]{1,0:T(8,128)(2,1)S(1)}, bf16[32,2048]{1,0:T(8,128)(2,1)S(1)}, u32[]{:S(2)}, u32[]{:S(2)}) %collective-permute-start.19) | collective-permute-done | bytes 131104 | tf_op jit(solution)/shard_map/ppermute | solution.py:233
  106.6 1.7 %collective-permute-done.22.refs_18_ = bf16[288,2048]{1,0:T(8,128)(2,1)S(1)} collective-permute-done((bf16[288,2048]{1,0:T(8,128)(2,1)S(1)}, bf16[288,2048]{1,0:T(8,128)(2,1)S(1)}, u32[]{:S(2)}, u32[]{:S(2)}) %collective-permute-start.22) | collective-permute-done | bytes 1179680 | tf_op jit(solution)/shard_map/ppermute | solution.py:233
  108.2 5.3 %collective-permute-done.23.refs_19_ = bf16[288,2048]{1,0:T(8,128)(2,1)S(1)} collective-permute-done((bf16[288,2048]{1,0:T(8,128)(2,1)S(1)}, bf16[288,2048]{1,0:T(8,128)(2,1)S(1)}, u32[]{:S(2)}, u32[]{:S(2)}) %collective-permute-start.23) | collective-permute-done | bytes 1179680 | tf_op jit(solution)/shard_map/ppermute | solution.py:233
  113.5 7.5 %experts.1 = (bf16[32,2048]{1,0:T(8,128)(2,1)S(1)}, bf16[32,2048]{1,0:T(8,128)(2,1)S(1)}, bf16[32,2048]{1,0:T(8,128)(2,1)S(1)}, bf16[32,2048]{1,0:T(8,128)(2,1)}...) custom-call(s32[4]{0:T(128)S(1)} %pad_add_fusion.where_ref, ...), custom_call_target="tpu_custom_call" | custom-call | flops 2415919104 | bytes 9437184 | tf_op jit(solution)/shard_map/experts/pallas_call | solution.py:507
  122.7 2.4 %collective-permute-start.25 = (bf16[32,2048]{1,0:T(8,128)(2,1)S(1)}, bf16[32,2048]{1,0:T(8,128)(2,1)S(1)}, u32[]{:S(2)}, u32[]{:S(2)}) collective-permute-start(bf16[32,2048]{1,0:T(8,128)(2,1)S(1)} %get-tuple-element.125), channel_id=1, source_target_pairs={{0,8},{1,9},{2,10},{3,11},{4,12},{5,13},{6,14},{7,15},{8,0},{9,1},... | collective-permute-start | bytes 393224 | tf_op jit(solution)/shard_map/ppermute | solution.py:233
  125.1 1.6 %collective-permute-start.27 = (bf16[32,2048]{1,0:T(8,128)(2,1)}, bf16[32,2048]{1,0:T(8,128)(2,1)S(1)}, u32[]{:S(2)}, u32[]{:S(2)}) collective-permute-start(bf16[32,2048]{1,0:T(8,128)(2,1)} %get-tuple-element.127), channel_id=1, source_target_pairs={{0,16},{1,17},{2,18},{3,19},{4,20},{5,21},{6,22},{7,23},{8,24},{9,... | collective-permute-start | bytes 393224 | tf_op jit(solution)/shard_map/ppermute | solution.py:233
  126.7 2.2 %collective-permute-start.28 = (bf16[32,2048]{1,0:T(8,128)(2,1)}, bf16[32,2048]{1,0:T(8,128)(2,1)S(1)}, u32[]{:S(2)}, u32[]{:S(2)}) collective-permute-start(bf16[32,2048]{1,0:T(8,128)(2,1)} %get-tuple-element.128), channel_id=1, source_target_pairs={{0,18},{1,19},{2,16},{3,17},{4,22},{5,23},{6,20},{7,21},{8,26},{9,... | collective-permute-start | bytes 393224 | tf_op jit(solution)/shard_map/ppermute | solution.py:233
  129.7 2.7 %collective-permute-done.25.refs_2_ = bf16[32,2048]{1,0:T(8,128)(2,1)S(1)} collective-permute-done((bf16[32,2048]{1,0:T(8,128)(2,1)S(1)}, bf16[32,2048]{1,0:T(8,128)(2,1)S(1)}, u32[]{:S(2)}, u32[]{:S(2)}) %collective-permute-start.25) | collective-permute-done | bytes 131104 | tf_op jit(solution)/shard_map/ppermute | solution.py:233
  132.5 1.6 %collective-permute-done.26.refs_3_ = bf16[32,2048]{1,0:T(8,128)(2,1)S(1)} collective-permute-done((bf16[32,2048]{1,0:T(8,128)(2,1)}, bf16[32,2048]{1,0:T(8,128)(2,1)S(1)}, u32[]{:S(2)}, u32[]{:S(2)}) %collective-permute-start.26) | collective-permute-done | bytes 131104 | tf_op jit(solution)/shard_map/ppermute | solution.py:233
  135.4 9.5 %collective-permute-done.28.refs_5_ = bf16[32,2048]{1,0:T(8,128)(2,1)S(1)} collective-permute-done((bf16[32,2048]{1,0:T(8,128)(2,1)}, bf16[32,2048]{1,0:T(8,128)(2,1)S(1)}, u32[]{:S(2)}, u32[]{:S(2)}) %collective-permute-start.28) | collective-permute-done | bytes 131104 | tf_op jit(solution)/shard_map/ppermute | solution.py:233
  144.9 4.8 %collective-permute-done.29.refs_6_ = bf16[32,2048]{1,0:T(8,128)(2,1)S(1)} collective-permute-done((bf16[32,2048]{1,0:T(8,128)(2,1)}, bf16[32,2048]{1,0:T(8,128)(2,1)S(1)}, u32[]{:S(2)}, u32[]{:S(2)}) %collective-permute-start.29) | collective-permute-done | bytes 131104 | tf_op jit(solution)/shard_map/ppermute | solution.py:233
  149.7 1.9 %collective-permute-done.30.refs_7_ = bf16[32,2048]{1,0:T(8,128)(2,1)S(1)} collective-permute-done((bf16[32,2048]{1,0:T(8,128)(2,1)}, bf16[32,2048]{1,0:T(8,128)(2,1)S(1)}, u32[]{:S(2)}, u32[]{:S(2)}) %collective-permute-start.30) | collective-permute-done | bytes 131104 | tf_op jit(solution)/shard_map/ppermute | solution.py:233
  153.7 1.8 %combine.1 = bf16[128,2048]{1,0:T(8,128)(2,1)} custom-call(s32[4]{0:T(128)S(1)} %pad_add_fusion.where_ref, s32[1,128]{1,0:T(1,128)S(1)} %bitcast.24, f32[128,1]{1,0:T(8,128)S(1)} %copy.10.route_ref, f32[128,2048]{1,0:T(8,128)S(1)} %copy-done.1, bf16[32,2048]{1,0:T(8,128)(2,1)S(1)} %copy-done.3, bf16[32,2048]{1,0:T(8,128)(2,1)S(1)} %collective-permute-done.24.refs_1_, ...), custom_call_target="tpu_custom_call" | custom-call | flops 134217728 | bytes 3145728 | tf_op jit(solution)/shard_map/combine/pallas_call | solution.py:527
  (92 shorter events, 33.9 us)
Async XLA Ops:
  1.0 3.1 %collective-permute-start = (bf16[128,512]{1,0:T(8,128)(2,1)S(1)}, bf16[128,512]{1,0:T(8,128)(2,1)S(1)}, u32[]{:S(2)}, u32[]{:S(2)}) collective-permute-start(bf16[128,512]{1,0:T(8,128)(2,1)S(1)} %pad_maximum_fusion.2.refs_0_), channel_id=1, source_target_pairs={{0,28},{1,29},{2,30},{3,31}} | collective-permute-start | bytes 393224 | tf_op jit(solution)/shard_map/ppermute | solution.py:233
  1.8 2.9 %collective-permute-start.1 = (bf16[128,512]{1,0:T(8,128)(2,1)S(1)}, bf16[128,512]{1,0:T(8,128)(2,1)S(1)}, u32[]{:S(2)}, u32[]{:S(2)}) collective-permute-start(bf16[128,512]{1,0:T(8,128)(2,1)S(1)} %pad_maximum_fusion.2.refs_0_), channel_id=1, source_target_pairs={{0,24},{1,25},{2,26},{3,27},{4,28},{5,29},{6,30},{7,31}} | collective-permute-start | bytes 393224 | tf_op jit(solution)/shard_map/ppermute | solution.py:233
  5.4 31.2 %collective-permute-start.2 = (bf16[288,2048]{1,0:T(8,128)(2,1)S(1)}, bf16[288,2048]{1,0:T(8,128)(2,1)S(1)}, u32[]{:S(2)}, u32[]{:S(2)}) collective-permute-start(bf16[288,2048]{1,0:T(8,128)(2,1)S(1)} %get-tuple-element.91.refs_8_), channel_id=1, source_target_pairs={{0,5},{1,9},{2,7},{3,11},{4,1},{5,13},{6,3},{7,15},{8,0},{9,12},{1... | collective-permute-start | bytes 3538952 | tf_op jit(solution)/shard_map/ppermute | solution.py:233
  14.2 11.3 %collective-permute-start.3 = (bf16[128,512]{1,0:T(8,128)(2,1)S(1)}, bf16[128,512]{1,0:T(8,128)(2,1)S(1)}, u32[]{:S(2)}, u32[]{:S(2)}) collective-permute-start(bf16[128,512]{1,0:T(8,128)(2,1)S(1)} %pad_maximum_fusion.2.refs_0_), channel_id=1, source_target_pairs={{0,4},{1,5},{2,6},{3,7},{4,8},{5,9},{6,10},{7,11},{8,12},{9,13},{1... | collective-permute-start | bytes 393224 | tf_op jit(solution)/shard_map/ppermute | solution.py:233
  16.1 11.7 %collective-permute-start.4 = (bf16[128,512]{1,0:T(8,128)(2,1)S(1)}, bf16[128,512]{1,0:T(8,128)(2,1)S(1)}, u32[]{:S(2)}, u32[]{:S(2)}) collective-permute-start(bf16[128,512]{1,0:T(8,128)(2,1)S(1)} %pad_maximum_fusion.2.refs_0_), channel_id=1, source_target_pairs={{0,8},{1,9},{2,10},{3,11},{4,12},{5,13},{6,14},{7,15},{8,16},{9,17... | collective-permute-start | bytes 393224 | tf_op jit(solution)/shard_map/ppermute | solution.py:233
  18.1 10.4 %collective-permute-start.5 = (bf16[128,512]{1,0:T(8,128)(2,1)S(1)}, bf16[128,512]{1,0:T(8,128)(2,1)S(1)}, u32[]{:S(2)}, u32[]{:S(2)}) collective-permute-start(bf16[128,512]{1,0:T(8,128)(2,1)S(1)} %pad_maximum_fusion.2.refs_0_), channel_id=1, source_target_pairs={{0,12},{1,13},{2,14},{3,15},{4,16},{5,17},{6,18},{7,19},{8,20},{9,... | collective-permute-start | bytes 393224 | tf_op jit(solution)/shard_map/ppermute | solution.py:233
  24.3 6.5 %collective-permute-start.6 = (bf16[128,512]{1,0:T(8,128)(2,1)S(1)}, bf16[128,512]{1,0:T(8,128)(2,1)S(1)}, u32[]{:S(2)}, u32[]{:S(2)}) collective-permute-start(bf16[128,512]{1,0:T(8,128)(2,1)S(1)} %pad_maximum_fusion.2.refs_0_), channel_id=1, source_target_pairs={{0,16},{1,17},{2,18},{3,19},{4,20},{5,21},{6,22},{7,23},{8,24},{9,... | collective-permute-start | bytes 393224 | tf_op jit(solution)/shard_map/ppermute | solution.py:233
  26.2 9.7 %collective-permute-start.7 = (bf16[128,512]{1,0:T(8,128)(2,1)S(1)}, bf16[128,512]{1,0:T(8,128)(2,1)S(1)}, u32[]{:S(2)}, u32[]{:S(2)}) collective-permute-start(bf16[128,512]{1,0:T(8,128)(2,1)S(1)} %pad_maximum_fusion.2.refs_0_), channel_id=1, source_target_pairs={{0,20},{1,21},{2,22},{3,23},{4,24},{5,25},{6,26},{7,27},{8,28},{9,... | collective-permute-start | bytes 393224 | tf_op jit(solution)/shard_map/ppermute | solution.py:233
  36.6 29.1 %collective-permute-start.10 = (bf16[288,2048]{1,0:T(8,128)(2,1)S(1)}, bf16[288,2048]{1,0:T(8,128)(2,1)}, u32[]{:S(2)}, u32[]{:S(2)}) collective-permute-start(bf16[288,2048]{1,0:T(8,128)(2,1)S(1)} %get-tuple-element.82.refs_9_), channel_id=1, source_target_pairs={{0,1},{2,3},{4,5},{6,7},{9,8},{11,10},{13,12},{15,14},{16,17},{18,... | collective-permute-start | bytes 3538952 | tf_op jit(solution)/shard_map/ppermute | solution.py:233
  37.9 27.8 %collective-permute-start.11 = (bf16[288,2048]{1,0:T(8,128)(2,1)S(1)}, bf16[288,2048]{1,0:T(8,128)(2,1)}, u32[]{:S(2)}, u32[]{:S(2)}) collective-permute-start(bf16[288,2048]{1,0:T(8,128)(2,1)S(1)} %collective-permute-done.2.refs_12_), channel_id=1, source_target_pairs={{0,1},{1,0},{2,3},{3,2},{4,5},{5,4},{6,7},{7,6},{8,9},{9,8},{10,11... | collective-permute-start | bytes 3538952 | tf_op jit(solution)/shard_map/ppermute | solution.py:233
  46.5 19.2 %collective-permute-start.9 = (bf16[288,2048]{1,0:T(8,128)(2,1)S(1)}, bf16[288,2048]{1,0:T(8,128)(2,1)}, u32[]{:S(2)}, u32[]{:S(2)}) collective-permute-start(bf16[288,2048]{1,0:T(8,128)(2,1)S(1)} %get-tuple-element.91.refs_8_), channel_id=1, source_target_pairs={{0,1},{2,3},{4,5},{6,7},{9,8},{11,10},{13,12},{15,14},{16,17},{18,... | collective-permute-start | bytes 3538952 | tf_op jit(solution)/shard_map/ppermute | solution.py:233
  47.8 24.1 %collective-permute-start.8 = (bf16[288,2048]{1,0:T(8,128)(2,1)S(1)}, bf16[288,2048]{1,0:T(8,128)(2,1)}, u32[]{:S(2)}, u32[]{:S(2)}) collective-permute-start(bf16[288,2048]{1,0:T(8,128)(2,1)S(1)} %get-tuple-element.82.refs_9_), channel_id=1, source_target_pairs={{0,5},{1,9},{2,7},{3,11},{4,1},{5,13},{6,3},{7,15},{8,0},{9,12},{1... | collective-permute-start | bytes 3538952 | tf_op jit(solution)/shard_map/ppermute | solution.py:233
  65.7 66.7 %copy-start.25 = (f32[1,128,1]{1,2,0:T(1,128)S(1)}, f32[1,128,1]{1,2,0:T(1,128)}, u32[]{:S(2)}) copy-start(f32[1,128,1]{1,2,0:T(1,128)} %param.14) | copy-start | bytes 1540
  65.7 6.3 %collective-permute-start.12 = (bf16[32,2048]{1,0:T(8,128)(2,1)S(1)}, bf16[32,2048]{1,0:T(8,128)(2,1)S(1)}, u32[]{:S(2)}, u32[]{:S(2)}) collective-permute-start(bf16[32,2048]{1,0:T(8,128)(2,1)S(1)} %get-tuple-element.93), channel_id=1, source_target_pairs={{0,2},{1,3},{2,0},{3,1},{4,6},{5,7},{6,4},{7,5},{8,10},{9,11},{10,... | collective-permute-start | bytes 393224 | tf_op jit(solution)/shard_map/ppermute | solution.py:233
  67.3 6.4 %collective-permute-start.13 = (bf16[32,2048]{1,0:T(8,128)(2,1)S(1)}, bf16[32,2048]{1,0:T(8,128)(2,1)S(1)}, u32[]{:S(2)}, u32[]{:S(2)}) collective-permute-start(bf16[32,2048]{1,0:T(8,128)(2,1)S(1)} %get-tuple-element.94), channel_id=1, source_target_pairs={{0,8},{1,9},{2,10},{3,11},{4,12},{5,13},{6,14},{7,15},{8,0},{9,1},... | collective-permute-start | bytes 393224 | tf_op jit(solution)/shard_map/ppermute | solution.py:233
  68.8 8.4 %collective-permute-start.14 = (bf16[32,2048]{1,0:T(8,128)(2,1)S(1)}, bf16[32,2048]{1,0:T(8,128)(2,1)S(1)}, u32[]{:S(2)}, u32[]{:S(2)}) collective-permute-start(bf16[32,2048]{1,0:T(8,128)(2,1)S(1)} %get-tuple-element.95), channel_id=1, source_target_pairs={{0,10},{1,11},{2,8},{3,9},{4,14},{5,15},{6,12},{7,13},{8,2},{9,3},... | collective-permute-start | bytes 393224 | tf_op jit(solution)/shard_map/ppermute | solution.py:233
  69.3 9.3 %collective-permute-start.15 = (bf16[32,2048]{1,0:T(8,128)(2,1)S(1)}, bf16[32,2048]{1,0:T(8,128)(2,1)S(1)}, u32[]{:S(2)}, u32[]{:S(2)}) collective-permute-start(bf16[32,2048]{1,0:T(8,128)(2,1)S(1)} %get-tuple-element.96), channel_id=1, source_target_pairs={{0,16},{1,17},{2,18},{3,19},{4,20},{5,21},{6,22},{7,23},{8,24},{9,... | collective-permute-start | bytes 393224 | tf_op jit(solution)/shard_map/ppermute | solution.py:233
  78.6 24.9 %collective-permute-start.16 = (bf16[288,2048]{1,0:T(8,128)(2,1)S(1)}, bf16[288,2048]{1,0:T(8,128)(2,1)S(1)}, u32[]{:S(2)}, u32[]{:S(2)}) collective-permute-start(bf16[288,2048]{1,0:T(8,128)(2,1)S(1)} %collective-permute-done.2.refs_12_), channel_id=1, source_target_pairs={{0,4},{2,6},{4,0},{6,2},{9,13},{11,15},{13,9},{15,11},{16,20},{18,... | collective-permute-start | bytes 3538952 | tf_op jit(solution)/shard_map/ppermute | solution.py:233
  79.3 25.5 %collective-permute-start.21 = (bf16[288,2048]{1,0:T(8,128)(2,1)}, bf16[288,2048]{1,0:T(8,128)(2,1)S(1)}, u32[]{:S(2)}, u32[]{:S(2)}) collective-permute-start(bf16[288,2048]{1,0:T(8,128)(2,1)} %collective-permute-done.8.refs_13_), channel_id=1, source_target_pairs={{0,4},{2,6},{4,0},{6,2},{9,13},{11,15},{13,9},{15,11},{16,20},{18,... | collective-permute-start | bytes 3538952 | tf_op jit(solution)/shard_map/ppermute | solution.py:233
  80.0 7.9 %collective-permute-start.17 = (bf16[32,2048]{1,0:T(8,128)(2,1)S(1)}, bf16[32,2048]{1,0:T(8,128)(2,1)S(1)}, u32[]{:S(2)}, u32[]{:S(2)}) collective-permute-start(bf16[32,2048]{1,0:T(8,128)(2,1)S(1)} %get-tuple-element.107), channel_id=1, source_target_pairs={{0,18},{1,19},{2,16},{3,17},{4,22},{5,23},{6,20},{7,21},{8,26},{9,... | collective-permute-start | bytes 393224 | tf_op jit(solution)/shard_map/ppermute | solution.py:233
  84.3 17.6 %collective-permute-start.18 = (bf16[32,2048]{1,0:T(8,128)(2,1)S(1)}, bf16[32,2048]{1,0:T(8,128)(2,1)S(1)}, u32[]{:S(2)}, u32[]{:S(2)}) collective-permute-start(bf16[32,2048]{1,0:T(8,128)(2,1)S(1)} %get-tuple-element.108), channel_id=1, source_target_pairs={{0,24},{1,25},{2,26},{3,27},{4,28},{5,29},{6,30},{7,31},{8,16},{9,... | collective-permute-start | bytes 393224 | tf_op jit(solution)/shard_map/ppermute | solution.py:233
  88.0 15.5 %collective-permute-start.19 = (bf16[32,2048]{1,0:T(8,128)(2,1)S(1)}, bf16[32,2048]{1,0:T(8,128)(2,1)S(1)}, u32[]{:S(2)}, u32[]{:S(2)}) collective-permute-start(bf16[32,2048]{1,0:T(8,128)(2,1)S(1)} %get-tuple-element.109), channel_id=1, source_target_pairs={{0,26},{1,27},{2,24},{3,25},{4,30},{5,31},{6,28},{7,29},{8,18},{9,... | collective-permute-start | bytes 393224 | tf_op jit(solution)/shard_map/ppermute | solution.py:233
  103.5 3.1 %collective-permute-start.20 = (bf16[288,2048]{1,0:T(8,128)(2,1)}, bf16[288,2048]{1,0:T(8,128)(2,1)S(1)}, u32[]{:S(2)}, u32[]{:S(2)}) collective-permute-start(bf16[288,2048]{1,0:T(8,128)(2,1)} %collective-permute-done.8.refs_13_), channel_id=1, source_target_pairs={{0,1},{1,0},{2,3},{3,2},{4,5},{5,4},{6,7},{7,6},{8,9},{9,8},{10,11... | collective-permute-start | bytes 3538952 | tf_op jit(solution)/shard_map/ppermute | solution.py:233
  103.5 4.7 %collective-permute-start.22 = (bf16[288,2048]{1,0:T(8,128)(2,1)S(1)}, bf16[288,2048]{1,0:T(8,128)(2,1)S(1)}, u32[]{:S(2)}, u32[]{:S(2)}) collective-permute-start(bf16[288,2048]{1,0:T(8,128)(2,1)S(1)} %collective-permute-done.16.refs_16_), channel_id=1, source_target_pairs={{0,1},{2,3},{4,5},{6,7},{9,8},{11,10},{13,12},{15,14},{16,17},{18,... | collective-permute-start | bytes 3538952 | tf_op jit(solution)/shard_map/ppermute | solution.py:233
  104.8 8.7 %collective-permute-start.23 = (bf16[288,2048]{1,0:T(8,128)(2,1)S(1)}, bf16[288,2048]{1,0:T(8,128)(2,1)S(1)}, u32[]{:S(2)}, u32[]{:S(2)}) collective-permute-start(bf16[288,2048]{1,0:T(8,128)(2,1)S(1)} %collective-permute-done.21.refs_17_), channel_id=1, source_target_pairs={{0,1},{2,3},{4,5},{6,7},{9,8},{11,10},{13,12},{15,14},{16,17},{18,... | collective-permute-start | bytes 3538952 | tf_op jit(solution)/shard_map/ppermute | solution.py:233
  121.6 7.3 %collective-permute-start.24 = (bf16[32,2048]{1,0:T(8,128)(2,1)S(1)}, bf16[32,2048]{1,0:T(8,128)(2,1)S(1)}, u32[]{:S(2)}, u32[]{:S(2)}) collective-permute-start(bf16[32,2048]{1,0:T(8,128)(2,1)S(1)} %get-tuple-element.124), channel_id=1, source_target_pairs={{0,2},{1,3},{2,0},{3,1},{4,6},{5,7},{6,4},{7,5},{8,10},{9,11},{10,... | collective-permute-start | bytes 393224 | tf_op jit(solution)/shard_map/ppermute | solution.py:233
  122.7 9.6 %collective-permute-start.25 = (bf16[32,2048]{1,0:T(8,128)(2,1)S(1)}, bf16[32,2048]{1,0:T(8,128)(2,1)S(1)}, u32[]{:S(2)}, u32[]{:S(2)}) collective-permute-start(bf16[32,2048]{1,0:T(8,128)(2,1)S(1)} %get-tuple-element.125), channel_id=1, source_target_pairs={{0,8},{1,9},{2,10},{3,11},{4,12},{5,13},{6,14},{7,15},{8,0},{9,1},... | collective-permute-start | bytes 393224 | tf_op jit(solution)/shard_map/ppermute | solution.py:233
  125.1 9.0 %collective-permute-start.26 = (bf16[32,2048]{1,0:T(8,128)(2,1)}, bf16[32,2048]{1,0:T(8,128)(2,1)S(1)}, u32[]{:S(2)}, u32[]{:S(2)}) collective-permute-start(bf16[32,2048]{1,0:T(8,128)(2,1)} %get-tuple-element.126), channel_id=1, source_target_pairs={{0,10},{1,11},{2,8},{3,9},{4,14},{5,15},{6,12},{7,13},{8,2},{9,3},... | collective-permute-start | bytes 393224 | tf_op jit(solution)/shard_map/ppermute | solution.py:233
  125.1 10.3 %collective-permute-start.27 = (bf16[32,2048]{1,0:T(8,128)(2,1)}, bf16[32,2048]{1,0:T(8,128)(2,1)S(1)}, u32[]{:S(2)}, u32[]{:S(2)}) collective-permute-start(bf16[32,2048]{1,0:T(8,128)(2,1)} %get-tuple-element.127), channel_id=1, source_target_pairs={{0,16},{1,17},{2,18},{3,19},{4,20},{5,21},{6,22},{7,23},{8,24},{9,... | collective-permute-start | bytes 393224 | tf_op jit(solution)/shard_map/ppermute | solution.py:233
  126.7 18.2 %collective-permute-start.28 = (bf16[32,2048]{1,0:T(8,128)(2,1)}, bf16[32,2048]{1,0:T(8,128)(2,1)S(1)}, u32[]{:S(2)}, u32[]{:S(2)}) collective-permute-start(bf16[32,2048]{1,0:T(8,128)(2,1)} %get-tuple-element.128), channel_id=1, source_target_pairs={{0,18},{1,19},{2,16},{3,17},{4,22},{5,23},{6,20},{7,21},{8,26},{9,... | collective-permute-start | bytes 393224 | tf_op jit(solution)/shard_map/ppermute | solution.py:233
  128.9 20.8 %collective-permute-start.29 = (bf16[32,2048]{1,0:T(8,128)(2,1)}, bf16[32,2048]{1,0:T(8,128)(2,1)S(1)}, u32[]{:S(2)}, u32[]{:S(2)}) collective-permute-start(bf16[32,2048]{1,0:T(8,128)(2,1)} %get-tuple-element.129), channel_id=1, source_target_pairs={{0,24},{1,25},{2,26},{3,27},{4,28},{5,29},{6,30},{7,31},{8,16},{9,... | collective-permute-start | bytes 393224 | tf_op jit(solution)/shard_map/ppermute | solution.py:233
  132.4 19.2 %collective-permute-start.30 = (bf16[32,2048]{1,0:T(8,128)(2,1)}, bf16[32,2048]{1,0:T(8,128)(2,1)S(1)}, u32[]{:S(2)}, u32[]{:S(2)}) collective-permute-start(bf16[32,2048]{1,0:T(8,128)(2,1)} %get-tuple-element.130), channel_id=1, source_target_pairs={{0,26},{1,27},{2,24},{3,25},{4,30},{5,31},{6,28},{7,29},{8,18},{9,... | collective-permute-start | bytes 393224 | tf_op jit(solution)/shard_map/ppermute | solution.py:233
  (25 other events, 95.0 us)

commit v3 on v2

--- a/solution.py
+++ b/solution.py
@@ -253,14 +253,6 @@
     return (z, x, y, 1 - core) if is_home(z, core) else None
 
 
-def pack_halves(gate, up, down):
-    half = gate.shape[0] // 2
-    return [
-        jnp.concatenate([w[k * half : (k + 1) * half] for w in (gate, up, down)], axis=0)
-        for k in range(2)
-    ]
-
-
 def slot_targets(ids_row, z_here, y_here, capacity):
     expert_count = 8
     token_count = ids_row.shape[1]
@@ -285,48 +277,66 @@
     return (rows == target).astype(jnp.bfloat16)
 
 
-def attend_kernel(where_ref, ids_ref, queries_ref, residual_ref, *refs):
-    kv_refs, summed_ref, out_refs = refs[:8], refs[8], refs[9:17]
-    keys_ref, values_ref, bias_ref, mixed_ref = refs[17:]
+def fetch_all(pairs, semaphores):
+    copies = [
+        pltpu.make_async_copy(source, target, semaphores.at[i])
+        for i, (source, target) in enumerate(pairs)
+    ]
+    for copy in copies:
+        copy.start()
+    return copies
+
+
+def attend_kernel(where_ref, ids_ref, queries_from, residual_from, *refs):
+    kv_from, summed_to, out_refs = refs[:8], refs[8], refs[9:17]
+    queries_ref, residual_ref, kv_ref, bias_ref, mixed_ref, summed_ref, semaphores = refs[17:]
     tokens = queries_ref.shape[0]
     group = HEADS // KV_HEADS
     ctx_here = where_ref[0]
+    copies = fetch_all(
+        [(queries_from, queries_ref), (residual_from, residual_ref)]
+        + [(kv_from[k], kv_ref.at[pl.ds(k * tokens, tokens)]) for k in range(8)],
+        semaphores,
+    )
     row = lax.broadcasted_iota(jnp.int32, (tokens, tokens), 0)
     column = lax.broadcasted_iota(jnp.int32, (tokens, tokens), 1)
     for k in range(8):
         span = slice(k * tokens, (k + 1) * tokens)
-        block = kv_refs[k][...]
-        keys_ref[span, :] = block[:, : KV_HEADS * HD]
-        values_ref[span, :] = block[:, KV_HEADS * HD :]
         if k == 0:
             bias_ref[:, span] = jnp.where(column <= row, 0.0, negative_fill)
         else:
             bias_ref[:, span] = jnp.full(
                 (tokens, tokens), jnp.where(ctx_here >= k, 0.0, negative_fill), jnp.float32
             )
+    for copy in copies[2:] + copies[:1]:
+        copy.wait()
     factor = math.log2(math.e) / math.sqrt(HD)
     heads_each = 2
     for first in range(0, HEADS, heads_each):
         kv_head = first // group
-        side = slice(kv_head * HD, (kv_head + 1) * HD)
+        key_side = slice(kv_head * HD, (kv_head + 1) * HD)
+        value_side = slice((KV_HEADS + kv_head) * HD, (KV_HEADS + kv_head + 1) * HD)
         rows = jnp.concatenate(
             [queries_ref[:, h * HD : (h + 1) * HD] for h in range(first, first + heads_each)], axis=0
         )
-        scores = contract_rows(rows, keys_ref[:, side])
+        scores = contract_rows(rows, kv_ref[:, key_side])
         scores = scores + jnp.concatenate([bias_ref[...]] * heads_each, axis=0)
         largest = jnp.max(scores, axis=1, keepdims=True)
         exponent = jnp.exp2((scores - largest) * factor)
         total = jnp.sum(exponent, axis=1, keepdims=True)
         product = jnp.dot(
-            exponent.astype(jnp.bfloat16), values_ref[:, side], preferred_element_type=jnp.float32
+            exponent.astype(jnp.bfloat16), kv_ref[:, value_side], preferred_element_type=jnp.float32
         )
         result = product / total
         for j in range(heads_each):
             mixed_ref[:, (first + j) * HD : (first + j + 1) * HD] = result[
                 j * tokens : (j + 1) * tokens
             ].astype(jnp.bfloat16)
+    copies[1].wait()
     summed = residual_ref[...].astype(jnp.float32) + mixed_ref[...].astype(jnp.float32)
     summed_ref[...] = summed
+    keep = pltpu.make_async_copy(summed_ref, summed_to, semaphores.at[10])
+    keep.start()
     scale = lax.rsqrt(jnp.mean(summed * summed, axis=1, keepdims=True) + epsilon)
     normed = (summed * scale).astype(jnp.bfloat16)
     capacity = out_refs[0].shape[0]
@@ -334,89 +344,103 @@
     slots = jnp.dot(choose, normed, preferred_element_type=jnp.float32).astype(jnp.bfloat16)
     for k in range(8):
         out_refs[k][...] = slots[k * capacity : (k + 1) * capacity]
-
-
-def expert_kernel(where_ref, *refs):
-    row_refs, pack_refs, out_refs = refs[:8], refs[8:20], refs[20:28]
-    gate_ref, up_ref, down_ref, semaphores = refs[28:]
-    own, own_twin, one, one_twin, last, last_twin = [pack_refs[2 * i : 2 * i + 2] for i in range(6)]
+    keep.wait()
+
+
+def load_pack(pack, place, strip, targets, semaphores):
+    return [
+        pltpu.make_async_copy(
+            pack.at[pl.ds(kind * strip, strip)],
+            targets[kind].at[pl.ds(place * strip, strip)],
+            semaphores.at[place, kind],
+        )
+        for kind in range(3)
+    ]
+
+
+def active_of(rows, gate, up):
+    gate_part = contract_rows(rows, gate)
+    up_part = contract_rows(rows, up)
+    silu = gate_part / (1.0 + jnp.exp(-gate_part))
+    return (silu * up_part).astype(jnp.bfloat16)
+
+
+def expert_kernel(places, where_ref, *refs):
+    row_from, pack_from, rest = refs[:8], refs[8 : 9 + places], refs[9 + places :]
+    continued = places == 1
+    if continued:
+        before_from, rest = rest[0], rest[1:]
+        out_refs, rest = rest[:8], rest[8:]
+    else:
+        out_refs, rest = rest[:1], rest[1:]
+    rows_ref, before_ref, gate_ref, up_ref, down_ref, row_semaphores, semaphores = rest
     at_home = where_ref[3] == 1
     away = jnp.logical_not(at_home)
-    strip = pack_refs[0].shape[0] // 3
+    strip = pack_from[0].shape[0] // 3
+    capacity = row_from[0].shape[0]
     targets = (gate_ref, up_ref, down_ref)
-
-    def copies_of(pair, place, kinds):
-        return [
-            pltpu.make_async_copy(
-                pair[h].at[pl.ds(kind * strip, strip)],
-                targets[kind].at[pl.ds((2 * place + h) * strip, strip)],
-                semaphores.at[kind, place, h],
-            )
-            for kind in kinds
-            for h in range(2)
-        ]
-
-    def start(pair, place):
-        for copy in copies_of(pair, place, range(3)):
-            copy.start()
-
-    def wait(pair, place, kinds):
-        for copy in copies_of(pair, place, kinds):
-            copy.wait()
+    loads = [(row_from[k], rows_ref.at[pl.ds(k * capacity, capacity)]) for k in range(8)]
+    if continued:
+        loads.append((before_from, before_ref))
+    row_copies = fetch_all(loads, row_semaphores)
 
     @pl.when(at_home)
     def _():
-        start(own, 0)
+        for copy in load_pack(pack_from[0], 0, strip, targets, semaphores):
+            copy.start()
 
     @pl.when(away)
     def _():
-        start(own_twin, 0)
-
-    start(one, 1)
-    start(one_twin, 2)
-
-    @pl.when(at_home)
-    def _():
-        start(last, 3)
-
-    @pl.when(away)
-    def _():
-        start(last_twin, 3)
-
-    rows = jnp.concatenate([ref[...] for ref in row_refs], axis=0)
-    sources = (own, one, one_twin, last)
+        for copy in load_pack(pack_from[1], 0, strip, targets, semaphores):
+            copy.start()
+
+    waits = [load_pack(pack_from[0], 0, strip, targets, semaphores)]
+    for place in range(1, places):
+        waits.append(load_pack(pack_from[place + 1], place, strip, targets, semaphores))
+        for copy in waits[place]:
+            copy.start()
+    for copy in row_copies:
+        copy.wait()
+    rows = rows_ref[...]
     actives = []
-    for half in range(2):
-        span = slice(half * 4 * strip, (half + 1) * 4 * strip)
-        for place in (2 * half, 2 * half + 1):
-            wait(sources[place], place, (0, 1))
-        gate_part = contract_rows(rows, gate_ref[span, :])
-        up_part = contract_rows(rows, up_ref[span, :])
-        silu = gate_part / (1.0 + jnp.exp(-gate_part))
-        actives.append((silu * up_part).astype(jnp.bfloat16))
-    for place in range(PIECES):
-        wait(sources[place], place, (2,))
-    active = jnp.concatenate(actives, axis=1)
-    capacity = out_refs[0].shape[0]
-    result = jnp.dot(active, down_ref[...], preferred_element_type=jnp.float32).astype(jnp.bfloat16)
-    for k in range(8):
-        out_refs[k][...] = result[k * capacity : (k + 1) * capacity]
-
-
-def combine_kernel(where_ref, ids_ref, route_ref, summed_ref, *refs):
-    row_refs, out_ref = refs[:8], refs[8]
-    capacity = row_refs[0].shape[0]
+    for place in range(places):
+        for copy in waits[place][:2]:
+            copy.wait()
+        span = slice(place * strip, (place + 1) * strip)
+        actives.append(active_of(rows, gate_ref[span, :], up_ref[span, :]))
+    for place in range(places):
+        for copy in waits[place][2:]:
+            copy.wait()
+    active = actives[0] if continued else jnp.concatenate(actives, axis=1)
+    result = jnp.dot(active, down_ref[...], preferred_element_type=jnp.float32)
+    if continued:
+        result = (result + before_ref[...]).astype(jnp.bfloat16)
+        for k in range(8):
+            out_refs[k][...] = result[k * capacity : (k + 1) * capacity]
+    else:
+        out_refs[0][...] = result
+
+
+def combine_kernel(where_ref, ids_ref, route_ref, summed_from, *refs):
+    row_from, out_ref, rows_ref, summed_ref, semaphores = refs[:8], *refs[8:]
+    capacity = row_from[0].shape[0]
+    copies = fetch_all(
+        [(row_from[k], rows_ref.at[pl.ds(k * capacity, capacity)]) for k in range(8)]
+        + [(summed_from, summed_ref)],
+        semaphores,
+    )
     choose = slot_matrix(ids_ref[...], where_ref[1], where_ref[2], capacity)
-    rows = jnp.concatenate([ref[...] for ref in row_refs], axis=0)
+    for copy in copies:
+        copy.wait()
     picked = lax.dot_general(
-        choose, rows, (((0,), (0,)), ((), ())), preferred_element_type=jnp.float32
+        choose, rows_ref[...], (((0,), (0,)), ((), ())), preferred_element_type=jnp.float32
     )
     out_ref[...] = (summed_ref[...] + picked * route_ref[...]).astype(jnp.bfloat16)
 
 
 IN_VMEM = pl.BlockSpec(memory_space=pltpu.VMEM)
 IN_SMEM = pl.BlockSpec(memory_space=pltpu.SMEM)
-ANYWHERE = pl.BlockSpec(memory_space=pl.ANY)
+IN_HBM = pl.BlockSpec(memory_space=pltpu.HBM)
 
 
 def shards_cube(
@@ -448,36 +472,35 @@
 
         kv_blocks[k] = move(block, later)
 
-    own = pack_halves(gate_weight[0, 0], up_weight[0, 0], down_weight[0, 0])
-    for k in (7, 6):
-        send_keys(kv_own, k)
-    own[0], own[1], kv_blocks[7], kv_blocks[6], kv_next = lax.optimization_barrier(
-        (own[0], own[1], kv_blocks[7], kv_blocks[6], kv_own)
-    )
-    one_first = move(own[0], first_hop)
-    for k in (4, 5, 3, 2, 1):
+    own = jnp.concatenate([gate_weight[0, 0], up_weight[0, 0], down_weight[0, 0]], axis=0)
+    send_keys(kv_own, 7)
+    own, kv_blocks[7], kv_next = lax.optimization_barrier((own, kv_blocks[7], kv_own))
+    one = move(own, first_hop)
+    for k in (4, 6, 5, 3, 2, 1):
         send_keys(kv_next, k)
     kv_list = [kv_blocks[k] for k in range(1, 8)]
-    one_first, own[0], own[1], *kv_list = lax.optimization_barrier(
-        (one_first, own[0], own[1], *kv_list)
-    )
-    one_second = move(own[1], first_hop)
-    own_twin = [move(w, home_to_twin) for w in own]
-    twin_first = move(one_first, to_twin)
+    one, own, *kv_list = lax.optimization_barrier((one, own, *kv_list))
+    last = move(one, second_hop)
+    own_twin = move(own, home_to_twin)
+    one_twin = move(one, to_twin)
     slot_shape = jax.ShapeDtypeStruct((capacity, width), jnp.bfloat16)
     keys_all = 8 * tokens
+    rows_all = 8 * capacity
     first_out = pl.pallas_call(
         attend_kernel,
         out_shape=[jax.ShapeDtypeStruct((tokens, width), jnp.float32)] + [slot_shape] * 8,
-        in_specs=[IN_SMEM] + [IN_VMEM] * 11,
-        out_specs=[IN_VMEM] * 9,
+        in_specs=[IN_SMEM, IN_VMEM] + [IN_HBM] * 10,
+        out_specs=[IN_HBM] + [IN_VMEM] * 8,
         scratch_shapes=[
-            pltpu.VMEM((keys_all, KV_HEADS * HD), jnp.bfloat16),
-            pltpu.VMEM((keys_all, KV_HEADS * HD), jnp.bfloat16),
+            pltpu.VMEM((tokens, width), jnp.bfloat16),
+            pltpu.VMEM((tokens, width), jnp.bfloat16),
+            pltpu.VMEM((keys_all, 2 * KV_HEADS * HD), jnp.bfloat16),
             pltpu.VMEM((tokens, keys_all), jnp.float32),
             pltpu.VMEM((tokens, width), jnp.bfloat16),
+            pltpu.VMEM((tokens, width), jnp.float32),
+            pltpu.SemaphoreType.DMA((11,)),
         ],
-        compiler_params=pltpu.CompilerParams(vmem_limit_bytes=16 << 20),
+        compiler_params=pltpu.CompilerParams(vmem_limit_bytes=58 << 20),
         cost_estimate=pl.CostEstimate(
             flops=4 * tokens * keys_all * HEADS * HD,
             bytes_accessed=8 * tokens * width,
@@ -492,44 +515,50 @@
             return array
         return move(array, lambda z, x, y, core: (z ^ (k >> 1), x, y ^ (k & 1), core))
 
-    early, late = (4, 2, 3, 1), (5, 6, 7)
-    held = lax.optimization_barrier((*outgoing, *own_twin, twin_first))
-    outgoing, own_twin, twin_first = list(held[:8]), list(held[8:10]), held[10]
-    arrived = [swap(outgoing[k], k) if k in early else outgoing[k] for k in range(8)]
-    one_first, one_second, *arrived = lax.optimization_barrier((one_first, one_second, *arrived))
-    one = [one_first, one_second]
-    last = [move(w, second_hop) for w in one]
-    arrived = [swap(arrived[k], k) if k in late else arrived[k] for k in range(8)]
-    last[0], one[1], *arrived = lax.optimization_barrier((last[0], one[1], *arrived))
-    one_twin = [twin_first, move(one[1], to_twin)]
-    last_twin = [move(w, home_to_twin) for w in last]
-    packs = own + own_twin + one + one_twin + last + last_twin
-    results = pl.pallas_call(
-        expert_kernel,
-        out_shape=[slot_shape] * 8,
-        in_specs=[IN_SMEM] + [IN_VMEM] * 8 + [ANYWHERE] * 12,
-        out_specs=[IN_VMEM] * 8,
-        scratch_shapes=[
-            pltpu.VMEM((PIECES * piece, width), jnp.bfloat16),
-            pltpu.VMEM((PIECES * piece, width), jnp.bfloat16),
-            pltpu.VMEM((PIECES * piece, width), jnp.bfloat16),
-            pltpu.SemaphoreType.DMA((3, PIECES, 2)),
-        ],
-        compiler_params=pltpu.CompilerParams(vmem_limit_bytes=24 << 20),
-        cost_estimate=pl.CostEstimate(
-            flops=6 * 8 * capacity * PIECES * piece * width,
-            bytes_accessed=6 * PIECES * piece * width,
-            transcendentals=8 * capacity * PIECES * piece,
-        ),
-        name="experts",
-    )(where, *[arrived[k] for k in range(8)], *packs)
+    own_twin, one_twin, *outgoing = lax.optimization_barrier((own_twin, one_twin, *outgoing))
+    arrived = [outgoing[0]] + [swap(outgoing[k], k) for k in range(1, 8)]
+    def run_expert(places, rows, packs, before):
+        total = jax.ShapeDtypeStruct((rows_all, width), jnp.float32)
+        inner = places * piece
+        return pl.pallas_call(
+            partial(expert_kernel, places),
+            out_shape=[slot_shape] * 8 if before else [total],
+            in_specs=[IN_SMEM] + [IN_HBM] * (8 + len(packs) + len(before)),
+            out_specs=[IN_VMEM] * (8 if before else 1),
+            scratch_shapes=[
+                pltpu.VMEM((rows_all, width), jnp.bfloat16),
+                pltpu.VMEM((rows_all if before else 8, width), jnp.float32),
+                pltpu.VMEM((inner, width), jnp.bfloat16),
+                pltpu.VMEM((inner, width), jnp.bfloat16),
+                pltpu.VMEM((inner, width), jnp.bfloat16),
+                pltpu.SemaphoreType.DMA((9,)),
+                pltpu.SemaphoreType.DMA((places, 3)),
+            ],
+            compiler_params=pltpu.CompilerParams(vmem_limit_bytes=24 << 20),
+            cost_estimate=pl.CostEstimate(
+                flops=6 * rows_all * inner * width,
+                bytes_accessed=6 * inner * width,
+                transcendentals=rows_all * inner,
+            ),
+            name="experts_%d" % places,
+        )(where, *rows, *packs, *before)
+
+    most = run_expert(3, arrived, [own, own_twin, one, one_twin], [])
+    last, *most = lax.optimization_barrier((last, *most))
+    last_twin = move(last, home_to_twin)
+    results = run_expert(1, arrived, [last, last_twin], most)
     returned = [swap(results[k], k) for k in range(8)]
     output = pl.pallas_call(
         combine_kernel,
         out_shape=jax.ShapeDtypeStruct((tokens, width), jnp.bfloat16),
-        in_specs=[IN_SMEM] + [IN_VMEM] * 11,
+        in_specs=[IN_SMEM, IN_VMEM, IN_VMEM] + [IN_HBM] * 9,
         out_specs=IN_VMEM,
-        compiler_params=pltpu.CompilerParams(vmem_limit_bytes=10 << 20),
+        scratch_shapes=[
+            pltpu.VMEM((rows_all, width), jnp.bfloat16),
+            pltpu.VMEM((tokens, width), jnp.float32),
+            pltpu.SemaphoreType.DMA((9,)),
+        ],
+        compiler_params=pltpu.CompilerParams(vmem_limit_bytes=12 << 20),
         cost_estimate=pl.CostEstimate(
             flops=2 * tokens * 8 * capacity * width,
             bytes_accessed=12 * tokens * width,

time: 157 us -> 154 us (0.981)
  local copies, waits for them, and re-layouts: 19 us -> 1.07 us
  starting transfers between devices: 62.9 us -> 71.8 us
  Pallas kernels: 14.5 us -> 22.2 us
  waiting for transfers between devices: 57.4 us -> 54.9 us
  other arithmetic: 1.31 us -> 3.24 us
    unnamed x52 -> x26, local copies, waits for them, and re-layouts: 17.7 us -> 0.96 us
    ppermute x31 -> x26, starting transfers between devices: 62.9 us -> 71.8 us  [move(): return lax.ppermute(array, AXES, pairs)]
    pallas_call x1, Pallas kernels: 5.22 us -> 8.55 us  [shards_cube(): pl.pallas_call(attend_kernel, out_shape=[jax.ShapeDtypeStruct((tokens, wi...]
    pallas_call x1 -> x2, Pallas kernels: 7.47 us -> 10.3 us  [run_expert(): pl.pallas_call(partial(expert_kernel, places), out_shape=[slot_shape] * 8...]
    ppermute x31 -> x26, waiting for transfers between devices: 57.4 us -> 54.9 us  [move(): return lax.ppermute(array, AXES, pairs)]
  transfers between devices with their start and end apart: 31 -> 26, of which waited for: 16 -> 13; matrix products, arithmetic and copies ran while one was open for 1% -> 2% of each run, Pallas kernels for 3% -> 10%
where the time goes in v3:
time: 154 us
  starting transfers between devices  71.8 us (47%)
  waiting for transfers between devices  54.9 us (36%)
  Pallas kernels  22.2 us (14%)
  other arithmetic  3.24 us (2%)
    ppermute x26, starting transfers between devices, move(): return lax.ppermute(array, AXES, pairs)  71.8 us
    ppermute x26, waiting for transfers between devices, move(): return lax.ppermute(array, AXES, pairs)  54.9 us
    pallas_call x2, Pallas kernels, run_expert(): pl.pallas_call(partial(expert_kernel, places), out_shape=[slot_shape] * 8...  10.3 us
    pallas_call x1, Pallas kernels, shards_cube(): pl.pallas_call(attend_kernel, out_shape=[jax.ShapeDtypeStruct((tokens, wi...  8.55 us
    pallas_call x1, Pallas kernels, shards_cube(): pl.pallas_call(combine_kernel, out_shape=jax.ShapeDtypeStruct((tokens, wi...  3.35 us
  transfers between devices with their start and end apart: 26, of which 13 were waited for; matrix products, arithmetic and copies ran while one was open for 2% of the time, Pallas kernels for 10%

profile of v3, /device:TPU:8, one launch (start us, length us, event | category | flops | bytes accessed | tf_op | source)
XLA Modules:
  0.0 153.6 jit_solution(7587874815700413353)
XLA Ops:
  1.6 1.8 %pad_maximum_fusion.refs_8_ = bf16[576,2048]{1,0:T(8,128)(2,1)S(1)} fusion(bf16[192,2048]{1,0:T(8,128)(2,1)} %bitcast.16, bf16[192,2048]{1,0:T(8,128)(2,1)} %bitcast.17, bf16[192,2048]{1,0:T(8,128)(2,1)} %bitcast.18), kind=kLoop, calls=%fused_computation | loop fusion | flops 7077888 | bytes 4718592 | tf_op jit(solution)/shard_map/concatenate | solution.py:475
  3.4 7.8 %collective-permute-start.1 = (bf16[576,2048]{1,0:T(8,128)(2,1)S(1)}, bf16[576,2048]{1,0:T(8,128)(2,1)}, u32[]{:S(2)}, u32[]{:S(2)}) collective-permute-start(bf16[576,2048]{1,0:T(8,128)(2,1)S(1)} %pad_maximum_fusion.refs_8_), channel_id=1, source_target_pairs={{0,5},{1,9},{2,7},{3,11},{4,1},{5,13},{6,3},{7,15},{8,0},{9,12},{1... | collective-permute-start | bytes 7077896 | tf_op jit(solution)/shard_map/ppermute | solution.py:233
  11.2 1.9 %collective-permute-start.2 = (bf16[128,512]{1,0:T(8,128)(2,1)S(1)}, bf16[128,512]{1,0:T(8,128)(2,1)S(1)}, u32[]{:S(2)}, u32[]{:S(2)}) collective-permute-start(bf16[128,512]{1,0:T(8,128)(2,1)S(1)} %pad_maximum_fusion.1.refs_0_), channel_id=1, source_target_pairs={{0,4},{1,5},{2,6},{3,7},{4,8},{5,9},{6,10},{7,11},{8,12},{9,13},{1... | collective-permute-start | bytes 393224 | tf_op jit(solution)/shard_map/ppermute | solution.py:233
  13.1 1.9 %collective-permute-start.3 = (bf16[128,512]{1,0:T(8,128)(2,1)S(1)}, bf16[128,512]{1,0:T(8,128)(2,1)S(1)}, u32[]{:S(2)}, u32[]{:S(2)}) collective-permute-start(bf16[128,512]{1,0:T(8,128)(2,1)S(1)} %pad_maximum_fusion.1.refs_0_), channel_id=1, source_target_pairs={{0,8},{1,9},{2,10},{3,11},{4,12},{5,13},{6,14},{7,15},{8,16},{9,17... | collective-permute-start | bytes 393224 | tf_op jit(solution)/shard_map/ppermute | solution.py:233
  15.0 5.6 %collective-permute-start.4 = (bf16[128,512]{1,0:T(8,128)(2,1)S(1)}, bf16[128,512]{1,0:T(8,128)(2,1)S(1)}, u32[]{:S(2)}, u32[]{:S(2)}) collective-permute-start(bf16[128,512]{1,0:T(8,128)(2,1)S(1)} %pad_maximum_fusion.1.refs_0_), channel_id=1, source_target_pairs={{0,12},{1,13},{2,14},{3,15},{4,16},{5,17},{6,18},{7,19},{8,20},{9,... | collective-permute-start | bytes 393224 | tf_op jit(solution)/shard_map/ppermute | solution.py:233
  21.9 3.2 %collective-permute-start.6 = (bf16[128,512]{1,0:T(8,128)(2,1)S(1)}, bf16[128,512]{1,0:T(8,128)(2,1)S(1)}, u32[]{:S(2)}, u32[]{:S(2)}) collective-permute-start(bf16[128,512]{1,0:T(8,128)(2,1)S(1)} %pad_maximum_fusion.1.refs_0_), channel_id=1, source_target_pairs={{0,20},{1,21},{2,22},{3,23},{4,24},{5,25},{6,26},{7,27},{8,28},{9,... | collective-permute-start | bytes 393224 | tf_op jit(solution)/shard_map/ppermute | solution.py:233
  26.5 3.6 %collective-permute-done.6.refs_5_ = bf16[128,512]{1,0:T(8,128)(2,1)S(1)} collective-permute-done((bf16[128,512]{1,0:T(8,128)(2,1)S(1)}, bf16[128,512]{1,0:T(8,128)(2,1)S(1)}, u32[]{:S(2)}, u32[]{:S(2)}) %collective-permute-start.6) | collective-permute-done | bytes 131104 | tf_op jit(solution)/shard_map/ppermute | solution.py:233
  30.1 7.4 %collective-permute-done.1.refs_10_ = bf16[576,2048]{1,0:T(8,128)(2,1)} collective-permute-done((bf16[576,2048]{1,0:T(8,128)(2,1)S(1)}, bf16[576,2048]{1,0:T(8,128)(2,1)}, u32[]{:S(2)}, u32[]{:S(2)}) %collective-permute-start.1) | collective-permute-done | bytes 2359328 | tf_op jit(solution)/shard_map/ppermute | solution.py:233
  37.5 16.1 %collective-permute-start.9 = (bf16[576,2048]{1,0:T(8,128)(2,1)}, bf16[576,2048]{1,0:T(8,128)(2,1)}, u32[]{:S(2)}, u32[]{:S(2)}) collective-permute-start(bf16[576,2048]{1,0:T(8,128)(2,1)} %collective-permute-done.1.refs_10_), channel_id=1, source_target_pairs={{0,1},{1,0},{2,3},{3,2},{4,5},{5,4},{6,7},{7,6},{8,9},{9,8},{10,11... | collective-permute-start | bytes 7077896 | tf_op jit(solution)/shard_map/ppermute | solution.py:233
  54.9 2.1 %collective-permute-start.17 = (bf16[576,2048]{1,0:T(8,128)(2,1)}, bf16[576,2048]{1,0:T(8,128)(2,1)}, u32[]{:S(2)}, u32[]{:S(2)}) collective-permute-start(bf16[576,2048]{1,0:T(8,128)(2,1)} %collective-permute-done.1.refs_10_), channel_id=1, source_target_pairs={{0,4},{2,6},{4,0},{6,2},{9,13},{11,15},{13,9},{15,11},{16,20},{18,... | collective-permute-start | bytes 7077896 | tf_op jit(solution)/shard_map/ppermute | solution.py:233
  57.7 8.6 %attend.1 = (f32[128,2048]{1,0:T(8,128)}, bf16[32,2048]{1,0:T(8,128)(2,1)}, bf16[32,2048]{1,0:T(8,128)(2,1)}, bf16[32,2048]{1,0:T(8,128)(2,1)}, bf16[32,2048]{1,...) custom-call(s32[4]{0:T(128)} %pad_add_fusion.where_ref, ...), custom_call_target="tpu_custom_call" | custom-call | flops 1073741824 | bytes 2097152 | tf_op jit(solution)/shard_map/attend/pallas_call | solution.py:489
  66.2 1.6 %collective-permute-start.10 = (bf16[32,2048]{1,0:T(8,128)(2,1)}, bf16[32,2048]{1,0:T(8,128)(2,1)S(1)}, u32[]{:S(2)}, u32[]{:S(2)}) collective-permute-start(bf16[32,2048]{1,0:T(8,128)(2,1)} %get-tuple-element.68), channel_id=1, source_target_pairs={{0,2},{1,3},{2,0},{3,1},{4,6},{5,7},{6,4},{7,5},{8,10},{9,11},{10,... | collective-permute-start | bytes 393224 | tf_op jit(solution)/shard_map/ppermute | solution.py:233
  67.8 8.3 %collective-permute-start.11 = (bf16[32,2048]{1,0:T(8,128)(2,1)}, bf16[32,2048]{1,0:T(8,128)(2,1)S(1)}, u32[]{:S(2)}, u32[]{:S(2)}) collective-permute-start(bf16[32,2048]{1,0:T(8,128)(2,1)} %get-tuple-element.69), channel_id=1, source_target_pairs={{0,8},{1,9},{2,10},{3,11},{4,12},{5,13},{6,14},{7,15},{8,0},{9,1},... | collective-permute-start | bytes 393224 | tf_op jit(solution)/shard_map/ppermute | solution.py:233
  77.1 2.8 %collective-permute-start.14 = (bf16[32,2048]{1,0:T(8,128)(2,1)}, bf16[32,2048]{1,0:T(8,128)(2,1)S(1)}, u32[]{:S(2)}, u32[]{:S(2)}) collective-permute-start(bf16[32,2048]{1,0:T(8,128)(2,1)} %get-tuple-element.72), channel_id=1, source_target_pairs={{0,18},{1,19},{2,16},{3,17},{4,22},{5,23},{6,20},{7,21},{8,26},{9,... | collective-permute-start | bytes 393224 | tf_op jit(solution)/shard_map/ppermute | solution.py:233
  79.9 2.2 %collective-permute-start.15 = (bf16[32,2048]{1,0:T(8,128)(2,1)}, bf16[32,2048]{1,0:T(8,128)(2,1)S(1)}, u32[]{:S(2)}, u32[]{:S(2)}) collective-permute-start(bf16[32,2048]{1,0:T(8,128)(2,1)} %get-tuple-element.73), channel_id=1, source_target_pairs={{0,24},{1,25},{2,26},{3,27},{4,28},{5,29},{6,30},{7,31},{8,16},{9,... | collective-permute-start | bytes 393224 | tf_op jit(solution)/shard_map/ppermute | solution.py:233
  84.8 9.7 %collective-permute-done.14.refs_5_ = bf16[32,2048]{1,0:T(8,128)(2,1)S(1)} collective-permute-done((bf16[32,2048]{1,0:T(8,128)(2,1)}, bf16[32,2048]{1,0:T(8,128)(2,1)S(1)}, u32[]{:S(2)}, u32[]{:S(2)}) %collective-permute-start.14) | collective-permute-done | bytes 131104 | tf_op jit(solution)/shard_map/ppermute | solution.py:233
  94.5 5.3 %collective-permute-done.15.refs_6_ = bf16[32,2048]{1,0:T(8,128)(2,1)S(1)} collective-permute-done((bf16[32,2048]{1,0:T(8,128)(2,1)}, bf16[32,2048]{1,0:T(8,128)(2,1)S(1)}, u32[]{:S(2)}, u32[]{:S(2)}) %collective-permute-start.15) | collective-permute-done | bytes 131104 | tf_op jit(solution)/shard_map/ppermute | solution.py:233
  99.8 3.5 %collective-permute-done.16.refs_7_ = bf16[32,2048]{1,0:T(8,128)(2,1)S(1)} collective-permute-done((bf16[32,2048]{1,0:T(8,128)(2,1)}, bf16[32,2048]{1,0:T(8,128)(2,1)S(1)}, u32[]{:S(2)}, u32[]{:S(2)}) %collective-permute-start.16) | collective-permute-done | bytes 131104 | tf_op jit(solution)/shard_map/ppermute | solution.py:233
  104.2 6.7 %experts_3.1.refs_10_ = f32[256,2048]{1,0:T(8,128)S(1)} custom-call(s32[4]{0:T(128)S(1)} %copy-done.2, bf16[32,2048]{1,0:T(8,128)(2,1)S(1)} %copy-done.1, bf16[32,2048]{1,0:T(8,128)(2,1)S(1)} %collective-permute-done.10.refs_1_, bf16[32,2048]{1,0:T(8,128)(2,1)S(1)} %collective-permute-done.11.refs_2_, bf16[32,2048]{1,0:T(8,128)(2,1)S(1)} %collective-permute-done.12.refs_3_, ...), custom_call_target="tpu_custom_call" | custom-call | flops 1811939328 | bytes 7077888 | tf_op jit(solution)/shard_map/experts_3/pallas_call | solution.py:523
  111.0 1.4 collective-permute-start.18
  112.4 5.3 %collective-permute-done.18.refs_9_ = bf16[576,2048]{1,0:T(8,128)(2,1)S(1)} collective-permute-done((bf16[576,2048]{1,0:T(8,128)(2,1)}, bf16[576,2048]{1,0:T(8,128)(2,1)S(1)}, u32[]{:S(2)}, u32[]{:S(2)}) %collective-permute-start.18) | collective-permute-done | bytes 2359328 | tf_op jit(solution)/shard_map/ppermute | solution.py:233
  117.7 3.7 %experts_1.1 = (bf16[32,2048]{1,0:T(8,128)(2,1)S(1)}, bf16[32,2048]{1,0:T(8,128)(2,1)S(1)}, bf16[32,2048]{1,0:T(8,128)(2,1)S(1)}, bf16[32,2048]{1,0:T(8,128)(2,1...) custom-call(s32[4]{0:T(128)S(1)} %copy-done.2, ...), custom_call_target="tpu_custom_call" | custom-call | flops 603979776 | bytes 2359296 | tf_op jit(solution)/shard_map/experts_1/pallas_call | solution.py:523
  122.1 2.9 %collective-permute-start.21 = (bf16[32,2048]{1,0:T(8,128)(2,1)S(1)}, bf16[32,2048]{1,0:T(8,128)(2,1)S(1)}, u32[]{:S(2)}, u32[]{:S(2)}) collective-permute-start(bf16[32,2048]{1,0:T(8,128)(2,1)S(1)} %get-tuple-element.82), channel_id=1, source_target_pairs={{0,10},{1,11},{2,8},{3,9},{4,14},{5,15},{6,12},{7,13},{8,2},{9,3},... | collective-permute-start | bytes 393224 | tf_op jit(solution)/shard_map/ppermute | solution.py:233
  125.0 1.3 collective-permute-start.22
  126.3 1.6 %collective-permute-start.23 = (bf16[32,2048]{1,0:T(8,128)(2,1)S(1)}, bf16[32,2048]{1,0:T(8,128)(2,1)S(1)}, u32[]{:S(2)}, u32[]{:S(2)}) collective-permute-start(bf16[32,2048]{1,0:T(8,128)(2,1)S(1)} %get-tuple-element.84), channel_id=1, source_target_pairs={{0,18},{1,19},{2,16},{3,17},{4,22},{5,23},{6,20},{7,21},{8,26},{9,... | collective-permute-start | bytes 393224 | tf_op jit(solution)/shard_map/ppermute | solution.py:233
  127.9 1.9 %collective-permute-start.24 = (bf16[32,2048]{1,0:T(8,128)(2,1)S(1)}, bf16[32,2048]{1,0:T(8,128)(2,1)S(1)}, u32[]{:S(2)}, u32[]{:S(2)}) collective-permute-start(bf16[32,2048]{1,0:T(8,128)(2,1)S(1)} %get-tuple-element.85), channel_id=1, source_target_pairs={{0,24},{1,25},{2,26},{3,27},{4,28},{5,29},{6,30},{7,31},{8,16},{9,... | collective-permute-start | bytes 393224 | tf_op jit(solution)/shard_map/ppermute | solution.py:233
  129.8 3.6 %collective-permute-start.25 = (bf16[32,2048]{1,0:T(8,128)(2,1)S(1)}, bf16[32,2048]{1,0:T(8,128)(2,1)S(1)}, u32[]{:S(2)}, u32[]{:S(2)}) collective-permute-start(bf16[32,2048]{1,0:T(8,128)(2,1)S(1)} %get-tuple-element.86), channel_id=1, source_target_pairs={{0,26},{1,27},{2,24},{3,25},{4,30},{5,31},{6,28},{7,29},{8,18},{9,... | collective-permute-start | bytes 393224 | tf_op jit(solution)/shard_map/ppermute | solution.py:233
  133.5 1.6 %collective-permute-done.22.refs_4_ = bf16[32,2048]{1,0:T(8,128)(2,1)S(1)} collective-permute-done((bf16[32,2048]{1,0:T(8,128)(2,1)S(1)}, bf16[32,2048]{1,0:T(8,128)(2,1)S(1)}, u32[]{:S(2)}, u32[]{:S(2)}) %collective-permute-start.22) | collective-permute-done | bytes 131104 | tf_op jit(solution)/shard_map/ppermute | solution.py:233
  135.0 8.5 %collective-permute-done.23.refs_5_ = bf16[32,2048]{1,0:T(8,128)(2,1)S(1)} collective-permute-done((bf16[32,2048]{1,0:T(8,128)(2,1)S(1)}, bf16[32,2048]{1,0:T(8,128)(2,1)S(1)}, u32[]{:S(2)}, u32[]{:S(2)}) %collective-permute-start.23) | collective-permute-done | bytes 131104 | tf_op jit(solution)/shard_map/ppermute | solution.py:233
  143.5 4.6 %collective-permute-done.24.refs_6_ = bf16[32,2048]{1,0:T(8,128)(2,1)S(1)} collective-permute-done((bf16[32,2048]{1,0:T(8,128)(2,1)S(1)}, bf16[32,2048]{1,0:T(8,128)(2,1)S(1)}, u32[]{:S(2)}, u32[]{:S(2)}) %collective-permute-start.24) | collective-permute-done | bytes 131104 | tf_op jit(solution)/shard_map/ppermute | solution.py:233
  148.1 2.2 %collective-permute-done.25.refs_7_ = bf16[32,2048]{1,0:T(8,128)(2,1)S(1)} collective-permute-done((bf16[32,2048]{1,0:T(8,128)(2,1)S(1)}, bf16[32,2048]{1,0:T(8,128)(2,1)S(1)}, u32[]{:S(2)}, u32[]{:S(2)}) %collective-permute-start.25) | collective-permute-done | bytes 131104 | tf_op jit(solution)/shard_map/ppermute | solution.py:233
  150.2 3.3 %combine.1 = bf16[128,2048]{1,0:T(8,128)(2,1)} custom-call(s32[4]{0:T(128)S(1)} %copy-done.2, s32[1,128]{1,0:T(1,128)S(1)} %bitcast.15, f32[128,1]{1,0:T(8,128)S(1)} %copy.10.route_ref, f32[128,2048]{1,0:T(8,128)S(1)} %copy-done, bf16[32,2048]{1,0:T(8,128)(2,1)S(1)} %get-tuple-element.79.refs_0_, bf16[32,2048]{1,0:T(8,128)(2,1)S(1)} %collective-permute-done.19.refs_1_, ...), custom_call_target="tpu_custom_call" | custom-call | flops 134217728 | bytes 3145728 | tf_op jit(solution)/shard_map/combine/pallas_call | solution.py:551
  (54 shorter events, 11.4 us)
Async XLA Ops:
  0.9 2.5 %collective-permute-start = (bf16[128,512]{1,0:T(8,128)(2,1)S(1)}, bf16[128,512]{1,0:T(8,128)(2,1)S(1)}, u32[]{:S(2)}, u32[]{:S(2)}) collective-permute-start(bf16[128,512]{1,0:T(8,128)(2,1)S(1)} %pad_maximum_fusion.1.refs_0_), channel_id=1, source_target_pairs={{0,28},{1,29},{2,30},{3,31}} | collective-permute-start | bytes 393224 | tf_op jit(solution)/shard_map/ppermute | solution.py:233
  3.4 54.2 %copy-start.6 = (bf16[128,512]{1,0:T(8,128)(2,1)}, bf16[128,512]{1,0:T(8,128)(2,1)S(1)}, u32[]{:S(2)}) copy-start(bf16[128,512]{1,0:T(8,128)(2,1)S(1)} %collective-permute-done.refs_7_) | copy-start | bytes 393220
  3.4 34.2 %collective-permute-start.1 = (bf16[576,2048]{1,0:T(8,128)(2,1)S(1)}, bf16[576,2048]{1,0:T(8,128)(2,1)}, u32[]{:S(2)}, u32[]{:S(2)}) collective-permute-start(bf16[576,2048]{1,0:T(8,128)(2,1)S(1)} %pad_maximum_fusion.refs_8_), channel_id=1, source_target_pairs={{0,5},{1,9},{2,7},{3,11},{4,1},{5,13},{6,3},{7,15},{8,0},{9,12},{1... | collective-permute-start | bytes 7077896 | tf_op jit(solution)/shard_map/ppermute | solution.py:233
  11.2 10.7 %collective-permute-start.2 = (bf16[128,512]{1,0:T(8,128)(2,1)S(1)}, bf16[128,512]{1,0:T(8,128)(2,1)S(1)}, u32[]{:S(2)}, u32[]{:S(2)}) collective-permute-start(bf16[128,512]{1,0:T(8,128)(2,1)S(1)} %pad_maximum_fusion.1.refs_0_), channel_id=1, source_target_pairs={{0,4},{1,5},{2,6},{3,7},{4,8},{5,9},{6,10},{7,11},{8,12},{9,13},{1... | collective-permute-start | bytes 393224 | tf_op jit(solution)/shard_map/ppermute | solution.py:233
  13.1 12.0 %collective-permute-start.3 = (bf16[128,512]{1,0:T(8,128)(2,1)S(1)}, bf16[128,512]{1,0:T(8,128)(2,1)S(1)}, u32[]{:S(2)}, u32[]{:S(2)}) collective-permute-start(bf16[128,512]{1,0:T(8,128)(2,1)S(1)} %pad_maximum_fusion.1.refs_0_), channel_id=1, source_target_pairs={{0,8},{1,9},{2,10},{3,11},{4,12},{5,13},{6,14},{7,15},{8,16},{9,17... | collective-permute-start | bytes 393224 | tf_op jit(solution)/shard_map/ppermute | solution.py:233
  15.0 10.8 %collective-permute-start.4 = (bf16[128,512]{1,0:T(8,128)(2,1)S(1)}, bf16[128,512]{1,0:T(8,128)(2,1)S(1)}, u32[]{:S(2)}, u32[]{:S(2)}) collective-permute-start(bf16[128,512]{1,0:T(8,128)(2,1)S(1)} %pad_maximum_fusion.1.refs_0_), channel_id=1, source_target_pairs={{0,12},{1,13},{2,14},{3,15},{4,16},{5,17},{6,18},{7,19},{8,20},{9,... | collective-permute-start | bytes 393224 | tf_op jit(solution)/shard_map/ppermute | solution.py:233
  20.6 5.9 %collective-permute-start.5 = (bf16[128,512]{1,0:T(8,128)(2,1)S(1)}, bf16[128,512]{1,0:T(8,128)(2,1)S(1)}, u32[]{:S(2)}, u32[]{:S(2)}) collective-permute-start(bf16[128,512]{1,0:T(8,128)(2,1)S(1)} %pad_maximum_fusion.1.refs_0_), channel_id=1, source_target_pairs={{0,16},{1,17},{2,18},{3,19},{4,20},{5,21},{6,22},{7,23},{8,24},{9,... | collective-permute-start | bytes 393224 | tf_op jit(solution)/shard_map/ppermute | solution.py:233
  21.9 35.7 %copy-start.7 = (bf16[128,512]{1,0:T(8,128)(2,1)}, bf16[128,512]{1,0:T(8,128)(2,1)S(1)}, u32[]{:S(2)}) copy-start(bf16[128,512]{1,0:T(8,128)(2,1)S(1)} %collective-permute-done.2.refs_1_) | copy-start | bytes 393220
  21.9 8.2 %collective-permute-start.6 = (bf16[128,512]{1,0:T(8,128)(2,1)S(1)}, bf16[128,512]{1,0:T(8,128)(2,1)S(1)}, u32[]{:S(2)}, u32[]{:S(2)}) collective-permute-start(bf16[128,512]{1,0:T(8,128)(2,1)S(1)} %pad_maximum_fusion.1.refs_0_), channel_id=1, source_target_pairs={{0,20},{1,21},{2,22},{3,23},{4,24},{5,25},{6,26},{7,27},{8,28},{9,... | collective-permute-start | bytes 393224 | tf_op jit(solution)/shard_map/ppermute | solution.py:233
  25.1 32.5 %copy-start.8 = (bf16[128,512]{1,0:T(8,128)(2,1)}, bf16[128,512]{1,0:T(8,128)(2,1)S(1)}, u32[]{:S(2)}) copy-start(bf16[128,512]{1,0:T(8,128)(2,1)S(1)} %collective-permute-done.3.refs_2_) | copy-start | bytes 393220
  25.1 5.0 %collective-permute-start.7 = (bf16[128,512]{1,0:T(8,128)(2,1)S(1)}, bf16[128,512]{1,0:T(8,128)(2,1)S(1)}, u32[]{:S(2)}, u32[]{:S(2)}) collective-permute-start(bf16[128,512]{1,0:T(8,128)(2,1)S(1)} %pad_maximum_fusion.1.refs_0_), channel_id=1, source_target_pairs={{0,24},{1,25},{2,26},{3,27},{4,28},{5,29},{6,30},{7,31}} | collective-permute-start | bytes 393224 | tf_op jit(solution)/shard_map/ppermute | solution.py:233
  37.5 28.7 %collective-permute-start.9 = (bf16[576,2048]{1,0:T(8,128)(2,1)}, bf16[576,2048]{1,0:T(8,128)(2,1)}, u32[]{:S(2)}, u32[]{:S(2)}) collective-permute-start(bf16[576,2048]{1,0:T(8,128)(2,1)} %collective-permute-done.1.refs_10_), channel_id=1, source_target_pairs={{0,1},{1,0},{2,3},{3,2},{4,5},{5,4},{6,7},{7,6},{8,9},{9,8},{10,11... | collective-permute-start | bytes 7077896 | tf_op jit(solution)/shard_map/ppermute | solution.py:233
  53.6 12.6 %collective-permute-start.8 = (bf16[576,2048]{1,0:T(8,128)(2,1)S(1)}, bf16[576,2048]{1,0:T(8,128)(2,1)}, u32[]{:S(2)}, u32[]{:S(2)}) collective-permute-start(bf16[576,2048]{1,0:T(8,128)(2,1)S(1)} %pad_maximum_fusion.refs_8_), channel_id=1, source_target_pairs={{0,1},{2,3},{4,5},{6,7},{9,8},{11,10},{13,12},{15,14},{16,17},{18,... | collective-permute-start | bytes 7077896 | tf_op jit(solution)/shard_map/ppermute | solution.py:233
  54.9 56.1 %collective-permute-start.17 = (bf16[576,2048]{1,0:T(8,128)(2,1)}, bf16[576,2048]{1,0:T(8,128)(2,1)}, u32[]{:S(2)}, u32[]{:S(2)}) collective-permute-start(bf16[576,2048]{1,0:T(8,128)(2,1)} %collective-permute-done.1.refs_10_), channel_id=1, source_target_pairs={{0,4},{2,6},{4,0},{6,2},{9,13},{11,15},{13,9},{15,11},{16,20},{18,... | collective-permute-start | bytes 7077896 | tf_op jit(solution)/shard_map/ppermute | solution.py:233
  57.6 45.7 %copy-start.2 = (s32[4]{0:T(128)S(1)}, s32[4]{0:T(128)}, u32[]{:S(2)}) copy-start(s32[4]{0:T(128)} %pad_add_fusion.where_ref) | copy-start | bytes 52
  66.2 10.9 %collective-permute-start.10 = (bf16[32,2048]{1,0:T(8,128)(2,1)}, bf16[32,2048]{1,0:T(8,128)(2,1)S(1)}, u32[]{:S(2)}, u32[]{:S(2)}) collective-permute-start(bf16[32,2048]{1,0:T(8,128)(2,1)} %get-tuple-element.68), channel_id=1, source_target_pairs={{0,2},{1,3},{2,0},{3,1},{4,6},{5,7},{6,4},{7,5},{8,10},{9,11},{10,... | collective-permute-start | bytes 393224 | tf_op jit(solution)/shard_map/ppermute | solution.py:233
  67.8 12.1 %collective-permute-start.11 = (bf16[32,2048]{1,0:T(8,128)(2,1)}, bf16[32,2048]{1,0:T(8,128)(2,1)S(1)}, u32[]{:S(2)}, u32[]{:S(2)}) collective-permute-start(bf16[32,2048]{1,0:T(8,128)(2,1)} %get-tuple-element.69), channel_id=1, source_target_pairs={{0,8},{1,9},{2,10},{3,11},{4,12},{5,13},{6,14},{7,15},{8,0},{9,1},... | collective-permute-start | bytes 393224 | tf_op jit(solution)/shard_map/ppermute | solution.py:233
  76.1 7.3 %collective-permute-start.12 = (bf16[32,2048]{1,0:T(8,128)(2,1)}, bf16[32,2048]{1,0:T(8,128)(2,1)S(1)}, u32[]{:S(2)}, u32[]{:S(2)}) collective-permute-start(bf16[32,2048]{1,0:T(8,128)(2,1)} %get-tuple-element.70), channel_id=1, source_target_pairs={{0,10},{1,11},{2,8},{3,9},{4,14},{5,15},{6,12},{7,13},{8,2},{9,3},... | collective-permute-start | bytes 393224 | tf_op jit(solution)/shard_map/ppermute | solution.py:233
  76.1 8.6 %collective-permute-start.13 = (bf16[32,2048]{1,0:T(8,128)(2,1)}, bf16[32,2048]{1,0:T(8,128)(2,1)S(1)}, u32[]{:S(2)}, u32[]{:S(2)}) collective-permute-start(bf16[32,2048]{1,0:T(8,128)(2,1)} %get-tuple-element.71), channel_id=1, source_target_pairs={{0,16},{1,17},{2,18},{3,19},{4,20},{5,21},{6,22},{7,23},{8,24},{9,... | collective-permute-start | bytes 393224 | tf_op jit(solution)/shard_map/ppermute | solution.py:233
  77.1 17.3 %collective-permute-start.14 = (bf16[32,2048]{1,0:T(8,128)(2,1)}, bf16[32,2048]{1,0:T(8,128)(2,1)S(1)}, u32[]{:S(2)}, u32[]{:S(2)}) collective-permute-start(bf16[32,2048]{1,0:T(8,128)(2,1)} %get-tuple-element.72), channel_id=1, source_target_pairs={{0,18},{1,19},{2,16},{3,17},{4,22},{5,23},{6,20},{7,21},{8,26},{9,... | collective-permute-start | bytes 393224 | tf_op jit(solution)/shard_map/ppermute | solution.py:233
  79.9 19.8 %collective-permute-start.15 = (bf16[32,2048]{1,0:T(8,128)(2,1)}, bf16[32,2048]{1,0:T(8,128)(2,1)S(1)}, u32[]{:S(2)}, u32[]{:S(2)}) collective-permute-start(bf16[32,2048]{1,0:T(8,128)(2,1)} %get-tuple-element.73), channel_id=1, source_target_pairs={{0,24},{1,25},{2,26},{3,27},{4,28},{5,29},{6,30},{7,31},{8,16},{9,... | collective-permute-start | bytes 393224 | tf_op jit(solution)/shard_map/ppermute | solution.py:233
  83.4 19.9 %collective-permute-start.16 = (bf16[32,2048]{1,0:T(8,128)(2,1)}, bf16[32,2048]{1,0:T(8,128)(2,1)S(1)}, u32[]{:S(2)}, u32[]{:S(2)}) collective-permute-start(bf16[32,2048]{1,0:T(8,128)(2,1)} %get-tuple-element.74), channel_id=1, source_target_pairs={{0,26},{1,27},{2,24},{3,25},{4,30},{5,31},{6,28},{7,29},{8,18},{9,... | collective-permute-start | bytes 393224 | tf_op jit(solution)/shard_map/ppermute | solution.py:233
  110.9 39.3 %copy-start = (f32[128,2048]{1,0:T(8,128)S(1)}, f32[128,2048]{1,0:T(8,128)}, u32[]{:S(2)}) copy-start(f32[128,2048]{1,0:T(8,128)} %get-tuple-element.56.summed_from) | copy-start | bytes 3145732
  111.0 39.3 %copy-start.3 = (s32[1,128,1]{1,2,0:T(1,128)S(1)}, s32[1,128,1]{1,2,0:T(1,128)}, u32[]{:S(2)}) copy-start(s32[1,128,1]{1,2,0:T(1,128)} %param.13) | copy-start | bytes 1540
  111.0 6.8 %collective-permute-start.18 = (bf16[576,2048]{1,0:T(8,128)(2,1)}, bf16[576,2048]{1,0:T(8,128)(2,1)S(1)}, u32[]{:S(2)}, u32[]{:S(2)}) collective-permute-start(bf16[576,2048]{1,0:T(8,128)(2,1)} %collective-permute-done.17.refs_8_), channel_id=1, source_target_pairs={{0,1},{2,3},{4,5},{6,7},{9,8},{11,10},{13,12},{15,14},{16,17},{18,... | collective-permute-start | bytes 7077896 | tf_op jit(solution)/shard_map/ppermute | solution.py:233
  121.4 6.5 %collective-permute-start.19 = (bf16[32,2048]{1,0:T(8,128)(2,1)S(1)}, bf16[32,2048]{1,0:T(8,128)(2,1)S(1)}, u32[]{:S(2)}, u32[]{:S(2)}) collective-permute-start(bf16[32,2048]{1,0:T(8,128)(2,1)S(1)} %get-tuple-element.80), channel_id=1, source_target_pairs={{0,2},{1,3},{2,0},{3,1},{4,6},{5,7},{6,4},{7,5},{8,10},{9,11},{10,... | collective-permute-start | bytes 393224 | tf_op jit(solution)/shard_map/ppermute | solution.py:233
  122.0 7.7 %collective-permute-start.20 = (bf16[32,2048]{1,0:T(8,128)(2,1)S(1)}, bf16[32,2048]{1,0:T(8,128)(2,1)S(1)}, u32[]{:S(2)}, u32[]{:S(2)}) collective-permute-start(bf16[32,2048]{1,0:T(8,128)(2,1)S(1)} %get-tuple-element.81), channel_id=1, source_target_pairs={{0,8},{1,9},{2,10},{3,11},{4,12},{5,13},{6,14},{7,15},{8,0},{9,1},... | collective-permute-start | bytes 393224 | tf_op jit(solution)/shard_map/ppermute | solution.py:233
  122.1 11.4 %collective-permute-start.21 = (bf16[32,2048]{1,0:T(8,128)(2,1)S(1)}, bf16[32,2048]{1,0:T(8,128)(2,1)S(1)}, u32[]{:S(2)}, u32[]{:S(2)}) collective-permute-start(bf16[32,2048]{1,0:T(8,128)(2,1)S(1)} %get-tuple-element.82), channel_id=1, source_target_pairs={{0,10},{1,11},{2,8},{3,9},{4,14},{5,15},{6,12},{7,13},{8,2},{9,3},... | collective-permute-start | bytes 393224 | tf_op jit(solution)/shard_map/ppermute | solution.py:233
  125.0 10.1 %collective-permute-start.22 = (bf16[32,2048]{1,0:T(8,128)(2,1)S(1)}, bf16[32,2048]{1,0:T(8,128)(2,1)S(1)}, u32[]{:S(2)}, u32[]{:S(2)}) collective-permute-start(bf16[32,2048]{1,0:T(8,128)(2,1)S(1)} %get-tuple-element.83), channel_id=1, source_target_pairs={{0,16},{1,17},{2,18},{3,19},{4,20},{5,21},{6,22},{7,23},{8,24},{9,... | collective-permute-start | bytes 393224 | tf_op jit(solution)/shard_map/ppermute | solution.py:233
  126.3 17.2 %collective-permute-start.23 = (bf16[32,2048]{1,0:T(8,128)(2,1)S(1)}, bf16[32,2048]{1,0:T(8,128)(2,1)S(1)}, u32[]{:S(2)}, u32[]{:S(2)}) collective-permute-start(bf16[32,2048]{1,0:T(8,128)(2,1)S(1)} %get-tuple-element.84), channel_id=1, source_target_pairs={{0,18},{1,19},{2,16},{3,17},{4,22},{5,23},{6,20},{7,21},{8,26},{9,... | collective-permute-start | bytes 393224 | tf_op jit(solution)/shard_map/ppermute | solution.py:233
  127.9 20.2 %collective-permute-start.24 = (bf16[32,2048]{1,0:T(8,128)(2,1)S(1)}, bf16[32,2048]{1,0:T(8,128)(2,1)S(1)}, u32[]{:S(2)}, u32[]{:S(2)}) collective-permute-start(bf16[32,2048]{1,0:T(8,128)(2,1)S(1)} %get-tuple-element.85), channel_id=1, source_target_pairs={{0,24},{1,25},{2,26},{3,27},{4,28},{5,29},{6,30},{7,31},{8,16},{9,... | collective-permute-start | bytes 393224 | tf_op jit(solution)/shard_map/ppermute | solution.py:233
  129.8 20.4 %collective-permute-start.25 = (bf16[32,2048]{1,0:T(8,128)(2,1)S(1)}, bf16[32,2048]{1,0:T(8,128)(2,1)S(1)}, u32[]{:S(2)}, u32[]{:S(2)}) collective-permute-start(bf16[32,2048]{1,0:T(8,128)(2,1)S(1)} %get-tuple-element.86), channel_id=1, source_target_pairs={{0,26},{1,27},{2,24},{3,25},{4,30},{5,31},{6,28},{7,29},{8,18},{9,... | collective-permute-start | bytes 393224 | tf_op jit(solution)/shard_map/ppermute | solution.py:233
  (7 other events, 165.6 us)

commit v4 on v3

--- a/solution.py
+++ b/solution.py
@@ -246,11 +246,12 @@
 
 
 def second_hop(z, x, y, core):
-    return (z, x ^ 1, y, core) if is_home(z, core) else None
-
-
-def home_to_twin(z, x, y, core):
-    return (z, x, y, 1 - core) if is_home(z, core) else None
+    return (z, x ^ 1, y, 1 - core) if is_home(z, core) else None
+
+
+def pack_half(half, *weights):
+    rows = weights[0].shape[0] // 2
+    return jnp.concatenate([w[half * rows : (half + 1) * rows] for w in weights], axis=0)
 
 
 def slot_targets(ids_row, z_here, y_here, capacity):
@@ -347,14 +348,15 @@
     keep.wait()
 
 
-def load_pack(pack, place, strip, targets, semaphores):
+def load_pack(pair, strip, targets, semaphores):
     return [
         pltpu.make_async_copy(
-            pack.at[pl.ds(kind * strip, strip)],
-            targets[kind].at[pl.ds(place * strip, strip)],
-            semaphores.at[place, kind],
+            pair[half].at[pl.ds(kind * strip, strip)],
+            targets[kind].at[pl.ds(half * strip, strip)],
+            semaphores.at[kind, half],
         )
         for kind in range(3)
+        for half in range(2)
     ]
 
 
@@ -365,60 +367,69 @@
     return (silu * up_part).astype(jnp.bfloat16)
 
 
-def expert_kernel(places, where_ref, *refs):
-    row_from, pack_from, rest = refs[:8], refs[8 : 9 + places], refs[9 + places :]
-    continued = places == 1
-    if continued:
-        before_from, rest = rest[0], rest[1:]
-        out_refs, rest = rest[:8], rest[8:]
+def expert_kernel(row_count, where_ref, *refs):
+    row_from, refs = refs[:row_count], refs[row_count:]
+    first_piece = len(refs) == 10
+    if first_piece:
+        pairs, (total_ref,), rest = [refs[:2]], refs[2:3], refs[3:]
     else:
-        out_refs, rest = rest[:1], rest[1:]
+        pairs, before_from, (mine_ref, twins_ref), rest = (
+            [refs[:2], refs[2:4]],
+            refs[4],
+            refs[5:7],
+            refs[7:],
+        )
     rows_ref, before_ref, gate_ref, up_ref, down_ref, row_semaphores, semaphores = rest
-    at_home = where_ref[3] == 1
-    away = jnp.logical_not(at_home)
-    strip = pack_from[0].shape[0] // 3
-    capacity = row_from[0].shape[0]
+    strip = pairs[0][0].shape[0] // 3
     targets = (gate_ref, up_ref, down_ref)
-    loads = [(row_from[k], rows_ref.at[pl.ds(k * capacity, capacity)]) for k in range(8)]
-    if continued:
+    loads = []
+    place = 0
+    for ref in row_from:
+        loads.append((ref, rows_ref.at[pl.ds(place, ref.shape[0])]))
+        place += ref.shape[0]
+    if not first_piece:
         loads.append((before_from, before_ref))
     row_copies = fetch_all(loads, row_semaphores)
-
-    @pl.when(at_home)
-    def _():
-        for copy in load_pack(pack_from[0], 0, strip, targets, semaphores):
+    weight_copies = load_pack(pairs[0], strip, targets, semaphores)
+    if first_piece:
+        for copy in weight_copies:
             copy.start()
-
-    @pl.when(away)
-    def _():
-        for copy in load_pack(pack_from[1], 0, strip, targets, semaphores):
-            copy.start()
-
-    waits = [load_pack(pack_from[0], 0, strip, targets, semaphores)]
-    for place in range(1, places):
-        waits.append(load_pack(pack_from[place + 1], place, strip, targets, semaphores))
-        for copy in waits[place]:
-            copy.start()
-    for copy in row_copies:
+    else:
+        at_home = where_ref[3] == 1
+
+        @pl.when(at_home)
+        def _():
+            for copy in load_pack(pairs[0], strip, targets, semaphores):
+                copy.start()
+
+        @pl.when(jnp.logical_not(at_home))
+        def _():
+            for copy in load_pack(pairs[1], strip, targets, semaphores):
+                copy.start()
+
+    for copy in row_copies + weight_copies[:4]:
         copy.wait()
-    rows = rows_ref[...]
-    actives = []
-    for place in range(places):
-        for copy in waits[place][:2]:
-            copy.wait()
-        span = slice(place * strip, (place + 1) * strip)
-        actives.append(active_of(rows, gate_ref[span, :], up_ref[span, :]))
-    for place in range(places):
-        for copy in waits[place][2:]:
-            copy.wait()
-    active = actives[0] if continued else jnp.concatenate(actives, axis=1)
+    active = active_of(rows_ref[...], gate_ref[...], up_ref[...])
+    for copy in weight_copies[4:]:
+        copy.wait()
     result = jnp.dot(active, down_ref[...], preferred_element_type=jnp.float32)
-    if continued:
-        result = (result + before_ref[...]).astype(jnp.bfloat16)
-        for k in range(8):
-            out_refs[k][...] = result[k * capacity : (k + 1) * capacity]
+    if first_piece:
+        total_ref[...] = result
     else:
-        out_refs[0][...] = result
+        result = result + before_ref[...]
+        half = result.shape[0] // 2
+        mine_ref[...] = result[:half]
+        twins_ref[...] = result[half:].astype(jnp.bfloat16)
+
+
+def join_kernel(mine_from, other_from, *refs):
+    out_refs, (mine_ref, other_ref, semaphores) = refs[:8], refs[8:]
+    capacity = out_refs[0].shape[0]
+    for copy in fetch_all([(mine_from, mine_ref), (other_from, other_ref)], semaphores):
+        copy.wait()
+    result = (mine_ref[...] + other_ref[...].astype(jnp.float32)).astype(jnp.bfloat16)
+    for k in range(8):
+        out_refs[k][...] = result[k * capacity : (k + 1) * capacity]
 
 
 def combine_kernel(where_ref, ids_ref, route_ref, summed_from, *refs):
@@ -472,17 +483,14 @@
 
         kv_blocks[k] = move(block, later)
 
-    own = jnp.concatenate([gate_weight[0, 0], up_weight[0, 0], down_weight[0, 0]], axis=0)
-    send_keys(kv_own, 7)
-    own, kv_blocks[7], kv_next = lax.optimization_barrier((own, kv_blocks[7], kv_own))
-    one = move(own, first_hop)
-    for k in (4, 6, 5, 3, 2, 1):
-        send_keys(kv_next, k)
+    own = [pack_half(half, gate_weight[0, 0], up_weight[0, 0], down_weight[0, 0]) for half in range(2)]
+    one_first = move(own[0], first_hop)
+    for k in (4, 5, 3, 2, 6, 1, 7):
+        send_keys(kv_own, k)
     kv_list = [kv_blocks[k] for k in range(1, 8)]
-    one, own, *kv_list = lax.optimization_barrier((one, own, *kv_list))
-    last = move(one, second_hop)
-    own_twin = move(own, home_to_twin)
-    one_twin = move(one, to_twin)
+    one_first, own[0], own[1], *kv_list = lax.optimization_barrier((one_first, *own, *kv_list))
+    one_second = move(own[1], first_hop)
+    last_first = move(one_first, second_hop)
     slot_shape = jax.ShapeDtypeStruct((capacity, width), jnp.bfloat16)
     keys_all = 8 * tokens
     rows_all = 8 * capacity
@@ -515,38 +523,67 @@
             return array
         return move(array, lambda z, x, y, core: (z ^ (k >> 1), x, y ^ (k & 1), core))
 
-    own_twin, one_twin, *outgoing = lax.optimization_barrier((own_twin, one_twin, *outgoing))
-    arrived = [outgoing[0]] + [swap(outgoing[k], k) for k in range(1, 8)]
-    def run_expert(places, rows, packs, before):
-        total = jax.ShapeDtypeStruct((rows_all, width), jnp.float32)
-        inner = places * piece
+    early, late = (4, 6, 2), (5, 7, 3, 1)
+    arrived = [swap(outgoing[k], k) if k in early else outgoing[k] for k in range(8)]
+    one_second, *held = lax.optimization_barrier((one_second, *[arrived[k] for k in late]))
+    for k, array in zip(late, held):
+        arrived[k] = swap(array, k)
+    last_second = move(one_second, second_hop)
+    order = (0, *early, *late)
+    row_parts = [jnp.concatenate([arrived[k] for k in group]) for group in (order[:4], order[4:])]
+    row_parts += [move(part, to_twin) for part in row_parts]
+    half_rows = row_parts[0].shape[0]
+
+    def run_expert(packs, before):
+        row_total = 2 * rows_all
+        mine = jax.ShapeDtypeStruct((rows_all, width), jnp.float32)
+        twins = jax.ShapeDtypeStruct((rows_all, width), jnp.bfloat16)
+        total = jax.ShapeDtypeStruct((row_total, width), jnp.float32)
         return pl.pallas_call(
-            partial(expert_kernel, places),
-            out_shape=[slot_shape] * 8 if before else [total],
-            in_specs=[IN_SMEM] + [IN_HBM] * (8 + len(packs) + len(before)),
-            out_specs=[IN_VMEM] * (8 if before else 1),
+            partial(expert_kernel, len(row_parts)),
+            out_shape=[mine, twins] if before else [total],
+            in_specs=[IN_SMEM] + [IN_HBM] * (len(row_parts) + len(packs) + len(before)),
+            out_specs=[IN_VMEM] * (2 if before else 1),
             scratch_shapes=[
-                pltpu.VMEM((rows_all, width), jnp.bfloat16),
-                pltpu.VMEM((rows_all if before else 8, width), jnp.float32),
-                pltpu.VMEM((inner, width), jnp.bfloat16),
-                pltpu.VMEM((inner, width), jnp.bfloat16),
-                pltpu.VMEM((inner, width), jnp.bfloat16),
-                pltpu.SemaphoreType.DMA((9,)),
-                pltpu.SemaphoreType.DMA((places, 3)),
+                pltpu.VMEM((row_total, width), jnp.bfloat16),
+                pltpu.VMEM((row_total if before else 8, width), jnp.float32),
+                pltpu.VMEM((piece, width), jnp.bfloat16),
+                pltpu.VMEM((piece, width), jnp.bfloat16),
+                pltpu.VMEM((piece, width), jnp.bfloat16),
+                pltpu.SemaphoreType.DMA((5,)),
+                pltpu.SemaphoreType.DMA((3, 2)),
             ],
-            compiler_params=pltpu.CompilerParams(vmem_limit_bytes=24 << 20),
+            compiler_params=pltpu.CompilerParams(vmem_limit_bytes=32 << 20),
             cost_estimate=pl.CostEstimate(
-                flops=6 * rows_all * inner * width,
-                bytes_accessed=6 * inner * width,
-                transcendentals=rows_all * inner,
+                flops=6 * row_total * piece * width,
+                bytes_accessed=6 * piece * width,
+                transcendentals=row_total * piece,
             ),
-            name="experts_%d" % places,
-        )(where, *rows, *packs, *before)
-
-    most = run_expert(3, arrived, [own, own_twin, one, one_twin], [])
-    last, *most = lax.optimization_barrier((last, *most))
-    last_twin = move(last, home_to_twin)
-    results = run_expert(1, arrived, [last, last_twin], most)
+            name="experts_rest" if before else "experts_first",
+        )(where, *row_parts, *packs, *before)
+
+    first_total = run_expert([one_first, one_second], [])
+    last_first, last_second, *first_total = lax.optimization_barrier(
+        (last_first, last_second, *first_total)
+    )
+    mine, twins = run_expert([*own, last_first, last_second], first_total)
+    joined = pl.pallas_call(
+        join_kernel,
+        out_shape=[slot_shape] * 8,
+        in_specs=[IN_HBM] * 2,
+        out_specs=[IN_VMEM] * 8,
+        scratch_shapes=[
+            pltpu.VMEM((rows_all, width), jnp.float32),
+            pltpu.VMEM((rows_all, width), jnp.bfloat16),
+            pltpu.SemaphoreType.DMA((2,)),
+        ],
+        compiler_params=pltpu.CompilerParams(vmem_limit_bytes=16 << 20),
+        cost_estimate=pl.CostEstimate(
+            flops=rows_all * width, bytes_accessed=8 * rows_all * width, transcendentals=0
+        ),
+        name="join",
+    )(mine, move(twins, to_twin))
+    results = [joined[order.index(k)] for k in range(8)]
     returned = [swap(results[k], k) for k in range(8)]
     output = pl.pallas_call(
         combine_kernel,

time: 154 us -> 136 us (0.88)
  starting transfers between devices: 71.8 us -> 57.3 us
  waiting for transfers between devices: 54.9 us -> 52.4 us
  local copies, waits for them, and re-layouts: 1.07 us -> 3.51 us
  other arithmetic: 3.24 us -> 0.89 us
    ppermute x26 -> x28, starting transfers between devices: 71.8 us -> 57.3 us  [move(): return lax.ppermute(array, AXES, pairs)]
    ppermute x26 -> x28, waiting for transfers between devices: 54.9 us -> 52.4 us  [move(): return lax.ppermute(array, AXES, pairs)]
    pallas_call x2 -> x3, Pallas kernels: 10.3 us -> 8.94 us  [the longest x2 8.53 us: run_expert(): pl.pallas_call(partial(expert_kernel, len(row_parts)), out_shape=[mine, t...]
  transfers between devices with their start and end apart: 26 -> 28, of which waited for: 13 -> 14; matrix products, arithmetic and copies ran while one was open for 2% -> 1% of each run, Pallas kernels for 10% -> 9%
where the time goes in v4:
time: 136 us; the launch traced here: 135 us
  starting transfers between devices  57.3 us (42%)
  waiting for transfers between devices  52.4 us (39%)
  Pallas kernels  20.8 us (15%)
  local copies, waits for them, and re-layouts  3.51 us (3%)
    ppermute x28, starting transfers between devices, move(): return lax.ppermute(array, AXES, pairs)  57.3 us
    ppermute x28, waiting for transfers between devices, move(): return lax.ppermute(array, AXES, pairs)  52.4 us
    pallas_call x2, Pallas kernels, run_expert(): pl.pallas_call(partial(expert_kernel, len(row_parts)), out_shape=[mine, t...  8.53 us
    pallas_call x1, Pallas kernels, shards_cube(): pl.pallas_call(attend_kernel, out_shape=[jax.ShapeDtypeStruct((tokens, wi...  8.48 us
    pallas_call x1, Pallas kernels, shards_cube(): pl.pallas_call(combine_kernel, out_shape=jax.ShapeDtypeStruct((tokens, wi...  3.35 us
  transfers between devices with their start and end apart: 28, of which 14 were waited for; matrix products, arithmetic and copies ran while one was open for 1% of the time, Pallas kernels for 9%

profile of v4, /device:TPU:8, one launch (start us, length us, event | category | flops | bytes accessed | tf_op | source)
XLA Modules:
  0.0 135.4 jit_solution(7592305072312650476)
XLA Ops:
  0.0 1.3 slice_bitcast_fusion.2
  2.6 3.4 %collective-permute-start.1 = (bf16[128,512]{1,0:T(8,128)(2,1)S(1)}, bf16[128,512]{1,0:T(8,128)(2,1)S(1)}, u32[]{:S(2)}, u32[]{:S(2)}) collective-permute-start(bf16[128,512]{1,0:T(8,128)(2,1)S(1)} %pad_maximum_fusion.2.refs_0_), channel_id=1, source_target_pairs={{0,4},{1,5},{2,6},{3,7},{4,8},{5,9},{6,10},{7,11},{8,12},{9,13},{1... | collective-permute-start | bytes 393224 | tf_op jit(solution)/shard_map/ppermute | solution.py:233
  6.0 3.5 %collective-permute-start.2 = (bf16[128,512]{1,0:T(8,128)(2,1)S(1)}, bf16[128,512]{1,0:T(8,128)(2,1)S(1)}, u32[]{:S(2)}, u32[]{:S(2)}) collective-permute-start(bf16[128,512]{1,0:T(8,128)(2,1)S(1)} %pad_maximum_fusion.2.refs_0_), channel_id=1, source_target_pairs={{0,8},{1,9},{2,10},{3,11},{4,12},{5,13},{6,14},{7,15},{8,16},{9,17... | collective-permute-start | bytes 393224 | tf_op jit(solution)/shard_map/ppermute | solution.py:233
  9.5 2.9 %collective-permute-start.3 = (bf16[128,512]{1,0:T(8,128)(2,1)S(1)}, bf16[128,512]{1,0:T(8,128)(2,1)S(1)}, u32[]{:S(2)}, u32[]{:S(2)}) collective-permute-start(bf16[128,512]{1,0:T(8,128)(2,1)S(1)} %pad_maximum_fusion.2.refs_0_), channel_id=1, source_target_pairs={{0,12},{1,13},{2,14},{3,15},{4,16},{5,17},{6,18},{7,19},{8,20},{9,... | collective-permute-start | bytes 393224 | tf_op jit(solution)/shard_map/ppermute | solution.py:233
  12.4 1.3 collective-permute-start.4
  13.8 2.6 %collective-permute-start.5 = (bf16[128,512]{1,0:T(8,128)(2,1)S(1)}, bf16[128,512]{1,0:T(8,128)(2,1)S(1)}, u32[]{:S(2)}, u32[]{:S(2)}) collective-permute-start(bf16[128,512]{1,0:T(8,128)(2,1)S(1)} %pad_maximum_fusion.2.refs_0_), channel_id=1, source_target_pairs={{0,20},{1,21},{2,22},{3,23},{4,24},{5,25},{6,26},{7,27},{8,28},{9,... | collective-permute-start | bytes 393224 | tf_op jit(solution)/shard_map/ppermute | solution.py:233
  17.9 1.9 %collective-permute-done.4.refs_4_ = bf16[128,512]{1,0:T(8,128)(2,1)S(1)} collective-permute-done((bf16[128,512]{1,0:T(8,128)(2,1)S(1)}, bf16[128,512]{1,0:T(8,128)(2,1)S(1)}, u32[]{:S(2)}, u32[]{:S(2)}) %collective-permute-start.4) | collective-permute-done | bytes 131104 | tf_op jit(solution)/shard_map/ppermute | solution.py:233
  19.8 1.9 %collective-permute-done.5.refs_5_ = bf16[128,512]{1,0:T(8,128)(2,1)S(1)} collective-permute-done((bf16[128,512]{1,0:T(8,128)(2,1)S(1)}, bf16[128,512]{1,0:T(8,128)(2,1)S(1)}, u32[]{:S(2)}, u32[]{:S(2)}) %collective-permute-start.5) | collective-permute-done | bytes 131104 | tf_op jit(solution)/shard_map/ppermute | solution.py:233
  21.7 12.6 %collective-permute-start.11 = (bf16[288,2048]{1,0:T(8,128)(2,1)S(1)}, bf16[288,2048]{1,0:T(8,128)(2,1)}, u32[]{:S(2)}, u32[]{:S(2)}) collective-permute-start(bf16[288,2048]{1,0:T(8,128)(2,1)S(1)} %pad_maximum_fusion.1.refs_5_), channel_id=1, source_target_pairs={{0,5},{1,9},{2,7},{3,11},{4,1},{5,13},{6,3},{7,15},{8,0},{9,12},{1... | collective-permute-start | bytes 3538952 | tf_op jit(solution)/shard_map/ppermute | solution.py:233
  35.0 8.5 %attend.1 = (f32[128,2048]{1,0:T(8,128)}, bf16[32,2048]{1,0:T(8,128)(2,1)}, bf16[32,2048]{1,0:T(8,128)(2,1)}, bf16[32,2048]{1,0:T(8,128)(2,1)}, bf16[32,2048]{1,...) custom-call(s32[4]{0:T(128)} %pad_add_fusion.where_ref, ...), custom_call_target="tpu_custom_call" | custom-call | flops 1073741824 | bytes 2097152 | tf_op jit(solution)/shard_map/attend/pallas_call | solution.py:497
  43.5 2.2 %collective-permute-start.8 = (bf16[32,2048]{1,0:T(8,128)(2,1)}, bf16[32,2048]{1,0:T(8,128)(2,1)S(1)}, u32[]{:S(2)}, u32[]{:S(2)}) collective-permute-start(bf16[32,2048]{1,0:T(8,128)(2,1)} %get-tuple-element.51), channel_id=1, source_target_pairs={{0,16},{1,17},{2,18},{3,19},{4,20},{5,21},{6,22},{7,23},{8,24},{9,... | collective-permute-start | bytes 393224 | tf_op jit(solution)/shard_map/ppermute | solution.py:233
  45.8 5.4 %collective-permute-start.9 = (bf16[32,2048]{1,0:T(8,128)(2,1)}, bf16[32,2048]{1,0:T(8,128)(2,1)S(1)}, u32[]{:S(2)}, u32[]{:S(2)}) collective-permute-start(bf16[32,2048]{1,0:T(8,128)(2,1)} %get-tuple-element.52), channel_id=1, source_target_pairs={{0,24},{1,25},{2,26},{3,27},{4,28},{5,29},{6,30},{7,31},{8,16},{9,... | collective-permute-start | bytes 393224 | tf_op jit(solution)/shard_map/ppermute | solution.py:233
  53.4 9.2 %collective-permute-done.9 = bf16[32,2048]{1,0:T(8,128)(2,1)S(1)} collective-permute-done((bf16[32,2048]{1,0:T(8,128)(2,1)}, bf16[32,2048]{1,0:T(8,128)(2,1)S(1)}, u32[]{:S(2)}, u32[]{:S(2)}) %collective-permute-start.9) | collective-permute-done | bytes 131104 | tf_op jit(solution)/shard_map/ppermute | solution.py:233
  62.8 2.2 %collective-permute-start.16 = (bf16[128,2048]{1,0:T(8,128)(2,1)S(1)}, bf16[128,2048]{1,0:T(8,128)(2,1)S(1)}, u32[]{:S(2)}, u32[]{:S(2)}) collective-permute-start(bf16[128,2048]{1,0:T(8,128)(2,1)S(1)} %constant_dynamic-update-slice_fusion.refs_0_), channel_id=1, source_target_pairs={{0,1},{1,0},{2,3},{3,2},{4,5},{5,4},{6,7},{7,6},{8,9},{9,8},{10,11... | collective-permute-start | bytes 1572872 | tf_op jit(solution)/shard_map/ppermute | solution.py:233
  65.0 4.1 %collective-permute-start.14 = (bf16[32,2048]{1,0:T(8,128)(2,1)}, bf16[32,2048]{1,0:T(8,128)(2,1)S(1)}, u32[]{:S(2)}, u32[]{:S(2)}) collective-permute-start(bf16[32,2048]{1,0:T(8,128)(2,1)} %get-tuple-element.61), channel_id=1, source_target_pairs={{0,10},{1,11},{2,8},{3,9},{4,14},{5,15},{6,12},{7,13},{8,2},{9,3},... | collective-permute-start | bytes 393224 | tf_op jit(solution)/shard_map/ppermute | solution.py:233
  69.1 1.6 %collective-permute-done.12 = bf16[32,2048]{1,0:T(8,128)(2,1)S(1)} collective-permute-done((bf16[32,2048]{1,0:T(8,128)(2,1)}, bf16[32,2048]{1,0:T(8,128)(2,1)S(1)}, u32[]{:S(2)}, u32[]{:S(2)}) %collective-permute-start.12) | collective-permute-done | bytes 131104 | tf_op jit(solution)/shard_map/ppermute | solution.py:233
  70.7 2.9 %collective-permute-start.15 = (bf16[32,2048]{1,0:T(8,128)(2,1)}, bf16[32,2048]{1,0:T(8,128)(2,1)S(1)}, u32[]{:S(2)}, u32[]{:S(2)}) collective-permute-start(bf16[32,2048]{1,0:T(8,128)(2,1)} %get-tuple-element.62), channel_id=1, source_target_pairs={{0,2},{1,3},{2,0},{3,1},{4,6},{5,7},{6,4},{7,5},{8,10},{9,11},{10,... | collective-permute-start | bytes 393224 | tf_op jit(solution)/shard_map/ppermute | solution.py:233
  73.6 5.4 %collective-permute-done.13 = bf16[32,2048]{1,0:T(8,128)(2,1)S(1)} collective-permute-done((bf16[32,2048]{1,0:T(8,128)(2,1)}, bf16[32,2048]{1,0:T(8,128)(2,1)S(1)}, u32[]{:S(2)}, u32[]{:S(2)}) %collective-permute-start.13) | collective-permute-done | bytes 131104 | tf_op jit(solution)/shard_map/ppermute | solution.py:233
  79.0 1.3 collective-permute-start.19
  82.2 1.5 %collective-permute-done.17.refs_3_ = bf16[128,2048]{1,0:T(8,128)(2,1)S(1)} collective-permute-done((bf16[128,2048]{1,0:T(8,128)(2,1)S(1)}, bf16[128,2048]{1,0:T(8,128)(2,1)S(1)}, u32[]{:S(2)}, u32[]{:S(2)}) %collective-permute-start.17) | collective-permute-done | bytes 524320 | tf_op jit(solution)/shard_map/ppermute | solution.py:233
  83.7 4.2 %experts_first.1.refs_8_ = f32[512,2048]{1,0:T(8,128)S(1)} custom-call(s32[4]{0:T(128)S(1)} %copy-done.1, bf16[128,2048]{1,0:T(8,128)(2,1)S(1)} %constant_dynamic-update-slice_fusion.refs_0_, bf16[128,2048]{1,0:T(8,128)(2,1)S(1)} %constant_dynamic-update-slice_fusion.4.refs_1_, bf16[128,2048]{1,0:T(8,128)(2,1)S(1)} %collective-permute-done.16.refs_2_, ...), custom_call_target="tpu_custom_call" | custom-call | flops 1207959552 | bytes 2359296 | tf_op jit(solution)/shard_map/experts_first/pallas_call | solution.py:542
  87.9 8.8 %collective-permute-done.19.refs_7_ = bf16[288,2048]{1,0:T(8,128)(2,1)S(1)} collective-permute-done((bf16[288,2048]{1,0:T(8,128)(2,1)}, bf16[288,2048]{1,0:T(8,128)(2,1)S(1)}, u32[]{:S(2)}, u32[]{:S(2)}) %collective-permute-start.19) | collective-permute-done | bytes 1179680 | tf_op jit(solution)/shard_map/ppermute | solution.py:233
  96.7 4.4 %experts_rest.1 = (f32[256,2048]{1,0:T(8,128)S(1)}, bf16[256,2048]{1,0:T(8,128)(2,1)S(1)}) custom-call(s32[4]{0:T(128)S(1)} %copy-done.1, bf16[128,2048]{1,0:T(8,128)(2,1)S(1)} %constant_dynamic-update-slice_fusion.refs_0_, bf16[128,2048]{1,0:T(8,128)(2,1)S(1)} %constant_dynamic-update-slice_fusion.4.refs_1_, ...), custom_call_target="tpu_custom_call" | custom-call | flops 1207959552 | bytes 2359296 | tf_op jit(solution)/shard_map/experts_rest/pallas_call | solution.py:542
  101.2 2.6 %collective-permute-done.20.other_from = bf16[256,2048]{1,0:T(8,128)(2,1)S(1)} collective-permute-done((bf16[256,2048]{1,0:T(8,128)(2,1)S(1)}, bf16[256,2048]{1,0:T(8,128)(2,1)S(1)}, u32[]{:S(2)}, u32[]{:S(2)}) %collective-permute-start.20) | collective-permute-done | bytes 1048608 | tf_op jit(solution)/shard_map/ppermute | solution.py:233
  104.5 3.2 %collective-permute-start.23 = (bf16[32,2048]{1,0:T(8,128)(2,1)S(1)}, bf16[32,2048]{1,0:T(8,128)(2,1)S(1)}, u32[]{:S(2)}, u32[]{:S(2)}) collective-permute-start(bf16[32,2048]{1,0:T(8,128)(2,1)S(1)} %get-tuple-element.74), channel_id=1, source_target_pairs={{0,10},{1,11},{2,8},{3,9},{4,14},{5,15},{6,12},{7,13},{8,2},{9,3},... | collective-permute-start | bytes 393224 | tf_op jit(solution)/shard_map/ppermute | solution.py:233
  107.8 2.6 %collective-permute-start.25 = (bf16[32,2048]{1,0:T(8,128)(2,1)S(1)}, bf16[32,2048]{1,0:T(8,128)(2,1)S(1)}, u32[]{:S(2)}, u32[]{:S(2)}) collective-permute-start(bf16[32,2048]{1,0:T(8,128)(2,1)S(1)} %get-tuple-element.76), channel_id=1, source_target_pairs={{0,18},{1,19},{2,16},{3,17},{4,22},{5,23},{6,20},{7,21},{8,26},{9,... | collective-permute-start | bytes 393224 | tf_op jit(solution)/shard_map/ppermute | solution.py:233
  111.2 2.4 %collective-permute-start.27 = (bf16[32,2048]{1,0:T(8,128)(2,1)S(1)}, bf16[32,2048]{1,0:T(8,128)(2,1)S(1)}, u32[]{:S(2)}, u32[]{:S(2)}) collective-permute-start(bf16[32,2048]{1,0:T(8,128)(2,1)S(1)} %get-tuple-element.78), channel_id=1, source_target_pairs={{0,26},{1,27},{2,24},{3,25},{4,30},{5,31},{6,28},{7,29},{8,18},{9,... | collective-permute-start | bytes 393224 | tf_op jit(solution)/shard_map/ppermute | solution.py:233
  114.9 1.9 %collective-permute-done.24.refs_4_ = bf16[32,2048]{1,0:T(8,128)(2,1)S(1)} collective-permute-done((bf16[32,2048]{1,0:T(8,128)(2,1)S(1)}, bf16[32,2048]{1,0:T(8,128)(2,1)S(1)}, u32[]{:S(2)}, u32[]{:S(2)}) %collective-permute-start.24) | collective-permute-done | bytes 131104 | tf_op jit(solution)/shard_map/ppermute | solution.py:233
  116.9 8.3 %collective-permute-done.25.refs_5_ = bf16[32,2048]{1,0:T(8,128)(2,1)S(1)} collective-permute-done((bf16[32,2048]{1,0:T(8,128)(2,1)S(1)}, bf16[32,2048]{1,0:T(8,128)(2,1)S(1)}, u32[]{:S(2)}, u32[]{:S(2)}) %collective-permute-start.25) | collective-permute-done | bytes 131104 | tf_op jit(solution)/shard_map/ppermute | solution.py:233
  125.2 5.2 %collective-permute-done.26.refs_6_ = bf16[32,2048]{1,0:T(8,128)(2,1)S(1)} collective-permute-done((bf16[32,2048]{1,0:T(8,128)(2,1)S(1)}, bf16[32,2048]{1,0:T(8,128)(2,1)S(1)}, u32[]{:S(2)}, u32[]{:S(2)}) %collective-permute-start.26) | collective-permute-done | bytes 131104 | tf_op jit(solution)/shard_map/ppermute | solution.py:233
  130.4 1.5 %collective-permute-done.27.refs_7_ = bf16[32,2048]{1,0:T(8,128)(2,1)S(1)} collective-permute-done((bf16[32,2048]{1,0:T(8,128)(2,1)S(1)}, bf16[32,2048]{1,0:T(8,128)(2,1)S(1)}, u32[]{:S(2)}, u32[]{:S(2)}) %collective-permute-start.27) | collective-permute-done | bytes 131104 | tf_op jit(solution)/shard_map/ppermute | solution.py:233
  131.9 3.3 %combine.1 = bf16[128,2048]{1,0:T(8,128)(2,1)} custom-call(s32[4]{0:T(128)S(1)} %copy-done.1, s32[1,128]{1,0:T(1,128)S(1)} %bitcast.24, f32[128,1]{1,0:T(8,128)S(1)} %copy.10.route_ref, f32[128,2048]{1,0:T(8,128)S(1)} %copy-done, bf16[32,2048]{1,0:T(8,128)(2,1)S(1)} %get-tuple-element.71.refs_0_, bf16[32,2048]{1,0:T(8,128)(2,1)S(1)} %collective-permute-done.21.refs_1_, ...), custom_call_target="tpu_custom_call" | custom-call | flops 134217728 | bytes 3145728 | tf_op jit(solution)/shard_map/combine/pallas_call | solution.py:588
  (76 shorter events, 10.6 us)
Async XLA Ops:
  1.9 19.9 %collective-permute-start = (bf16[288,2048]{1,0:T(8,128)(2,1)S(1)}, bf16[288,2048]{1,0:T(8,128)(2,1)S(1)}, u32[]{:S(2)}, u32[]{:S(2)}) collective-permute-start(bf16[288,2048]{1,0:T(8,128)(2,1)S(1)} %pad_maximum_fusion.refs_4_), channel_id=1, source_target_pairs={{0,5},{1,9},{2,7},{3,11},{4,1},{5,13},{6,3},{7,15},{8,0},{9,12},{1... | collective-permute-start | bytes 3538952 | tf_op jit(solution)/shard_map/ppermute | solution.py:233
  2.6 15.3 %copy-start.5 = (bf16[128,512]{1,0:T(8,128)(2,1)}, bf16[128,512]{1,0:T(8,128)(2,1)S(1)}, u32[]{:S(2)}) copy-start(bf16[128,512]{1,0:T(8,128)(2,1)S(1)} %pad_maximum_fusion.2.refs_0_) | copy-start | bytes 393220
  2.6 11.1 %collective-permute-start.1 = (bf16[128,512]{1,0:T(8,128)(2,1)S(1)}, bf16[128,512]{1,0:T(8,128)(2,1)S(1)}, u32[]{:S(2)}, u32[]{:S(2)}) collective-permute-start(bf16[128,512]{1,0:T(8,128)(2,1)S(1)} %pad_maximum_fusion.2.refs_0_), channel_id=1, source_target_pairs={{0,4},{1,5},{2,6},{3,7},{4,8},{5,9},{6,10},{7,11},{8,12},{9,13},{1... | collective-permute-start | bytes 393224 | tf_op jit(solution)/shard_map/ppermute | solution.py:233
  6.0 10.4 %collective-permute-start.2 = (bf16[128,512]{1,0:T(8,128)(2,1)S(1)}, bf16[128,512]{1,0:T(8,128)(2,1)S(1)}, u32[]{:S(2)}, u32[]{:S(2)}) collective-permute-start(bf16[128,512]{1,0:T(8,128)(2,1)S(1)} %pad_maximum_fusion.2.refs_0_), channel_id=1, source_target_pairs={{0,8},{1,9},{2,10},{3,11},{4,12},{5,13},{6,14},{7,15},{8,16},{9,17... | collective-permute-start | bytes 393224 | tf_op jit(solution)/shard_map/ppermute | solution.py:233
  9.5 7.6 %collective-permute-start.3 = (bf16[128,512]{1,0:T(8,128)(2,1)S(1)}, bf16[128,512]{1,0:T(8,128)(2,1)S(1)}, u32[]{:S(2)}, u32[]{:S(2)}) collective-permute-start(bf16[128,512]{1,0:T(8,128)(2,1)S(1)} %pad_maximum_fusion.2.refs_0_), channel_id=1, source_target_pairs={{0,12},{1,13},{2,14},{3,15},{4,16},{5,17},{6,18},{7,19},{8,20},{9,... | collective-permute-start | bytes 393224 | tf_op jit(solution)/shard_map/ppermute | solution.py:233
  12.4 7.4 %collective-permute-start.4 = (bf16[128,512]{1,0:T(8,128)(2,1)S(1)}, bf16[128,512]{1,0:T(8,128)(2,1)S(1)}, u32[]{:S(2)}, u32[]{:S(2)}) collective-permute-start(bf16[128,512]{1,0:T(8,128)(2,1)S(1)} %pad_maximum_fusion.2.refs_0_), channel_id=1, source_target_pairs={{0,16},{1,17},{2,18},{3,19},{4,20},{5,21},{6,22},{7,23},{8,24},{9,... | collective-permute-start | bytes 393224 | tf_op jit(solution)/shard_map/ppermute | solution.py:233
  13.8 7.9 %collective-permute-start.5 = (bf16[128,512]{1,0:T(8,128)(2,1)S(1)}, bf16[128,512]{1,0:T(8,128)(2,1)S(1)}, u32[]{:S(2)}, u32[]{:S(2)}) collective-permute-start(bf16[128,512]{1,0:T(8,128)(2,1)S(1)} %pad_maximum_fusion.2.refs_0_), channel_id=1, source_target_pairs={{0,20},{1,21},{2,22},{3,23},{4,24},{5,25},{6,26},{7,27},{8,28},{9,... | collective-permute-start | bytes 393224 | tf_op jit(solution)/shard_map/ppermute | solution.py:233
  16.4 5.3 %collective-permute-start.6 = (bf16[128,512]{1,0:T(8,128)(2,1)S(1)}, bf16[128,512]{1,0:T(8,128)(2,1)S(1)}, u32[]{:S(2)}, u32[]{:S(2)}) collective-permute-start(bf16[128,512]{1,0:T(8,128)(2,1)S(1)} %pad_maximum_fusion.2.refs_0_), channel_id=1, source_target_pairs={{0,24},{1,25},{2,26},{3,27},{4,28},{5,29},{6,30},{7,31}} | collective-permute-start | bytes 393224 | tf_op jit(solution)/shard_map/ppermute | solution.py:233
  17.1 4.6 %collective-permute-start.7 = (bf16[128,512]{1,0:T(8,128)(2,1)S(1)}, bf16[128,512]{1,0:T(8,128)(2,1)S(1)}, u32[]{:S(2)}, u32[]{:S(2)}) collective-permute-start(bf16[128,512]{1,0:T(8,128)(2,1)S(1)} %pad_maximum_fusion.2.refs_0_), channel_id=1, source_target_pairs={{0,28},{1,29},{2,30},{3,31}} | collective-permute-start | bytes 393224 | tf_op jit(solution)/shard_map/ppermute | solution.py:233
  21.7 40.9 %collective-permute-start.11 = (bf16[288,2048]{1,0:T(8,128)(2,1)S(1)}, bf16[288,2048]{1,0:T(8,128)(2,1)}, u32[]{:S(2)}, u32[]{:S(2)}) collective-permute-start(bf16[288,2048]{1,0:T(8,128)(2,1)S(1)} %pad_maximum_fusion.1.refs_5_), channel_id=1, source_target_pairs={{0,5},{1,9},{2,7},{3,11},{4,1},{5,13},{6,3},{7,15},{8,0},{9,12},{1... | collective-permute-start | bytes 3538952 | tf_op jit(solution)/shard_map/ppermute | solution.py:233
  43.5 40.2 %copy-start.1 = (s32[4]{0:T(128)S(1)}, s32[4]{0:T(128)}, u32[]{:S(2)}) copy-start(s32[4]{0:T(128)} %pad_add_fusion.where_ref) | copy-start | bytes 52
  43.5 9.9 %collective-permute-start.8 = (bf16[32,2048]{1,0:T(8,128)(2,1)}, bf16[32,2048]{1,0:T(8,128)(2,1)S(1)}, u32[]{:S(2)}, u32[]{:S(2)}) collective-permute-start(bf16[32,2048]{1,0:T(8,128)(2,1)} %get-tuple-element.51), channel_id=1, source_target_pairs={{0,16},{1,17},{2,18},{3,19},{4,20},{5,21},{6,22},{7,23},{8,24},{9,... | collective-permute-start | bytes 393224 | tf_op jit(solution)/shard_map/ppermute | solution.py:233
  45.8 16.9 %collective-permute-start.9 = (bf16[32,2048]{1,0:T(8,128)(2,1)}, bf16[32,2048]{1,0:T(8,128)(2,1)S(1)}, u32[]{:S(2)}, u32[]{:S(2)}) collective-permute-start(bf16[32,2048]{1,0:T(8,128)(2,1)} %get-tuple-element.52), channel_id=1, source_target_pairs={{0,24},{1,25},{2,26},{3,27},{4,28},{5,29},{6,30},{7,31},{8,16},{9,... | collective-permute-start | bytes 393224 | tf_op jit(solution)/shard_map/ppermute | solution.py:233
  51.2 11.5 %collective-permute-start.10 = (bf16[32,2048]{1,0:T(8,128)(2,1)}, bf16[32,2048]{1,0:T(8,128)(2,1)S(1)}, u32[]{:S(2)}, u32[]{:S(2)}) collective-permute-start(bf16[32,2048]{1,0:T(8,128)(2,1)} %get-tuple-element.53), channel_id=1, source_target_pairs={{0,8},{1,9},{2,10},{3,11},{4,12},{5,13},{6,14},{7,15},{8,0},{9,1},... | collective-permute-start | bytes 393224 | tf_op jit(solution)/shard_map/ppermute | solution.py:233
  51.2 36.7 %collective-permute-start.18 = (bf16[288,2048]{1,0:T(8,128)(2,1)S(1)}, bf16[288,2048]{1,0:T(8,128)(2,1)S(1)}, u32[]{:S(2)}, u32[]{:S(2)}) collective-permute-start(bf16[288,2048]{1,0:T(8,128)(2,1)S(1)} %collective-permute-done.refs_4_), channel_id=1, source_target_pairs={{0,5},{2,7},{4,1},{6,3},{9,12},{11,14},{13,8},{15,10},{16,21},{18,... | collective-permute-start | bytes 3538952 | tf_op jit(solution)/shard_map/ppermute | solution.py:233
  62.7 8.0 %collective-permute-start.12 = (bf16[32,2048]{1,0:T(8,128)(2,1)}, bf16[32,2048]{1,0:T(8,128)(2,1)S(1)}, u32[]{:S(2)}, u32[]{:S(2)}) collective-permute-start(bf16[32,2048]{1,0:T(8,128)(2,1)} %get-tuple-element.59), channel_id=1, source_target_pairs={{0,18},{1,19},{2,16},{3,17},{4,22},{5,23},{6,20},{7,21},{8,26},{9,... | collective-permute-start | bytes 393224 | tf_op jit(solution)/shard_map/ppermute | solution.py:233
  62.8 19.4 %collective-permute-start.16 = (bf16[128,2048]{1,0:T(8,128)(2,1)S(1)}, bf16[128,2048]{1,0:T(8,128)(2,1)S(1)}, u32[]{:S(2)}, u32[]{:S(2)}) collective-permute-start(bf16[128,2048]{1,0:T(8,128)(2,1)S(1)} %constant_dynamic-update-slice_fusion.refs_0_), channel_id=1, source_target_pairs={{0,1},{1,0},{2,3},{3,2},{4,5},{5,4},{6,7},{7,6},{8,9},{9,8},{10,11... | collective-permute-start | bytes 1572872 | tf_op jit(solution)/shard_map/ppermute | solution.py:233
  65.0 14.0 %collective-permute-start.13 = (bf16[32,2048]{1,0:T(8,128)(2,1)}, bf16[32,2048]{1,0:T(8,128)(2,1)S(1)}, u32[]{:S(2)}, u32[]{:S(2)}) collective-permute-start(bf16[32,2048]{1,0:T(8,128)(2,1)} %get-tuple-element.60), channel_id=1, source_target_pairs={{0,26},{1,27},{2,24},{3,25},{4,30},{5,31},{6,28},{7,29},{8,18},{9,... | collective-permute-start | bytes 393224 | tf_op jit(solution)/shard_map/ppermute | solution.py:233
  65.0 15.3 %collective-permute-start.14 = (bf16[32,2048]{1,0:T(8,128)(2,1)}, bf16[32,2048]{1,0:T(8,128)(2,1)S(1)}, u32[]{:S(2)}, u32[]{:S(2)}) collective-permute-start(bf16[32,2048]{1,0:T(8,128)(2,1)} %get-tuple-element.61), channel_id=1, source_target_pairs={{0,10},{1,11},{2,8},{3,9},{4,14},{5,15},{6,12},{7,13},{8,2},{9,3},... | collective-permute-start | bytes 393224 | tf_op jit(solution)/shard_map/ppermute | solution.py:233
  70.7 10.9 %collective-permute-start.15 = (bf16[32,2048]{1,0:T(8,128)(2,1)}, bf16[32,2048]{1,0:T(8,128)(2,1)S(1)}, u32[]{:S(2)}, u32[]{:S(2)}) collective-permute-start(bf16[32,2048]{1,0:T(8,128)(2,1)} %get-tuple-element.62), channel_id=1, source_target_pairs={{0,2},{1,3},{2,0},{3,1},{4,6},{5,7},{6,4},{7,5},{8,10},{9,11},{10,... | collective-permute-start | bytes 393224 | tf_op jit(solution)/shard_map/ppermute | solution.py:233
  79.0 17.7 %collective-permute-start.19 = (bf16[288,2048]{1,0:T(8,128)(2,1)}, bf16[288,2048]{1,0:T(8,128)(2,1)S(1)}, u32[]{:S(2)}, u32[]{:S(2)}) collective-permute-start(bf16[288,2048]{1,0:T(8,128)(2,1)} %collective-permute-done.11.refs_5_), channel_id=1, source_target_pairs={{0,5},{2,7},{4,1},{6,3},{9,12},{11,14},{13,8},{15,10},{16,21},{18,... | collective-permute-start | bytes 3538952 | tf_op jit(solution)/shard_map/ppermute | solution.py:233
  81.6 2.1 %collective-permute-start.17 = (bf16[128,2048]{1,0:T(8,128)(2,1)S(1)}, bf16[128,2048]{1,0:T(8,128)(2,1)S(1)}, u32[]{:S(2)}, u32[]{:S(2)}) collective-permute-start(bf16[128,2048]{1,0:T(8,128)(2,1)S(1)} %constant_dynamic-update-slice_fusion.4.refs_1_), channel_id=1, source_target_pairs={{0,1},{1,0},{2,3},{3,2},{4,5},{5,4},{6,7},{7,6},{8,9},{9,8},{10,11... | collective-permute-start | bytes 1572872 | tf_op jit(solution)/shard_map/ppermute | solution.py:233
  101.1 2.7 %collective-permute-start.20 = (bf16[256,2048]{1,0:T(8,128)(2,1)S(1)}, bf16[256,2048]{1,0:T(8,128)(2,1)S(1)}, u32[]{:S(2)}, u32[]{:S(2)}) collective-permute-start(bf16[256,2048]{1,0:T(8,128)(2,1)S(1)} %get-tuple-element.70), channel_id=1, source_target_pairs={{0,1},{1,0},{2,3},{3,2},{4,5},{5,4},{6,7},{7,6},{8,9},{9,8},{10,11... | collective-permute-start | bytes 3145736 | tf_op jit(solution)/shard_map/ppermute | solution.py:233
  103.8 28.1 %copy-start = (f32[128,2048]{1,0:T(8,128)S(1)}, f32[128,2048]{1,0:T(8,128)}, u32[]{:S(2)}) copy-start(f32[128,2048]{1,0:T(8,128)} %get-tuple-element.49.summed_from) | copy-start | bytes 3145732
  103.8 28.1 %copy-start.2 = (s32[1,128,1]{1,2,0:T(1,128)S(1)}, s32[1,128,1]{1,2,0:T(1,128)}, u32[]{:S(2)}) copy-start(s32[1,128,1]{1,2,0:T(1,128)} %param.13) | copy-start | bytes 1540
  104.2 6.2 %collective-permute-start.21 = (bf16[32,2048]{1,0:T(8,128)(2,1)S(1)}, bf16[32,2048]{1,0:T(8,128)(2,1)S(1)}, u32[]{:S(2)}, u32[]{:S(2)}) collective-permute-start(bf16[32,2048]{1,0:T(8,128)(2,1)S(1)} %get-tuple-element.72), channel_id=1, source_target_pairs={{0,2},{1,3},{2,0},{3,1},{4,6},{5,7},{6,4},{7,5},{8,10},{9,11},{10,... | collective-permute-start | bytes 393224 | tf_op jit(solution)/shard_map/ppermute | solution.py:233
  104.5 6.7 %collective-permute-start.22 = (bf16[32,2048]{1,0:T(8,128)(2,1)S(1)}, bf16[32,2048]{1,0:T(8,128)(2,1)S(1)}, u32[]{:S(2)}, u32[]{:S(2)}) collective-permute-start(bf16[32,2048]{1,0:T(8,128)(2,1)S(1)} %get-tuple-element.73), channel_id=1, source_target_pairs={{0,8},{1,9},{2,10},{3,11},{4,12},{5,13},{6,14},{7,15},{8,0},{9,1},... | collective-permute-start | bytes 393224 | tf_op jit(solution)/shard_map/ppermute | solution.py:233
  104.5 10.4 %collective-permute-start.23 = (bf16[32,2048]{1,0:T(8,128)(2,1)S(1)}, bf16[32,2048]{1,0:T(8,128)(2,1)S(1)}, u32[]{:S(2)}, u32[]{:S(2)}) collective-permute-start(bf16[32,2048]{1,0:T(8,128)(2,1)S(1)} %get-tuple-element.74), channel_id=1, source_target_pairs={{0,10},{1,11},{2,8},{3,9},{4,14},{5,15},{6,12},{7,13},{8,2},{9,3},... | collective-permute-start | bytes 393224 | tf_op jit(solution)/shard_map/ppermute | solution.py:233
  107.8 9.1 %collective-permute-start.24 = (bf16[32,2048]{1,0:T(8,128)(2,1)S(1)}, bf16[32,2048]{1,0:T(8,128)(2,1)S(1)}, u32[]{:S(2)}, u32[]{:S(2)}) collective-permute-start(bf16[32,2048]{1,0:T(8,128)(2,1)S(1)} %get-tuple-element.75), channel_id=1, source_target_pairs={{0,16},{1,17},{2,18},{3,19},{4,20},{5,21},{6,22},{7,23},{8,24},{9,... | collective-permute-start | bytes 393224 | tf_op jit(solution)/shard_map/ppermute | solution.py:233
  107.8 17.4 %collective-permute-start.25 = (bf16[32,2048]{1,0:T(8,128)(2,1)S(1)}, bf16[32,2048]{1,0:T(8,128)(2,1)S(1)}, u32[]{:S(2)}, u32[]{:S(2)}) collective-permute-start(bf16[32,2048]{1,0:T(8,128)(2,1)S(1)} %get-tuple-element.76), channel_id=1, source_target_pairs={{0,18},{1,19},{2,16},{3,17},{4,22},{5,23},{6,20},{7,21},{8,26},{9,... | collective-permute-start | bytes 393224 | tf_op jit(solution)/shard_map/ppermute | solution.py:233
  110.4 20.0 %collective-permute-start.26 = (bf16[32,2048]{1,0:T(8,128)(2,1)S(1)}, bf16[32,2048]{1,0:T(8,128)(2,1)S(1)}, u32[]{:S(2)}, u32[]{:S(2)}) collective-permute-start(bf16[32,2048]{1,0:T(8,128)(2,1)S(1)} %get-tuple-element.77), channel_id=1, source_target_pairs={{0,24},{1,25},{2,26},{3,27},{4,28},{5,29},{6,30},{7,31},{8,16},{9,... | collective-permute-start | bytes 393224 | tf_op jit(solution)/shard_map/ppermute | solution.py:233
  111.2 20.7 %collective-permute-start.27 = (bf16[32,2048]{1,0:T(8,128)(2,1)S(1)}, bf16[32,2048]{1,0:T(8,128)(2,1)S(1)}, u32[]{:S(2)}, u32[]{:S(2)}) collective-permute-start(bf16[32,2048]{1,0:T(8,128)(2,1)S(1)} %get-tuple-element.78), channel_id=1, source_target_pairs={{0,26},{1,27},{2,24},{3,25},{4,30},{5,31},{6,28},{7,29},{8,18},{9,... | collective-permute-start | bytes 393224 | tf_op jit(solution)/shard_map/ppermute | solution.py:233
  (12 other events, 61.0 us)

commit v5 on v4

--- a/solution.py
+++ b/solution.py
@@ -247,11 +247,6 @@
 
 def second_hop(z, x, y, core):
     return (z, x ^ 1, y, 1 - core) if is_home(z, core) else None
-
-
-def pack_half(half, *weights):
-    rows = weights[0].shape[0] // 2
-    return jnp.concatenate([w[half * rows : (half + 1) * rows] for w in weights], axis=0)
 
 
 def slot_targets(ids_row, z_here, y_here, capacity):
@@ -348,15 +343,12 @@
     keep.wait()
 
 
-def load_pack(pair, strip, targets, semaphores):
+def load_pack(pack, strip, targets, semaphores):
     return [
         pltpu.make_async_copy(
-            pair[half].at[pl.ds(kind * strip, strip)],
-            targets[kind].at[pl.ds(half * strip, strip)],
-            semaphores.at[kind, half],
+            pack.at[pl.ds(kind * strip, strip)], targets[kind], semaphores.at[kind]
         )
         for kind in range(3)
-        for half in range(2)
     ]
 
 
@@ -369,18 +361,13 @@
 
 def expert_kernel(row_count, where_ref, *refs):
     row_from, refs = refs[:row_count], refs[row_count:]
-    first_piece = len(refs) == 10
+    first_piece = len(refs) == 9
     if first_piece:
-        pairs, (total_ref,), rest = [refs[:2]], refs[2:3], refs[3:]
+        packs, (total_ref,), rest = refs[:1], refs[1:2], refs[2:]
     else:
-        pairs, before_from, (mine_ref, twins_ref), rest = (
-            [refs[:2], refs[2:4]],
-            refs[4],
-            refs[5:7],
-            refs[7:],
-        )
+        packs, before_from, (mine_ref, twins_ref), rest = refs[:2], refs[2], refs[3:5], refs[5:]
     rows_ref, before_ref, gate_ref, up_ref, down_ref, row_semaphores, semaphores = rest
-    strip = pairs[0][0].shape[0] // 3
+    strip = packs[0].shape[0] // 3
     targets = (gate_ref, up_ref, down_ref)
     loads = []
     place = 0
@@ -390,7 +377,7 @@
     if not first_piece:
         loads.append((before_from, before_ref))
     row_copies = fetch_all(loads, row_semaphores)
-    weight_copies = load_pack(pairs[0], strip, targets, semaphores)
+    weight_copies = load_pack(packs[0], strip, targets, semaphores)
     if first_piece:
         for copy in weight_copies:
             copy.start()
@@ -399,18 +386,18 @@
 
         @pl.when(at_home)
         def _():
-            for copy in load_pack(pairs[0], strip, targets, semaphores):
+            for copy in load_pack(packs[0], strip, targets, semaphores):
                 copy.start()
 
         @pl.when(jnp.logical_not(at_home))
         def _():
-            for copy in load_pack(pairs[1], strip, targets, semaphores):
+            for copy in load_pack(packs[1], strip, targets, semaphores):
                 copy.start()
 
-    for copy in row_copies + weight_copies[:4]:
+    for copy in row_copies + weight_copies[:2]:
         copy.wait()
     active = active_of(rows_ref[...], gate_ref[...], up_ref[...])
-    for copy in weight_copies[4:]:
+    for copy in weight_copies[2:]:
         copy.wait()
     result = jnp.dot(active, down_ref[...], preferred_element_type=jnp.float32)
     if first_piece:
@@ -432,19 +419,13 @@
         out_refs[k][...] = result[k * capacity : (k + 1) * capacity]
 
 
-def combine_kernel(where_ref, ids_ref, route_ref, summed_from, *refs):
-    row_from, out_ref, rows_ref, summed_ref, semaphores = refs[:8], *refs[8:]
-    capacity = row_from[0].shape[0]
-    copies = fetch_all(
-        [(row_from[k], rows_ref.at[pl.ds(k * capacity, capacity)]) for k in range(8)]
-        + [(summed_from, summed_ref)],
-        semaphores,
-    )
+def combine_kernel(where_ref, ids_ref, route_ref, summed_ref, *refs):
+    row_refs, out_ref = refs[:8], refs[8]
+    capacity = row_refs[0].shape[0]
     choose = slot_matrix(ids_ref[...], where_ref[1], where_ref[2], capacity)
-    for copy in copies:
-        copy.wait()
+    rows = jnp.concatenate([ref[...] for ref in row_refs], axis=0)
     picked = lax.dot_general(
-        choose, rows_ref[...], (((0,), (0,)), ((), ())), preferred_element_type=jnp.float32
+        choose, rows, (((0,), (0,)), ((), ())), preferred_element_type=jnp.float32
     )
     out_ref[...] = (summed_ref[...] + picked * route_ref[...]).astype(jnp.bfloat16)
 
@@ -483,14 +464,13 @@
 
         kv_blocks[k] = move(block, later)
 
-    own = [pack_half(half, gate_weight[0, 0], up_weight[0, 0], down_weight[0, 0]) for half in range(2)]
-    one_first = move(own[0], first_hop)
+    own = jnp.concatenate([gate_weight[0, 0], up_weight[0, 0], down_weight[0, 0]], axis=0)
+    one = move(own, first_hop)
     for k in (4, 5, 3, 2, 6, 1, 7):
         send_keys(kv_own, k)
     kv_list = [kv_blocks[k] for k in range(1, 8)]
-    one_first, own[0], own[1], *kv_list = lax.optimization_barrier((one_first, *own, *kv_list))
-    one_second = move(own[1], first_hop)
-    last_first = move(one_first, second_hop)
+    one, *kv_list = lax.optimization_barrier((one, *kv_list))
+    last = move(one, second_hop)
     slot_shape = jax.ShapeDtypeStruct((capacity, width), jnp.bfloat16)
     keys_all = 8 * tokens
     rows_all = 8 * capacity
@@ -523,16 +503,12 @@
             return array
         return move(array, lambda z, x, y, core: (z ^ (k >> 1), x, y ^ (k & 1), core))
 
-    early, late = (4, 6, 2), (5, 7, 3, 1)
-    arrived = [swap(outgoing[k], k) if k in early else outgoing[k] for k in range(8)]
-    one_second, *held = lax.optimization_barrier((one_second, *[arrived[k] for k in late]))
-    for k, array in zip(late, held):
-        arrived[k] = swap(array, k)
-    last_second = move(one_second, second_hop)
-    order = (0, *early, *late)
+    arrived = {0: outgoing[0]}
+    for k in (4, 6, 5, 7, 2, 3, 1):
+        arrived[k] = swap(outgoing[k], k)
+    order = (0, 2, 3, 1, 4, 6, 5, 7)
     row_parts = [jnp.concatenate([arrived[k] for k in group]) for group in (order[:4], order[4:])]
     row_parts += [move(part, to_twin) for part in row_parts]
-    half_rows = row_parts[0].shape[0]
 
     def run_expert(packs, before):
         row_total = 2 * rows_all
@@ -551,7 +527,7 @@
                 pltpu.VMEM((piece, width), jnp.bfloat16),
                 pltpu.VMEM((piece, width), jnp.bfloat16),
                 pltpu.SemaphoreType.DMA((5,)),
-                pltpu.SemaphoreType.DMA((3, 2)),
+                pltpu.SemaphoreType.DMA((3,)),
             ],
             compiler_params=pltpu.CompilerParams(vmem_limit_bytes=32 << 20),
             cost_estimate=pl.CostEstimate(
@@ -562,11 +538,9 @@
             name="experts_rest" if before else "experts_first",
         )(where, *row_parts, *packs, *before)
 
-    first_total = run_expert([one_first, one_second], [])
-    last_first, last_second, *first_total = lax.optimization_barrier(
-        (last_first, last_second, *first_total)
-    )
-    mine, twins = run_expert([*own, last_first, last_second], first_total)
+    first_total = run_expert([one], [])
+    last, *first_total = lax.optimization_barrier((last, *first_total))
+    mine, twins = run_expert([own, last], first_total)
     joined = pl.pallas_call(
         join_kernel,
         out_shape=[slot_shape] * 8,
@@ -588,13 +562,8 @@
     output = pl.pallas_call(
         combine_kernel,
         out_shape=jax.ShapeDtypeStruct((tokens, width), jnp.bfloat16),
-        in_specs=[IN_SMEM, IN_VMEM, IN_VMEM] + [IN_HBM] * 9,
+        in_specs=[IN_SMEM] + [IN_VMEM] * 11,
         out_specs=IN_VMEM,
-        scratch_shapes=[
-            pltpu.VMEM((rows_all, width), jnp.bfloat16),
-            pltpu.VMEM((tokens, width), jnp.float32),
-            pltpu.SemaphoreType.DMA((9,)),
-        ],
         compiler_params=pltpu.CompilerParams(vmem_limit_bytes=12 << 20),
         cost_estimate=pl.CostEstimate(
             flops=2 * tokens * 8 * capacity * width,

time: 136 us -> 137 us (level)
  starting transfers between devices: 57.3 us -> 61.8 us
  Pallas kernels: 20.8 us -> 18.1 us
  local copies, waits for them, and re-layouts: 3.51 us -> 1.16 us
  other arithmetic: 0.89 us -> 2.48 us
    ppermute x28 -> x26, starting transfers between devices: 57.3 us -> 61.8 us  [move(): return lax.ppermute(array, AXES, pairs)]
    concatenate x2 -> x1, other arithmetic: 0.23 us -> 1.8 us  [shards_cube(): jnp.concatenate([gate_weight[0, 0], up_weight[0, 0], down_weight[0, 0]],...]
    pallas_call x1, Pallas kernels: 3.35 us -> 1.82 us  [shards_cube(): pl.pallas_call(combine_kernel, out_shape=jax.ShapeDtypeStruct((tokens, wi...]
    slice x2 -> x0, local copies, waits for them, and re-layouts: 1.39 us -> none  [pack_half(): w[half * rows:(half + 1) * rows]]
    ppermute x28 -> x26, waiting for transfers between devices: 52.4 us -> 51.8 us  [move(): return lax.ppermute(array, AXES, pairs)]
  transfers between devices with their start and end apart: 28 -> 26, of which waited for: 14 -> 16; matrix products, arithmetic and copies ran while one was open for 1% -> 1% of each run, Pallas kernels for 9% -> 3%
where the time goes in v5:
time: 137 us; the launch traced here: 136 us
  starting transfers between devices  61.8 us (45%)
  waiting for transfers between devices  51.8 us (38%)
  Pallas kernels  18.1 us (13%)
  other arithmetic  2.48 us (2%)
    ppermute x26, starting transfers between devices, move(): return lax.ppermute(array, AXES, pairs)  61.8 us
    ppermute x26, waiting for transfers between devices, move(): return lax.ppermute(array, AXES, pairs)  51.8 us
    pallas_call x1, Pallas kernels, shards_cube(): pl.pallas_call(attend_kernel, out_shape=[jax.ShapeDtypeStruct((tokens, wi...  8.56 us
    pallas_call x2, Pallas kernels, run_expert(): pl.pallas_call(partial(expert_kernel, len(row_parts)), out_shape=[mine, t...  7.31 us
  transfers between devices with their start and end apart: 26, of which 16 were waited for; matrix products, arithmetic and copies ran while one was open for 1% of the time, Pallas kernels for 3%

profile of v5, /device:TPU:8, one launch (start us, length us, event | category | flops | bytes accessed | tf_op | source)
XLA Modules:
  0.0 135.7 jit_solution(7800937624334772207)
XLA Ops:
  0.0 1.8 %pad_maximum_fusion.refs_4_ = bf16[576,2048]{1,0:T(8,128)(2,1)S(1)} fusion(bf16[192,2048]{1,0:T(8,128)(2,1)} %bitcast.16, bf16[192,2048]{1,0:T(8,128)(2,1)} %bitcast.17, bf16[192,2048]{1,0:T(8,128)(2,1)} %bitcast.18), kind=kLoop, calls=%fused_computation | loop fusion | flops 7077888 | bytes 4718592 | tf_op jit(solution)/shard_map/concatenate | solution.py:467
  1.9 3.8 %collective-permute-start.1 = (bf16[128,512]{1,0:T(8,128)(2,1)S(1)}, bf16[128,512]{1,0:T(8,128)(2,1)S(1)}, u32[]{:S(2)}, u32[]{:S(2)}) collective-permute-start(bf16[128,512]{1,0:T(8,128)(2,1)S(1)} %pad_maximum_fusion.1.refs_0_), channel_id=1, source_target_pairs={{0,4},{1,5},{2,6},{3,7},{4,8},{5,9},{6,10},{7,11},{8,12},{9,13},{1... | collective-permute-start | bytes 393224 | tf_op jit(solution)/shard_map/ppermute | solution.py:233
  5.8 3.1 %collective-permute-start.2 = (bf16[128,512]{1,0:T(8,128)(2,1)S(1)}, bf16[128,512]{1,0:T(8,128)(2,1)S(1)}, u32[]{:S(2)}, u32[]{:S(2)}) collective-permute-start(bf16[128,512]{1,0:T(8,128)(2,1)S(1)} %pad_maximum_fusion.1.refs_0_), channel_id=1, source_target_pairs={{0,8},{1,9},{2,10},{3,11},{4,12},{5,13},{6,14},{7,15},{8,16},{9,17... | collective-permute-start | bytes 393224 | tf_op jit(solution)/shard_map/ppermute | solution.py:233
  8.8 3.3 %collective-permute-start.3 = (bf16[128,512]{1,0:T(8,128)(2,1)S(1)}, bf16[128,512]{1,0:T(8,128)(2,1)S(1)}, u32[]{:S(2)}, u32[]{:S(2)}) collective-permute-start(bf16[128,512]{1,0:T(8,128)(2,1)S(1)} %pad_maximum_fusion.1.refs_0_), channel_id=1, source_target_pairs={{0,12},{1,13},{2,14},{3,15},{4,16},{5,17},{6,18},{7,19},{8,20},{9,... | collective-permute-start | bytes 393224 | tf_op jit(solution)/shard_map/ppermute | solution.py:233
  13.5 2.6 %collective-permute-start.5 = (bf16[128,512]{1,0:T(8,128)(2,1)S(1)}, bf16[128,512]{1,0:T(8,128)(2,1)S(1)}, u32[]{:S(2)}, u32[]{:S(2)}) collective-permute-start(bf16[128,512]{1,0:T(8,128)(2,1)S(1)} %pad_maximum_fusion.1.refs_0_), channel_id=1, source_target_pairs={{0,20},{1,21},{2,22},{3,23},{4,24},{5,25},{6,26},{7,27},{8,28},{9,... | collective-permute-start | bytes 393224 | tf_op jit(solution)/shard_map/ppermute | solution.py:233
  18.2 1.8 %collective-permute-done.4.refs_4_ = bf16[128,512]{1,0:T(8,128)(2,1)S(1)} collective-permute-done((bf16[128,512]{1,0:T(8,128)(2,1)S(1)}, bf16[128,512]{1,0:T(8,128)(2,1)S(1)}, u32[]{:S(2)}, u32[]{:S(2)}) %collective-permute-start.4) | collective-permute-done | bytes 131104 | tf_op jit(solution)/shard_map/ppermute | solution.py:233
  20.0 1.7 %collective-permute-done.5.refs_5_ = bf16[128,512]{1,0:T(8,128)(2,1)S(1)} collective-permute-done((bf16[128,512]{1,0:T(8,128)(2,1)S(1)}, bf16[128,512]{1,0:T(8,128)(2,1)S(1)}, u32[]{:S(2)}, u32[]{:S(2)}) %collective-permute-start.5) | collective-permute-done | bytes 131104 | tf_op jit(solution)/shard_map/ppermute | solution.py:233
  21.7 10.0 %collective-permute-done.refs_4_ = bf16[576,2048]{1,0:T(8,128)(2,1)} collective-permute-done((bf16[576,2048]{1,0:T(8,128)(2,1)S(1)}, bf16[576,2048]{1,0:T(8,128)(2,1)}, u32[]{:S(2)}, u32[]{:S(2)}) %collective-permute-start) | collective-permute-done | bytes 2359328 | tf_op jit(solution)/shard_map/ppermute | solution.py:233
  31.7 8.6 %attend.1 = (f32[128,2048]{1,0:T(8,128)}, bf16[32,2048]{1,0:T(8,128)(2,1)}, bf16[32,2048]{1,0:T(8,128)(2,1)}, bf16[32,2048]{1,0:T(8,128)(2,1)}, bf16[32,2048]{1,...) custom-call(s32[4]{0:T(128)} %pad_add_fusion.where_ref, ...), custom_call_target="tpu_custom_call" | custom-call | flops 1073741824 | bytes 2097152 | tf_op jit(solution)/shard_map/attend/pallas_call | solution.py:477
  40.3 17.5 %collective-permute-start.11 = (bf16[32,2048]{1,0:T(8,128)(2,1)}, bf16[32,2048]{1,0:T(8,128)(2,1)S(1)}, u32[]{:S(2)}, u32[]{:S(2)}) collective-permute-start(bf16[32,2048]{1,0:T(8,128)(2,1)} %get-tuple-element.46), channel_id=1, source_target_pairs={{0,16},{1,17},{2,18},{3,19},{4,20},{5,21},{6,22},{7,23},{8,24},{9,... | collective-permute-start | bytes 393224 | tf_op jit(solution)/shard_map/ppermute | solution.py:233
  57.8 1.9 %collective-permute-start.13 = (bf16[32,2048]{1,0:T(8,128)(2,1)}, bf16[32,2048]{1,0:T(8,128)(2,1)S(1)}, u32[]{:S(2)}, u32[]{:S(2)}) collective-permute-start(bf16[32,2048]{1,0:T(8,128)(2,1)} %get-tuple-element.48), channel_id=1, source_target_pairs={{0,18},{1,19},{2,16},{3,17},{4,22},{5,23},{6,20},{7,21},{8,26},{9,... | collective-permute-start | bytes 393224 | tf_op jit(solution)/shard_map/ppermute | solution.py:233
  59.6 2.0 %collective-permute-start.14 = (bf16[32,2048]{1,0:T(8,128)(2,1)}, bf16[32,2048]{1,0:T(8,128)(2,1)S(1)}, u32[]{:S(2)}, u32[]{:S(2)}) collective-permute-start(bf16[32,2048]{1,0:T(8,128)(2,1)} %get-tuple-element.49), channel_id=1, source_target_pairs={{0,26},{1,27},{2,24},{3,25},{4,30},{5,31},{6,28},{7,29},{8,18},{9,... | collective-permute-start | bytes 393224 | tf_op jit(solution)/shard_map/ppermute | solution.py:233
  63.9 9.8 %collective-permute-start.8 = (bf16[32,2048]{1,0:T(8,128)(2,1)}, bf16[32,2048]{1,0:T(8,128)(2,1)S(1)}, u32[]{:S(2)}, u32[]{:S(2)}) collective-permute-start(bf16[32,2048]{1,0:T(8,128)(2,1)} %get-tuple-element.43), channel_id=1, source_target_pairs={{0,8},{1,9},{2,10},{3,11},{4,12},{5,13},{6,14},{7,15},{8,0},{9,1},... | collective-permute-start | bytes 393224 | tf_op jit(solution)/shard_map/ppermute | solution.py:233
  75.1 2.3 %collective-permute-start.10 = (bf16[32,2048]{1,0:T(8,128)(2,1)}, bf16[32,2048]{1,0:T(8,128)(2,1)S(1)}, u32[]{:S(2)}, u32[]{:S(2)}) collective-permute-start(bf16[32,2048]{1,0:T(8,128)(2,1)} %get-tuple-element.45), channel_id=1, source_target_pairs={{0,2},{1,3},{2,0},{3,1},{4,6},{5,7},{6,4},{7,5},{8,10},{9,11},{10,... | collective-permute-start | bytes 393224 | tf_op jit(solution)/shard_map/ppermute | solution.py:233
  77.4 5.2 %collective-permute-done.14 = bf16[32,2048]{1,0:T(8,128)(2,1)S(1)} collective-permute-done((bf16[32,2048]{1,0:T(8,128)(2,1)}, bf16[32,2048]{1,0:T(8,128)(2,1)S(1)}, u32[]{:S(2)}, u32[]{:S(2)}) %collective-permute-start.14) | collective-permute-done | bytes 131104 | tf_op jit(solution)/shard_map/ppermute | solution.py:233
  82.6 2.3 %collective-permute-start.16 = (bf16[128,2048]{1,0:T(8,128)(2,1)S(1)}, bf16[128,2048]{1,0:T(8,128)(2,1)S(1)}, u32[]{:S(2)}, u32[]{:S(2)}) collective-permute-start(bf16[128,2048]{1,0:T(8,128)(2,1)S(1)} %constant_dynamic-update-slice_fusion.4.refs_1_), channel_id=1, source_target_pairs={{0,1},{1,0},{2,3},{3,2},{4,5},{5,4},{6,7},{7,6},{8,9},{9,8},{10,11... | collective-permute-start | bytes 1572872 | tf_op jit(solution)/shard_map/ppermute | solution.py:233
  84.9 2.0 %collective-permute-done.10 = bf16[32,2048]{1,0:T(8,128)(2,1)S(1)} collective-permute-done((bf16[32,2048]{1,0:T(8,128)(2,1)}, bf16[32,2048]{1,0:T(8,128)(2,1)S(1)}, u32[]{:S(2)}, u32[]{:S(2)}) %collective-permute-start.10) | collective-permute-done | bytes 131104 | tf_op jit(solution)/shard_map/ppermute | solution.py:233
  87.6 1.5 %collective-permute-done.15.refs_2_ = bf16[128,2048]{1,0:T(8,128)(2,1)S(1)} collective-permute-done((bf16[128,2048]{1,0:T(8,128)(2,1)S(1)}, bf16[128,2048]{1,0:T(8,128)(2,1)S(1)}, u32[]{:S(2)}, u32[]{:S(2)}) %collective-permute-start.15) | collective-permute-done | bytes 524320 | tf_op jit(solution)/shard_map/ppermute | solution.py:233
  89.2 4.1 %experts_first.1.refs_6_ = f32[512,2048]{1,0:T(8,128)S(1)} custom-call(s32[4]{0:T(128)S(1)} %copy-done.1, bf16[128,2048]{1,0:T(8,128)(2,1)S(1)} %constant_dynamic-update-slice_fusion.refs_0_, bf16[128,2048]{1,0:T(8,128)(2,1)S(1)} %constant_dynamic-update-slice_fusion.4.refs_1_, bf16[128,2048]{1,0:T(8,128)(2,1)S(1)} %collective-permute-done.15.refs_2_, ...), custom_call_target="tpu_custom_call" | custom-call | flops 1207959552 | bytes 2359296 | tf_op jit(solution)/shard_map/experts_first/pallas_call | solution.py:518
  93.3 3.9 %collective-permute-done.17.refs_5_ = bf16[576,2048]{1,0:T(8,128)(2,1)S(1)} collective-permute-done((bf16[576,2048]{1,0:T(8,128)(2,1)}, bf16[576,2048]{1,0:T(8,128)(2,1)S(1)}, u32[]{:S(2)}, u32[]{:S(2)}) %collective-permute-start.17) | collective-permute-done | bytes 2359328 | tf_op jit(solution)/shard_map/ppermute | solution.py:233
  97.2 3.2 %experts_rest.1 = (f32[256,2048]{1,0:T(8,128)S(1)}, bf16[256,2048]{1,0:T(8,128)(2,1)S(1)}) custom-call(s32[4]{0:T(128)S(1)} %copy-done.1, bf16[128,2048]{1,0:T(8,128)(2,1)S(1)} %constant_dynamic-update-slice_fusion.refs_0_, bf16[128,2048]{1,0:T(8,128)(2,1)S(1)} %constant_dynamic-update-slice_fusion.4.refs_1_, ...), custom_call_target="tpu_custom_call" | custom-call | flops 1207959552 | bytes 2359296 | tf_op jit(solution)/shard_map/experts_rest/pallas_call | solution.py:518
  100.5 2.6 %collective-permute-done.18.other_from = bf16[256,2048]{1,0:T(8,128)(2,1)S(1)} collective-permute-done((bf16[256,2048]{1,0:T(8,128)(2,1)S(1)}, bf16[256,2048]{1,0:T(8,128)(2,1)S(1)}, u32[]{:S(2)}, u32[]{:S(2)}) %collective-permute-start.18) | collective-permute-done | bytes 1048608 | tf_op jit(solution)/shard_map/ppermute | solution.py:233
  103.6 1.6 %collective-permute-start.19 = (bf16[32,2048]{1,0:T(8,128)(2,1)S(1)}, bf16[32,2048]{1,0:T(8,128)(2,1)S(1)}, u32[]{:S(2)}, u32[]{:S(2)}) collective-permute-start(bf16[32,2048]{1,0:T(8,128)(2,1)S(1)} %get-tuple-element.56), channel_id=1, source_target_pairs={{0,2},{1,3},{2,0},{3,1},{4,6},{5,7},{6,4},{7,5},{8,10},{9,11},{10,... | collective-permute-start | bytes 393224 | tf_op jit(solution)/shard_map/ppermute | solution.py:233
  105.2 1.9 %collective-permute-start.20 = (bf16[32,2048]{1,0:T(8,128)(2,1)S(1)}, bf16[32,2048]{1,0:T(8,128)(2,1)S(1)}, u32[]{:S(2)}, u32[]{:S(2)}) collective-permute-start(bf16[32,2048]{1,0:T(8,128)(2,1)S(1)} %get-tuple-element.57), channel_id=1, source_target_pairs={{0,8},{1,9},{2,10},{3,11},{4,12},{5,13},{6,14},{7,15},{8,0},{9,1},... | collective-permute-start | bytes 393224 | tf_op jit(solution)/shard_map/ppermute | solution.py:233
  107.1 2.6 %collective-permute-start.22 = (bf16[32,2048]{1,0:T(8,128)(2,1)S(1)}, bf16[32,2048]{1,0:T(8,128)(2,1)S(1)}, u32[]{:S(2)}, u32[]{:S(2)}) collective-permute-start(bf16[32,2048]{1,0:T(8,128)(2,1)S(1)} %get-tuple-element.59), channel_id=1, source_target_pairs={{0,16},{1,17},{2,18},{3,19},{4,20},{5,21},{6,22},{7,23},{8,24},{9,... | collective-permute-start | bytes 393224 | tf_op jit(solution)/shard_map/ppermute | solution.py:233
  112.1 2.3 %collective-permute-done.20.refs_2_ = bf16[32,2048]{1,0:T(8,128)(2,1)S(1)} collective-permute-done((bf16[32,2048]{1,0:T(8,128)(2,1)S(1)}, bf16[32,2048]{1,0:T(8,128)(2,1)S(1)}, u32[]{:S(2)}, u32[]{:S(2)}) %collective-permute-start.20) | collective-permute-done | bytes 131104 | tf_op jit(solution)/shard_map/ppermute | solution.py:233
  114.6 1.7 %collective-permute-done.21.refs_3_ = bf16[32,2048]{1,0:T(8,128)(2,1)S(1)} collective-permute-done((bf16[32,2048]{1,0:T(8,128)(2,1)S(1)}, bf16[32,2048]{1,0:T(8,128)(2,1)S(1)}, u32[]{:S(2)}, u32[]{:S(2)}) %collective-permute-start.21) | collective-permute-done | bytes 131104 | tf_op jit(solution)/shard_map/ppermute | solution.py:233
  116.3 8.6 %collective-permute-done.22.refs_4_ = bf16[32,2048]{1,0:T(8,128)(2,1)S(1)} collective-permute-done((bf16[32,2048]{1,0:T(8,128)(2,1)S(1)}, bf16[32,2048]{1,0:T(8,128)(2,1)S(1)}, u32[]{:S(2)}, u32[]{:S(2)}) %collective-permute-start.22) | collective-permute-done | bytes 131104 | tf_op jit(solution)/shard_map/ppermute | solution.py:233
  124.9 2.8 %collective-permute-done.23.refs_5_ = bf16[32,2048]{1,0:T(8,128)(2,1)S(1)} collective-permute-done((bf16[32,2048]{1,0:T(8,128)(2,1)S(1)}, bf16[32,2048]{1,0:T(8,128)(2,1)S(1)}, u32[]{:S(2)}, u32[]{:S(2)}) %collective-permute-start.23) | collective-permute-done | bytes 131104 | tf_op jit(solution)/shard_map/ppermute | solution.py:233
  127.7 3.9 %collective-permute-done.24.refs_6_ = bf16[32,2048]{1,0:T(8,128)(2,1)S(1)} collective-permute-done((bf16[32,2048]{1,0:T(8,128)(2,1)S(1)}, bf16[32,2048]{1,0:T(8,128)(2,1)S(1)}, u32[]{:S(2)}, u32[]{:S(2)}) %collective-permute-start.24) | collective-permute-done | bytes 131104 | tf_op jit(solution)/shard_map/ppermute | solution.py:233
  131.7 2.2 %collective-permute-done.25.refs_7_ = bf16[32,2048]{1,0:T(8,128)(2,1)S(1)} collective-permute-done((bf16[32,2048]{1,0:T(8,128)(2,1)S(1)}, bf16[32,2048]{1,0:T(8,128)(2,1)S(1)}, u32[]{:S(2)}, u32[]{:S(2)}) %collective-permute-start.25) | collective-permute-done | bytes 131104 | tf_op jit(solution)/shard_map/ppermute | solution.py:233
  133.9 1.8 %combine.1 = bf16[128,2048]{1,0:T(8,128)(2,1)} custom-call(s32[4]{0:T(128)S(1)} %copy-done.1, s32[1,128]{1,0:T(1,128)S(1)} %bitcast.15, f32[128,1]{1,0:T(8,128)S(1)} %copy.10.route_ref, f32[128,2048]{1,0:T(8,128)S(1)} %copy-done, bf16[32,2048]{1,0:T(8,128)(2,1)S(1)} %get-tuple-element.55.refs_0_, bf16[32,2048]{1,0:T(8,128)(2,1)S(1)} %collective-permute-done.19.refs_1_, ...), custom_call_target="tpu_custom_call" | custom-call | flops 134217728 | bytes 3145728 | tf_op jit(solution)/shard_map/combine/pallas_call | solution.py:562
  (65 shorter events, 10.8 us)
Async XLA Ops:
  1.8 29.8 %collective-permute-start = (bf16[576,2048]{1,0:T(8,128)(2,1)S(1)}, bf16[576,2048]{1,0:T(8,128)(2,1)}, u32[]{:S(2)}, u32[]{:S(2)}) collective-permute-start(bf16[576,2048]{1,0:T(8,128)(2,1)S(1)} %pad_maximum_fusion.refs_4_), channel_id=1, source_target_pairs={{0,5},{1,9},{2,7},{3,11},{4,1},{5,13},{6,3},{7,15},{8,0},{9,12},{1... | collective-permute-start | bytes 7077896 | tf_op jit(solution)/shard_map/ppermute | solution.py:233
  1.9 29.7 %copy-start.3 = (bf16[128,512]{1,0:T(8,128)(2,1)}, bf16[128,512]{1,0:T(8,128)(2,1)S(1)}, u32[]{:S(2)}) copy-start(bf16[128,512]{1,0:T(8,128)(2,1)S(1)} %pad_maximum_fusion.1.refs_0_) | copy-start | bytes 393220
  1.9 11.5 %collective-permute-start.1 = (bf16[128,512]{1,0:T(8,128)(2,1)S(1)}, bf16[128,512]{1,0:T(8,128)(2,1)S(1)}, u32[]{:S(2)}, u32[]{:S(2)}) collective-permute-start(bf16[128,512]{1,0:T(8,128)(2,1)S(1)} %pad_maximum_fusion.1.refs_0_), channel_id=1, source_target_pairs={{0,4},{1,5},{2,6},{3,7},{4,8},{5,9},{6,10},{7,11},{8,12},{9,13},{1... | collective-permute-start | bytes 393224 | tf_op jit(solution)/shard_map/ppermute | solution.py:233
  5.8 10.4 %collective-permute-start.2 = (bf16[128,512]{1,0:T(8,128)(2,1)S(1)}, bf16[128,512]{1,0:T(8,128)(2,1)S(1)}, u32[]{:S(2)}, u32[]{:S(2)}) collective-permute-start(bf16[128,512]{1,0:T(8,128)(2,1)S(1)} %pad_maximum_fusion.1.refs_0_), channel_id=1, source_target_pairs={{0,8},{1,9},{2,10},{3,11},{4,12},{5,13},{6,14},{7,15},{8,16},{9,17... | collective-permute-start | bytes 393224 | tf_op jit(solution)/shard_map/ppermute | solution.py:233
  8.8 8.0 %collective-permute-start.3 = (bf16[128,512]{1,0:T(8,128)(2,1)S(1)}, bf16[128,512]{1,0:T(8,128)(2,1)S(1)}, u32[]{:S(2)}, u32[]{:S(2)}) collective-permute-start(bf16[128,512]{1,0:T(8,128)(2,1)S(1)} %pad_maximum_fusion.1.refs_0_), channel_id=1, source_target_pairs={{0,12},{1,13},{2,14},{3,15},{4,16},{5,17},{6,18},{7,19},{8,20},{9,... | collective-permute-start | bytes 393224 | tf_op jit(solution)/shard_map/ppermute | solution.py:233
  12.2 7.8 %collective-permute-start.4 = (bf16[128,512]{1,0:T(8,128)(2,1)S(1)}, bf16[128,512]{1,0:T(8,128)(2,1)S(1)}, u32[]{:S(2)}, u32[]{:S(2)}) collective-permute-start(bf16[128,512]{1,0:T(8,128)(2,1)S(1)} %pad_maximum_fusion.1.refs_0_), channel_id=1, source_target_pairs={{0,16},{1,17},{2,18},{3,19},{4,20},{5,21},{6,22},{7,23},{8,24},{9,... | collective-permute-start | bytes 393224 | tf_op jit(solution)/shard_map/ppermute | solution.py:233
  13.5 18.2 %copy-start.7 = (bf16[128,512]{1,0:T(8,128)(2,1)}, bf16[128,512]{1,0:T(8,128)(2,1)S(1)}, u32[]{:S(2)}) copy-start(bf16[128,512]{1,0:T(8,128)(2,1)S(1)} %collective-permute-done.1.refs_1_) | copy-start | bytes 393220
  13.5 8.2 %collective-permute-start.5 = (bf16[128,512]{1,0:T(8,128)(2,1)S(1)}, bf16[128,512]{1,0:T(8,128)(2,1)S(1)}, u32[]{:S(2)}, u32[]{:S(2)}) collective-permute-start(bf16[128,512]{1,0:T(8,128)(2,1)S(1)} %pad_maximum_fusion.1.refs_0_), channel_id=1, source_target_pairs={{0,20},{1,21},{2,22},{3,23},{4,24},{5,25},{6,26},{7,27},{8,28},{9,... | collective-permute-start | bytes 393224 | tf_op jit(solution)/shard_map/ppermute | solution.py:233
  16.1 15.5 %copy-start.8 = (bf16[128,512]{1,0:T(8,128)(2,1)}, bf16[128,512]{1,0:T(8,128)(2,1)S(1)}, u32[]{:S(2)}) copy-start(bf16[128,512]{1,0:T(8,128)(2,1)S(1)} %collective-permute-done.2.refs_2_) | copy-start | bytes 393220
  16.1 5.5 %collective-permute-start.6 = (bf16[128,512]{1,0:T(8,128)(2,1)S(1)}, bf16[128,512]{1,0:T(8,128)(2,1)S(1)}, u32[]{:S(2)}, u32[]{:S(2)}) collective-permute-start(bf16[128,512]{1,0:T(8,128)(2,1)S(1)} %pad_maximum_fusion.1.refs_0_), channel_id=1, source_target_pairs={{0,24},{1,25},{2,26},{3,27},{4,28},{5,29},{6,30},{7,31}} | collective-permute-start | bytes 393224 | tf_op jit(solution)/shard_map/ppermute | solution.py:233
  16.8 4.8 %collective-permute-start.7 = (bf16[128,512]{1,0:T(8,128)(2,1)S(1)}, bf16[128,512]{1,0:T(8,128)(2,1)S(1)}, u32[]{:S(2)}, u32[]{:S(2)}) collective-permute-start(bf16[128,512]{1,0:T(8,128)(2,1)S(1)} %pad_maximum_fusion.1.refs_0_), channel_id=1, source_target_pairs={{0,28},{1,29},{2,30},{3,31}} | collective-permute-start | bytes 393224 | tf_op jit(solution)/shard_map/ppermute | solution.py:233
  31.7 57.4 %copy-start.1 = (s32[4]{0:T(128)S(1)}, s32[4]{0:T(128)}, u32[]{:S(2)}) copy-start(s32[4]{0:T(128)} %pad_add_fusion.where_ref) | copy-start | bytes 52
  40.3 23.6 %collective-permute-start.11 = (bf16[32,2048]{1,0:T(8,128)(2,1)}, bf16[32,2048]{1,0:T(8,128)(2,1)S(1)}, u32[]{:S(2)}, u32[]{:S(2)}) collective-permute-start(bf16[32,2048]{1,0:T(8,128)(2,1)} %get-tuple-element.46), channel_id=1, source_target_pairs={{0,16},{1,17},{2,18},{3,19},{4,20},{5,21},{6,22},{7,23},{8,24},{9,... | collective-permute-start | bytes 393224 | tf_op jit(solution)/shard_map/ppermute | solution.py:233
  57.8 17.2 %collective-permute-start.12 = (bf16[32,2048]{1,0:T(8,128)(2,1)}, bf16[32,2048]{1,0:T(8,128)(2,1)S(1)}, u32[]{:S(2)}, u32[]{:S(2)}) collective-permute-start(bf16[32,2048]{1,0:T(8,128)(2,1)} %get-tuple-element.47), channel_id=1, source_target_pairs={{0,24},{1,25},{2,26},{3,27},{4,28},{5,29},{6,30},{7,31},{8,16},{9,... | collective-permute-start | bytes 393224 | tf_op jit(solution)/shard_map/ppermute | solution.py:233
  57.8 17.3 %collective-permute-start.13 = (bf16[32,2048]{1,0:T(8,128)(2,1)}, bf16[32,2048]{1,0:T(8,128)(2,1)S(1)}, u32[]{:S(2)}, u32[]{:S(2)}) collective-permute-start(bf16[32,2048]{1,0:T(8,128)(2,1)} %get-tuple-element.48), channel_id=1, source_target_pairs={{0,18},{1,19},{2,16},{3,17},{4,22},{5,23},{6,20},{7,21},{8,26},{9,... | collective-permute-start | bytes 393224 | tf_op jit(solution)/shard_map/ppermute | solution.py:233
  59.6 22.9 %collective-permute-start.14 = (bf16[32,2048]{1,0:T(8,128)(2,1)}, bf16[32,2048]{1,0:T(8,128)(2,1)S(1)}, u32[]{:S(2)}, u32[]{:S(2)}) collective-permute-start(bf16[32,2048]{1,0:T(8,128)(2,1)} %get-tuple-element.49), channel_id=1, source_target_pairs={{0,26},{1,27},{2,24},{3,25},{4,30},{5,31},{6,28},{7,29},{8,18},{9,... | collective-permute-start | bytes 393224 | tf_op jit(solution)/shard_map/ppermute | solution.py:233
  61.7 35.5 %collective-permute-start.17 = (bf16[576,2048]{1,0:T(8,128)(2,1)}, bf16[576,2048]{1,0:T(8,128)(2,1)S(1)}, u32[]{:S(2)}, u32[]{:S(2)}) collective-permute-start(bf16[576,2048]{1,0:T(8,128)(2,1)} %collective-permute-done.refs_4_), channel_id=1, source_target_pairs={{0,5},{2,7},{4,1},{6,3},{9,12},{11,14},{13,8},{15,10},{16,21},{18,... | collective-permute-start | bytes 7077896 | tf_op jit(solution)/shard_map/ppermute | solution.py:233
  63.9 21.0 %collective-permute-start.8 = (bf16[32,2048]{1,0:T(8,128)(2,1)}, bf16[32,2048]{1,0:T(8,128)(2,1)S(1)}, u32[]{:S(2)}, u32[]{:S(2)}) collective-permute-start(bf16[32,2048]{1,0:T(8,128)(2,1)} %get-tuple-element.43), channel_id=1, source_target_pairs={{0,8},{1,9},{2,10},{3,11},{4,12},{5,13},{6,14},{7,15},{8,0},{9,1},... | collective-permute-start | bytes 393224 | tf_op jit(solution)/shard_map/ppermute | solution.py:233
  75.0 9.9 %collective-permute-start.9 = (bf16[32,2048]{1,0:T(8,128)(2,1)}, bf16[32,2048]{1,0:T(8,128)(2,1)S(1)}, u32[]{:S(2)}, u32[]{:S(2)}) collective-permute-start(bf16[32,2048]{1,0:T(8,128)(2,1)} %get-tuple-element.44), channel_id=1, source_target_pairs={{0,10},{1,11},{2,8},{3,9},{4,14},{5,15},{6,12},{7,13},{8,2},{9,3},... | collective-permute-start | bytes 393224 | tf_op jit(solution)/shard_map/ppermute | solution.py:233
  75.1 11.9 %collective-permute-start.10 = (bf16[32,2048]{1,0:T(8,128)(2,1)}, bf16[32,2048]{1,0:T(8,128)(2,1)S(1)}, u32[]{:S(2)}, u32[]{:S(2)}) collective-permute-start(bf16[32,2048]{1,0:T(8,128)(2,1)} %get-tuple-element.45), channel_id=1, source_target_pairs={{0,2},{1,3},{2,0},{3,1},{4,6},{5,7},{6,4},{7,5},{8,10},{9,11},{10,... | collective-permute-start | bytes 393224 | tf_op jit(solution)/shard_map/ppermute | solution.py:233
  82.6 5.0 %collective-permute-start.16 = (bf16[128,2048]{1,0:T(8,128)(2,1)S(1)}, bf16[128,2048]{1,0:T(8,128)(2,1)S(1)}, u32[]{:S(2)}, u32[]{:S(2)}) collective-permute-start(bf16[128,2048]{1,0:T(8,128)(2,1)S(1)} %constant_dynamic-update-slice_fusion.4.refs_1_), channel_id=1, source_target_pairs={{0,1},{1,0},{2,3},{3,2},{4,5},{5,4},{6,7},{7,6},{8,9},{9,8},{10,11... | collective-permute-start | bytes 1572872 | tf_op jit(solution)/shard_map/ppermute | solution.py:233
  87.0 2.2 %collective-permute-start.15 = (bf16[128,2048]{1,0:T(8,128)(2,1)S(1)}, bf16[128,2048]{1,0:T(8,128)(2,1)S(1)}, u32[]{:S(2)}, u32[]{:S(2)}) collective-permute-start(bf16[128,2048]{1,0:T(8,128)(2,1)S(1)} %constant_dynamic-update-slice_fusion.refs_0_), channel_id=1, source_target_pairs={{0,1},{1,0},{2,3},{3,2},{4,5},{5,4},{6,7},{7,6},{8,9},{9,8},{10,11... | collective-permute-start | bytes 1572872 | tf_op jit(solution)/shard_map/ppermute | solution.py:233
  100.4 33.5 %copy-start = (f32[128,2048]{1,0:T(8,128)S(1)}, f32[128,2048]{1,0:T(8,128)}, u32[]{:S(2)}) copy-start(f32[128,2048]{1,0:T(8,128)} %get-tuple-element.41.summed_ref) | copy-start | bytes 3145732
  100.4 33.4 %copy-start.2 = (s32[1,128,1]{1,2,0:T(1,128)S(1)}, s32[1,128,1]{1,2,0:T(1,128)}, u32[]{:S(2)}) copy-start(s32[1,128,1]{1,2,0:T(1,128)} %param.13) | copy-start | bytes 1540
  100.4 2.7 %collective-permute-start.18 = (bf16[256,2048]{1,0:T(8,128)(2,1)S(1)}, bf16[256,2048]{1,0:T(8,128)(2,1)S(1)}, u32[]{:S(2)}, u32[]{:S(2)}) collective-permute-start(bf16[256,2048]{1,0:T(8,128)(2,1)S(1)} %get-tuple-element.54), channel_id=1, source_target_pairs={{0,1},{1,0},{2,3},{3,2},{4,5},{5,4},{6,7},{7,6},{8,9},{9,8},{10,11... | collective-permute-start | bytes 3145736 | tf_op jit(solution)/shard_map/ppermute | solution.py:233
  103.6 7.4 %collective-permute-start.19 = (bf16[32,2048]{1,0:T(8,128)(2,1)S(1)}, bf16[32,2048]{1,0:T(8,128)(2,1)S(1)}, u32[]{:S(2)}, u32[]{:S(2)}) collective-permute-start(bf16[32,2048]{1,0:T(8,128)(2,1)S(1)} %get-tuple-element.56), channel_id=1, source_target_pairs={{0,2},{1,3},{2,0},{3,1},{4,6},{5,7},{6,4},{7,5},{8,10},{9,11},{10,... | collective-permute-start | bytes 393224 | tf_op jit(solution)/shard_map/ppermute | solution.py:233
  105.2 9.3 %collective-permute-start.20 = (bf16[32,2048]{1,0:T(8,128)(2,1)S(1)}, bf16[32,2048]{1,0:T(8,128)(2,1)S(1)}, u32[]{:S(2)}, u32[]{:S(2)}) collective-permute-start(bf16[32,2048]{1,0:T(8,128)(2,1)S(1)} %get-tuple-element.57), channel_id=1, source_target_pairs={{0,8},{1,9},{2,10},{3,11},{4,12},{5,13},{6,14},{7,15},{8,0},{9,1},... | collective-permute-start | bytes 393224 | tf_op jit(solution)/shard_map/ppermute | solution.py:233
  107.1 9.2 %collective-permute-start.21 = (bf16[32,2048]{1,0:T(8,128)(2,1)S(1)}, bf16[32,2048]{1,0:T(8,128)(2,1)S(1)}, u32[]{:S(2)}, u32[]{:S(2)}) collective-permute-start(bf16[32,2048]{1,0:T(8,128)(2,1)S(1)} %get-tuple-element.58), channel_id=1, source_target_pairs={{0,10},{1,11},{2,8},{3,9},{4,14},{5,15},{6,12},{7,13},{8,2},{9,3},... | collective-permute-start | bytes 393224 | tf_op jit(solution)/shard_map/ppermute | solution.py:233
  107.1 17.8 %collective-permute-start.22 = (bf16[32,2048]{1,0:T(8,128)(2,1)S(1)}, bf16[32,2048]{1,0:T(8,128)(2,1)S(1)}, u32[]{:S(2)}, u32[]{:S(2)}) collective-permute-start(bf16[32,2048]{1,0:T(8,128)(2,1)S(1)} %get-tuple-element.59), channel_id=1, source_target_pairs={{0,16},{1,17},{2,18},{3,19},{4,20},{5,21},{6,22},{7,23},{8,24},{9,... | collective-permute-start | bytes 393224 | tf_op jit(solution)/shard_map/ppermute | solution.py:233
  109.7 18.0 %collective-permute-start.23 = (bf16[32,2048]{1,0:T(8,128)(2,1)S(1)}, bf16[32,2048]{1,0:T(8,128)(2,1)S(1)}, u32[]{:S(2)}, u32[]{:S(2)}) collective-permute-start(bf16[32,2048]{1,0:T(8,128)(2,1)S(1)} %get-tuple-element.60), channel_id=1, source_target_pairs={{0,18},{1,19},{2,16},{3,17},{4,22},{5,23},{6,20},{7,21},{8,26},{9,... | collective-permute-start | bytes 393224 | tf_op jit(solution)/shard_map/ppermute | solution.py:233
  111.0 20.6 %collective-permute-start.24 = (bf16[32,2048]{1,0:T(8,128)(2,1)S(1)}, bf16[32,2048]{1,0:T(8,128)(2,1)S(1)}, u32[]{:S(2)}, u32[]{:S(2)}) collective-permute-start(bf16[32,2048]{1,0:T(8,128)(2,1)S(1)} %get-tuple-element.61), channel_id=1, source_target_pairs={{0,24},{1,25},{2,26},{3,27},{4,28},{5,29},{6,30},{7,31},{8,16},{9,... | collective-permute-start | bytes 393224 | tf_op jit(solution)/shard_map/ppermute | solution.py:233
  114.4 19.4 %collective-permute-start.25 = (bf16[32,2048]{1,0:T(8,128)(2,1)S(1)}, bf16[32,2048]{1,0:T(8,128)(2,1)S(1)}, u32[]{:S(2)}, u32[]{:S(2)}) collective-permute-start(bf16[32,2048]{1,0:T(8,128)(2,1)S(1)} %get-tuple-element.62), channel_id=1, source_target_pairs={{0,26},{1,27},{2,24},{3,25},{4,30},{5,31},{6,28},{7,29},{8,18},{9,... | collective-permute-start | bytes 393224 | tf_op jit(solution)/shard_map/ppermute | solution.py:233
  (8 other events, 74.5 us)

commit v6 on v5

--- a/solution.py
+++ b/solution.py
@@ -288,7 +288,6 @@
     queries_ref, residual_ref, kv_ref, bias_ref, mixed_ref, summed_ref, semaphores = refs[17:]
     tokens = queries_ref.shape[0]
     group = HEADS // KV_HEADS
-    ctx_here = where_ref[0]
     copies = fetch_all(
         [(queries_from, queries_ref), (residual_from, residual_ref)]
         + [(kv_from[k], kv_ref.at[pl.ds(k * tokens, tokens)]) for k in range(8)],
@@ -301,8 +300,9 @@
         if k == 0:
             bias_ref[:, span] = jnp.where(column <= row, 0.0, negative_fill)
         else:
+            seen = where_ref[0] == 1 if k == 1 else where_ref[1] >= k // 2
             bias_ref[:, span] = jnp.full(
-                (tokens, tokens), jnp.where(ctx_here >= k, 0.0, negative_fill), jnp.float32
+                (tokens, tokens), jnp.where(seen, 0.0, negative_fill), jnp.float32
             )
     for copy in copies[2:] + copies[:1]:
         copy.wait()
@@ -365,7 +365,8 @@
     if first_piece:
         packs, (total_ref,), rest = refs[:1], refs[1:2], refs[2:]
     else:
-        packs, before_from, (mine_ref, twins_ref), rest = refs[:2], refs[2], refs[3:5], refs[5:]
+        packs, own_from, before_from = refs[:1], refs[1:4], refs[4]
+        (mine_ref, twins_ref), rest = refs[5:7], refs[7:]
     rows_ref, before_ref, gate_ref, up_ref, down_ref, row_semaphores, semaphores = rest
     strip = packs[0].shape[0] // 3
     targets = (gate_ref, up_ref, down_ref)
@@ -386,12 +387,12 @@
 
         @pl.when(at_home)
         def _():
-            for copy in load_pack(packs[0], strip, targets, semaphores):
-                copy.start()
+            for kind in range(3):
+                pltpu.make_async_copy(own_from[kind], targets[kind], semaphores.at[kind]).start()
 
         @pl.when(jnp.logical_not(at_home))
         def _():
-            for copy in load_pack(packs[1], strip, targets, semaphores):
+            for copy in weight_copies:
                 copy.start()
 
     for copy in row_copies + weight_copies[:2]:
@@ -449,28 +450,34 @@
     ctx_here = lax.axis_index("ctx")
     exp_here = lax.axis_index("exp")
     home = ((ctx_here // 2) % 2 == exp_here % 2).astype(jnp.int32)
-    where = jnp.stack([ctx_here, ctx_here // 2, exp_here // 2, home]).astype(jnp.int32)
+    where = jnp.stack([ctx_here % 2, ctx_here // 2, exp_here // 2, home]).astype(jnp.int32)
     tokens, width = residual.shape[1:]
     piece = gate_weight.shape[2]
     capacity = max(2, 2 * tokens * TOPK // 8)
     ids_row = expert_ids[0].reshape(1, tokens)
     kv_own = jnp.concatenate([key_states[0], value_states[0]], axis=1)
-    kv_blocks = {0: kv_own}
-
-    def send_keys(block, k):
-        def later(z, x, y, core):
-            ctx = 2 * z + x + k
-            return (ctx // 2, ctx % 2, y, core) if ctx < 8 else None
-
-        kv_blocks[k] = move(block, later)
-
-    own = jnp.concatenate([gate_weight[0, 0], up_weight[0, 0], down_weight[0, 0]], axis=0)
-    one = move(own, first_hop)
-    for k in (4, 5, 3, 2, 6, 1, 7):
-        send_keys(kv_own, k)
-    kv_list = [kv_blocks[k] for k in range(1, 8)]
-    one, *kv_list = lax.optimization_barrier((one, *kv_list))
-    last = move(one, second_hop)
+    weights = (gate_weight[0, 0], up_weight[0, 0], down_weight[0, 0])
+    own_first = jnp.concatenate([weights[0], weights[1]], axis=0)
+    own_second = weights[2]
+
+    def along_z(steps):
+        return move(
+            kv_own, lambda z, x, y, core: (z + steps, x, y, core) if z + steps < 4 else None
+        )
+
+    def over_x(block, steps):
+        def rule(z, x, y, core):
+            return (z, 1 - x, y, core) if z >= steps and (steps or x == 0) else None
+
+        return move(block, rule)
+
+    one_first = move(own_first, first_hop)
+    kv_along = [kv_own] + [along_z(steps) for steps in (1, 2, 3)]
+    kv_list = []
+    for steps in range(4):
+        kv_list += [kv_along[steps], over_x(kv_along[steps], steps)]
+    one_first, own_second, *kv_list = lax.optimization_barrier((one_first, own_second, *kv_list))
+    one_second = move(own_second, first_hop)
     slot_shape = jax.ShapeDtypeStruct((capacity, width), jnp.bfloat16)
     keys_all = 8 * tokens
     rows_all = 8 * capacity
@@ -495,7 +502,7 @@
             transcendentals=tokens * keys_all * HEADS,
         ),
         name="attend",
-    )(where, ids_row, queries[0], residual[0], kv_own, *kv_list)
+    )(where, ids_row, queries[0], residual[0], *kv_list)
     summed, outgoing = first_out[0], list(first_out[1:])
 
     def swap(array, k):
@@ -503,6 +510,9 @@
             return array
         return move(array, lambda z, x, y, core: (z ^ (k >> 1), x, y ^ (k & 1), core))
 
+    one_second, *outgoing = lax.optimization_barrier((one_second, *outgoing))
+    one = jnp.concatenate([one_first, one_second], axis=0)
+    last = move(one, second_hop)
     arrived = {0: outgoing[0]}
     for k in (4, 6, 5, 7, 2, 3, 1):
         arrived[k] = swap(outgoing[k], k)
@@ -540,7 +550,7 @@
 
     first_total = run_expert([one], [])
     last, *first_total = lax.optimization_barrier((last, *first_total))
-    mine, twins = run_expert([own, last], first_total)
+    mine, twins = run_expert([last, *weights], first_total)
     joined = pl.pallas_call(
         join_kernel,
         out_shape=[slot_shape] * 8,

time: 137 us -> 127 us (0.927)
  starting transfers between devices: 61.8 us -> 43.1 us
  waiting for transfers between devices: 51.8 us -> 62.4 us
    ppermute x26 -> x27, starting transfers between devices: 61.8 us -> 43.1 us  [move(): return lax.ppermute(array, AXES, pairs)]
    ppermute x26 -> x27, waiting for transfers between devices: 51.8 us -> 62.4 us  [move(): return lax.ppermute(array, AXES, pairs)]
  transfers between devices with their start and end apart: 26 -> 27, of which waited for: 16 -> 19; matrix products, arithmetic and copies ran while one was open for 1% -> 1% of each run, Pallas kernels for 3% -> 9%
where the time goes in v6:
time: 127 us; the launch traced here: 126 us
  waiting for transfers between devices  62.4 us (49%)
  starting transfers between devices  43.1 us (34%)
  Pallas kernels  16.8 us (13%)
  other arithmetic  2.22 us (2%)
    ppermute x27, waiting for transfers between devices, move(): return lax.ppermute(array, AXES, pairs)  62.4 us
    ppermute x27, starting transfers between devices, move(): return lax.ppermute(array, AXES, pairs)  43.1 us
    pallas_call x1, Pallas kernels, shards_cube(): pl.pallas_call(attend_kernel, out_shape=[jax.ShapeDtypeStruct((tokens, wi...  8.49 us
    pallas_call x2, Pallas kernels, run_expert(): pl.pallas_call(partial(expert_kernel, len(row_parts)), out_shape=[mine, t...  6.11 us
  transfers between devices with their start and end apart: 27, of which 19 were waited for; matrix products, arithmetic and copies ran while one was open for 1% of the time, Pallas kernels for 9%

profile of v6, /device:TPU:8, one launch (start us, length us, event | category | flops | bytes accessed | tf_op | source)
XLA Modules:
  0.0 125.5 jit_solution(1558209284593941472)
XLA Ops:
  0.0 1.6 %pad_maximum_fusion = bf16[384,2048]{1,0:T(8,128)(2,1)S(1)} fusion(bf16[192,2048]{1,0:T(8,128)(2,1)} %bitcast.14, bf16[192,2048]{1,0:T(8,128)(2,1)} %bitcast.16), kind=kLoop, calls=%fused_computation | loop fusion | flops 3145728 | bytes 3145728 | tf_op jit(solution)/shard_map/concatenate | solution.py:460
  1.7 4.4 %collective-permute-start.2 = (bf16[128,512]{1,0:T(8,128)(2,1)S(1)}, bf16[128,512]{1,0:T(8,128)(2,1)S(1)}, u32[]{:S(2)}, u32[]{:S(2)}) collective-permute-start(bf16[128,512]{1,0:T(8,128)(2,1)S(1)} %pad_maximum_fusion.1.refs_0_), channel_id=1, source_target_pairs={{0,8},{1,9},{2,10},{3,11},{4,12},{5,13},{6,14},{7,15},{8,16},{9,17... | collective-permute-start | bytes 393224 | tf_op jit(solution)/shard_map/ppermute | solution.py:233
  6.1 1.8 %collective-permute-start.4 = (bf16[128,512]{1,0:T(8,128)(2,1)S(1)}, bf16[128,512]{1,0:T(8,128)(2,1)S(1)}, u32[]{:S(2)}, u32[]{:S(2)}) collective-permute-start(bf16[128,512]{1,0:T(8,128)(2,1)S(1)} %pad_maximum_fusion.1.refs_0_), channel_id=1, source_target_pairs={{0,16},{1,17},{2,18},{3,19},{4,20},{5,21},{6,22},{7,23},{8,24},{9,... | collective-permute-start | bytes 393224 | tf_op jit(solution)/shard_map/ppermute | solution.py:233
  8.6 3.4 %collective-permute-start.1 = (bf16[128,512]{1,0:T(8,128)(2,1)S(1)}, bf16[128,512]{1,0:T(8,128)(2,1)S(1)}, u32[]{:S(2)}, u32[]{:S(2)}) collective-permute-start(bf16[128,512]{1,0:T(8,128)(2,1)S(1)} %pad_maximum_fusion.1.refs_0_), channel_id=1, source_target_pairs={{0,4},{1,5},{2,6},{3,7},{8,12},{9,13},{10,14},{11,15},{16,20},{17,... | collective-permute-start | bytes 393224 | tf_op jit(solution)/shard_map/ppermute | solution.py:233
  12.0 1.9 %collective-permute-start.3 = (bf16[128,512]{1,0:T(8,128)(2,1)S(1)}, bf16[128,512]{1,0:T(8,128)(2,1)S(1)}, u32[]{:S(2)}, u32[]{:S(2)}) collective-permute-start(bf16[128,512]{1,0:T(8,128)(2,1)S(1)} %collective-permute-done.2.refs_2_), channel_id=1, source_target_pairs={{8,12},{9,13},{10,14},{11,15},{12,8},{13,9},{14,10},{15,11},{16,20... | collective-permute-start | bytes 393224 | tf_op jit(solution)/shard_map/ppermute | solution.py:233
  15.9 4.4 %collective-permute-done.3.refs_3_ = bf16[128,512]{1,0:T(8,128)(2,1)S(1)} collective-permute-done((bf16[128,512]{1,0:T(8,128)(2,1)S(1)}, bf16[128,512]{1,0:T(8,128)(2,1)S(1)}, u32[]{:S(2)}, u32[]{:S(2)}) %collective-permute-start.3) | collective-permute-done | bytes 131104 | tf_op jit(solution)/shard_map/ppermute | solution.py:233
  20.4 2.5 %collective-permute-done = bf16[384,2048]{1,0:T(8,128)(2,1)S(1)} collective-permute-done((bf16[384,2048]{1,0:T(8,128)(2,1)S(1)}, bf16[384,2048]{1,0:T(8,128)(2,1)S(1)}, u32[]{:S(2)}, u32[]{:S(2)}) %collective-permute-start) | collective-permute-done | bytes 1572896 | tf_op jit(solution)/shard_map/ppermute | solution.py:233
  22.9 1.7 %collective-permute-start.8 = (bf16[192,2048]{1,0:T(8,128)(2,1)S(1)}, bf16[192,2048]{1,0:T(8,128)(2,1)S(1)}, u32[]{:S(2)}, u32[]{:S(2)}) collective-permute-start(bf16[192,2048]{1,0:T(8,128)(2,1)S(1)} %bitcast.18), channel_id=1, source_target_pairs={{0,5},{1,9},{2,7},{3,11},{4,1},{5,13},{6,3},{7,15},{8,0},{9,12},{1... | collective-permute-start | bytes 2359304 | tf_op jit(solution)/shard_map/ppermute | solution.py:233
  25.2 8.5 %attend.1 = (f32[128,2048]{1,0:T(8,128)}, bf16[32,2048]{1,0:T(8,128)(2,1)}, bf16[32,2048]{1,0:T(8,128)(2,1)}, bf16[32,2048]{1,0:T(8,128)(2,1)}, bf16[32,2048]{1,...) custom-call(s32[4]{0:T(128)} %pad_add_fusion.where_ref, ...), custom_call_target="tpu_custom_call" | custom-call | flops 1073741824 | bytes 2097152 | tf_op jit(solution)/shard_map/attend/pallas_call | solution.py:484
  33.9 9.6 %collective-permute-done.8 = bf16[192,2048]{1,0:T(8,128)(2,1)S(1)} collective-permute-done((bf16[192,2048]{1,0:T(8,128)(2,1)S(1)}, bf16[192,2048]{1,0:T(8,128)(2,1)S(1)}, u32[]{:S(2)}, u32[]{:S(2)}) %collective-permute-start.8) | collective-permute-done | bytes 786464 | tf_op jit(solution)/shard_map/ppermute | solution.py:233
  43.6 10.6 %collective-permute-start.12 = (bf16[32,2048]{1,0:T(8,128)(2,1)S(1)}, bf16[32,2048]{1,0:T(8,128)(2,1)S(1)}, u32[]{:S(2)}, u32[]{:S(2)}) collective-permute-start(bf16[32,2048]{1,0:T(8,128)(2,1)S(1)} %copy-done.24), channel_id=1, source_target_pairs={{0,16},{1,17},{2,18},{3,19},{4,20},{5,21},{6,22},{7,23},{8,24},{9,... | collective-permute-start | bytes 393224 | tf_op jit(solution)/shard_map/ppermute | solution.py:233
  55.3 2.8 %collective-permute-start.15 = (bf16[32,2048]{1,0:T(8,128)(2,1)S(1)}, bf16[32,2048]{1,0:T(8,128)(2,1)S(1)}, u32[]{:S(2)}, u32[]{:S(2)}) collective-permute-start(bf16[32,2048]{1,0:T(8,128)(2,1)S(1)} %copy-done.21), channel_id=1, source_target_pairs={{0,26},{1,27},{2,24},{3,25},{4,30},{5,31},{6,28},{7,29},{8,18},{9,... | collective-permute-start | bytes 393224 | tf_op jit(solution)/shard_map/ppermute | solution.py:233
  59.5 8.0 %collective-permute-done.12 = bf16[32,2048]{1,0:T(8,128)(2,1)S(1)} collective-permute-done((bf16[32,2048]{1,0:T(8,128)(2,1)S(1)}, bf16[32,2048]{1,0:T(8,128)(2,1)S(1)}, u32[]{:S(2)}, u32[]{:S(2)}) %collective-permute-start.12) | collective-permute-done | bytes 131104 | tf_op jit(solution)/shard_map/ppermute | solution.py:233
  67.6 2.8 %collective-permute-done.13 = bf16[32,2048]{1,0:T(8,128)(2,1)S(1)} collective-permute-done((bf16[32,2048]{1,0:T(8,128)(2,1)S(1)}, bf16[32,2048]{1,0:T(8,128)(2,1)S(1)}, u32[]{:S(2)}, u32[]{:S(2)}) %collective-permute-start.13) | collective-permute-done | bytes 131104 | tf_op jit(solution)/shard_map/ppermute | solution.py:233
  70.6 2.6 %collective-permute-done.14 = bf16[32,2048]{1,0:T(8,128)(2,1)S(1)} collective-permute-done((bf16[32,2048]{1,0:T(8,128)(2,1)S(1)}, bf16[32,2048]{1,0:T(8,128)(2,1)S(1)}, u32[]{:S(2)}, u32[]{:S(2)}) %collective-permute-start.14) | collective-permute-done | bytes 131104 | tf_op jit(solution)/shard_map/ppermute | solution.py:233
  73.2 1.5 %collective-permute-start.11 = (bf16[32,2048]{1,0:T(8,128)(2,1)S(1)}, bf16[32,2048]{1,0:T(8,128)(2,1)S(1)}, u32[]{:S(2)}, u32[]{:S(2)}) collective-permute-start(bf16[32,2048]{1,0:T(8,128)(2,1)S(1)} %copy-done.18), channel_id=1, source_target_pairs={{0,2},{1,3},{2,0},{3,1},{4,6},{5,7},{6,4},{7,5},{8,10},{9,11},{10,... | collective-permute-start | bytes 393224 | tf_op jit(solution)/shard_map/ppermute | solution.py:233
  74.7 2.9 %collective-permute-done.15 = bf16[32,2048]{1,0:T(8,128)(2,1)S(1)} collective-permute-done((bf16[32,2048]{1,0:T(8,128)(2,1)S(1)}, bf16[32,2048]{1,0:T(8,128)(2,1)S(1)}, u32[]{:S(2)}, u32[]{:S(2)}) %collective-permute-start.15) | collective-permute-done | bytes 131104 | tf_op jit(solution)/shard_map/ppermute | solution.py:233
  79.6 2.7 %collective-permute-done.11 = bf16[32,2048]{1,0:T(8,128)(2,1)S(1)} collective-permute-done((bf16[32,2048]{1,0:T(8,128)(2,1)S(1)}, bf16[32,2048]{1,0:T(8,128)(2,1)S(1)}, u32[]{:S(2)}, u32[]{:S(2)}) %collective-permute-start.11) | collective-permute-done | bytes 131104 | tf_op jit(solution)/shard_map/ppermute | solution.py:233
  82.4 1.9 %collective-permute-done.16.refs_2_ = bf16[128,2048]{1,0:T(8,128)(2,1)S(1)} collective-permute-done((bf16[128,2048]{1,0:T(8,128)(2,1)S(1)}, bf16[128,2048]{1,0:T(8,128)(2,1)S(1)}, u32[]{:S(2)}, u32[]{:S(2)}) %collective-permute-start.16) | collective-permute-done | bytes 524320 | tf_op jit(solution)/shard_map/ppermute | solution.py:233
  84.3 2.9 %experts_first.1.refs_8_ = f32[512,2048]{1,0:T(8,128)S(1)} custom-call(s32[4]{0:T(128)S(1)} %copy-done.4, bf16[128,2048]{1,0:T(8,128)(2,1)S(1)} %constant_dynamic-update-slice_fusion.refs_0_, bf16[128,2048]{1,0:T(8,128)(2,1)S(1)} %constant_dynamic-update-slice_fusion.4.refs_1_, bf16[128,2048]{1,0:T(8,128)(2,1)S(1)} %collective-permute-done.16.refs_2_, ...), custom_call_target="tpu_custom_call" | custom-call | flops 1207959552 | bytes 2359296 | tf_op jit(solution)/shard_map/experts_first/pallas_call | solution.py:528
  88.4 3.2 %experts_rest.1 = (f32[256,2048]{1,0:T(8,128)S(1)}, bf16[256,2048]{1,0:T(8,128)(2,1)S(1)}) custom-call(s32[4]{0:T(128)S(1)} %copy-done.4, bf16[128,2048]{1,0:T(8,128)(2,1)S(1)} %constant_dynamic-update-slice_fusion.refs_0_, bf16[128,2048]{1,0:T(8,128)(2,1)S(1)} %constant_dynamic-update-slice_fusion.4.refs_1_, ...), custom_call_target="tpu_custom_call" | custom-call | flops 1207959552 | bytes 2359296 | tf_op jit(solution)/shard_map/experts_rest/pallas_call | solution.py:528
  91.7 2.6 %collective-permute-done.19.other_from = bf16[256,2048]{1,0:T(8,128)(2,1)S(1)} collective-permute-done((bf16[256,2048]{1,0:T(8,128)(2,1)S(1)}, bf16[256,2048]{1,0:T(8,128)(2,1)S(1)}, u32[]{:S(2)}, u32[]{:S(2)}) %collective-permute-start.19) | collective-permute-done | bytes 1048608 | tf_op jit(solution)/shard_map/ppermute | solution.py:233
  94.7 1.6 %collective-permute-start.20 = (bf16[32,2048]{1,0:T(8,128)(2,1)S(1)}, bf16[32,2048]{1,0:T(8,128)(2,1)S(1)}, u32[]{:S(2)}, u32[]{:S(2)}) collective-permute-start(bf16[32,2048]{1,0:T(8,128)(2,1)S(1)} %get-tuple-element.78), channel_id=1, source_target_pairs={{0,2},{1,3},{2,0},{3,1},{4,6},{5,7},{6,4},{7,5},{8,10},{9,11},{10,... | collective-permute-start | bytes 393224 | tf_op jit(solution)/shard_map/ppermute | solution.py:233
  96.7 1.6 %collective-permute-start.22 = (bf16[32,2048]{1,0:T(8,128)(2,1)S(1)}, bf16[32,2048]{1,0:T(8,128)(2,1)S(1)}, u32[]{:S(2)}, u32[]{:S(2)}) collective-permute-start(bf16[32,2048]{1,0:T(8,128)(2,1)S(1)} %get-tuple-element.80), channel_id=1, source_target_pairs={{0,10},{1,11},{2,8},{3,9},{4,14},{5,15},{6,12},{7,13},{8,2},{9,3},... | collective-permute-start | bytes 393224 | tf_op jit(solution)/shard_map/ppermute | solution.py:233
  98.3 2.9 %collective-permute-start.23 = (bf16[32,2048]{1,0:T(8,128)(2,1)S(1)}, bf16[32,2048]{1,0:T(8,128)(2,1)S(1)}, u32[]{:S(2)}, u32[]{:S(2)}) collective-permute-start(bf16[32,2048]{1,0:T(8,128)(2,1)S(1)} %get-tuple-element.81), channel_id=1, source_target_pairs={{0,16},{1,17},{2,18},{3,19},{4,20},{5,21},{6,22},{7,23},{8,24},{9,... | collective-permute-start | bytes 393224 | tf_op jit(solution)/shard_map/ppermute | solution.py:233
  102.2 1.4 %collective-permute-start.25 = (bf16[32,2048]{1,0:T(8,128)(2,1)S(1)}, bf16[32,2048]{1,0:T(8,128)(2,1)S(1)}, u32[]{:S(2)}, u32[]{:S(2)}) collective-permute-start(bf16[32,2048]{1,0:T(8,128)(2,1)S(1)} %get-tuple-element.83), channel_id=1, source_target_pairs={{0,24},{1,25},{2,26},{3,27},{4,28},{5,29},{6,30},{7,31},{8,16},{9,... | collective-permute-start | bytes 393224 | tf_op jit(solution)/shard_map/ppermute | solution.py:233
  104.8 2.2 %collective-permute-done.22.refs_3_ = bf16[32,2048]{1,0:T(8,128)(2,1)S(1)} collective-permute-done((bf16[32,2048]{1,0:T(8,128)(2,1)S(1)}, bf16[32,2048]{1,0:T(8,128)(2,1)S(1)}, u32[]{:S(2)}, u32[]{:S(2)}) %collective-permute-start.22) | collective-permute-done | bytes 131104 | tf_op jit(solution)/shard_map/ppermute | solution.py:233
  107.0 9.3 %collective-permute-done.23.refs_4_ = bf16[32,2048]{1,0:T(8,128)(2,1)S(1)} collective-permute-done((bf16[32,2048]{1,0:T(8,128)(2,1)S(1)}, bf16[32,2048]{1,0:T(8,128)(2,1)S(1)}, u32[]{:S(2)}, u32[]{:S(2)}) %collective-permute-start.23) | collective-permute-done | bytes 131104 | tf_op jit(solution)/shard_map/ppermute | solution.py:233
  116.3 2.8 %collective-permute-done.24.refs_5_ = bf16[32,2048]{1,0:T(8,128)(2,1)S(1)} collective-permute-done((bf16[32,2048]{1,0:T(8,128)(2,1)S(1)}, bf16[32,2048]{1,0:T(8,128)(2,1)S(1)}, u32[]{:S(2)}, u32[]{:S(2)}) %collective-permute-start.24) | collective-permute-done | bytes 131104 | tf_op jit(solution)/shard_map/ppermute | solution.py:233
  119.1 2.6 %collective-permute-done.25.refs_6_ = bf16[32,2048]{1,0:T(8,128)(2,1)S(1)} collective-permute-done((bf16[32,2048]{1,0:T(8,128)(2,1)S(1)}, bf16[32,2048]{1,0:T(8,128)(2,1)S(1)}, u32[]{:S(2)}, u32[]{:S(2)}) %collective-permute-start.25) | collective-permute-done | bytes 131104 | tf_op jit(solution)/shard_map/ppermute | solution.py:233
  121.8 1.9 %collective-permute-done.26.refs_7_ = bf16[32,2048]{1,0:T(8,128)(2,1)S(1)} collective-permute-done((bf16[32,2048]{1,0:T(8,128)(2,1)S(1)}, bf16[32,2048]{1,0:T(8,128)(2,1)S(1)}, u32[]{:S(2)}, u32[]{:S(2)}) %collective-permute-start.26) | collective-permute-done | bytes 131104 | tf_op jit(solution)/shard_map/ppermute | solution.py:233
  123.7 1.8 %combine.1 = bf16[128,2048]{1,0:T(8,128)(2,1)} custom-call(s32[4]{0:T(128)S(1)} %copy-done.4, s32[1,128]{1,0:T(1,128)S(1)} %bitcast.21, f32[128,1]{1,0:T(8,128)S(1)} %copy.10.route_ref, f32[128,2048]{1,0:T(8,128)S(1)} %copy-done.2, bf16[32,2048]{1,0:T(8,128)(2,1)S(1)} %get-tuple-element.77.refs_0_, bf16[32,2048]{1,0:T(8,128)(2,1)S(1)} %collective-permute-done.20.refs_1_, ...), custom_call_target="tpu_custom_call" | custom-call | flops 134217728 | bytes 3145728 | tf_op jit(solution)/shard_map/combine/pallas_call | solution.py:572
  (91 shorter events, 12.6 us)
Async XLA Ops:
  1.6 21.3 %collective-permute-start = (bf16[384,2048]{1,0:T(8,128)(2,1)S(1)}, bf16[384,2048]{1,0:T(8,128)(2,1)S(1)}, u32[]{:S(2)}, u32[]{:S(2)}) collective-permute-start(bf16[384,2048]{1,0:T(8,128)(2,1)S(1)} %pad_maximum_fusion), channel_id=1, source_target_pairs={{0,5},{1,9},{2,7},{3,11},{4,1},{5,13},{6,3},{7,15},{8,0},{9,12},{1... | collective-permute-start | bytes 4718600 | tf_op jit(solution)/shard_map/ppermute | solution.py:233
  1.7 10.3 %collective-permute-start.2 = (bf16[128,512]{1,0:T(8,128)(2,1)S(1)}, bf16[128,512]{1,0:T(8,128)(2,1)S(1)}, u32[]{:S(2)}, u32[]{:S(2)}) collective-permute-start(bf16[128,512]{1,0:T(8,128)(2,1)S(1)} %pad_maximum_fusion.1.refs_0_), channel_id=1, source_target_pairs={{0,8},{1,9},{2,10},{3,11},{4,12},{5,13},{6,14},{7,15},{8,16},{9,17... | collective-permute-start | bytes 393224 | tf_op jit(solution)/shard_map/ppermute | solution.py:233
  6.1 7.9 %collective-permute-start.4 = (bf16[128,512]{1,0:T(8,128)(2,1)S(1)}, bf16[128,512]{1,0:T(8,128)(2,1)S(1)}, u32[]{:S(2)}, u32[]{:S(2)}) collective-permute-start(bf16[128,512]{1,0:T(8,128)(2,1)S(1)} %pad_maximum_fusion.1.refs_0_), channel_id=1, source_target_pairs={{0,16},{1,17},{2,18},{3,19},{4,20},{5,21},{6,22},{7,23},{8,24},{9,... | collective-permute-start | bytes 393224 | tf_op jit(solution)/shard_map/ppermute | solution.py:233
  7.9 6.7 %collective-permute-start.6 = (bf16[128,512]{1,0:T(8,128)(2,1)S(1)}, bf16[128,512]{1,0:T(8,128)(2,1)S(1)}, u32[]{:S(2)}, u32[]{:S(2)}) collective-permute-start(bf16[128,512]{1,0:T(8,128)(2,1)S(1)} %pad_maximum_fusion.1.refs_0_), channel_id=1, source_target_pairs={{0,24},{1,25},{2,26},{3,27},{4,28},{5,29},{6,30},{7,31}} | collective-permute-start | bytes 393224 | tf_op jit(solution)/shard_map/ppermute | solution.py:233
  8.6 7.3 %collective-permute-start.1 = (bf16[128,512]{1,0:T(8,128)(2,1)S(1)}, bf16[128,512]{1,0:T(8,128)(2,1)S(1)}, u32[]{:S(2)}, u32[]{:S(2)}) collective-permute-start(bf16[128,512]{1,0:T(8,128)(2,1)S(1)} %pad_maximum_fusion.1.refs_0_), channel_id=1, source_target_pairs={{0,4},{1,5},{2,6},{3,7},{8,12},{9,13},{10,14},{11,15},{16,20},{17,... | collective-permute-start | bytes 393224 | tf_op jit(solution)/shard_map/ppermute | solution.py:233
  12.0 8.3 %collective-permute-start.3 = (bf16[128,512]{1,0:T(8,128)(2,1)S(1)}, bf16[128,512]{1,0:T(8,128)(2,1)S(1)}, u32[]{:S(2)}, u32[]{:S(2)}) collective-permute-start(bf16[128,512]{1,0:T(8,128)(2,1)S(1)} %collective-permute-done.2.refs_2_), channel_id=1, source_target_pairs={{8,12},{9,13},{10,14},{11,15},{12,8},{13,9},{14,10},{15,11},{16,20... | collective-permute-start | bytes 393224 | tf_op jit(solution)/shard_map/ppermute | solution.py:233
  14.0 6.4 %collective-permute-start.5 = (bf16[128,512]{1,0:T(8,128)(2,1)S(1)}, bf16[128,512]{1,0:T(8,128)(2,1)S(1)}, u32[]{:S(2)}, u32[]{:S(2)}) collective-permute-start(bf16[128,512]{1,0:T(8,128)(2,1)S(1)} %collective-permute-done.4.refs_4_), channel_id=1, source_target_pairs={{16,20},{17,21},{18,22},{19,23},{20,16},{21,17},{22,18},{23,19},{2... | collective-permute-start | bytes 393224 | tf_op jit(solution)/shard_map/ppermute | solution.py:233
  14.7 5.7 %collective-permute-start.7 = (bf16[128,512]{1,0:T(8,128)(2,1)S(1)}, bf16[128,512]{1,0:T(8,128)(2,1)S(1)}, u32[]{:S(2)}, u32[]{:S(2)}) collective-permute-start(bf16[128,512]{1,0:T(8,128)(2,1)S(1)} %collective-permute-done.6.refs_6_), channel_id=1, source_target_pairs={{24,28},{25,29},{26,30},{27,31},{28,24},{29,25},{30,26},{31,27}} | collective-permute-start | bytes 393224 | tf_op jit(solution)/shard_map/ppermute | solution.py:233
  22.9 20.7 %collective-permute-start.8 = (bf16[192,2048]{1,0:T(8,128)(2,1)S(1)}, bf16[192,2048]{1,0:T(8,128)(2,1)S(1)}, u32[]{:S(2)}, u32[]{:S(2)}) collective-permute-start(bf16[192,2048]{1,0:T(8,128)(2,1)S(1)} %bitcast.18), channel_id=1, source_target_pairs={{0,5},{1,9},{2,7},{3,11},{4,1},{5,13},{6,3},{7,15},{8,0},{9,12},{1... | collective-permute-start | bytes 2359304 | tf_op jit(solution)/shard_map/ppermute | solution.py:233
  33.8 33.7 %copy-start.20 = (bf16[32,2048]{1,0:T(8,128)(2,1)S(1)}, bf16[32,2048]{1,0:T(8,128)(2,1)}, u32[]{:S(2)}) copy-start(bf16[32,2048]{1,0:T(8,128)(2,1)} %get-tuple-element.64) | copy-start | bytes 393220
  33.8 36.5 %copy-start.19 = (bf16[32,2048]{1,0:T(8,128)(2,1)S(1)}, bf16[32,2048]{1,0:T(8,128)(2,1)}, u32[]{:S(2)}) copy-start(bf16[32,2048]{1,0:T(8,128)(2,1)} %get-tuple-element.65) | copy-start | bytes 393220
  33.8 39.4 %copy-start.18 = (bf16[32,2048]{1,0:T(8,128)(2,1)S(1)}, bf16[32,2048]{1,0:T(8,128)(2,1)}, u32[]{:S(2)}) copy-start(bf16[32,2048]{1,0:T(8,128)(2,1)} %get-tuple-element.66) | copy-start | bytes 393220
  33.9 50.3 %copy-start.4 = (s32[4]{0:T(128)S(1)}, s32[4]{0:T(128)}, u32[]{:S(2)}) copy-start(s32[4]{0:T(128)} %pad_add_fusion.where_ref) | copy-start | bytes 52
  43.6 23.9 %collective-permute-start.12 = (bf16[32,2048]{1,0:T(8,128)(2,1)S(1)}, bf16[32,2048]{1,0:T(8,128)(2,1)S(1)}, u32[]{:S(2)}, u32[]{:S(2)}) collective-permute-start(bf16[32,2048]{1,0:T(8,128)(2,1)S(1)} %copy-done.24), channel_id=1, source_target_pairs={{0,16},{1,17},{2,18},{3,19},{4,20},{5,21},{6,22},{7,23},{8,24},{9,... | collective-permute-start | bytes 393224 | tf_op jit(solution)/shard_map/ppermute | solution.py:233
  54.2 16.1 %collective-permute-start.13 = (bf16[32,2048]{1,0:T(8,128)(2,1)S(1)}, bf16[32,2048]{1,0:T(8,128)(2,1)S(1)}, u32[]{:S(2)}, u32[]{:S(2)}) collective-permute-start(bf16[32,2048]{1,0:T(8,128)(2,1)S(1)} %copy-done.23), channel_id=1, source_target_pairs={{0,24},{1,25},{2,26},{3,27},{4,28},{5,29},{6,30},{7,31},{8,16},{9,... | collective-permute-start | bytes 393224 | tf_op jit(solution)/shard_map/ppermute | solution.py:233
  54.2 19.0 %collective-permute-start.14 = (bf16[32,2048]{1,0:T(8,128)(2,1)S(1)}, bf16[32,2048]{1,0:T(8,128)(2,1)S(1)}, u32[]{:S(2)}, u32[]{:S(2)}) collective-permute-start(bf16[32,2048]{1,0:T(8,128)(2,1)S(1)} %copy-done.22), channel_id=1, source_target_pairs={{0,18},{1,19},{2,16},{3,17},{4,22},{5,23},{6,20},{7,21},{8,26},{9,... | collective-permute-start | bytes 393224 | tf_op jit(solution)/shard_map/ppermute | solution.py:233
  55.3 22.3 %collective-permute-start.15 = (bf16[32,2048]{1,0:T(8,128)(2,1)S(1)}, bf16[32,2048]{1,0:T(8,128)(2,1)S(1)}, u32[]{:S(2)}, u32[]{:S(2)}) collective-permute-start(bf16[32,2048]{1,0:T(8,128)(2,1)S(1)} %copy-done.21), channel_id=1, source_target_pairs={{0,26},{1,27},{2,24},{3,25},{4,30},{5,31},{6,28},{7,29},{8,18},{9,... | collective-permute-start | bytes 393224 | tf_op jit(solution)/shard_map/ppermute | solution.py:233
  58.2 30.2 %collective-permute-start.18 = (bf16[576,2048]{1,0:T(8,128)(2,1)S(1)}, bf16[576,2048]{1,0:T(8,128)(2,1)S(1)}, u32[]{:S(2)}, u32[]{:S(2)}) collective-permute-start(bf16[576,2048]{1,0:T(8,128)(2,1)S(1)} %constant_dynamic-update-slice_fusion.8.refs_4_), channel_id=1, source_target_pairs={{0,5},{2,7},{4,1},{6,3},{9,12},{11,14},{13,8},{15,10},{16,21},{18,... | collective-permute-start | bytes 7077896 | tf_op jit(solution)/shard_map/ppermute | solution.py:233
  67.5 11.4 %collective-permute-start.9 = (bf16[32,2048]{1,0:T(8,128)(2,1)S(1)}, bf16[32,2048]{1,0:T(8,128)(2,1)S(1)}, u32[]{:S(2)}, u32[]{:S(2)}) collective-permute-start(bf16[32,2048]{1,0:T(8,128)(2,1)S(1)} %copy-done.20), channel_id=1, source_target_pairs={{0,8},{1,9},{2,10},{3,11},{4,12},{5,13},{6,14},{7,15},{8,0},{9,1},... | collective-permute-start | bytes 393224 | tf_op jit(solution)/shard_map/ppermute | solution.py:233
  70.3 9.2 %collective-permute-start.10 = (bf16[32,2048]{1,0:T(8,128)(2,1)S(1)}, bf16[32,2048]{1,0:T(8,128)(2,1)S(1)}, u32[]{:S(2)}, u32[]{:S(2)}) collective-permute-start(bf16[32,2048]{1,0:T(8,128)(2,1)S(1)} %copy-done.19), channel_id=1, source_target_pairs={{0,10},{1,11},{2,8},{3,9},{4,14},{5,15},{6,12},{7,13},{8,2},{9,3},... | collective-permute-start | bytes 393224 | tf_op jit(solution)/shard_map/ppermute | solution.py:233
  73.2 9.0 %collective-permute-start.11 = (bf16[32,2048]{1,0:T(8,128)(2,1)S(1)}, bf16[32,2048]{1,0:T(8,128)(2,1)S(1)}, u32[]{:S(2)}, u32[]{:S(2)}) collective-permute-start(bf16[32,2048]{1,0:T(8,128)(2,1)S(1)} %copy-done.18), channel_id=1, source_target_pairs={{0,2},{1,3},{2,0},{3,1},{4,6},{5,7},{6,4},{7,5},{8,10},{9,11},{10,... | collective-permute-start | bytes 393224 | tf_op jit(solution)/shard_map/ppermute | solution.py:233
  77.6 4.7 %collective-permute-start.17 = (bf16[128,2048]{1,0:T(8,128)(2,1)S(1)}, bf16[128,2048]{1,0:T(8,128)(2,1)S(1)}, u32[]{:S(2)}, u32[]{:S(2)}) collective-permute-start(bf16[128,2048]{1,0:T(8,128)(2,1)S(1)} %constant_dynamic-update-slice_fusion.4.refs_1_), channel_id=1, source_target_pairs={{0,1},{1,0},{2,3},{3,2},{4,5},{5,4},{6,7},{7,6},{8,9},{9,8},{10,11... | collective-permute-start | bytes 1572872 | tf_op jit(solution)/shard_map/ppermute | solution.py:233
  82.3 2.0 %collective-permute-start.16 = (bf16[128,2048]{1,0:T(8,128)(2,1)S(1)}, bf16[128,2048]{1,0:T(8,128)(2,1)S(1)}, u32[]{:S(2)}, u32[]{:S(2)}) collective-permute-start(bf16[128,2048]{1,0:T(8,128)(2,1)S(1)} %constant_dynamic-update-slice_fusion.refs_0_), channel_id=1, source_target_pairs={{0,1},{1,0},{2,3},{3,2},{4,5},{5,4},{6,7},{7,6},{8,9},{9,8},{10,11... | collective-permute-start | bytes 1572872 | tf_op jit(solution)/shard_map/ppermute | solution.py:233
  91.6 32.1 %copy-start.2 = (f32[128,2048]{1,0:T(8,128)S(1)}, f32[128,2048]{1,0:T(8,128)}, u32[]{:S(2)}) copy-start(f32[128,2048]{1,0:T(8,128)} %get-tuple-element.53.summed_ref) | copy-start | bytes 3145732
  91.6 2.7 %collective-permute-start.19 = (bf16[256,2048]{1,0:T(8,128)(2,1)S(1)}, bf16[256,2048]{1,0:T(8,128)(2,1)S(1)}, u32[]{:S(2)}, u32[]{:S(2)}) collective-permute-start(bf16[256,2048]{1,0:T(8,128)(2,1)S(1)} %get-tuple-element.76), channel_id=1, source_target_pairs={{0,1},{1,0},{2,3},{3,2},{4,5},{5,4},{6,7},{7,6},{8,9},{9,8},{10,11... | collective-permute-start | bytes 3145736 | tf_op jit(solution)/shard_map/ppermute | solution.py:233
  94.7 7.4 %collective-permute-start.20 = (bf16[32,2048]{1,0:T(8,128)(2,1)S(1)}, bf16[32,2048]{1,0:T(8,128)(2,1)S(1)}, u32[]{:S(2)}, u32[]{:S(2)}) collective-permute-start(bf16[32,2048]{1,0:T(8,128)(2,1)S(1)} %get-tuple-element.78), channel_id=1, source_target_pairs={{0,2},{1,3},{2,0},{3,1},{4,6},{5,7},{6,4},{7,5},{8,10},{9,11},{10,... | collective-permute-start | bytes 393224 | tf_op jit(solution)/shard_map/ppermute | solution.py:233
  96.3 8.4 %collective-permute-start.21 = (bf16[32,2048]{1,0:T(8,128)(2,1)S(1)}, bf16[32,2048]{1,0:T(8,128)(2,1)S(1)}, u32[]{:S(2)}, u32[]{:S(2)}) collective-permute-start(bf16[32,2048]{1,0:T(8,128)(2,1)S(1)} %get-tuple-element.79), channel_id=1, source_target_pairs={{0,8},{1,9},{2,10},{3,11},{4,12},{5,13},{6,14},{7,15},{8,0},{9,1},... | collective-permute-start | bytes 393224 | tf_op jit(solution)/shard_map/ppermute | solution.py:233
  96.7 10.3 %collective-permute-start.22 = (bf16[32,2048]{1,0:T(8,128)(2,1)S(1)}, bf16[32,2048]{1,0:T(8,128)(2,1)S(1)}, u32[]{:S(2)}, u32[]{:S(2)}) collective-permute-start(bf16[32,2048]{1,0:T(8,128)(2,1)S(1)} %get-tuple-element.80), channel_id=1, source_target_pairs={{0,10},{1,11},{2,8},{3,9},{4,14},{5,15},{6,12},{7,13},{8,2},{9,3},... | collective-permute-start | bytes 393224 | tf_op jit(solution)/shard_map/ppermute | solution.py:233
  98.3 18.0 %collective-permute-start.23 = (bf16[32,2048]{1,0:T(8,128)(2,1)S(1)}, bf16[32,2048]{1,0:T(8,128)(2,1)S(1)}, u32[]{:S(2)}, u32[]{:S(2)}) collective-permute-start(bf16[32,2048]{1,0:T(8,128)(2,1)S(1)} %get-tuple-element.81), channel_id=1, source_target_pairs={{0,16},{1,17},{2,18},{3,19},{4,20},{5,21},{6,22},{7,23},{8,24},{9,... | collective-permute-start | bytes 393224 | tf_op jit(solution)/shard_map/ppermute | solution.py:233
  101.1 18.0 %collective-permute-start.24 = (bf16[32,2048]{1,0:T(8,128)(2,1)S(1)}, bf16[32,2048]{1,0:T(8,128)(2,1)S(1)}, u32[]{:S(2)}, u32[]{:S(2)}) collective-permute-start(bf16[32,2048]{1,0:T(8,128)(2,1)S(1)} %get-tuple-element.82), channel_id=1, source_target_pairs={{0,18},{1,19},{2,16},{3,17},{4,22},{5,23},{6,20},{7,21},{8,26},{9,... | collective-permute-start | bytes 393224 | tf_op jit(solution)/shard_map/ppermute | solution.py:233
  102.2 19.6 %collective-permute-start.25 = (bf16[32,2048]{1,0:T(8,128)(2,1)S(1)}, bf16[32,2048]{1,0:T(8,128)(2,1)S(1)}, u32[]{:S(2)}, u32[]{:S(2)}) collective-permute-start(bf16[32,2048]{1,0:T(8,128)(2,1)S(1)} %get-tuple-element.83), channel_id=1, source_target_pairs={{0,24},{1,25},{2,26},{3,27},{4,28},{5,29},{6,30},{7,31},{8,16},{9,... | collective-permute-start | bytes 393224 | tf_op jit(solution)/shard_map/ppermute | solution.py:233
  104.7 19.0 %collective-permute-start.26 = (bf16[32,2048]{1,0:T(8,128)(2,1)S(1)}, bf16[32,2048]{1,0:T(8,128)(2,1)S(1)}, u32[]{:S(2)}, u32[]{:S(2)}) collective-permute-start(bf16[32,2048]{1,0:T(8,128)(2,1)S(1)} %get-tuple-element.84), channel_id=1, source_target_pairs={{0,26},{1,27},{2,24},{3,25},{4,30},{5,31},{6,28},{7,29},{8,18},{9,... | collective-permute-start | bytes 393224 | tf_op jit(solution)/shard_map/ppermute | solution.py:233
  (20 other events, 252.5 us)

commit v7 on v6

--- a/solution.py
+++ b/solution.py
@@ -241,8 +241,12 @@
     return z, x, y, 1 - core
 
 
-def first_hop(z, x, y, core):
-    return (z, x ^ 1, y, 1 - core) if is_home(z, core) else (z ^ 1, x, y, core)
+def aside(z, x, y, core):
+    return (z, x ^ 1, y, 1 - core) if is_home(z, core) else None
+
+
+def homeward(z, x, y, core):
+    return None if is_home(z, core) else (z ^ 1, x, y, core)
 
 
 def second_hop(z, x, y, core):
@@ -289,8 +293,8 @@
     tokens = queries_ref.shape[0]
     group = HEADS // KV_HEADS
     copies = fetch_all(
-        [(queries_from, queries_ref), (residual_from, residual_ref)]
-        + [(kv_from[k], kv_ref.at[pl.ds(k * tokens, tokens)]) for k in range(8)],
+        [(kv_from[k], kv_ref.at[pl.ds(k * tokens, tokens)]) for k in range(8)]
+        + [(queries_from, queries_ref), (residual_from, residual_ref)],
         semaphores,
     )
     row = lax.broadcasted_iota(jnp.int32, (tokens, tokens), 0)
@@ -304,10 +308,10 @@
             bias_ref[:, span] = jnp.full(
                 (tokens, tokens), jnp.where(seen, 0.0, negative_fill), jnp.float32
             )
-    for copy in copies[2:] + copies[:1]:
+    for copy in copies[:9]:
         copy.wait()
     factor = math.log2(math.e) / math.sqrt(HD)
-    heads_each = 2
+    heads_each = 4
     for first in range(0, HEADS, heads_each):
         kv_head = first // group
         key_side = slice(kv_head * HD, (kv_head + 1) * HD)
@@ -328,7 +332,7 @@
             mixed_ref[:, (first + j) * HD : (first + j + 1) * HD] = result[
                 j * tokens : (j + 1) * tokens
             ].astype(jnp.bfloat16)
-    copies[1].wait()
+    copies[9].wait()
     summed = residual_ref[...].astype(jnp.float32) + mixed_ref[...].astype(jnp.float32)
     summed_ref[...] = summed
     keep = pltpu.make_async_copy(summed_ref, summed_to, semaphores.at[10])
@@ -343,11 +347,13 @@
     keep.wait()
 
 
-def load_pack(pack, strip, targets, semaphores):
+def strips(pack, strip, count):
+    return [pack.at[pl.ds(i * strip, strip)] for i in range(count)]
+
+
+def load(sources, targets, semaphores):
     return [
-        pltpu.make_async_copy(
-            pack.at[pl.ds(kind * strip, strip)], targets[kind], semaphores.at[kind]
-        )
+        pltpu.make_async_copy(sources[kind], targets[kind], semaphores.at[kind])
         for kind in range(3)
     ]
 
@@ -361,14 +367,16 @@
 
 def expert_kernel(row_count, where_ref, *refs):
     row_from, refs = refs[:row_count], refs[row_count:]
-    first_piece = len(refs) == 9
+    first_piece = len(refs) == 12
+    strip = refs[-4].shape[0]
     if first_piece:
-        packs, (total_ref,), rest = refs[:1], refs[1:2], refs[2:]
+        at_home_from = strips(refs[0], strip, 3)
+        away_from = refs[1:4]
+        (total_ref,), rest = refs[4:5], refs[5:]
     else:
-        packs, own_from, before_from = refs[:1], refs[1:4], refs[4]
+        away_from, at_home_from, before_from = strips(refs[0], strip, 3), refs[1:4], refs[4]
         (mine_ref, twins_ref), rest = refs[5:7], refs[7:]
     rows_ref, before_ref, gate_ref, up_ref, down_ref, row_semaphores, semaphores = rest
-    strip = packs[0].shape[0] // 3
     targets = (gate_ref, up_ref, down_ref)
     loads = []
     place = 0
@@ -378,22 +386,18 @@
     if not first_piece:
         loads.append((before_from, before_ref))
     row_copies = fetch_all(loads, row_semaphores)
-    weight_copies = load_pack(packs[0], strip, targets, semaphores)
-    if first_piece:
+    weight_copies = load(at_home_from, targets, semaphores)
+    at_home = where_ref[3] == 1
+
+    @pl.when(at_home)
+    def _():
         for copy in weight_copies:
             copy.start()
-    else:
-        at_home = where_ref[3] == 1
-
-        @pl.when(at_home)
-        def _():
-            for kind in range(3):
-                pltpu.make_async_copy(own_from[kind], targets[kind], semaphores.at[kind]).start()
-
-        @pl.when(jnp.logical_not(at_home))
-        def _():
-            for copy in weight_copies:
-                copy.start()
+
+    @pl.when(jnp.logical_not(at_home))
+    def _():
+        for copy in load(away_from, targets, semaphores):
+            copy.start()
 
     for copy in row_copies + weight_copies[:2]:
         copy.wait()
@@ -449,17 +453,14 @@
 ):
     ctx_here = lax.axis_index("ctx")
     exp_here = lax.axis_index("exp")
-    home = ((ctx_here // 2) % 2 == exp_here % 2).astype(jnp.int32)
-    where = jnp.stack([ctx_here % 2, ctx_here // 2, exp_here // 2, home]).astype(jnp.int32)
+    at_home = ((ctx_here // 2) % 2 == exp_here % 2).astype(jnp.int32)
+    where = jnp.stack([ctx_here % 2, ctx_here // 2, exp_here // 2, at_home]).astype(jnp.int32)
     tokens, width = residual.shape[1:]
     piece = gate_weight.shape[2]
     capacity = max(2, 2 * tokens * TOPK // 8)
     ids_row = expert_ids[0].reshape(1, tokens)
     kv_own = jnp.concatenate([key_states[0], value_states[0]], axis=1)
     weights = (gate_weight[0, 0], up_weight[0, 0], down_weight[0, 0])
-    own_first = jnp.concatenate([weights[0], weights[1]], axis=0)
-    own_second = weights[2]
-
     def along_z(steps):
         return move(
             kv_own, lambda z, x, y, core: (z + steps, x, y, core) if z + steps < 4 else None
@@ -471,13 +472,18 @@
 
         return move(block, rule)
 
-    one_first = move(own_first, first_hop)
+    beside = [move(w, aside) for w in weights[:2]]
     kv_along = [kv_own] + [along_z(steps) for steps in (1, 2, 3)]
+    own = jnp.concatenate(weights, axis=0)
+    own, where, beside[0], beside[1], *kv_along = lax.optimization_barrier(
+        (own, where, *beside, *kv_along)
+    )
+    home = move(own, homeward)
     kv_list = []
     for steps in range(4):
         kv_list += [kv_along[steps], over_x(kv_along[steps], steps)]
-    one_first, own_second, *kv_list = lax.optimization_barrier((one_first, own_second, *kv_list))
-    one_second = move(own_second, first_hop)
+    rest, *kv_list = lax.optimization_barrier((weights[2], *kv_list))
+    beside_rest = move(rest, aside)
     slot_shape = jax.ShapeDtypeStruct((capacity, width), jnp.bfloat16)
     keys_all = 8 * tokens
     rows_all = 8 * capacity
@@ -510,10 +516,9 @@
             return array
         return move(array, lambda z, x, y, core: (z ^ (k >> 1), x, y ^ (k & 1), core))
 
-    one_second, *outgoing = lax.optimization_barrier((one_second, *outgoing))
-    one = jnp.concatenate([one_first, one_second], axis=0)
-    last = move(one, second_hop)
+    last = move(home, second_hop)
     arrived = {0: outgoing[0]}
+    beside_rest, *outgoing = lax.optimization_barrier((beside_rest, *outgoing))
     for k in (4, 6, 5, 7, 2, 3, 1):
         arrived[k] = swap(outgoing[k], k)
     order = (0, 2, 3, 1, 4, 6, 5, 7)
@@ -548,7 +553,7 @@
             name="experts_rest" if before else "experts_first",
         )(where, *row_parts, *packs, *before)
 
-    first_total = run_expert([one], [])
+    first_total = run_expert([home, *beside, beside_rest], [])
     last, *first_total = lax.optimization_barrier((last, *first_total))
     mine, twins = run_expert([last, *weights], first_total)
     joined = pl.pallas_call(

time: 127 us -> 125 us (0.984)
  waiting for transfers between devices: 62.4 us -> 54.9 us
  starting transfers between devices: 43.1 us -> 46.7 us
  other arithmetic: 2.22 us -> 4.96 us
  local copies, waits for them, and re-layouts: 0.46 us -> 1.85 us
    ppermute x27 -> x29, waiting for transfers between devices: 62.4 us -> 54.9 us  [move(): return lax.ppermute(array, AXES, pairs)]
    ppermute x27 -> x29, starting transfers between devices: 43.1 us -> 46.7 us  [move(): return lax.ppermute(array, AXES, pairs)]
    concatenate x1, other arithmetic: 1.55 us -> 3.41 us  [shards_cube(): own = jnp.concatenate(weights, axis=0)]
    unnamed x57 -> x34, local copies, waits for them, and re-layouts: 0.27 us -> 1.72 us
  transfers between devices with their start and end apart: 27 -> 29, of which waited for: 19 -> 15; matrix products, arithmetic and copies ran while one was open for 1% -> 5% of each run, Pallas kernels for 9% -> 8%
where the time goes in v7:
time: 125 us
  waiting for transfers between devices  54.9 us (44%)
  starting transfers between devices  46.7 us (37%)
  Pallas kernels  15.9 us (13%)
  other arithmetic  4.96 us (4%)
  local copies, waits for them, and re-layouts  1.85 us (1%)
    ppermute x29, waiting for transfers between devices, move(): return lax.ppermute(array, AXES, pairs)  54.9 us
    ppermute x29, starting transfers between devices, move(): return lax.ppermute(array, AXES, pairs)  46.7 us
    pallas_call x1, Pallas kernels, shards_cube(): pl.pallas_call(attend_kernel, out_shape=[jax.ShapeDtypeStruct((tokens, wi...  7.55 us
    pallas_call x2, Pallas kernels, run_expert(): pl.pallas_call(partial(expert_kernel, len(row_parts)), out_shape=[mine, t...  6.12 us
    concatenate x1, other arithmetic, shards_cube(): own = jnp.concatenate(weights, axis=0)  3.41 us
  transfers between devices with their start and end apart: 29, of which 15 were waited for; matrix products, arithmetic and copies ran while one was open for 5% of the time, Pallas kernels for 8%

profile of v7, /device:TPU:8, one launch (start us, length us, event | category | flops | bytes accessed | tf_op | source)
XLA Modules:
  0.0 124.6 jit_solution(8954419014784557377)
XLA Ops:
  3.5 5.1 %collective-permute-start.2 = (bf16[128,512]{1,0:T(8,128)(2,1)S(1)}, bf16[128,512]{1,0:T(8,128)(2,1)S(1)}, u32[]{:S(2)}, u32[]{:S(2)}) collective-permute-start(bf16[128,512]{1,0:T(8,128)(2,1)S(1)} %pad_maximum_fusion.1.refs_0_), channel_id=1, source_target_pairs={{0,8},{1,9},{2,10},{3,11},{4,12},{5,13},{6,14},{7,15},{8,16},{9,17... | collective-permute-start | bytes 393224 | tf_op jit(solution)/shard_map/ppermute | solution.py:233
  10.6 3.4 %pad_maximum_fusion = bf16[576,2048]{1,0:T(8,128)(2,1)} fusion(bf16[192,2048]{1,0:T(8,128)(2,1)} %bitcast.14, bf16[192,2048]{1,0:T(8,128)(2,1)} %bitcast.18, bf16[192,2048]{1,0:T(8,128)(2,1)} %bitcast.21), kind=kLoop, calls=%fused_computation | loop fusion | flops 7077888 | bytes 4718592 | tf_op jit(solution)/shard_map/concatenate | solution.py:477
  14.7 4.0 %collective-permute-done.3.refs_4_ = bf16[128,512]{1,0:T(8,128)(2,1)S(1)} collective-permute-done((bf16[128,512]{1,0:T(8,128)(2,1)S(1)}, bf16[128,512]{1,0:T(8,128)(2,1)S(1)}, u32[]{:S(2)}, u32[]{:S(2)}) %collective-permute-start.3) | collective-permute-done | bytes 131104 | tf_op jit(solution)/shard_map/ppermute | solution.py:233
  18.7 3.2 %collective-permute-done.1.refs_6_ = bf16[192,2048]{1,0:T(8,128)(2,1)S(1)} collective-permute-done((bf16[192,2048]{1,0:T(8,128)(2,1)}, bf16[192,2048]{1,0:T(8,128)(2,1)S(1)}, u32[]{:S(2)}, u32[]{:S(2)}) %collective-permute-start.1) | collective-permute-done | bytes 786464 | tf_op jit(solution)/shard_map/ppermute | solution.py:233
  21.9 1.6 %collective-permute-start.19 = (bf16[576,2048]{1,0:T(8,128)(2,1)}, bf16[576,2048]{1,0:T(8,128)(2,1)S(1)}, u32[]{:S(2)}, u32[]{:S(2)}) collective-permute-start(bf16[576,2048]{1,0:T(8,128)(2,1)} %pad_maximum_fusion), channel_id=1, source_target_pairs={{1,9},{3,11},{5,13},{7,15},{8,0},{10,2},{12,4},{14,6},{17,25},{19,... | collective-permute-start | bytes 7077896 | tf_op jit(solution)/shard_map/ppermute | solution.py:233
  23.6 3.2 %collective-permute-start.5 = (bf16[128,512]{1,0:T(8,128)(2,1)S(1)}, bf16[128,512]{1,0:T(8,128)(2,1)S(1)}, u32[]{:S(2)}, u32[]{:S(2)}) collective-permute-start(bf16[128,512]{1,0:T(8,128)(2,1)S(1)} %pad_maximum_fusion.1.refs_0_), channel_id=1, source_target_pairs={{0,4},{1,5},{2,6},{3,7},{8,12},{9,13},{10,14},{11,15},{16,20},{17,... | collective-permute-start | bytes 393224 | tf_op jit(solution)/shard_map/ppermute | solution.py:233
  26.8 1.9 %collective-permute-start.6 = (bf16[128,512]{1,0:T(8,128)(2,1)S(1)}, bf16[128,512]{1,0:T(8,128)(2,1)S(1)}, u32[]{:S(2)}, u32[]{:S(2)}) collective-permute-start(bf16[128,512]{1,0:T(8,128)(2,1)S(1)} %collective-permute-done.2.refs_2_), channel_id=1, source_target_pairs={{8,12},{9,13},{10,14},{11,15},{12,8},{13,9},{14,10},{15,11},{16,20... | collective-permute-start | bytes 393224 | tf_op jit(solution)/shard_map/ppermute | solution.py:233
  30.7 2.9 %collective-permute-done.6.refs_3_ = bf16[128,512]{1,0:T(8,128)(2,1)S(1)} collective-permute-done((bf16[128,512]{1,0:T(8,128)(2,1)S(1)}, bf16[128,512]{1,0:T(8,128)(2,1)S(1)}, u32[]{:S(2)}, u32[]{:S(2)}) %collective-permute-start.6) | collective-permute-done | bytes 131104 | tf_op jit(solution)/shard_map/ppermute | solution.py:233
  35.7 7.6 %attend.1 = (f32[128,2048]{1,0:T(8,128)}, bf16[32,2048]{1,0:T(8,128)(2,1)}, bf16[32,2048]{1,0:T(8,128)(2,1)}, bf16[32,2048]{1,0:T(8,128)(2,1)}, bf16[32,2048]{1,...) custom-call(s32[4]{0:T(128)} %pad_add_fusion.where_ref, ...), custom_call_target="tpu_custom_call" | custom-call | flops 1073741824 | bytes 2097152 | tf_op jit(solution)/shard_map/attend/pallas_call | solution.py:490
  43.3 4.4 %collective-permute-done.9.refs_7_ = bf16[192,2048]{1,0:T(8,128)(2,1)S(1)} collective-permute-done((bf16[192,2048]{1,0:T(8,128)(2,1)S(1)}, bf16[192,2048]{1,0:T(8,128)(2,1)S(1)}, u32[]{:S(2)}, u32[]{:S(2)}) %collective-permute-start.9) | collective-permute-done | bytes 786464 | tf_op jit(solution)/shard_map/ppermute | solution.py:233
  47.7 7.8 %collective-permute-start.13 = (bf16[32,2048]{1,0:T(8,128)(2,1)}, bf16[32,2048]{1,0:T(8,128)(2,1)S(1)}, u32[]{:S(2)}, u32[]{:S(2)}) collective-permute-start(bf16[32,2048]{1,0:T(8,128)(2,1)} %get-tuple-element.77), channel_id=1, source_target_pairs={{0,16},{1,17},{2,18},{3,19},{4,20},{5,21},{6,22},{7,23},{8,24},{9,... | collective-permute-start | bytes 393224 | tf_op jit(solution)/shard_map/ppermute | solution.py:233
  57.8 2.3 %collective-permute-start.15 = (bf16[32,2048]{1,0:T(8,128)(2,1)}, bf16[32,2048]{1,0:T(8,128)(2,1)S(1)}, u32[]{:S(2)}, u32[]{:S(2)}) collective-permute-start(bf16[32,2048]{1,0:T(8,128)(2,1)} %get-tuple-element.79), channel_id=1, source_target_pairs={{0,18},{1,19},{2,16},{3,17},{4,22},{5,23},{6,20},{7,21},{8,26},{9,... | collective-permute-start | bytes 393224 | tf_op jit(solution)/shard_map/ppermute | solution.py:233
  60.1 1.5 %collective-permute-start.16 = (bf16[32,2048]{1,0:T(8,128)(2,1)}, bf16[32,2048]{1,0:T(8,128)(2,1)S(1)}, u32[]{:S(2)}, u32[]{:S(2)}) collective-permute-start(bf16[32,2048]{1,0:T(8,128)(2,1)} %get-tuple-element.80), channel_id=1, source_target_pairs={{0,26},{1,27},{2,24},{3,25},{4,30},{5,31},{6,28},{7,29},{8,18},{9,... | collective-permute-start | bytes 393224 | tf_op jit(solution)/shard_map/ppermute | solution.py:233
  61.6 1.5 %collective-permute-start.10 = (bf16[32,2048]{1,0:T(8,128)(2,1)}, bf16[32,2048]{1,0:T(8,128)(2,1)S(1)}, u32[]{:S(2)}, u32[]{:S(2)}) collective-permute-start(bf16[32,2048]{1,0:T(8,128)(2,1)} %get-tuple-element.74), channel_id=1, source_target_pairs={{0,8},{1,9},{2,10},{3,11},{4,12},{5,13},{6,14},{7,15},{8,0},{9,1},... | collective-permute-start | bytes 393224 | tf_op jit(solution)/shard_map/ppermute | solution.py:233
  63.2 7.8 %collective-permute-done.14 = bf16[32,2048]{1,0:T(8,128)(2,1)S(1)} collective-permute-done((bf16[32,2048]{1,0:T(8,128)(2,1)}, bf16[32,2048]{1,0:T(8,128)(2,1)S(1)}, u32[]{:S(2)}, u32[]{:S(2)}) %collective-permute-start.14) | collective-permute-done | bytes 131104 | tf_op jit(solution)/shard_map/ppermute | solution.py:233
  71.0 2.0 %collective-permute-done.15 = bf16[32,2048]{1,0:T(8,128)(2,1)S(1)} collective-permute-done((bf16[32,2048]{1,0:T(8,128)(2,1)}, bf16[32,2048]{1,0:T(8,128)(2,1)S(1)}, u32[]{:S(2)}, u32[]{:S(2)}) %collective-permute-start.15) | collective-permute-done | bytes 131104 | tf_op jit(solution)/shard_map/ppermute | solution.py:233
  73.0 1.5 %collective-permute-start.12 = (bf16[32,2048]{1,0:T(8,128)(2,1)}, bf16[32,2048]{1,0:T(8,128)(2,1)S(1)}, u32[]{:S(2)}, u32[]{:S(2)}) collective-permute-start(bf16[32,2048]{1,0:T(8,128)(2,1)} %get-tuple-element.76), channel_id=1, source_target_pairs={{0,2},{1,3},{2,0},{3,1},{4,6},{5,7},{6,4},{7,5},{8,10},{9,11},{10,... | collective-permute-start | bytes 393224 | tf_op jit(solution)/shard_map/ppermute | solution.py:233
  74.6 5.8 %collective-permute-done.16 = bf16[32,2048]{1,0:T(8,128)(2,1)S(1)} collective-permute-done((bf16[32,2048]{1,0:T(8,128)(2,1)}, bf16[32,2048]{1,0:T(8,128)(2,1)S(1)}, u32[]{:S(2)}, u32[]{:S(2)}) %collective-permute-start.16) | collective-permute-done | bytes 131104 | tf_op jit(solution)/shard_map/ppermute | solution.py:233
  80.6 2.6 %collective-permute-done.12 = bf16[32,2048]{1,0:T(8,128)(2,1)S(1)} collective-permute-done((bf16[32,2048]{1,0:T(8,128)(2,1)}, bf16[32,2048]{1,0:T(8,128)(2,1)S(1)}, u32[]{:S(2)}, u32[]{:S(2)}) %collective-permute-start.12) | collective-permute-done | bytes 131104 | tf_op jit(solution)/shard_map/ppermute | solution.py:233
  83.3 1.8 %collective-permute-done.17.refs_2_ = bf16[128,2048]{1,0:T(8,128)(2,1)S(1)} collective-permute-done((bf16[128,2048]{1,0:T(8,128)(2,1)S(1)}, bf16[128,2048]{1,0:T(8,128)(2,1)S(1)}, u32[]{:S(2)}, u32[]{:S(2)}) %collective-permute-start.17) | collective-permute-done | bytes 524320 | tf_op jit(solution)/shard_map/ppermute | solution.py:233
  85.2 2.9 %experts_first.1.refs_8_ = f32[512,2048]{1,0:T(8,128)S(1)} custom-call(s32[4]{0:T(128)S(1)} %copy-done.4, bf16[128,2048]{1,0:T(8,128)(2,1)S(1)} %constant_dynamic-update-slice_fusion.refs_0_, bf16[128,2048]{1,0:T(8,128)(2,1)S(1)} %constant_dynamic-update-slice_fusion.4.refs_1_, bf16[128,2048]{1,0:T(8,128)(2,1)S(1)} %collective-permute-done.17.refs_2_, ...), custom_call_target="tpu_custom_call" | custom-call | flops 1207959552 | bytes 2359296 | tf_op jit(solution)/shard_map/experts_first/pallas_call | solution.py:533
  88.1 3.2 %experts_rest.1 = (f32[256,2048]{1,0:T(8,128)S(1)}, bf16[256,2048]{1,0:T(8,128)(2,1)S(1)}) custom-call(s32[4]{0:T(128)S(1)} %copy-done.4, bf16[128,2048]{1,0:T(8,128)(2,1)S(1)} %constant_dynamic-update-slice_fusion.refs_0_, bf16[128,2048]{1,0:T(8,128)(2,1)S(1)} %constant_dynamic-update-slice_fusion.4.refs_1_, ...), custom_call_target="tpu_custom_call" | custom-call | flops 1207959552 | bytes 2359296 | tf_op jit(solution)/shard_map/experts_rest/pallas_call | solution.py:533
  91.6 2.5 %collective-permute-done.21.other_from = bf16[256,2048]{1,0:T(8,128)(2,1)S(1)} collective-permute-done((bf16[256,2048]{1,0:T(8,128)(2,1)S(1)}, bf16[256,2048]{1,0:T(8,128)(2,1)S(1)}, u32[]{:S(2)}, u32[]{:S(2)}) %collective-permute-start.21) | collective-permute-done | bytes 1048608 | tf_op jit(solution)/shard_map/ppermute | solution.py:233
  95.1 3.0 %collective-permute-start.24 = (bf16[32,2048]{1,0:T(8,128)(2,1)S(1)}, bf16[32,2048]{1,0:T(8,128)(2,1)S(1)}, u32[]{:S(2)}, u32[]{:S(2)}) collective-permute-start(bf16[32,2048]{1,0:T(8,128)(2,1)S(1)} %get-tuple-element.92), channel_id=1, source_target_pairs={{0,10},{1,11},{2,8},{3,9},{4,14},{5,15},{6,12},{7,13},{8,2},{9,3},... | collective-permute-start | bytes 393224 | tf_op jit(solution)/shard_map/ppermute | solution.py:233
  99.1 1.8 %collective-permute-start.26 = (bf16[32,2048]{1,0:T(8,128)(2,1)S(1)}, bf16[32,2048]{1,0:T(8,128)(2,1)S(1)}, u32[]{:S(2)}, u32[]{:S(2)}) collective-permute-start(bf16[32,2048]{1,0:T(8,128)(2,1)S(1)} %get-tuple-element.94), channel_id=1, source_target_pairs={{0,18},{1,19},{2,16},{3,17},{4,22},{5,23},{6,20},{7,21},{8,26},{9,... | collective-permute-start | bytes 393224 | tf_op jit(solution)/shard_map/ppermute | solution.py:233
  101.0 1.8 %collective-permute-start.27 = (bf16[32,2048]{1,0:T(8,128)(2,1)S(1)}, bf16[32,2048]{1,0:T(8,128)(2,1)S(1)}, u32[]{:S(2)}, u32[]{:S(2)}) collective-permute-start(bf16[32,2048]{1,0:T(8,128)(2,1)S(1)} %get-tuple-element.95), channel_id=1, source_target_pairs={{0,24},{1,25},{2,26},{3,27},{4,28},{5,29},{6,30},{7,31},{8,16},{9,... | collective-permute-start | bytes 393224 | tf_op jit(solution)/shard_map/ppermute | solution.py:233
  102.8 2.3 %collective-permute-start.28 = (bf16[32,2048]{1,0:T(8,128)(2,1)S(1)}, bf16[32,2048]{1,0:T(8,128)(2,1)S(1)}, u32[]{:S(2)}, u32[]{:S(2)}) collective-permute-start(bf16[32,2048]{1,0:T(8,128)(2,1)S(1)} %get-tuple-element.96), channel_id=1, source_target_pairs={{0,26},{1,27},{2,24},{3,25},{4,30},{5,31},{6,28},{7,29},{8,18},{9,... | collective-permute-start | bytes 393224 | tf_op jit(solution)/shard_map/ppermute | solution.py:233
  105.5 8.8 %collective-permute-done.25.refs_4_ = bf16[32,2048]{1,0:T(8,128)(2,1)S(1)} collective-permute-done((bf16[32,2048]{1,0:T(8,128)(2,1)S(1)}, bf16[32,2048]{1,0:T(8,128)(2,1)S(1)}, u32[]{:S(2)}, u32[]{:S(2)}) %collective-permute-start.25) | collective-permute-done | bytes 131104 | tf_op jit(solution)/shard_map/ppermute | solution.py:233
  114.3 2.8 %collective-permute-done.26.refs_5_ = bf16[32,2048]{1,0:T(8,128)(2,1)S(1)} collective-permute-done((bf16[32,2048]{1,0:T(8,128)(2,1)S(1)}, bf16[32,2048]{1,0:T(8,128)(2,1)S(1)}, u32[]{:S(2)}, u32[]{:S(2)}) %collective-permute-start.26) | collective-permute-done | bytes 131104 | tf_op jit(solution)/shard_map/ppermute | solution.py:233
  117.1 3.6 %collective-permute-done.27.refs_6_ = bf16[32,2048]{1,0:T(8,128)(2,1)S(1)} collective-permute-done((bf16[32,2048]{1,0:T(8,128)(2,1)S(1)}, bf16[32,2048]{1,0:T(8,128)(2,1)S(1)}, u32[]{:S(2)}, u32[]{:S(2)}) %collective-permute-start.27) | collective-permute-done | bytes 131104 | tf_op jit(solution)/shard_map/ppermute | solution.py:233
  120.7 2.0 %collective-permute-done.28.refs_7_ = bf16[32,2048]{1,0:T(8,128)(2,1)S(1)} collective-permute-done((bf16[32,2048]{1,0:T(8,128)(2,1)S(1)}, bf16[32,2048]{1,0:T(8,128)(2,1)S(1)}, u32[]{:S(2)}, u32[]{:S(2)}) %collective-permute-start.28) | collective-permute-done | bytes 131104 | tf_op jit(solution)/shard_map/ppermute | solution.py:233
  122.8 1.8 %combine.1 = bf16[128,2048]{1,0:T(8,128)(2,1)} custom-call(s32[4]{0:T(128)S(1)} %copy-done.4, s32[1,128]{1,0:T(1,128)S(1)} %bitcast.24, f32[128,1]{1,0:T(8,128)S(1)} %copy.10.route_ref, f32[128,2048]{1,0:T(8,128)S(1)} %copy-done.3, bf16[32,2048]{1,0:T(8,128)(2,1)S(1)} %get-tuple-element.89.refs_0_, bf16[32,2048]{1,0:T(8,128)(2,1)S(1)} %collective-permute-done.22.refs_1_, ...), custom_call_target="tpu_custom_call" | custom-call | flops 134217728 | bytes 3145728 | tf_op jit(solution)/shard_map/combine/pallas_call | solution.py:577
  (71 shorter events, 15.4 us)
Async XLA Ops:
  0.0 18.7 %collective-permute-start = (bf16[192,2048]{1,0:T(8,128)(2,1)}, bf16[192,2048]{1,0:T(8,128)(2,1)S(1)}, u32[]{:S(2)}, u32[]{:S(2)}) collective-permute-start(bf16[192,2048]{1,0:T(8,128)(2,1)} %bitcast.20), channel_id=1, source_target_pairs={{0,5},{2,7},{4,1},{6,3},{9,12},{11,14},{13,8},{15,10},{16,21},{18,... | collective-permute-start | bytes 2359304 | tf_op jit(solution)/shard_map/ppermute | solution.py:233
  1.3 20.6 %collective-permute-start.1 = (bf16[192,2048]{1,0:T(8,128)(2,1)}, bf16[192,2048]{1,0:T(8,128)(2,1)S(1)}, u32[]{:S(2)}, u32[]{:S(2)}) collective-permute-start(bf16[192,2048]{1,0:T(8,128)(2,1)} %bitcast.17), channel_id=1, source_target_pairs={{0,5},{2,7},{4,1},{6,3},{9,12},{11,14},{13,8},{15,10},{16,21},{18,... | collective-permute-start | bytes 2359304 | tf_op jit(solution)/shard_map/ppermute | solution.py:233
  3.5 11.2 %collective-permute-start.2 = (bf16[128,512]{1,0:T(8,128)(2,1)S(1)}, bf16[128,512]{1,0:T(8,128)(2,1)S(1)}, u32[]{:S(2)}, u32[]{:S(2)}) collective-permute-start(bf16[128,512]{1,0:T(8,128)(2,1)S(1)} %pad_maximum_fusion.1.refs_0_), channel_id=1, source_target_pairs={{0,8},{1,9},{2,10},{3,11},{4,12},{5,13},{6,14},{7,15},{8,16},{9,17... | collective-permute-start | bytes 393224 | tf_op jit(solution)/shard_map/ppermute | solution.py:233
  8.6 10.1 %collective-permute-start.3 = (bf16[128,512]{1,0:T(8,128)(2,1)S(1)}, bf16[128,512]{1,0:T(8,128)(2,1)S(1)}, u32[]{:S(2)}, u32[]{:S(2)}) collective-permute-start(bf16[128,512]{1,0:T(8,128)(2,1)S(1)} %pad_maximum_fusion.1.refs_0_), channel_id=1, source_target_pairs={{0,16},{1,17},{2,18},{3,19},{4,20},{5,21},{6,22},{7,23},{8,24},{9,... | collective-permute-start | bytes 393224 | tf_op jit(solution)/shard_map/ppermute | solution.py:233
  9.9 8.8 %collective-permute-start.4 = (bf16[128,512]{1,0:T(8,128)(2,1)S(1)}, bf16[128,512]{1,0:T(8,128)(2,1)S(1)}, u32[]{:S(2)}, u32[]{:S(2)}) collective-permute-start(bf16[128,512]{1,0:T(8,128)(2,1)S(1)} %pad_maximum_fusion.1.refs_0_), channel_id=1, source_target_pairs={{0,24},{1,25},{2,26},{3,27},{4,28},{5,29},{6,30},{7,31}} | collective-permute-start | bytes 393224 | tf_op jit(solution)/shard_map/ppermute | solution.py:233
  21.9 33.6 %collective-permute-start.19 = (bf16[576,2048]{1,0:T(8,128)(2,1)}, bf16[576,2048]{1,0:T(8,128)(2,1)S(1)}, u32[]{:S(2)}, u32[]{:S(2)}) collective-permute-start(bf16[576,2048]{1,0:T(8,128)(2,1)} %pad_maximum_fusion), channel_id=1, source_target_pairs={{1,9},{3,11},{5,13},{7,15},{8,0},{10,2},{12,4},{14,6},{17,25},{19,... | collective-permute-start | bytes 7077896 | tf_op jit(solution)/shard_map/ppermute | solution.py:233
  23.6 7.1 %collective-permute-start.5 = (bf16[128,512]{1,0:T(8,128)(2,1)S(1)}, bf16[128,512]{1,0:T(8,128)(2,1)S(1)}, u32[]{:S(2)}, u32[]{:S(2)}) collective-permute-start(bf16[128,512]{1,0:T(8,128)(2,1)S(1)} %pad_maximum_fusion.1.refs_0_), channel_id=1, source_target_pairs={{0,4},{1,5},{2,6},{3,7},{8,12},{9,13},{10,14},{11,15},{16,20},{17,... | collective-permute-start | bytes 393224 | tf_op jit(solution)/shard_map/ppermute | solution.py:233
  26.8 6.9 %collective-permute-start.6 = (bf16[128,512]{1,0:T(8,128)(2,1)S(1)}, bf16[128,512]{1,0:T(8,128)(2,1)S(1)}, u32[]{:S(2)}, u32[]{:S(2)}) collective-permute-start(bf16[128,512]{1,0:T(8,128)(2,1)S(1)} %collective-permute-done.2.refs_2_), channel_id=1, source_target_pairs={{8,12},{9,13},{10,14},{11,15},{12,8},{13,9},{14,10},{15,11},{16,20... | collective-permute-start | bytes 393224 | tf_op jit(solution)/shard_map/ppermute | solution.py:233
  28.7 4.9 %collective-permute-start.7 = (bf16[128,512]{1,0:T(8,128)(2,1)S(1)}, bf16[128,512]{1,0:T(8,128)(2,1)S(1)}, u32[]{:S(2)}, u32[]{:S(2)}) collective-permute-start(bf16[128,512]{1,0:T(8,128)(2,1)S(1)} %collective-permute-done.3.refs_4_), channel_id=1, source_target_pairs={{16,20},{17,21},{18,22},{19,23},{20,16},{21,17},{22,18},{23,19},{2... | collective-permute-start | bytes 393224 | tf_op jit(solution)/shard_map/ppermute | solution.py:233
  29.4 5.0 %collective-permute-start.8 = (bf16[128,512]{1,0:T(8,128)(2,1)S(1)}, bf16[128,512]{1,0:T(8,128)(2,1)}, u32[]{:S(2)}, u32[]{:S(2)}) collective-permute-start(bf16[128,512]{1,0:T(8,128)(2,1)S(1)} %collective-permute-done.4.refs_6_), channel_id=1, source_target_pairs={{24,28},{25,29},{26,30},{27,31},{28,24},{29,25},{30,26},{31,27}} | collective-permute-start | bytes 393224 | tf_op jit(solution)/shard_map/ppermute | solution.py:233
  34.4 13.3 %collective-permute-start.9 = (bf16[192,2048]{1,0:T(8,128)(2,1)S(1)}, bf16[192,2048]{1,0:T(8,128)(2,1)S(1)}, u32[]{:S(2)}, u32[]{:S(2)}) collective-permute-start(bf16[192,2048]{1,0:T(8,128)(2,1)S(1)} %bitcast.15), channel_id=1, source_target_pairs={{0,5},{2,7},{4,1},{6,3},{9,12},{11,14},{13,8},{15,10},{16,21},{18,... | collective-permute-start | bytes 2359304 | tf_op jit(solution)/shard_map/ppermute | solution.py:233
  35.7 49.5 %copy-start.4 = (s32[4]{0:T(128)S(1)}, s32[4]{0:T(128)}, u32[]{:S(2)}) copy-start(s32[4]{0:T(128)} %pad_add_fusion.where_ref) | copy-start | bytes 52
  47.7 13.9 %collective-permute-start.13 = (bf16[32,2048]{1,0:T(8,128)(2,1)}, bf16[32,2048]{1,0:T(8,128)(2,1)S(1)}, u32[]{:S(2)}, u32[]{:S(2)}) collective-permute-start(bf16[32,2048]{1,0:T(8,128)(2,1)} %get-tuple-element.77), channel_id=1, source_target_pairs={{0,16},{1,17},{2,18},{3,19},{4,20},{5,21},{6,22},{7,23},{8,24},{9,... | collective-permute-start | bytes 393224 | tf_op jit(solution)/shard_map/ppermute | solution.py:233
  55.5 32.6 %collective-permute-start.20 = (bf16[576,2048]{1,0:T(8,128)(2,1)S(1)}, bf16[576,2048]{1,0:T(8,128)(2,1)S(1)}, u32[]{:S(2)}, u32[]{:S(2)}) collective-permute-start(bf16[576,2048]{1,0:T(8,128)(2,1)S(1)} %collective-permute-done.19.refs_4_), channel_id=1, source_target_pairs={{0,5},{2,7},{4,1},{6,3},{9,12},{11,14},{13,8},{15,10},{16,21},{18,... | collective-permute-start | bytes 7077896 | tf_op jit(solution)/shard_map/ppermute | solution.py:233
  57.7 13.3 %collective-permute-start.14 = (bf16[32,2048]{1,0:T(8,128)(2,1)}, bf16[32,2048]{1,0:T(8,128)(2,1)S(1)}, u32[]{:S(2)}, u32[]{:S(2)}) collective-permute-start(bf16[32,2048]{1,0:T(8,128)(2,1)} %get-tuple-element.78), channel_id=1, source_target_pairs={{0,24},{1,25},{2,26},{3,27},{4,28},{5,29},{6,30},{7,31},{8,16},{9,... | collective-permute-start | bytes 393224 | tf_op jit(solution)/shard_map/ppermute | solution.py:233
  57.8 15.2 %collective-permute-start.15 = (bf16[32,2048]{1,0:T(8,128)(2,1)}, bf16[32,2048]{1,0:T(8,128)(2,1)S(1)}, u32[]{:S(2)}, u32[]{:S(2)}) collective-permute-start(bf16[32,2048]{1,0:T(8,128)(2,1)} %get-tuple-element.79), channel_id=1, source_target_pairs={{0,18},{1,19},{2,16},{3,17},{4,22},{5,23},{6,20},{7,21},{8,26},{9,... | collective-permute-start | bytes 393224 | tf_op jit(solution)/shard_map/ppermute | solution.py:233
  60.1 20.3 %collective-permute-start.16 = (bf16[32,2048]{1,0:T(8,128)(2,1)}, bf16[32,2048]{1,0:T(8,128)(2,1)S(1)}, u32[]{:S(2)}, u32[]{:S(2)}) collective-permute-start(bf16[32,2048]{1,0:T(8,128)(2,1)} %get-tuple-element.80), channel_id=1, source_target_pairs={{0,26},{1,27},{2,24},{3,25},{4,30},{5,31},{6,28},{7,29},{8,18},{9,... | collective-permute-start | bytes 393224 | tf_op jit(solution)/shard_map/ppermute | solution.py:233
  61.6 18.9 %collective-permute-start.10 = (bf16[32,2048]{1,0:T(8,128)(2,1)}, bf16[32,2048]{1,0:T(8,128)(2,1)S(1)}, u32[]{:S(2)}, u32[]{:S(2)}) collective-permute-start(bf16[32,2048]{1,0:T(8,128)(2,1)} %get-tuple-element.74), channel_id=1, source_target_pairs={{0,8},{1,9},{2,10},{3,11},{4,12},{5,13},{6,14},{7,15},{8,0},{9,1},... | collective-permute-start | bytes 393224 | tf_op jit(solution)/shard_map/ppermute | solution.py:233
  71.0 9.6 %collective-permute-start.11 = (bf16[32,2048]{1,0:T(8,128)(2,1)}, bf16[32,2048]{1,0:T(8,128)(2,1)S(1)}, u32[]{:S(2)}, u32[]{:S(2)}) collective-permute-start(bf16[32,2048]{1,0:T(8,128)(2,1)} %get-tuple-element.75), channel_id=1, source_target_pairs={{0,10},{1,11},{2,8},{3,9},{4,14},{5,15},{6,12},{7,13},{8,2},{9,3},... | collective-permute-start | bytes 393224 | tf_op jit(solution)/shard_map/ppermute | solution.py:233
  73.0 10.1 %collective-permute-start.12 = (bf16[32,2048]{1,0:T(8,128)(2,1)}, bf16[32,2048]{1,0:T(8,128)(2,1)S(1)}, u32[]{:S(2)}, u32[]{:S(2)}) collective-permute-start(bf16[32,2048]{1,0:T(8,128)(2,1)} %get-tuple-element.76), channel_id=1, source_target_pairs={{0,2},{1,3},{2,0},{3,1},{4,6},{5,7},{6,4},{7,5},{8,10},{9,11},{10,... | collective-permute-start | bytes 393224 | tf_op jit(solution)/shard_map/ppermute | solution.py:233
  80.4 2.9 %collective-permute-start.18 = (bf16[128,2048]{1,0:T(8,128)(2,1)S(1)}, bf16[128,2048]{1,0:T(8,128)(2,1)S(1)}, u32[]{:S(2)}, u32[]{:S(2)}) collective-permute-start(bf16[128,2048]{1,0:T(8,128)(2,1)S(1)} %constant_dynamic-update-slice_fusion.4.refs_1_), channel_id=1, source_target_pairs={{0,1},{1,0},{2,3},{3,2},{4,5},{5,4},{6,7},{7,6},{8,9},{9,8},{10,11... | collective-permute-start | bytes 1572872 | tf_op jit(solution)/shard_map/ppermute | solution.py:233
  83.2 2.0 %collective-permute-start.17 = (bf16[128,2048]{1,0:T(8,128)(2,1)S(1)}, bf16[128,2048]{1,0:T(8,128)(2,1)S(1)}, u32[]{:S(2)}, u32[]{:S(2)}) collective-permute-start(bf16[128,2048]{1,0:T(8,128)(2,1)S(1)} %constant_dynamic-update-slice_fusion.refs_0_), channel_id=1, source_target_pairs={{0,1},{1,0},{2,3},{3,2},{4,5},{5,4},{6,7},{7,6},{8,9},{9,8},{10,11... | collective-permute-start | bytes 1572872 | tf_op jit(solution)/shard_map/ppermute | solution.py:233
  91.4 31.4 %copy-start.3 = (f32[128,2048]{1,0:T(8,128)S(1)}, f32[128,2048]{1,0:T(8,128)}, u32[]{:S(2)}) copy-start(f32[128,2048]{1,0:T(8,128)} %get-tuple-element.64.summed_ref) | copy-start | bytes 3145732
  91.4 31.4 %copy-start.5 = (s32[1,128,1]{1,2,0:T(1,128)S(1)}, s32[1,128,1]{1,2,0:T(1,128)}, u32[]{:S(2)}) copy-start(s32[1,128,1]{1,2,0:T(1,128)} %param.13) | copy-start | bytes 1540
  91.4 2.7 %collective-permute-start.21 = (bf16[256,2048]{1,0:T(8,128)(2,1)S(1)}, bf16[256,2048]{1,0:T(8,128)(2,1)S(1)}, u32[]{:S(2)}, u32[]{:S(2)}) collective-permute-start(bf16[256,2048]{1,0:T(8,128)(2,1)S(1)} %get-tuple-element.88), channel_id=1, source_target_pairs={{0,1},{1,0},{2,3},{3,2},{4,5},{5,4},{6,7},{7,6},{8,9},{9,8},{10,11... | collective-permute-start | bytes 3145736 | tf_op jit(solution)/shard_map/ppermute | solution.py:233
  94.5 6.4 %collective-permute-start.22 = (bf16[32,2048]{1,0:T(8,128)(2,1)S(1)}, bf16[32,2048]{1,0:T(8,128)(2,1)S(1)}, u32[]{:S(2)}, u32[]{:S(2)}) collective-permute-start(bf16[32,2048]{1,0:T(8,128)(2,1)S(1)} %get-tuple-element.90), channel_id=1, source_target_pairs={{0,2},{1,3},{2,0},{3,1},{4,6},{5,7},{6,4},{7,5},{8,10},{9,11},{10,... | collective-permute-start | bytes 393224 | tf_op jit(solution)/shard_map/ppermute | solution.py:233
  95.1 7.7 %collective-permute-start.23 = (bf16[32,2048]{1,0:T(8,128)(2,1)S(1)}, bf16[32,2048]{1,0:T(8,128)(2,1)S(1)}, u32[]{:S(2)}, u32[]{:S(2)}) collective-permute-start(bf16[32,2048]{1,0:T(8,128)(2,1)S(1)} %get-tuple-element.91), channel_id=1, source_target_pairs={{0,8},{1,9},{2,10},{3,11},{4,12},{5,13},{6,14},{7,15},{8,0},{9,1},... | collective-permute-start | bytes 393224 | tf_op jit(solution)/shard_map/ppermute | solution.py:233
  95.1 10.4 %collective-permute-start.24 = (bf16[32,2048]{1,0:T(8,128)(2,1)S(1)}, bf16[32,2048]{1,0:T(8,128)(2,1)S(1)}, u32[]{:S(2)}, u32[]{:S(2)}) collective-permute-start(bf16[32,2048]{1,0:T(8,128)(2,1)S(1)} %get-tuple-element.92), channel_id=1, source_target_pairs={{0,10},{1,11},{2,8},{3,9},{4,14},{5,15},{6,12},{7,13},{8,2},{9,3},... | collective-permute-start | bytes 393224 | tf_op jit(solution)/shard_map/ppermute | solution.py:233
  98.1 16.2 %collective-permute-start.25 = (bf16[32,2048]{1,0:T(8,128)(2,1)S(1)}, bf16[32,2048]{1,0:T(8,128)(2,1)S(1)}, u32[]{:S(2)}, u32[]{:S(2)}) collective-permute-start(bf16[32,2048]{1,0:T(8,128)(2,1)S(1)} %get-tuple-element.93), channel_id=1, source_target_pairs={{0,16},{1,17},{2,18},{3,19},{4,20},{5,21},{6,22},{7,23},{8,24},{9,... | collective-permute-start | bytes 393224 | tf_op jit(solution)/shard_map/ppermute | solution.py:233
  99.1 18.0 %collective-permute-start.26 = (bf16[32,2048]{1,0:T(8,128)(2,1)S(1)}, bf16[32,2048]{1,0:T(8,128)(2,1)S(1)}, u32[]{:S(2)}, u32[]{:S(2)}) collective-permute-start(bf16[32,2048]{1,0:T(8,128)(2,1)S(1)} %get-tuple-element.94), channel_id=1, source_target_pairs={{0,18},{1,19},{2,16},{3,17},{4,22},{5,23},{6,20},{7,21},{8,26},{9,... | collective-permute-start | bytes 393224 | tf_op jit(solution)/shard_map/ppermute | solution.py:233
  101.0 19.8 %collective-permute-start.27 = (bf16[32,2048]{1,0:T(8,128)(2,1)S(1)}, bf16[32,2048]{1,0:T(8,128)(2,1)S(1)}, u32[]{:S(2)}, u32[]{:S(2)}) collective-permute-start(bf16[32,2048]{1,0:T(8,128)(2,1)S(1)} %get-tuple-element.95), channel_id=1, source_target_pairs={{0,24},{1,25},{2,26},{3,27},{4,28},{5,29},{6,30},{7,31},{8,16},{9,... | collective-permute-start | bytes 393224 | tf_op jit(solution)/shard_map/ppermute | solution.py:233
  102.8 20.0 %collective-permute-start.28 = (bf16[32,2048]{1,0:T(8,128)(2,1)S(1)}, bf16[32,2048]{1,0:T(8,128)(2,1)S(1)}, u32[]{:S(2)}, u32[]{:S(2)}) collective-permute-start(bf16[32,2048]{1,0:T(8,128)(2,1)S(1)} %get-tuple-element.96), channel_id=1, source_target_pairs={{0,26},{1,27},{2,24},{3,25},{4,30},{5,31},{6,28},{7,29},{8,18},{9,... | collective-permute-start | bytes 393224 | tf_op jit(solution)/shard_map/ppermute | solution.py:233
  (11 other events, 128.1 us)

commit v8 on v7

--- a/solution.py
+++ b/solution.py
@@ -288,12 +288,12 @@
 
 
 def attend_kernel(where_ref, ids_ref, queries_from, residual_from, *refs):
-    kv_from, summed_to, out_refs = refs[:8], refs[8], refs[9:17]
-    queries_ref, residual_ref, kv_ref, bias_ref, mixed_ref, summed_ref, semaphores = refs[17:]
+    kv_from, summed_to, out_refs = refs[:2], refs[2], refs[3:11]
+    queries_ref, residual_ref, kv_ref, bias_ref, mixed_ref, summed_ref, semaphores = refs[11:]
     tokens = queries_ref.shape[0]
     group = HEADS // KV_HEADS
     copies = fetch_all(
-        [(kv_from[k], kv_ref.at[pl.ds(k * tokens, tokens)]) for k in range(8)]
+        [(kv_from[k], kv_ref.at[pl.ds(4 * k * tokens, 4 * tokens)]) for k in range(2)]
         + [(queries_from, queries_ref), (residual_from, residual_ref)],
         semaphores,
     )
@@ -304,14 +304,14 @@
         if k == 0:
             bias_ref[:, span] = jnp.where(column <= row, 0.0, negative_fill)
         else:
-            seen = where_ref[0] == 1 if k == 1 else where_ref[1] >= k // 2
+            seen = where_ref[0] == 1 if k == 4 else where_ref[1] >= k % 4
             bias_ref[:, span] = jnp.full(
                 (tokens, tokens), jnp.where(seen, 0.0, negative_fill), jnp.float32
             )
-    for copy in copies[:9]:
+    for copy in copies[:3]:
         copy.wait()
     factor = math.log2(math.e) / math.sqrt(HD)
-    heads_each = 4
+    heads_each = 8
     for first in range(0, HEADS, heads_each):
         kv_head = first // group
         key_side = slice(kv_head * HD, (kv_head + 1) * HD)
@@ -332,10 +332,10 @@
             mixed_ref[:, (first + j) * HD : (first + j + 1) * HD] = result[
                 j * tokens : (j + 1) * tokens
             ].astype(jnp.bfloat16)
-    copies[9].wait()
+    copies[3].wait()
     summed = residual_ref[...].astype(jnp.float32) + mixed_ref[...].astype(jnp.float32)
     summed_ref[...] = summed
-    keep = pltpu.make_async_copy(summed_ref, summed_to, semaphores.at[10])
+    keep = pltpu.make_async_copy(summed_ref, summed_to, semaphores.at[4])
     keep.start()
     scale = lax.rsqrt(jnp.mean(summed * summed, axis=1, keepdims=True) + epsilon)
     normed = (summed * scale).astype(jnp.bfloat16)
@@ -367,7 +367,7 @@
 
 def expert_kernel(row_count, where_ref, *refs):
     row_from, refs = refs[:row_count], refs[row_count:]
-    first_piece = len(refs) == 12
+    first_piece = len(refs) == 11
     strip = refs[-4].shape[0]
     if first_piece:
         at_home_from = strips(refs[0], strip, 3)
@@ -376,15 +376,13 @@
     else:
         away_from, at_home_from, before_from = strips(refs[0], strip, 3), refs[1:4], refs[4]
         (mine_ref, twins_ref), rest = refs[5:7], refs[7:]
-    rows_ref, before_ref, gate_ref, up_ref, down_ref, row_semaphores, semaphores = rest
+    rows_ref, gate_ref, up_ref, down_ref, row_semaphores, semaphores = rest
     targets = (gate_ref, up_ref, down_ref)
     loads = []
     place = 0
     for ref in row_from:
         loads.append((ref, rows_ref.at[pl.ds(place, ref.shape[0])]))
         place += ref.shape[0]
-    if not first_piece:
-        loads.append((before_from, before_ref))
     row_copies = fetch_all(loads, row_semaphores)
     weight_copies = load(at_home_from, targets, semaphores)
     at_home = where_ref[3] == 1
@@ -408,7 +406,7 @@
     if first_piece:
         total_ref[...] = result
     else:
-        result = result + before_ref[...]
+        result = result + before_from[...]
         half = result.shape[0] // 2
         mine_ref[...] = result[:half]
         twins_ref[...] = result[half:].astype(jnp.bfloat16)
@@ -466,12 +464,6 @@
             kv_own, lambda z, x, y, core: (z + steps, x, y, core) if z + steps < 4 else None
         )
 
-    def over_x(block, steps):
-        def rule(z, x, y, core):
-            return (z, 1 - x, y, core) if z >= steps and (steps or x == 0) else None
-
-        return move(block, rule)
-
     beside = [move(w, aside) for w in weights[:2]]
     kv_along = [kv_own] + [along_z(steps) for steps in (1, 2, 3)]
     own = jnp.concatenate(weights, axis=0)
@@ -479,9 +471,8 @@
         (own, where, *beside, *kv_along)
     )
     home = move(own, homeward)
-    kv_list = []
-    for steps in range(4):
-        kv_list += [kv_along[steps], over_x(kv_along[steps], steps)]
+    kv_here = jnp.concatenate(kv_along, axis=0)
+    kv_list = [kv_here, move(kv_here, lambda z, x, y, core: (z, 1 - x, y, core))]
     rest, *kv_list = lax.optimization_barrier((weights[2], *kv_list))
     beside_rest = move(rest, aside)
     slot_shape = jax.ShapeDtypeStruct((capacity, width), jnp.bfloat16)
@@ -490,7 +481,7 @@
     first_out = pl.pallas_call(
         attend_kernel,
         out_shape=[jax.ShapeDtypeStruct((tokens, width), jnp.float32)] + [slot_shape] * 8,
-        in_specs=[IN_SMEM, IN_VMEM] + [IN_HBM] * 10,
+        in_specs=[IN_SMEM, IN_VMEM] + [IN_HBM] * 4,
         out_specs=[IN_HBM] + [IN_VMEM] * 8,
         scratch_shapes=[
             pltpu.VMEM((tokens, width), jnp.bfloat16),
@@ -499,7 +490,7 @@
             pltpu.VMEM((tokens, keys_all), jnp.float32),
             pltpu.VMEM((tokens, width), jnp.bfloat16),
             pltpu.VMEM((tokens, width), jnp.float32),
-            pltpu.SemaphoreType.DMA((11,)),
+            pltpu.SemaphoreType.DMA((5,)),
         ],
         compiler_params=pltpu.CompilerParams(vmem_limit_bytes=58 << 20),
         cost_estimate=pl.CostEstimate(
@@ -533,15 +524,16 @@
         return pl.pallas_call(
             partial(expert_kernel, len(row_parts)),
             out_shape=[mine, twins] if before else [total],
-            in_specs=[IN_SMEM] + [IN_HBM] * (len(row_parts) + len(packs) + len(before)),
+            in_specs=[IN_SMEM]
+            + [IN_HBM] * (len(row_parts) + len(packs))
+            + [IN_VMEM] * len(before),
             out_specs=[IN_VMEM] * (2 if before else 1),
             scratch_shapes=[
                 pltpu.VMEM((row_total, width), jnp.bfloat16),
-                pltpu.VMEM((row_total if before else 8, width), jnp.float32),
                 pltpu.VMEM((piece, width), jnp.bfloat16),
                 pltpu.VMEM((piece, width), jnp.bfloat16),
                 pltpu.VMEM((piece, width), jnp.bfloat16),
-                pltpu.SemaphoreType.DMA((5,)),
+                pltpu.SemaphoreType.DMA((4,)),
                 pltpu.SemaphoreType.DMA((3,)),
             ],
             compiler_params=pltpu.CompilerParams(vmem_limit_bytes=32 << 20),

time: 125 us -> 123 us (0.984)
  starting transfers between devices: 46.7 us -> 37.6 us
  waiting for transfers between devices: 54.9 us -> 63 us
    ppermute x29 -> x26, starting transfers between devices: 46.7 us -> 37.6 us  [move(): return lax.ppermute(array, AXES, pairs)]
    ppermute x29 -> x26, waiting for transfers between devices: 54.9 us -> 63 us  [move(): return lax.ppermute(array, AXES, pairs)]
  transfers between devices with their start and end apart: 29 -> 26, of which waited for: 15 -> 16; matrix products, arithmetic and copies ran while one was open for 5% -> 5% of each run, Pallas kernels for 8% -> 9%
where the time goes in v8:
time: 123 us
  waiting for transfers between devices  63 us (51%)
  starting transfers between devices  37.6 us (31%)
  Pallas kernels  15.6 us (13%)
  other arithmetic  4.9 us (4%)
    ppermute x26, waiting for transfers between devices, move(): return lax.ppermute(array, AXES, pairs)  63 us
    ppermute x26, starting transfers between devices, move(): return lax.ppermute(array, AXES, pairs)  37.6 us
    pallas_call x1, Pallas kernels, shards_cube(): pl.pallas_call(attend_kernel, out_shape=[jax.ShapeDtypeStruct((tokens, wi...  7.54 us
    pallas_call x2, Pallas kernels, run_expert(): pl.pallas_call(partial(expert_kernel, len(row_parts)), out_shape=[mine, t...  5.82 us
    concatenate x1, other arithmetic, shards_cube(): own = jnp.concatenate(weights, axis=0)  3.38 us
  transfers between devices with their start and end apart: 26, of which 16 were waited for; matrix products, arithmetic and copies ran while one was open for 5% of the time, Pallas kernels for 9%

profile of v8, /device:TPU:8, one launch (start us, length us, event | category | flops | bytes accessed | tf_op | source)
XLA Modules:
  0.0 122.6 jit_solution(13999755213543874737)
XLA Ops:
  3.5 5.1 %collective-permute-start.2 = (bf16[128,512]{1,0:T(8,128)(2,1)S(1)}, bf16[128,512]{1,0:T(8,128)(2,1)S(1)}, u32[]{:S(2)}, u32[]{:S(2)}) collective-permute-start(bf16[128,512]{1,0:T(8,128)(2,1)S(1)} %pad_maximum_fusion.1), channel_id=1, source_target_pairs={{0,8},{1,9},{2,10},{3,11},{4,12},{5,13},{6,14},{7,15},{8,16},{9,17... | collective-permute-start | bytes 393224 | tf_op jit(solution)/shard_map/ppermute | solution.py:233
  8.6 1.3 %collective-permute-start.3 = (bf16[128,512]{1,0:T(8,128)(2,1)S(1)}, bf16[128,512]{1,0:T(8,128)(2,1)S(1)}, u32[]{:S(2)}, u32[]{:S(2)}) collective-permute-start(bf16[128,512]{1,0:T(8,128)(2,1)S(1)} %pad_maximum_fusion.1), channel_id=1, source_target_pairs={{0,16},{1,17},{2,18},{3,19},{4,20},{5,21},{6,22},{7,23},{8,24},{9,... | collective-permute-start | bytes 393224 | tf_op jit(solution)/shard_map/ppermute | solution.py:233
  10.6 3.4 %pad_maximum_fusion = bf16[576,2048]{1,0:T(8,128)(2,1)} fusion(bf16[192,2048]{1,0:T(8,128)(2,1)} %bitcast.14, bf16[192,2048]{1,0:T(8,128)(2,1)} %bitcast.18, bf16[192,2048]{1,0:T(8,128)(2,1)} %bitcast.21), kind=kLoop, calls=%fused_computation | loop fusion | flops 7077888 | bytes 4718592 | tf_op jit(solution)/shard_map/concatenate | solution.py:469
  14.6 4.0 %collective-permute-done.3 = bf16[128,512]{1,0:T(8,128)(2,1)S(1)} collective-permute-done((bf16[128,512]{1,0:T(8,128)(2,1)S(1)}, bf16[128,512]{1,0:T(8,128)(2,1)S(1)}, u32[]{:S(2)}, u32[]{:S(2)}) %collective-permute-start.3) | collective-permute-done | bytes 131104 | tf_op jit(solution)/shard_map/ppermute | solution.py:233
  18.7 3.3 %collective-permute-done.1.refs_6_ = bf16[192,2048]{1,0:T(8,128)(2,1)S(1)} collective-permute-done((bf16[192,2048]{1,0:T(8,128)(2,1)}, bf16[192,2048]{1,0:T(8,128)(2,1)S(1)}, u32[]{:S(2)}, u32[]{:S(2)}) %collective-permute-start.1) | collective-permute-done | bytes 786464 | tf_op jit(solution)/shard_map/ppermute | solution.py:233
  21.9 1.6 %collective-permute-start.16 = (bf16[576,2048]{1,0:T(8,128)(2,1)}, bf16[576,2048]{1,0:T(8,128)(2,1)S(1)}, u32[]{:S(2)}, u32[]{:S(2)}) collective-permute-start(bf16[576,2048]{1,0:T(8,128)(2,1)} %pad_maximum_fusion), channel_id=1, source_target_pairs={{1,9},{3,11},{5,13},{7,15},{8,0},{10,2},{12,4},{14,6},{17,25},{19,... | collective-permute-start | bytes 7077896 | tf_op jit(solution)/shard_map/ppermute | solution.py:233
  23.7 1.4 %collective-permute-start.5 = (bf16[512,512]{1,0:T(8,128)(2,1)S(1)}, bf16[512,512]{1,0:T(8,128)(2,1)S(1)}, u32[]{:S(2)}, u32[]{:S(2)}) collective-permute-start(bf16[512,512]{1,0:T(8,128)(2,1)S(1)} %constant_dynamic-update-slice_fusion.refs_0_), channel_id=1, source_target_pairs={{0,4},{1,5},{2,6},{3,7},{4,0},{5,1},{6,2},{7,3},{8,12},{9,13},{10,... | collective-permute-start | bytes 1572872 | tf_op jit(solution)/shard_map/ppermute | solution.py:233
  25.0 11.4 %collective-permute-done.5.refs_1_ = bf16[512,512]{1,0:T(8,128)(2,1)S(1)} collective-permute-done((bf16[512,512]{1,0:T(8,128)(2,1)S(1)}, bf16[512,512]{1,0:T(8,128)(2,1)S(1)}, u32[]{:S(2)}, u32[]{:S(2)}) %collective-permute-start.5) | collective-permute-done | bytes 524320 | tf_op jit(solution)/shard_map/ppermute | solution.py:233
  37.8 7.5 %attend.1 = (f32[128,2048]{1,0:T(8,128)}, bf16[32,2048]{1,0:T(8,128)(2,1)}, bf16[32,2048]{1,0:T(8,128)(2,1)}, bf16[32,2048]{1,0:T(8,128)(2,1)}, bf16[32,2048]{1,...) custom-call(s32[4]{0:T(128)} %pad_add_fusion.where_ref, ...), custom_call_target="tpu_custom_call" | custom-call | flops 1073741824 | bytes 2097152 | tf_op jit(solution)/shard_map/attend/pallas_call | solution.py:481
  45.3 4.4 %collective-permute-done.6.refs_7_ = bf16[192,2048]{1,0:T(8,128)(2,1)S(1)} collective-permute-done((bf16[192,2048]{1,0:T(8,128)(2,1)S(1)}, bf16[192,2048]{1,0:T(8,128)(2,1)S(1)}, u32[]{:S(2)}, u32[]{:S(2)}) %collective-permute-start.6) | collective-permute-done | bytes 786464 | tf_op jit(solution)/shard_map/ppermute | solution.py:233
  49.7 2.6 %collective-permute-start.10 = (bf16[32,2048]{1,0:T(8,128)(2,1)}, bf16[32,2048]{1,0:T(8,128)(2,1)S(1)}, u32[]{:S(2)}, u32[]{:S(2)}) collective-permute-start(bf16[32,2048]{1,0:T(8,128)(2,1)} %get-tuple-element.65), channel_id=1, source_target_pairs={{0,16},{1,17},{2,18},{3,19},{4,20},{5,21},{6,22},{7,23},{8,24},{9,... | collective-permute-start | bytes 393224 | tf_op jit(solution)/shard_map/ppermute | solution.py:233
  54.5 2.8 %collective-permute-start.11 = (bf16[32,2048]{1,0:T(8,128)(2,1)}, bf16[32,2048]{1,0:T(8,128)(2,1)S(1)}, u32[]{:S(2)}, u32[]{:S(2)}) collective-permute-start(bf16[32,2048]{1,0:T(8,128)(2,1)} %get-tuple-element.66), channel_id=1, source_target_pairs={{0,24},{1,25},{2,26},{3,27},{4,28},{5,29},{6,30},{7,31},{8,16},{9,... | collective-permute-start | bytes 393224 | tf_op jit(solution)/shard_map/ppermute | solution.py:233
  57.3 2.9 %collective-permute-start.12 = (bf16[32,2048]{1,0:T(8,128)(2,1)}, bf16[32,2048]{1,0:T(8,128)(2,1)S(1)}, u32[]{:S(2)}, u32[]{:S(2)}) collective-permute-start(bf16[32,2048]{1,0:T(8,128)(2,1)} %get-tuple-element.67), channel_id=1, source_target_pairs={{0,18},{1,19},{2,16},{3,17},{4,22},{5,23},{6,20},{7,21},{8,26},{9,... | collective-permute-start | bytes 393224 | tf_op jit(solution)/shard_map/ppermute | solution.py:233
  60.3 2.3 %collective-permute-start.7 = (bf16[32,2048]{1,0:T(8,128)(2,1)}, bf16[32,2048]{1,0:T(8,128)(2,1)S(1)}, u32[]{:S(2)}, u32[]{:S(2)}) collective-permute-start(bf16[32,2048]{1,0:T(8,128)(2,1)} %get-tuple-element.62), channel_id=1, source_target_pairs={{0,8},{1,9},{2,10},{3,11},{4,12},{5,13},{6,14},{7,15},{8,0},{9,1},... | collective-permute-start | bytes 393224 | tf_op jit(solution)/shard_map/ppermute | solution.py:233
  62.6 7.7 %collective-permute-done.11 = bf16[32,2048]{1,0:T(8,128)(2,1)S(1)} collective-permute-done((bf16[32,2048]{1,0:T(8,128)(2,1)}, bf16[32,2048]{1,0:T(8,128)(2,1)S(1)}, u32[]{:S(2)}, u32[]{:S(2)}) %collective-permute-start.11) | collective-permute-done | bytes 131104 | tf_op jit(solution)/shard_map/ppermute | solution.py:233
  70.3 2.2 %collective-permute-done.12 = bf16[32,2048]{1,0:T(8,128)(2,1)S(1)} collective-permute-done((bf16[32,2048]{1,0:T(8,128)(2,1)}, bf16[32,2048]{1,0:T(8,128)(2,1)S(1)}, u32[]{:S(2)}, u32[]{:S(2)}) %collective-permute-start.12) | collective-permute-done | bytes 131104 | tf_op jit(solution)/shard_map/ppermute | solution.py:233
  72.6 1.6 %collective-permute-start.9 = (bf16[32,2048]{1,0:T(8,128)(2,1)}, bf16[32,2048]{1,0:T(8,128)(2,1)S(1)}, u32[]{:S(2)}, u32[]{:S(2)}) collective-permute-start(bf16[32,2048]{1,0:T(8,128)(2,1)} %get-tuple-element.64), channel_id=1, source_target_pairs={{0,2},{1,3},{2,0},{3,1},{4,6},{5,7},{6,4},{7,5},{8,10},{9,11},{10,... | collective-permute-start | bytes 393224 | tf_op jit(solution)/shard_map/ppermute | solution.py:233
  74.2 5.1 %collective-permute-done.13 = bf16[32,2048]{1,0:T(8,128)(2,1)S(1)} collective-permute-done((bf16[32,2048]{1,0:T(8,128)(2,1)}, bf16[32,2048]{1,0:T(8,128)(2,1)S(1)}, u32[]{:S(2)}, u32[]{:S(2)}) %collective-permute-start.13) | collective-permute-done | bytes 131104 | tf_op jit(solution)/shard_map/ppermute | solution.py:233
  79.5 1.8 %collective-permute-done.9 = bf16[32,2048]{1,0:T(8,128)(2,1)S(1)} collective-permute-done((bf16[32,2048]{1,0:T(8,128)(2,1)}, bf16[32,2048]{1,0:T(8,128)(2,1)S(1)}, u32[]{:S(2)}, u32[]{:S(2)}) %collective-permute-start.9) | collective-permute-done | bytes 131104 | tf_op jit(solution)/shard_map/ppermute | solution.py:233
  81.4 1.9 %collective-permute-done.14.refs_2_ = bf16[128,2048]{1,0:T(8,128)(2,1)S(1)} collective-permute-done((bf16[128,2048]{1,0:T(8,128)(2,1)S(1)}, bf16[128,2048]{1,0:T(8,128)(2,1)S(1)}, u32[]{:S(2)}, u32[]{:S(2)}) %collective-permute-start.14) | collective-permute-done | bytes 524320 | tf_op jit(solution)/shard_map/ppermute | solution.py:233
  83.3 2.9 %experts_first.1.refs_8_ = f32[512,2048]{1,0:T(8,128)S(1)} custom-call(s32[4]{0:T(128)S(1)} %copy-done.4, bf16[128,2048]{1,0:T(8,128)(2,1)S(1)} %constant_dynamic-update-slice_fusion.4.refs_0_, bf16[128,2048]{1,0:T(8,128)(2,1)S(1)} %constant_dynamic-update-slice_fusion.8.refs_1_, bf16[128,2048]{1,0:T(8,128)(2,1)S(1)} %collective-permute-done.14.refs_2_, ...), custom_call_target="tpu_custom_call" | custom-call | flops 1207959552 | bytes 2359296 | tf_op jit(solution)/shard_map/experts_first/pallas_call | solution.py:524
  86.2 2.9 %experts_rest.1 = (f32[256,2048]{1,0:T(8,128)S(1)}, bf16[256,2048]{1,0:T(8,128)(2,1)S(1)}) custom-call(s32[4]{0:T(128)S(1)} %copy-done.4, bf16[128,2048]{1,0:T(8,128)(2,1)S(1)} %constant_dynamic-update-slice_fusion.4.refs_0_, bf16[128,2048]{1,0:T(8,128)(2,1)S(1)} %constant_dynamic-update-slice_fusion.8.refs_1_, ...), custom_call_target="tpu_custom_call" | custom-call | flops 1207959552 | bytes 2359296 | tf_op jit(solution)/shard_map/experts_rest/pallas_call | solution.py:524
  89.4 2.5 %collective-permute-done.18.other_from = bf16[256,2048]{1,0:T(8,128)(2,1)S(1)} collective-permute-done((bf16[256,2048]{1,0:T(8,128)(2,1)S(1)}, bf16[256,2048]{1,0:T(8,128)(2,1)S(1)}, u32[]{:S(2)}, u32[]{:S(2)}) %collective-permute-start.18) | collective-permute-done | bytes 1048608 | tf_op jit(solution)/shard_map/ppermute | solution.py:233
  92.3 1.4 %collective-permute-start.19 = (bf16[32,2048]{1,0:T(8,128)(2,1)S(1)}, bf16[32,2048]{1,0:T(8,128)(2,1)S(1)}, u32[]{:S(2)}, u32[]{:S(2)}) collective-permute-start(bf16[32,2048]{1,0:T(8,128)(2,1)S(1)} %get-tuple-element.78), channel_id=1, source_target_pairs={{0,2},{1,3},{2,0},{3,1},{4,6},{5,7},{6,4},{7,5},{8,10},{9,11},{10,... | collective-permute-start | bytes 393224 | tf_op jit(solution)/shard_map/ppermute | solution.py:233
  93.7 2.1 %collective-permute-start.21 = (bf16[32,2048]{1,0:T(8,128)(2,1)S(1)}, bf16[32,2048]{1,0:T(8,128)(2,1)S(1)}, u32[]{:S(2)}, u32[]{:S(2)}) collective-permute-start(bf16[32,2048]{1,0:T(8,128)(2,1)S(1)} %get-tuple-element.80), channel_id=1, source_target_pairs={{0,10},{1,11},{2,8},{3,9},{4,14},{5,15},{6,12},{7,13},{8,2},{9,3},... | collective-permute-start | bytes 393224 | tf_op jit(solution)/shard_map/ppermute | solution.py:233
  96.7 2.9 %collective-permute-start.23 = (bf16[32,2048]{1,0:T(8,128)(2,1)S(1)}, bf16[32,2048]{1,0:T(8,128)(2,1)S(1)}, u32[]{:S(2)}, u32[]{:S(2)}) collective-permute-start(bf16[32,2048]{1,0:T(8,128)(2,1)S(1)} %get-tuple-element.82), channel_id=1, source_target_pairs={{0,18},{1,19},{2,16},{3,17},{4,22},{5,23},{6,20},{7,21},{8,26},{9,... | collective-permute-start | bytes 393224 | tf_op jit(solution)/shard_map/ppermute | solution.py:233
  100.8 2.5 %collective-permute-start.25 = (bf16[32,2048]{1,0:T(8,128)(2,1)S(1)}, bf16[32,2048]{1,0:T(8,128)(2,1)S(1)}, u32[]{:S(2)}, u32[]{:S(2)}) collective-permute-start(bf16[32,2048]{1,0:T(8,128)(2,1)S(1)} %get-tuple-element.84), channel_id=1, source_target_pairs={{0,26},{1,27},{2,24},{3,25},{4,30},{5,31},{6,28},{7,29},{8,18},{9,... | collective-permute-start | bytes 393224 | tf_op jit(solution)/shard_map/ppermute | solution.py:233
  103.4 1.9 %collective-permute-done.22.refs_4_ = bf16[32,2048]{1,0:T(8,128)(2,1)S(1)} collective-permute-done((bf16[32,2048]{1,0:T(8,128)(2,1)S(1)}, bf16[32,2048]{1,0:T(8,128)(2,1)S(1)}, u32[]{:S(2)}, u32[]{:S(2)}) %collective-permute-start.22) | collective-permute-done | bytes 131104 | tf_op jit(solution)/shard_map/ppermute | solution.py:233
  105.3 9.0 %collective-permute-done.23.refs_5_ = bf16[32,2048]{1,0:T(8,128)(2,1)S(1)} collective-permute-done((bf16[32,2048]{1,0:T(8,128)(2,1)S(1)}, bf16[32,2048]{1,0:T(8,128)(2,1)S(1)}, u32[]{:S(2)}, u32[]{:S(2)}) %collective-permute-start.23) | collective-permute-done | bytes 131104 | tf_op jit(solution)/shard_map/ppermute | solution.py:233
  114.3 4.1 %collective-permute-done.24.refs_6_ = bf16[32,2048]{1,0:T(8,128)(2,1)S(1)} collective-permute-done((bf16[32,2048]{1,0:T(8,128)(2,1)S(1)}, bf16[32,2048]{1,0:T(8,128)(2,1)S(1)}, u32[]{:S(2)}, u32[]{:S(2)}) %collective-permute-start.24) | collective-permute-done | bytes 131104 | tf_op jit(solution)/shard_map/ppermute | solution.py:233
  118.4 2.4 %collective-permute-done.25.refs_7_ = bf16[32,2048]{1,0:T(8,128)(2,1)S(1)} collective-permute-done((bf16[32,2048]{1,0:T(8,128)(2,1)S(1)}, bf16[32,2048]{1,0:T(8,128)(2,1)S(1)}, u32[]{:S(2)}, u32[]{:S(2)}) %collective-permute-start.25) | collective-permute-done | bytes 131104 | tf_op jit(solution)/shard_map/ppermute | solution.py:233
  120.8 1.8 %combine.1 = bf16[128,2048]{1,0:T(8,128)(2,1)} custom-call(s32[4]{0:T(128)S(1)} %copy-done.4, s32[1,128]{1,0:T(1,128)S(1)} %bitcast.24, f32[128,1]{1,0:T(8,128)S(1)} %copy.10.route_ref, f32[128,2048]{1,0:T(8,128)S(1)} %copy-done.3, bf16[32,2048]{1,0:T(8,128)(2,1)S(1)} %get-tuple-element.77.refs_0_, bf16[32,2048]{1,0:T(8,128)(2,1)S(1)} %collective-permute-done.19.refs_1_, ...), custom_call_target="tpu_custom_call" | custom-call | flops 134217728 | bytes 3145728 | tf_op jit(solution)/shard_map/combine/pallas_call | solution.py:569
  (59 shorter events, 11.4 us)
Async XLA Ops:
  0.0 18.7 %collective-permute-start = (bf16[192,2048]{1,0:T(8,128)(2,1)}, bf16[192,2048]{1,0:T(8,128)(2,1)S(1)}, u32[]{:S(2)}, u32[]{:S(2)}) collective-permute-start(bf16[192,2048]{1,0:T(8,128)(2,1)} %bitcast.20), channel_id=1, source_target_pairs={{0,5},{2,7},{4,1},{6,3},{9,12},{11,14},{13,8},{15,10},{16,21},{18,... | collective-permute-start | bytes 2359304 | tf_op jit(solution)/shard_map/ppermute | solution.py:233
  1.3 20.6 %collective-permute-start.1 = (bf16[192,2048]{1,0:T(8,128)(2,1)}, bf16[192,2048]{1,0:T(8,128)(2,1)S(1)}, u32[]{:S(2)}, u32[]{:S(2)}) collective-permute-start(bf16[192,2048]{1,0:T(8,128)(2,1)} %bitcast.17), channel_id=1, source_target_pairs={{0,5},{2,7},{4,1},{6,3},{9,12},{11,14},{13,8},{15,10},{16,21},{18,... | collective-permute-start | bytes 2359304 | tf_op jit(solution)/shard_map/ppermute | solution.py:233
  3.5 11.2 %collective-permute-start.2 = (bf16[128,512]{1,0:T(8,128)(2,1)S(1)}, bf16[128,512]{1,0:T(8,128)(2,1)S(1)}, u32[]{:S(2)}, u32[]{:S(2)}) collective-permute-start(bf16[128,512]{1,0:T(8,128)(2,1)S(1)} %pad_maximum_fusion.1), channel_id=1, source_target_pairs={{0,8},{1,9},{2,10},{3,11},{4,12},{5,13},{6,14},{7,15},{8,16},{9,17... | collective-permute-start | bytes 393224 | tf_op jit(solution)/shard_map/ppermute | solution.py:233
  8.6 10.1 %collective-permute-start.3 = (bf16[128,512]{1,0:T(8,128)(2,1)S(1)}, bf16[128,512]{1,0:T(8,128)(2,1)S(1)}, u32[]{:S(2)}, u32[]{:S(2)}) collective-permute-start(bf16[128,512]{1,0:T(8,128)(2,1)S(1)} %pad_maximum_fusion.1), channel_id=1, source_target_pairs={{0,16},{1,17},{2,18},{3,19},{4,20},{5,21},{6,22},{7,23},{8,24},{9,... | collective-permute-start | bytes 393224 | tf_op jit(solution)/shard_map/ppermute | solution.py:233
  9.9 8.8 %collective-permute-start.4 = (bf16[128,512]{1,0:T(8,128)(2,1)S(1)}, bf16[128,512]{1,0:T(8,128)(2,1)S(1)}, u32[]{:S(2)}, u32[]{:S(2)}) collective-permute-start(bf16[128,512]{1,0:T(8,128)(2,1)S(1)} %pad_maximum_fusion.1), channel_id=1, source_target_pairs={{0,24},{1,25},{2,26},{3,27},{4,28},{5,29},{6,30},{7,31}} | collective-permute-start | bytes 393224 | tf_op jit(solution)/shard_map/ppermute | solution.py:233
  10.6 25.8 %copy-start = (bf16[1,1,192,2048]{3,2,1,0:T(8,128)(2,1)S(1)}, bf16[1,1,192,2048]{3,2,1,0:T(8,128)(2,1)}, u32[]{:S(2)}) copy-start(bf16[1,1,192,2048]{3,2,1,0:T(8,128)(2,1)} %param.17) | copy-start | bytes 2359300
  21.9 30.4 %collective-permute-start.16 = (bf16[576,2048]{1,0:T(8,128)(2,1)}, bf16[576,2048]{1,0:T(8,128)(2,1)S(1)}, u32[]{:S(2)}, u32[]{:S(2)}) collective-permute-start(bf16[576,2048]{1,0:T(8,128)(2,1)} %pad_maximum_fusion), channel_id=1, source_target_pairs={{1,9},{3,11},{5,13},{7,15},{8,0},{10,2},{12,4},{14,6},{17,25},{19,... | collective-permute-start | bytes 7077896 | tf_op jit(solution)/shard_map/ppermute | solution.py:233
  23.6 14.1 %copy-start.6 = (bf16[512,512]{1,0:T(8,128)(2,1)}, bf16[512,512]{1,0:T(8,128)(2,1)S(1)}, u32[]{:S(2)}) copy-start(bf16[512,512]{1,0:T(8,128)(2,1)S(1)} %constant_dynamic-update-slice_fusion.refs_0_) | copy-start | bytes 1572868
  23.7 12.8 %collective-permute-start.5 = (bf16[512,512]{1,0:T(8,128)(2,1)S(1)}, bf16[512,512]{1,0:T(8,128)(2,1)S(1)}, u32[]{:S(2)}, u32[]{:S(2)}) collective-permute-start(bf16[512,512]{1,0:T(8,128)(2,1)S(1)} %constant_dynamic-update-slice_fusion.refs_0_), channel_id=1, source_target_pairs={{0,4},{1,5},{2,6},{3,7},{4,0},{5,1},{6,2},{7,3},{8,12},{9,13},{10,... | collective-permute-start | bytes 1572872 | tf_op jit(solution)/shard_map/ppermute | solution.py:233
  36.4 13.3 %collective-permute-start.6 = (bf16[192,2048]{1,0:T(8,128)(2,1)S(1)}, bf16[192,2048]{1,0:T(8,128)(2,1)S(1)}, u32[]{:S(2)}, u32[]{:S(2)}) collective-permute-start(bf16[192,2048]{1,0:T(8,128)(2,1)S(1)} %bitcast.15), channel_id=1, source_target_pairs={{0,5},{2,7},{4,1},{6,3},{9,12},{11,14},{13,8},{15,10},{16,21},{18,... | collective-permute-start | bytes 2359304 | tf_op jit(solution)/shard_map/ppermute | solution.py:233
  37.8 45.5 %copy-start.4 = (s32[4]{0:T(128)S(1)}, s32[4]{0:T(128)}, u32[]{:S(2)}) copy-start(s32[4]{0:T(128)} %pad_add_fusion.where_ref) | copy-start | bytes 52
  49.7 10.5 %collective-permute-start.10 = (bf16[32,2048]{1,0:T(8,128)(2,1)}, bf16[32,2048]{1,0:T(8,128)(2,1)S(1)}, u32[]{:S(2)}, u32[]{:S(2)}) collective-permute-start(bf16[32,2048]{1,0:T(8,128)(2,1)} %get-tuple-element.65), channel_id=1, source_target_pairs={{0,16},{1,17},{2,18},{3,19},{4,20},{5,21},{6,22},{7,23},{8,24},{9,... | collective-permute-start | bytes 393224 | tf_op jit(solution)/shard_map/ppermute | solution.py:233
  52.3 33.9 %collective-permute-start.17 = (bf16[576,2048]{1,0:T(8,128)(2,1)S(1)}, bf16[576,2048]{1,0:T(8,128)(2,1)S(1)}, u32[]{:S(2)}, u32[]{:S(2)}) collective-permute-start(bf16[576,2048]{1,0:T(8,128)(2,1)S(1)} %collective-permute-done.16.refs_4_), channel_id=1, source_target_pairs={{0,5},{2,7},{4,1},{6,3},{9,12},{11,14},{13,8},{15,10},{16,21},{18,... | collective-permute-start | bytes 7077896 | tf_op jit(solution)/shard_map/ppermute | solution.py:233
  54.5 15.8 %collective-permute-start.11 = (bf16[32,2048]{1,0:T(8,128)(2,1)}, bf16[32,2048]{1,0:T(8,128)(2,1)S(1)}, u32[]{:S(2)}, u32[]{:S(2)}) collective-permute-start(bf16[32,2048]{1,0:T(8,128)(2,1)} %get-tuple-element.66), channel_id=1, source_target_pairs={{0,24},{1,25},{2,26},{3,27},{4,28},{5,29},{6,30},{7,31},{8,16},{9,... | collective-permute-start | bytes 393224 | tf_op jit(solution)/shard_map/ppermute | solution.py:233
  57.3 15.2 %collective-permute-start.12 = (bf16[32,2048]{1,0:T(8,128)(2,1)}, bf16[32,2048]{1,0:T(8,128)(2,1)S(1)}, u32[]{:S(2)}, u32[]{:S(2)}) collective-permute-start(bf16[32,2048]{1,0:T(8,128)(2,1)} %get-tuple-element.67), channel_id=1, source_target_pairs={{0,18},{1,19},{2,16},{3,17},{4,22},{5,23},{6,20},{7,21},{8,26},{9,... | collective-permute-start | bytes 393224 | tf_op jit(solution)/shard_map/ppermute | solution.py:233
  60.3 19.0 %collective-permute-start.13 = (bf16[32,2048]{1,0:T(8,128)(2,1)}, bf16[32,2048]{1,0:T(8,128)(2,1)S(1)}, u32[]{:S(2)}, u32[]{:S(2)}) collective-permute-start(bf16[32,2048]{1,0:T(8,128)(2,1)} %get-tuple-element.68), channel_id=1, source_target_pairs={{0,26},{1,27},{2,24},{3,25},{4,30},{5,31},{6,28},{7,29},{8,18},{9,... | collective-permute-start | bytes 393224 | tf_op jit(solution)/shard_map/ppermute | solution.py:233
  60.3 19.1 %collective-permute-start.7 = (bf16[32,2048]{1,0:T(8,128)(2,1)}, bf16[32,2048]{1,0:T(8,128)(2,1)S(1)}, u32[]{:S(2)}, u32[]{:S(2)}) collective-permute-start(bf16[32,2048]{1,0:T(8,128)(2,1)} %get-tuple-element.62), channel_id=1, source_target_pairs={{0,8},{1,9},{2,10},{3,11},{4,12},{5,13},{6,14},{7,15},{8,0},{9,1},... | collective-permute-start | bytes 393224 | tf_op jit(solution)/shard_map/ppermute | solution.py:233
  70.3 9.1 %collective-permute-start.8 = (bf16[32,2048]{1,0:T(8,128)(2,1)}, bf16[32,2048]{1,0:T(8,128)(2,1)S(1)}, u32[]{:S(2)}, u32[]{:S(2)}) collective-permute-start(bf16[32,2048]{1,0:T(8,128)(2,1)} %get-tuple-element.63), channel_id=1, source_target_pairs={{0,10},{1,11},{2,8},{3,9},{4,14},{5,15},{6,12},{7,13},{8,2},{9,3},... | collective-permute-start | bytes 393224 | tf_op jit(solution)/shard_map/ppermute | solution.py:233
  72.6 8.7 %collective-permute-start.9 = (bf16[32,2048]{1,0:T(8,128)(2,1)}, bf16[32,2048]{1,0:T(8,128)(2,1)S(1)}, u32[]{:S(2)}, u32[]{:S(2)}) collective-permute-start(bf16[32,2048]{1,0:T(8,128)(2,1)} %get-tuple-element.64), channel_id=1, source_target_pairs={{0,2},{1,3},{2,0},{3,1},{4,6},{5,7},{6,4},{7,5},{8,10},{9,11},{10,... | collective-permute-start | bytes 393224 | tf_op jit(solution)/shard_map/ppermute | solution.py:233
  79.3 2.1 %collective-permute-start.15 = (bf16[128,2048]{1,0:T(8,128)(2,1)S(1)}, bf16[128,2048]{1,0:T(8,128)(2,1)S(1)}, u32[]{:S(2)}, u32[]{:S(2)}) collective-permute-start(bf16[128,2048]{1,0:T(8,128)(2,1)S(1)} %constant_dynamic-update-slice_fusion.8.refs_1_), channel_id=1, source_target_pairs={{0,1},{1,0},{2,3},{3,2},{4,5},{5,4},{6,7},{7,6},{8,9},{9,8},{10,11... | collective-permute-start | bytes 1572872 | tf_op jit(solution)/shard_map/ppermute | solution.py:233
  81.3 2.0 %collective-permute-start.14 = (bf16[128,2048]{1,0:T(8,128)(2,1)S(1)}, bf16[128,2048]{1,0:T(8,128)(2,1)S(1)}, u32[]{:S(2)}, u32[]{:S(2)}) collective-permute-start(bf16[128,2048]{1,0:T(8,128)(2,1)S(1)} %constant_dynamic-update-slice_fusion.4.refs_0_), channel_id=1, source_target_pairs={{0,1},{1,0},{2,3},{3,2},{4,5},{5,4},{6,7},{7,6},{8,9},{9,8},{10,11... | collective-permute-start | bytes 1572872 | tf_op jit(solution)/shard_map/ppermute | solution.py:233
  89.2 14.1 %copy-start.7 = (f32[1,128,1]{1,2,0:T(1,128)S(1)}, f32[1,128,1]{1,2,0:T(1,128)}, u32[]{:S(2)}) copy-start(f32[1,128,1]{1,2,0:T(1,128)} %param.14) | copy-start | bytes 1540
  89.2 31.6 %copy-start.3 = (f32[128,2048]{1,0:T(8,128)S(1)}, f32[128,2048]{1,0:T(8,128)}, u32[]{:S(2)}) copy-start(f32[128,2048]{1,0:T(8,128)} %get-tuple-element.52.summed_ref) | copy-start | bytes 3145732
  89.2 31.6 %copy-start.5 = (s32[1,128,1]{1,2,0:T(1,128)S(1)}, s32[1,128,1]{1,2,0:T(1,128)}, u32[]{:S(2)}) copy-start(s32[1,128,1]{1,2,0:T(1,128)} %param.13) | copy-start | bytes 1540
  89.2 2.7 %collective-permute-start.18 = (bf16[256,2048]{1,0:T(8,128)(2,1)S(1)}, bf16[256,2048]{1,0:T(8,128)(2,1)S(1)}, u32[]{:S(2)}, u32[]{:S(2)}) collective-permute-start(bf16[256,2048]{1,0:T(8,128)(2,1)S(1)} %get-tuple-element.76), channel_id=1, source_target_pairs={{0,1},{1,0},{2,3},{3,2},{4,5},{5,4},{6,7},{7,6},{8,9},{9,8},{10,11... | collective-permute-start | bytes 3145736 | tf_op jit(solution)/shard_map/ppermute | solution.py:233
  92.3 7.3 %collective-permute-start.19 = (bf16[32,2048]{1,0:T(8,128)(2,1)S(1)}, bf16[32,2048]{1,0:T(8,128)(2,1)S(1)}, u32[]{:S(2)}, u32[]{:S(2)}) collective-permute-start(bf16[32,2048]{1,0:T(8,128)(2,1)S(1)} %get-tuple-element.78), channel_id=1, source_target_pairs={{0,2},{1,3},{2,0},{3,1},{4,6},{5,7},{6,4},{7,5},{8,10},{9,11},{10,... | collective-permute-start | bytes 393224 | tf_op jit(solution)/shard_map/ppermute | solution.py:233
  93.7 7.0 %collective-permute-start.20 = (bf16[32,2048]{1,0:T(8,128)(2,1)S(1)}, bf16[32,2048]{1,0:T(8,128)(2,1)S(1)}, u32[]{:S(2)}, u32[]{:S(2)}) collective-permute-start(bf16[32,2048]{1,0:T(8,128)(2,1)S(1)} %get-tuple-element.79), channel_id=1, source_target_pairs={{0,8},{1,9},{2,10},{3,11},{4,12},{5,13},{6,14},{7,15},{8,0},{9,1},... | collective-permute-start | bytes 393224 | tf_op jit(solution)/shard_map/ppermute | solution.py:233
  93.7 9.7 %collective-permute-start.21 = (bf16[32,2048]{1,0:T(8,128)(2,1)S(1)}, bf16[32,2048]{1,0:T(8,128)(2,1)S(1)}, u32[]{:S(2)}, u32[]{:S(2)}) collective-permute-start(bf16[32,2048]{1,0:T(8,128)(2,1)S(1)} %get-tuple-element.80), channel_id=1, source_target_pairs={{0,10},{1,11},{2,8},{3,9},{4,14},{5,15},{6,12},{7,13},{8,2},{9,3},... | collective-permute-start | bytes 393224 | tf_op jit(solution)/shard_map/ppermute | solution.py:233
  95.9 9.4 %collective-permute-start.22 = (bf16[32,2048]{1,0:T(8,128)(2,1)S(1)}, bf16[32,2048]{1,0:T(8,128)(2,1)S(1)}, u32[]{:S(2)}, u32[]{:S(2)}) collective-permute-start(bf16[32,2048]{1,0:T(8,128)(2,1)S(1)} %get-tuple-element.81), channel_id=1, source_target_pairs={{0,16},{1,17},{2,18},{3,19},{4,20},{5,21},{6,22},{7,23},{8,24},{9,... | collective-permute-start | bytes 393224 | tf_op jit(solution)/shard_map/ppermute | solution.py:233
  96.7 17.6 %collective-permute-start.23 = (bf16[32,2048]{1,0:T(8,128)(2,1)S(1)}, bf16[32,2048]{1,0:T(8,128)(2,1)S(1)}, u32[]{:S(2)}, u32[]{:S(2)}) collective-permute-start(bf16[32,2048]{1,0:T(8,128)(2,1)S(1)} %get-tuple-element.82), channel_id=1, source_target_pairs={{0,18},{1,19},{2,16},{3,17},{4,22},{5,23},{6,20},{7,21},{8,26},{9,... | collective-permute-start | bytes 393224 | tf_op jit(solution)/shard_map/ppermute | solution.py:233
  99.6 18.8 %collective-permute-start.24 = (bf16[32,2048]{1,0:T(8,128)(2,1)S(1)}, bf16[32,2048]{1,0:T(8,128)(2,1)S(1)}, u32[]{:S(2)}, u32[]{:S(2)}) collective-permute-start(bf16[32,2048]{1,0:T(8,128)(2,1)S(1)} %get-tuple-element.83), channel_id=1, source_target_pairs={{0,24},{1,25},{2,26},{3,27},{4,28},{5,29},{6,30},{7,31},{8,16},{9,... | collective-permute-start | bytes 393224 | tf_op jit(solution)/shard_map/ppermute | solution.py:233
  100.8 20.0 %collective-permute-start.25 = (bf16[32,2048]{1,0:T(8,128)(2,1)S(1)}, bf16[32,2048]{1,0:T(8,128)(2,1)S(1)}, u32[]{:S(2)}, u32[]{:S(2)}) collective-permute-start(bf16[32,2048]{1,0:T(8,128)(2,1)S(1)} %get-tuple-element.84), channel_id=1, source_target_pairs={{0,26},{1,27},{2,24},{3,25},{4,30},{5,31},{6,28},{7,29},{8,18},{9,... | collective-permute-start | bytes 393224 | tf_op jit(solution)/shard_map/ppermute | solution.py:233
  (3 other events, 11.2 us)

commit v9 on v8

--- a/solution.py
+++ b/solution.py
@@ -509,8 +509,10 @@
 
     last = move(home, second_hop)
     arrived = {0: outgoing[0]}
+    arrived[4] = swap(outgoing[4], 4)
+    arrived[6] = swap(outgoing[6], 6)
     beside_rest, *outgoing = lax.optimization_barrier((beside_rest, *outgoing))
-    for k in (4, 6, 5, 7, 2, 3, 1):
+    for k in (5, 7, 2, 3, 1):
         arrived[k] = swap(outgoing[k], k)
     order = (0, 2, 3, 1, 4, 6, 5, 7)
     row_parts = [jnp.concatenate([arrived[k] for k in group]) for group in (order[:4], order[4:])]

time: 123 us -> 122 us (level); the launches traced: 123 us -> 120 us
  waiting for transfers between devices: 63 us -> 59.5 us
    ppermute x26, waiting for transfers between devices: 63 us -> 59.5 us  [move(): return lax.ppermute(array, AXES, pairs)]
  transfers between devices with their start and end apart: 26 -> 26, of which waited for: 16 -> 17; matrix products, arithmetic and copies ran while one was open for 5% -> 5% of each run, Pallas kernels for 9% -> 9%
where the time goes in v9:
time: 122 us; the launch traced here: 120 us
  waiting for transfers between devices  59.5 us (49%)
  starting transfers between devices  38.6 us (32%)
  Pallas kernels  15.6 us (13%)
  other arithmetic  4.9 us (4%)
    ppermute x26, waiting for transfers between devices, move(): return lax.ppermute(array, AXES, pairs)  59.5 us
    ppermute x26, starting transfers between devices, move(): return lax.ppermute(array, AXES, pairs)  38.6 us
    pallas_call x1, Pallas kernels, shards_cube(): pl.pallas_call(attend_kernel, out_shape=[jax.ShapeDtypeStruct((tokens, wi...  7.54 us
    pallas_call x2, Pallas kernels, run_expert(): pl.pallas_call(partial(expert_kernel, len(row_parts)), out_shape=[mine, t...  5.83 us
    concatenate x1, other arithmetic, shards_cube(): own = jnp.concatenate(weights, axis=0)  3.38 us
  transfers between devices with their start and end apart: 26, of which 17 were waited for; matrix products, arithmetic and copies ran while one was open for 5% of the time, Pallas kernels for 9%

profile of v9, /device:TPU:8, one launch (start us, length us, event | category | flops | bytes accessed | tf_op | source)
XLA Modules:
  0.0 120.1 jit_solution(3406854140368475275)
XLA Ops:
  1.3 1.3 %collective-permute-start.1 = (bf16[192,2048]{1,0:T(8,128)(2,1)}, bf16[192,2048]{1,0:T(8,128)(2,1)S(1)}, u32[]{:S(2)}, u32[]{:S(2)}) collective-permute-start(bf16[192,2048]{1,0:T(8,128)(2,1)} %bitcast.17), channel_id=1, source_target_pairs={{0,5},{2,7},{4,1},{6,3},{9,12},{11,14},{13,8},{15,10},{16,21},{18,... | collective-permute-start | bytes 2359304 | tf_op jit(solution)/shard_map/ppermute | solution.py:233
  3.5 5.1 %collective-permute-start.2 = (bf16[128,512]{1,0:T(8,128)(2,1)S(1)}, bf16[128,512]{1,0:T(8,128)(2,1)S(1)}, u32[]{:S(2)}, u32[]{:S(2)}) collective-permute-start(bf16[128,512]{1,0:T(8,128)(2,1)S(1)} %pad_maximum_fusion.1), channel_id=1, source_target_pairs={{0,8},{1,9},{2,10},{3,11},{4,12},{5,13},{6,14},{7,15},{8,16},{9,17... | collective-permute-start | bytes 393224 | tf_op jit(solution)/shard_map/ppermute | solution.py:233
  8.6 1.3 %collective-permute-start.3 = (bf16[128,512]{1,0:T(8,128)(2,1)S(1)}, bf16[128,512]{1,0:T(8,128)(2,1)S(1)}, u32[]{:S(2)}, u32[]{:S(2)}) collective-permute-start(bf16[128,512]{1,0:T(8,128)(2,1)S(1)} %pad_maximum_fusion.1), channel_id=1, source_target_pairs={{0,16},{1,17},{2,18},{3,19},{4,20},{5,21},{6,22},{7,23},{8,24},{9,... | collective-permute-start | bytes 393224 | tf_op jit(solution)/shard_map/ppermute | solution.py:233
  10.6 3.4 %pad_maximum_fusion = bf16[576,2048]{1,0:T(8,128)(2,1)} fusion(bf16[192,2048]{1,0:T(8,128)(2,1)} %bitcast.14, bf16[192,2048]{1,0:T(8,128)(2,1)} %bitcast.18, bf16[192,2048]{1,0:T(8,128)(2,1)} %bitcast.21), kind=kLoop, calls=%fused_computation | loop fusion | flops 7077888 | bytes 4718592 | tf_op jit(solution)/shard_map/concatenate | solution.py:469
  14.6 4.0 %collective-permute-done.3 = bf16[128,512]{1,0:T(8,128)(2,1)S(1)} collective-permute-done((bf16[128,512]{1,0:T(8,128)(2,1)S(1)}, bf16[128,512]{1,0:T(8,128)(2,1)S(1)}, u32[]{:S(2)}, u32[]{:S(2)}) %collective-permute-start.3) | collective-permute-done | bytes 131104 | tf_op jit(solution)/shard_map/ppermute | solution.py:233
  18.7 3.3 %collective-permute-done.1.refs_6_ = bf16[192,2048]{1,0:T(8,128)(2,1)S(1)} collective-permute-done((bf16[192,2048]{1,0:T(8,128)(2,1)}, bf16[192,2048]{1,0:T(8,128)(2,1)S(1)}, u32[]{:S(2)}, u32[]{:S(2)}) %collective-permute-start.1) | collective-permute-done | bytes 786464 | tf_op jit(solution)/shard_map/ppermute | solution.py:233
  21.9 1.6 %collective-permute-start.16 = (bf16[576,2048]{1,0:T(8,128)(2,1)}, bf16[576,2048]{1,0:T(8,128)(2,1)S(1)}, u32[]{:S(2)}, u32[]{:S(2)}) collective-permute-start(bf16[576,2048]{1,0:T(8,128)(2,1)} %pad_maximum_fusion), channel_id=1, source_target_pairs={{1,9},{3,11},{5,13},{7,15},{8,0},{10,2},{12,4},{14,6},{17,25},{19,... | collective-permute-start | bytes 7077896 | tf_op jit(solution)/shard_map/ppermute | solution.py:233
  23.7 1.4 %collective-permute-start.5 = (bf16[512,512]{1,0:T(8,128)(2,1)S(1)}, bf16[512,512]{1,0:T(8,128)(2,1)S(1)}, u32[]{:S(2)}, u32[]{:S(2)}) collective-permute-start(bf16[512,512]{1,0:T(8,128)(2,1)S(1)} %constant_dynamic-update-slice_fusion.refs_0_), channel_id=1, source_target_pairs={{0,4},{1,5},{2,6},{3,7},{4,0},{5,1},{6,2},{7,3},{8,12},{9,13},{10,... | collective-permute-start | bytes 1572872 | tf_op jit(solution)/shard_map/ppermute | solution.py:233
  25.0 11.4 %collective-permute-done.5.refs_1_ = bf16[512,512]{1,0:T(8,128)(2,1)S(1)} collective-permute-done((bf16[512,512]{1,0:T(8,128)(2,1)S(1)}, bf16[512,512]{1,0:T(8,128)(2,1)S(1)}, u32[]{:S(2)}, u32[]{:S(2)}) %collective-permute-start.5) | collective-permute-done | bytes 524320 | tf_op jit(solution)/shard_map/ppermute | solution.py:233
  37.8 7.5 %attend.1 = (f32[128,2048]{1,0:T(8,128)}, bf16[32,2048]{1,0:T(8,128)(2,1)}, bf16[32,2048]{1,0:T(8,128)(2,1)}, bf16[32,2048]{1,0:T(8,128)(2,1)}, bf16[32,2048]{1,...) custom-call(s32[4]{0:T(128)} %pad_add_fusion.where_ref, ...), custom_call_target="tpu_custom_call" | custom-call | flops 1073741824 | bytes 2097152 | tf_op jit(solution)/shard_map/attend/pallas_call | solution.py:481
  45.3 2.7 %collective-permute-start.10 = (bf16[32,2048]{1,0:T(8,128)(2,1)}, bf16[32,2048]{1,0:T(8,128)(2,1)S(1)}, u32[]{:S(2)}, u32[]{:S(2)}) collective-permute-start(bf16[32,2048]{1,0:T(8,128)(2,1)} %get-tuple-element.56), channel_id=1, source_target_pairs={{0,16},{1,17},{2,18},{3,19},{4,20},{5,21},{6,22},{7,23},{8,24},{9,... | collective-permute-start | bytes 393224 | tf_op jit(solution)/shard_map/ppermute | solution.py:233
  48.8 3.7 %collective-permute-done.16.refs_4_ = bf16[576,2048]{1,0:T(8,128)(2,1)S(1)} collective-permute-done((bf16[576,2048]{1,0:T(8,128)(2,1)}, bf16[576,2048]{1,0:T(8,128)(2,1)S(1)}, u32[]{:S(2)}, u32[]{:S(2)}) %collective-permute-start.16) | collective-permute-done | bytes 2359328 | tf_op jit(solution)/shard_map/ppermute | solution.py:233
  54.7 2.7 %collective-permute-done.10 = bf16[32,2048]{1,0:T(8,128)(2,1)S(1)} collective-permute-done((bf16[32,2048]{1,0:T(8,128)(2,1)}, bf16[32,2048]{1,0:T(8,128)(2,1)S(1)}, u32[]{:S(2)}, u32[]{:S(2)}) %collective-permute-start.10) | collective-permute-done | bytes 131104 | tf_op jit(solution)/shard_map/ppermute | solution.py:233
  57.5 5.7 %collective-permute-start.12 = (bf16[32,2048]{1,0:T(8,128)(2,1)}, bf16[32,2048]{1,0:T(8,128)(2,1)S(1)}, u32[]{:S(2)}, u32[]{:S(2)}) collective-permute-start(bf16[32,2048]{1,0:T(8,128)(2,1)} %get-tuple-element.63), channel_id=1, source_target_pairs={{0,18},{1,19},{2,16},{3,17},{4,22},{5,23},{6,20},{7,21},{8,26},{9,... | collective-permute-start | bytes 393224 | tf_op jit(solution)/shard_map/ppermute | solution.py:233
  63.2 3.3 %collective-permute-start.13 = (bf16[32,2048]{1,0:T(8,128)(2,1)}, bf16[32,2048]{1,0:T(8,128)(2,1)S(1)}, u32[]{:S(2)}, u32[]{:S(2)}) collective-permute-start(bf16[32,2048]{1,0:T(8,128)(2,1)} %get-tuple-element.64), channel_id=1, source_target_pairs={{0,26},{1,27},{2,24},{3,25},{4,30},{5,31},{6,28},{7,29},{8,18},{9,... | collective-permute-start | bytes 393224 | tf_op jit(solution)/shard_map/ppermute | solution.py:233
  67.0 3.1 %collective-permute-done.12 = bf16[32,2048]{1,0:T(8,128)(2,1)S(1)} collective-permute-done((bf16[32,2048]{1,0:T(8,128)(2,1)}, bf16[32,2048]{1,0:T(8,128)(2,1)S(1)}, u32[]{:S(2)}, u32[]{:S(2)}) %collective-permute-start.12) | collective-permute-done | bytes 131104 | tf_op jit(solution)/shard_map/ppermute | solution.py:233
  70.3 3.9 %collective-permute-done.13 = bf16[32,2048]{1,0:T(8,128)(2,1)S(1)} collective-permute-done((bf16[32,2048]{1,0:T(8,128)(2,1)}, bf16[32,2048]{1,0:T(8,128)(2,1)S(1)}, u32[]{:S(2)}, u32[]{:S(2)}) %collective-permute-start.13) | collective-permute-done | bytes 131104 | tf_op jit(solution)/shard_map/ppermute | solution.py:233
  74.3 1.8 %collective-permute-done.8 = bf16[32,2048]{1,0:T(8,128)(2,1)S(1)} collective-permute-done((bf16[32,2048]{1,0:T(8,128)(2,1)}, bf16[32,2048]{1,0:T(8,128)(2,1)S(1)}, u32[]{:S(2)}, u32[]{:S(2)}) %collective-permute-start.8) | collective-permute-done | bytes 131104 | tf_op jit(solution)/shard_map/ppermute | solution.py:233
  76.1 2.7 %collective-permute-done.9 = bf16[32,2048]{1,0:T(8,128)(2,1)S(1)} collective-permute-done((bf16[32,2048]{1,0:T(8,128)(2,1)}, bf16[32,2048]{1,0:T(8,128)(2,1)S(1)}, u32[]{:S(2)}, u32[]{:S(2)}) %collective-permute-start.9) | collective-permute-done | bytes 131104 | tf_op jit(solution)/shard_map/ppermute | solution.py:233
  78.9 1.9 %collective-permute-done.14.refs_2_ = bf16[128,2048]{1,0:T(8,128)(2,1)S(1)} collective-permute-done((bf16[128,2048]{1,0:T(8,128)(2,1)S(1)}, bf16[128,2048]{1,0:T(8,128)(2,1)S(1)}, u32[]{:S(2)}, u32[]{:S(2)}) %collective-permute-start.14) | collective-permute-done | bytes 524320 | tf_op jit(solution)/shard_map/ppermute | solution.py:233
  80.8 2.9 %experts_first.1.refs_8_ = f32[512,2048]{1,0:T(8,128)S(1)} custom-call(s32[4]{0:T(128)S(1)} %copy-done.4, bf16[128,2048]{1,0:T(8,128)(2,1)S(1)} %constant_dynamic-update-slice_fusion.4.refs_0_, bf16[128,2048]{1,0:T(8,128)(2,1)S(1)} %constant_dynamic-update-slice_fusion.8.refs_1_, bf16[128,2048]{1,0:T(8,128)(2,1)S(1)} %collective-permute-done.14.refs_2_, ...), custom_call_target="tpu_custom_call" | custom-call | flops 1207959552 | bytes 2359296 | tf_op jit(solution)/shard_map/experts_first/pallas_call | solution.py:526
  83.7 2.9 %experts_rest.1 = (f32[256,2048]{1,0:T(8,128)S(1)}, bf16[256,2048]{1,0:T(8,128)(2,1)S(1)}) custom-call(s32[4]{0:T(128)S(1)} %copy-done.4, bf16[128,2048]{1,0:T(8,128)(2,1)S(1)} %constant_dynamic-update-slice_fusion.4.refs_0_, bf16[128,2048]{1,0:T(8,128)(2,1)S(1)} %constant_dynamic-update-slice_fusion.8.refs_1_, ...), custom_call_target="tpu_custom_call" | custom-call | flops 1207959552 | bytes 2359296 | tf_op jit(solution)/shard_map/experts_rest/pallas_call | solution.py:526
  86.9 2.5 %collective-permute-done.18.other_from = bf16[256,2048]{1,0:T(8,128)(2,1)S(1)} collective-permute-done((bf16[256,2048]{1,0:T(8,128)(2,1)S(1)}, bf16[256,2048]{1,0:T(8,128)(2,1)S(1)}, u32[]{:S(2)}, u32[]{:S(2)}) %collective-permute-start.18) | collective-permute-done | bytes 1048608 | tf_op jit(solution)/shard_map/ppermute | solution.py:233
  91.2 2.2 %collective-permute-start.21 = (bf16[32,2048]{1,0:T(8,128)(2,1)S(1)}, bf16[32,2048]{1,0:T(8,128)(2,1)S(1)}, u32[]{:S(2)}, u32[]{:S(2)}) collective-permute-start(bf16[32,2048]{1,0:T(8,128)(2,1)S(1)} %get-tuple-element.76), channel_id=1, source_target_pairs={{0,10},{1,11},{2,8},{3,9},{4,14},{5,15},{6,12},{7,13},{8,2},{9,3},... | collective-permute-start | bytes 393224 | tf_op jit(solution)/shard_map/ppermute | solution.py:233
  93.4 2.9 %collective-permute-start.22 = (bf16[32,2048]{1,0:T(8,128)(2,1)S(1)}, bf16[32,2048]{1,0:T(8,128)(2,1)S(1)}, u32[]{:S(2)}, u32[]{:S(2)}) collective-permute-start(bf16[32,2048]{1,0:T(8,128)(2,1)S(1)} %get-tuple-element.77), channel_id=1, source_target_pairs={{0,16},{1,17},{2,18},{3,19},{4,20},{5,21},{6,22},{7,23},{8,24},{9,... | collective-permute-start | bytes 393224 | tf_op jit(solution)/shard_map/ppermute | solution.py:233
  96.9 1.4 %collective-permute-start.24 = (bf16[32,2048]{1,0:T(8,128)(2,1)S(1)}, bf16[32,2048]{1,0:T(8,128)(2,1)S(1)}, u32[]{:S(2)}, u32[]{:S(2)}) collective-permute-start(bf16[32,2048]{1,0:T(8,128)(2,1)S(1)} %get-tuple-element.79), channel_id=1, source_target_pairs={{0,24},{1,25},{2,26},{3,27},{4,28},{5,29},{6,30},{7,31},{8,16},{9,... | collective-permute-start | bytes 393224 | tf_op jit(solution)/shard_map/ppermute | solution.py:233
  99.1 1.4 %collective-permute-start.25 = (bf16[32,2048]{1,0:T(8,128)(2,1)S(1)}, bf16[32,2048]{1,0:T(8,128)(2,1)S(1)}, u32[]{:S(2)}, u32[]{:S(2)}) collective-permute-start(bf16[32,2048]{1,0:T(8,128)(2,1)S(1)} %get-tuple-element.80), channel_id=1, source_target_pairs={{0,26},{1,27},{2,24},{3,25},{4,30},{5,31},{6,28},{7,29},{8,18},{9,... | collective-permute-start | bytes 393224 | tf_op jit(solution)/shard_map/ppermute | solution.py:233
  101.5 9.8 %collective-permute-done.22.refs_4_ = bf16[32,2048]{1,0:T(8,128)(2,1)S(1)} collective-permute-done((bf16[32,2048]{1,0:T(8,128)(2,1)S(1)}, bf16[32,2048]{1,0:T(8,128)(2,1)S(1)}, u32[]{:S(2)}, u32[]{:S(2)}) %collective-permute-start.22) | collective-permute-done | bytes 131104 | tf_op jit(solution)/shard_map/ppermute | solution.py:233
  111.3 2.8 %collective-permute-done.23.refs_5_ = bf16[32,2048]{1,0:T(8,128)(2,1)S(1)} collective-permute-done((bf16[32,2048]{1,0:T(8,128)(2,1)S(1)}, bf16[32,2048]{1,0:T(8,128)(2,1)S(1)}, u32[]{:S(2)}, u32[]{:S(2)}) %collective-permute-start.23) | collective-permute-done | bytes 131104 | tf_op jit(solution)/shard_map/ppermute | solution.py:233
  114.1 2.8 %collective-permute-done.24.refs_6_ = bf16[32,2048]{1,0:T(8,128)(2,1)S(1)} collective-permute-done((bf16[32,2048]{1,0:T(8,128)(2,1)S(1)}, bf16[32,2048]{1,0:T(8,128)(2,1)S(1)}, u32[]{:S(2)}, u32[]{:S(2)}) %collective-permute-start.24) | collective-permute-done | bytes 131104 | tf_op jit(solution)/shard_map/ppermute | solution.py:233
  116.8 1.5 %collective-permute-done.25.refs_7_ = bf16[32,2048]{1,0:T(8,128)(2,1)S(1)} collective-permute-done((bf16[32,2048]{1,0:T(8,128)(2,1)S(1)}, bf16[32,2048]{1,0:T(8,128)(2,1)S(1)}, u32[]{:S(2)}, u32[]{:S(2)}) %collective-permute-start.25) | collective-permute-done | bytes 131104 | tf_op jit(solution)/shard_map/ppermute | solution.py:233
  118.3 1.8 %combine.1 = bf16[128,2048]{1,0:T(8,128)(2,1)} custom-call(s32[4]{0:T(128)S(1)} %copy-done.4, s32[1,128]{1,0:T(1,128)S(1)} %bitcast.24, f32[128,1]{1,0:T(8,128)S(1)} %copy.10.route_ref, f32[128,2048]{1,0:T(8,128)S(1)} %copy-done.3, bf16[32,2048]{1,0:T(8,128)(2,1)S(1)} %get-tuple-element.73.refs_0_, bf16[32,2048]{1,0:T(8,128)(2,1)S(1)} %collective-permute-done.19.refs_1_, ...), custom_call_target="tpu_custom_call" | custom-call | flops 134217728 | bytes 3145728 | tf_op jit(solution)/shard_map/combine/pallas_call | solution.py:571
  (59 shorter events, 13.1 us)
Async XLA Ops:
  0.0 18.7 %collective-permute-start = (bf16[192,2048]{1,0:T(8,128)(2,1)}, bf16[192,2048]{1,0:T(8,128)(2,1)S(1)}, u32[]{:S(2)}, u32[]{:S(2)}) collective-permute-start(bf16[192,2048]{1,0:T(8,128)(2,1)} %bitcast.20), channel_id=1, source_target_pairs={{0,5},{2,7},{4,1},{6,3},{9,12},{11,14},{13,8},{15,10},{16,21},{18,... | collective-permute-start | bytes 2359304 | tf_op jit(solution)/shard_map/ppermute | solution.py:233
  1.3 20.6 %collective-permute-start.1 = (bf16[192,2048]{1,0:T(8,128)(2,1)}, bf16[192,2048]{1,0:T(8,128)(2,1)S(1)}, u32[]{:S(2)}, u32[]{:S(2)}) collective-permute-start(bf16[192,2048]{1,0:T(8,128)(2,1)} %bitcast.17), channel_id=1, source_target_pairs={{0,5},{2,7},{4,1},{6,3},{9,12},{11,14},{13,8},{15,10},{16,21},{18,... | collective-permute-start | bytes 2359304 | tf_op jit(solution)/shard_map/ppermute | solution.py:233
  3.5 11.2 %collective-permute-start.2 = (bf16[128,512]{1,0:T(8,128)(2,1)S(1)}, bf16[128,512]{1,0:T(8,128)(2,1)S(1)}, u32[]{:S(2)}, u32[]{:S(2)}) collective-permute-start(bf16[128,512]{1,0:T(8,128)(2,1)S(1)} %pad_maximum_fusion.1), channel_id=1, source_target_pairs={{0,8},{1,9},{2,10},{3,11},{4,12},{5,13},{6,14},{7,15},{8,16},{9,17... | collective-permute-start | bytes 393224 | tf_op jit(solution)/shard_map/ppermute | solution.py:233
  8.6 10.1 %collective-permute-start.3 = (bf16[128,512]{1,0:T(8,128)(2,1)S(1)}, bf16[128,512]{1,0:T(8,128)(2,1)S(1)}, u32[]{:S(2)}, u32[]{:S(2)}) collective-permute-start(bf16[128,512]{1,0:T(8,128)(2,1)S(1)} %pad_maximum_fusion.1), channel_id=1, source_target_pairs={{0,16},{1,17},{2,18},{3,19},{4,20},{5,21},{6,22},{7,23},{8,24},{9,... | collective-permute-start | bytes 393224 | tf_op jit(solution)/shard_map/ppermute | solution.py:233
  9.9 8.8 %collective-permute-start.4 = (bf16[128,512]{1,0:T(8,128)(2,1)S(1)}, bf16[128,512]{1,0:T(8,128)(2,1)S(1)}, u32[]{:S(2)}, u32[]{:S(2)}) collective-permute-start(bf16[128,512]{1,0:T(8,128)(2,1)S(1)} %pad_maximum_fusion.1), channel_id=1, source_target_pairs={{0,24},{1,25},{2,26},{3,27},{4,28},{5,29},{6,30},{7,31}} | collective-permute-start | bytes 393224 | tf_op jit(solution)/shard_map/ppermute | solution.py:233
  10.6 25.8 %copy-start = (bf16[1,1,192,2048]{3,2,1,0:T(8,128)(2,1)S(1)}, bf16[1,1,192,2048]{3,2,1,0:T(8,128)(2,1)}, u32[]{:S(2)}) copy-start(bf16[1,1,192,2048]{3,2,1,0:T(8,128)(2,1)} %param.17) | copy-start | bytes 2359300
  21.9 30.6 %collective-permute-start.16 = (bf16[576,2048]{1,0:T(8,128)(2,1)}, bf16[576,2048]{1,0:T(8,128)(2,1)S(1)}, u32[]{:S(2)}, u32[]{:S(2)}) collective-permute-start(bf16[576,2048]{1,0:T(8,128)(2,1)} %pad_maximum_fusion), channel_id=1, source_target_pairs={{1,9},{3,11},{5,13},{7,15},{8,0},{10,2},{12,4},{14,6},{17,25},{19,... | collective-permute-start | bytes 7077896 | tf_op jit(solution)/shard_map/ppermute | solution.py:233
  23.6 14.1 %copy-start.6 = (bf16[512,512]{1,0:T(8,128)(2,1)}, bf16[512,512]{1,0:T(8,128)(2,1)S(1)}, u32[]{:S(2)}) copy-start(bf16[512,512]{1,0:T(8,128)(2,1)S(1)} %constant_dynamic-update-slice_fusion.refs_0_) | copy-start | bytes 1572868
  23.7 12.8 %collective-permute-start.5 = (bf16[512,512]{1,0:T(8,128)(2,1)S(1)}, bf16[512,512]{1,0:T(8,128)(2,1)S(1)}, u32[]{:S(2)}, u32[]{:S(2)}) collective-permute-start(bf16[512,512]{1,0:T(8,128)(2,1)S(1)} %constant_dynamic-update-slice_fusion.refs_0_), channel_id=1, source_target_pairs={{0,4},{1,5},{2,6},{3,7},{4,0},{5,1},{6,2},{7,3},{8,12},{9,13},{10,... | collective-permute-start | bytes 1572872 | tf_op jit(solution)/shard_map/ppermute | solution.py:233
  36.4 21.0 %collective-permute-start.6 = (bf16[192,2048]{1,0:T(8,128)(2,1)S(1)}, bf16[192,2048]{1,0:T(8,128)(2,1)S(1)}, u32[]{:S(2)}, u32[]{:S(2)}) collective-permute-start(bf16[192,2048]{1,0:T(8,128)(2,1)S(1)} %bitcast.15), channel_id=1, source_target_pairs={{0,5},{2,7},{4,1},{6,3},{9,12},{11,14},{13,8},{15,10},{16,21},{18,... | collective-permute-start | bytes 2359304 | tf_op jit(solution)/shard_map/ppermute | solution.py:233
  37.8 43.0 %copy-start.4 = (s32[4]{0:T(128)S(1)}, s32[4]{0:T(128)}, u32[]{:S(2)}) copy-start(s32[4]{0:T(128)} %pad_add_fusion.where_ref) | copy-start | bytes 52
  45.3 12.1 %collective-permute-start.10 = (bf16[32,2048]{1,0:T(8,128)(2,1)}, bf16[32,2048]{1,0:T(8,128)(2,1)S(1)}, u32[]{:S(2)}, u32[]{:S(2)}) collective-permute-start(bf16[32,2048]{1,0:T(8,128)(2,1)} %get-tuple-element.56), channel_id=1, source_target_pairs={{0,16},{1,17},{2,18},{3,19},{4,20},{5,21},{6,22},{7,23},{8,24},{9,... | collective-permute-start | bytes 393224 | tf_op jit(solution)/shard_map/ppermute | solution.py:233
  48.0 15.2 %collective-permute-start.11 = (bf16[32,2048]{1,0:T(8,128)(2,1)}, bf16[32,2048]{1,0:T(8,128)(2,1)S(1)}, u32[]{:S(2)}, u32[]{:S(2)}) collective-permute-start(bf16[32,2048]{1,0:T(8,128)(2,1)} %get-tuple-element.58), channel_id=1, source_target_pairs={{0,24},{1,25},{2,26},{3,27},{4,28},{5,29},{6,30},{7,31},{8,16},{9,... | collective-permute-start | bytes 393224 | tf_op jit(solution)/shard_map/ppermute | solution.py:233
  52.5 31.2 %collective-permute-start.17 = (bf16[576,2048]{1,0:T(8,128)(2,1)S(1)}, bf16[576,2048]{1,0:T(8,128)(2,1)S(1)}, u32[]{:S(2)}, u32[]{:S(2)}) collective-permute-start(bf16[576,2048]{1,0:T(8,128)(2,1)S(1)} %collective-permute-done.16.refs_4_), channel_id=1, source_target_pairs={{0,5},{2,7},{4,1},{6,3},{9,12},{11,14},{13,8},{15,10},{16,21},{18,... | collective-permute-start | bytes 7077896 | tf_op jit(solution)/shard_map/ppermute | solution.py:233
  57.5 12.7 %collective-permute-start.12 = (bf16[32,2048]{1,0:T(8,128)(2,1)}, bf16[32,2048]{1,0:T(8,128)(2,1)S(1)}, u32[]{:S(2)}, u32[]{:S(2)}) collective-permute-start(bf16[32,2048]{1,0:T(8,128)(2,1)} %get-tuple-element.63), channel_id=1, source_target_pairs={{0,18},{1,19},{2,16},{3,17},{4,22},{5,23},{6,20},{7,21},{8,26},{9,... | collective-permute-start | bytes 393224 | tf_op jit(solution)/shard_map/ppermute | solution.py:233
  63.2 11.0 %collective-permute-start.13 = (bf16[32,2048]{1,0:T(8,128)(2,1)}, bf16[32,2048]{1,0:T(8,128)(2,1)S(1)}, u32[]{:S(2)}, u32[]{:S(2)}) collective-permute-start(bf16[32,2048]{1,0:T(8,128)(2,1)} %get-tuple-element.64), channel_id=1, source_target_pairs={{0,26},{1,27},{2,24},{3,25},{4,30},{5,31},{6,28},{7,29},{8,18},{9,... | collective-permute-start | bytes 393224 | tf_op jit(solution)/shard_map/ppermute | solution.py:233
  66.5 7.8 %collective-permute-start.7 = (bf16[32,2048]{1,0:T(8,128)(2,1)}, bf16[32,2048]{1,0:T(8,128)(2,1)S(1)}, u32[]{:S(2)}, u32[]{:S(2)}) collective-permute-start(bf16[32,2048]{1,0:T(8,128)(2,1)} %get-tuple-element.60), channel_id=1, source_target_pairs={{0,8},{1,9},{2,10},{3,11},{4,12},{5,13},{6,14},{7,15},{8,0},{9,1},... | collective-permute-start | bytes 393224 | tf_op jit(solution)/shard_map/ppermute | solution.py:233
  66.5 9.6 %collective-permute-start.8 = (bf16[32,2048]{1,0:T(8,128)(2,1)}, bf16[32,2048]{1,0:T(8,128)(2,1)S(1)}, u32[]{:S(2)}, u32[]{:S(2)}) collective-permute-start(bf16[32,2048]{1,0:T(8,128)(2,1)} %get-tuple-element.61), channel_id=1, source_target_pairs={{0,10},{1,11},{2,8},{3,9},{4,14},{5,15},{6,12},{7,13},{8,2},{9,3},... | collective-permute-start | bytes 393224 | tf_op jit(solution)/shard_map/ppermute | solution.py:233
  70.1 8.6 %collective-permute-start.9 = (bf16[32,2048]{1,0:T(8,128)(2,1)}, bf16[32,2048]{1,0:T(8,128)(2,1)S(1)}, u32[]{:S(2)}, u32[]{:S(2)}) collective-permute-start(bf16[32,2048]{1,0:T(8,128)(2,1)} %get-tuple-element.62), channel_id=1, source_target_pairs={{0,2},{1,3},{2,0},{3,1},{4,6},{5,7},{6,4},{7,5},{8,10},{9,11},{10,... | collective-permute-start | bytes 393224 | tf_op jit(solution)/shard_map/ppermute | solution.py:233
  74.2 4.7 %collective-permute-start.15 = (bf16[128,2048]{1,0:T(8,128)(2,1)S(1)}, bf16[128,2048]{1,0:T(8,128)(2,1)S(1)}, u32[]{:S(2)}, u32[]{:S(2)}) collective-permute-start(bf16[128,2048]{1,0:T(8,128)(2,1)S(1)} %constant_dynamic-update-slice_fusion.8.refs_1_), channel_id=1, source_target_pairs={{0,1},{1,0},{2,3},{3,2},{4,5},{5,4},{6,7},{7,6},{8,9},{9,8},{10,11... | collective-permute-start | bytes 1572872 | tf_op jit(solution)/shard_map/ppermute | solution.py:233
  78.8 2.0 %collective-permute-start.14 = (bf16[128,2048]{1,0:T(8,128)(2,1)S(1)}, bf16[128,2048]{1,0:T(8,128)(2,1)S(1)}, u32[]{:S(2)}, u32[]{:S(2)}) collective-permute-start(bf16[128,2048]{1,0:T(8,128)(2,1)S(1)} %constant_dynamic-update-slice_fusion.4.refs_0_), channel_id=1, source_target_pairs={{0,1},{1,0},{2,3},{3,2},{4,5},{5,4},{6,7},{7,6},{8,9},{9,8},{10,11... | collective-permute-start | bytes 1572872 | tf_op jit(solution)/shard_map/ppermute | solution.py:233
  86.7 13.8 %copy-start.7 = (f32[1,128,1]{1,2,0:T(1,128)S(1)}, f32[1,128,1]{1,2,0:T(1,128)}, u32[]{:S(2)}) copy-start(f32[1,128,1]{1,2,0:T(1,128)} %param.14) | copy-start | bytes 1540
  86.7 31.6 %copy-start.3 = (f32[128,2048]{1,0:T(8,128)S(1)}, f32[128,2048]{1,0:T(8,128)}, u32[]{:S(2)}) copy-start(f32[128,2048]{1,0:T(8,128)} %get-tuple-element.50.summed_ref) | copy-start | bytes 3145732
  86.7 31.6 %copy-start.5 = (s32[1,128,1]{1,2,0:T(1,128)S(1)}, s32[1,128,1]{1,2,0:T(1,128)}, u32[]{:S(2)}) copy-start(s32[1,128,1]{1,2,0:T(1,128)} %param.13) | copy-start | bytes 1540
  86.7 2.7 %collective-permute-start.18 = (bf16[256,2048]{1,0:T(8,128)(2,1)S(1)}, bf16[256,2048]{1,0:T(8,128)(2,1)S(1)}, u32[]{:S(2)}, u32[]{:S(2)}) collective-permute-start(bf16[256,2048]{1,0:T(8,128)(2,1)S(1)} %get-tuple-element.72), channel_id=1, source_target_pairs={{0,1},{1,0},{2,3},{3,2},{4,5},{5,4},{6,7},{7,6},{8,9},{9,8},{10,11... | collective-permute-start | bytes 3145736 | tf_op jit(solution)/shard_map/ppermute | solution.py:233
  89.8 7.0 %collective-permute-start.19 = (bf16[32,2048]{1,0:T(8,128)(2,1)S(1)}, bf16[32,2048]{1,0:T(8,128)(2,1)S(1)}, u32[]{:S(2)}, u32[]{:S(2)}) collective-permute-start(bf16[32,2048]{1,0:T(8,128)(2,1)S(1)} %get-tuple-element.74), channel_id=1, source_target_pairs={{0,2},{1,3},{2,0},{3,1},{4,6},{5,7},{6,4},{7,5},{8,10},{9,11},{10,... | collective-permute-start | bytes 393224 | tf_op jit(solution)/shard_map/ppermute | solution.py:233
  91.0 8.1 %collective-permute-start.20 = (bf16[32,2048]{1,0:T(8,128)(2,1)S(1)}, bf16[32,2048]{1,0:T(8,128)(2,1)S(1)}, u32[]{:S(2)}, u32[]{:S(2)}) collective-permute-start(bf16[32,2048]{1,0:T(8,128)(2,1)S(1)} %get-tuple-element.75), channel_id=1, source_target_pairs={{0,8},{1,9},{2,10},{3,11},{4,12},{5,13},{6,14},{7,15},{8,0},{9,1},... | collective-permute-start | bytes 393224 | tf_op jit(solution)/shard_map/ppermute | solution.py:233
  91.2 10.3 %collective-permute-start.21 = (bf16[32,2048]{1,0:T(8,128)(2,1)S(1)}, bf16[32,2048]{1,0:T(8,128)(2,1)S(1)}, u32[]{:S(2)}, u32[]{:S(2)}) collective-permute-start(bf16[32,2048]{1,0:T(8,128)(2,1)S(1)} %get-tuple-element.76), channel_id=1, source_target_pairs={{0,10},{1,11},{2,8},{3,9},{4,14},{5,15},{6,12},{7,13},{8,2},{9,3},... | collective-permute-start | bytes 393224 | tf_op jit(solution)/shard_map/ppermute | solution.py:233
  93.4 17.9 %collective-permute-start.22 = (bf16[32,2048]{1,0:T(8,128)(2,1)S(1)}, bf16[32,2048]{1,0:T(8,128)(2,1)S(1)}, u32[]{:S(2)}, u32[]{:S(2)}) collective-permute-start(bf16[32,2048]{1,0:T(8,128)(2,1)S(1)} %get-tuple-element.77), channel_id=1, source_target_pairs={{0,16},{1,17},{2,18},{3,19},{4,20},{5,21},{6,22},{7,23},{8,24},{9,... | collective-permute-start | bytes 393224 | tf_op jit(solution)/shard_map/ppermute | solution.py:233
  96.3 17.8 %collective-permute-start.23 = (bf16[32,2048]{1,0:T(8,128)(2,1)S(1)}, bf16[32,2048]{1,0:T(8,128)(2,1)S(1)}, u32[]{:S(2)}, u32[]{:S(2)}) collective-permute-start(bf16[32,2048]{1,0:T(8,128)(2,1)S(1)} %get-tuple-element.78), channel_id=1, source_target_pairs={{0,18},{1,19},{2,16},{3,17},{4,22},{5,23},{6,20},{7,21},{8,26},{9,... | collective-permute-start | bytes 393224 | tf_op jit(solution)/shard_map/ppermute | solution.py:233
  96.9 19.9 %collective-permute-start.24 = (bf16[32,2048]{1,0:T(8,128)(2,1)S(1)}, bf16[32,2048]{1,0:T(8,128)(2,1)S(1)}, u32[]{:S(2)}, u32[]{:S(2)}) collective-permute-start(bf16[32,2048]{1,0:T(8,128)(2,1)S(1)} %get-tuple-element.79), channel_id=1, source_target_pairs={{0,24},{1,25},{2,26},{3,27},{4,28},{5,29},{6,30},{7,31},{8,16},{9,... | collective-permute-start | bytes 393224 | tf_op jit(solution)/shard_map/ppermute | solution.py:233
  99.1 19.2 %collective-permute-start.25 = (bf16[32,2048]{1,0:T(8,128)(2,1)S(1)}, bf16[32,2048]{1,0:T(8,128)(2,1)S(1)}, u32[]{:S(2)}, u32[]{:S(2)}) collective-permute-start(bf16[32,2048]{1,0:T(8,128)(2,1)S(1)} %get-tuple-element.80), channel_id=1, source_target_pairs={{0,26},{1,27},{2,24},{3,25},{4,30},{5,31},{6,28},{7,29},{8,18},{9,... | collective-permute-start | bytes 393224 | tf_op jit(solution)/shard_map/ppermute | solution.py:233
  (3 other events, 11.2 us)
